TPU v7x, 128 devices: a whole 4x4x4 slice. The times are simulated.
128 devices in a mesh: req: 16 (over x, z), exp: 8 (over y, core).
Axes of the slice: x: 4, y: 4, z: 4, core: 2. Of those that a mesh axis runs over, the one named last changes fastest.
Arguments:
- tokens: bfloat16 [16384, 2048], P('req'), may hold values from -40 to 40
- routes: int32 [16384, 2], P('req'), may hold values from 0 to 7, all different within a row; in each aligned block of 1024 rows (0 to 1023, 1024 to 2047, ...) at most 320 rows name the same one
- lengths: int32 [64], P('req'), may hold values from 1 to 256, 8192 in all
- cached_prefix_length: int32 [64], P('req'), may hold values from 0 to 64, as said below
- prefix_cache_row: int32 [64], replicated, may hold values from 0 to 15, as said below
- adapter_per_request: int32 [64], P('req'), may hold values from 0 to 63
- adapter_storage_slot: int32 [64], replicated, may hold values from 0 to 63, each once
- router_weight: bfloat16 [2048, 8], replicated, may hold values from -0.125 to 0.125
- key_value_weight: bfloat16 [2048, 4096], P('req', 'exp'), may hold values from -0.125 to 0.125
- expert_query_weight: bfloat16 [2048, 8, 2048], P('req', None, 'exp'), may hold values from -0.125 to 0.125
- expert_output_weight: bfloat16 [8, 2048, 2048], P(None, 'exp', 'req'), may hold values from -0.125 to 0.125
- adapter_down_maps: bfloat16 [64, 2048, 16], P('req'), may hold values from -0.125 to 0.125
- adapter_up_maps: bfloat16 [64, 16, 4096], P('req', None, 'exp'), may hold values from -1.5 to 1.5
- prefix_cache_store: bfloat16 [64, 64, 4096], P('req', None, 'exp'), may hold values from -6 to 6
Outputs:
- attention_out: bfloat16 [16384, 2048], P('req', 'exp')
Inputs may be any that keep to these rules, and one draw needn't show every extreme that they name: `routes`: in each aligned block of 1024 rows (one group) no expert is named by more than 320 rows, and one is named by exactly 320. The lengths sum to 8192 and some request has exactly 256. `cached_prefix_length`: exactly 32 requests have no cached prefix; some request has exactly 64. `prefix_cache_row`: request j of a group keeps its cache in slot j of its row; each row holds exactly one cache in each slot, and no row holds two caches of one group. `adapter_storage_slot`: each slot holds one adapter.
All inputs are finite; a program needn't handle non-finite values. No bound on the sum of `lengths` on one device may be relied on, other than what follows from the above.
Results may differ from a plain program's by a relative error of at most 0.017.
The roundings to bfloat16 on the way count: a program that leaves them out, or rounds other values in their place, can miss the bound.
Values may be sent and summed in bfloat16 or wider, within the bound.
No kernel may reach another device: no remote copies, remote signals or barrier semaphores. Data moves between devices by JAX's collectives and lax.ppermute only.
A program may use at most 128 MiB of HBM per device.

v0:
```python
import functools

import jax
import jax.numpy as jnp
from jax import lax
from jax.experimental import pallas as pl
from jax.experimental.pallas import tpu as pltpu
from jax.sharding import PartitionSpec as P

HD = 128
NE = 8
TOPK = 2
SIDE = 4
BF = jnp.bfloat16
F32 = jnp.float32
NEG = -1e30
adapter_scale = 0.5

ROW_KV = 512
SHARD_ROWS = 640
ROW_UP, ROW_DN, SENT_ROWS = 64, 128, 160
PLACES = []
for _piece, _off in ((0, 0), (1, -1), (2, 1)):
    for _i, _near in enumerate((0, -1, 1, 2)):
        PLACES.append((_piece, _i, _near, _off))
EARLY = list(PLACES)
LATE = [(0, 0, 0, 2), (0, 1, -1, 2), (1, 0, 1, 2), (1, 1, 2, 2)]


def torus(dx, dz):
    return [
        (i, ((i // SIDE + dx) % SIDE) * SIDE + (i % SIDE + dz) % SIDE) for i in range(SIDE * SIDE)
    ]


def send(value, along, step):
    return lax.ppermute(value, "req", torus(step, 0) if along == 0 else torus(0, step))


def first_step(value, along):
    return send(value, along, 1), send(value, along, -1)


def second_step(before, after, along):
    half = before.shape[0] // 2
    return send(before[:half], along, 1), send(after[half:], along, -1)


def source(group, half, first, second):
    x, z = group // SIDE, group % SIDE
    dx, dz = (first, second) if half == 0 else (second, first)
    return ((x + dx + SIDE) % SIDE) * SIDE + (z + dz + SIDE) % SIDE


def cost(us):
    return pl.CostEstimate(flops=int(us * 1.15e9), bytes_accessed=2**20, transcendentals=0)


ANY = pl.BlockSpec(memory_space=pl.ANY)
HBM = pl.BlockSpec(memory_space=pltpu.HBM)
WHOLE = pl.BlockSpec(memory_space=pltpu.VMEM)
SCALARS = pl.BlockSpec(memory_space=pltpu.SMEM)


def pack_kernel(index_ref, store_ref, up_ref, down_ref, out_ref):
    def one(i, carry):
        out_ref[i, 0:ROW_UP, :] = store_ref[index_ref[i]]
        out_ref[i, ROW_UP:ROW_DN, :] = up_ref[...]
        for side in range(2):
            out_ref[i, ROW_DN:SENT_ROWS, side * 256 : side * 256 + 256] = down_ref[
                side * 32 : side * 32 + 32, :
            ]
        return carry

    lax.fori_loop(0, out_ref.shape[0], one, 0)


def pack(index, store, up, down):
    return pl.pallas_call(
        pack_kernel,
        out_shape=jax.ShapeDtypeStruct((16, SENT_ROWS, 512), BF),
        in_specs=[SCALARS] + [WHOLE] * 3,
        out_specs=WHOLE,
        cost_estimate=cost(3),
        name="pack",
    )(index, store, up, down)


def pick_down_kernel(info_ref, recv_ref, out_ref, sem):
    for j in range(4):
        slot = info_ref[1 + j]
        owner, inner = slot // 4, slot % 4
        start = pl.multiple_of(ROW_DN + (inner % 2) * 16, 16)
        for side in range(2):

            @pl.when(inner // 2 == side)
            def _(side=side, j=j, owner=owner, start=start):
                pltpu.make_async_copy(
                    recv_ref.at[owner, pl.ds(start, 16), pl.ds(side * 256, 256)],
                    out_ref.at[j],
                    sem.at[j],
                ).start()

    for j in range(4):
        pltpu.make_async_copy(out_ref.at[j], out_ref.at[j], sem.at[j]).wait()


def pick_down(info, recv):
    return pl.pallas_call(
        pick_down_kernel,
        out_shape=jax.ShapeDtypeStruct((4, 16, 256), BF),
        in_specs=[SCALARS, ANY],
        out_specs=WHOLE,
        scratch_shapes=[pltpu.SemaphoreType.DMA((4,))],
        cost_estimate=cost(2),
        name="pick_down",
    )(info, recv)


def products(group, x_ref, routes_ref, pieces, shards, half):
    count = len(pieces) // 2
    x = jnp.concatenate(
        [
            x_ref[:, pl.ds(pl.multiple_of(source(group, half, first, second) * 128, 128), 128)]
            for _, _, first, second in shards
        ],
        axis=1,
    )

    def product(row):
        weight = jnp.concatenate(
            [
                pieces[half * count + piece][pl.ds(shard * SHARD_ROWS + row, 128), :]
                for piece, shard, _, _ in shards
            ],
            axis=0,
        )
        return jnp.dot(x, weight, preferred_element_type=F32)

    chosen = [jnp.zeros((256, 256), F32)] * TOPK
    for i in range(4):
        value = product(i * 128)
        for k in range(TOPK):
            chosen[k] = jnp.where(routes_ref[:, k : k + 1] == half * 4 + i, value, chosen[k])
    return chosen, product(ROW_KV)


def early_kernel(info_ref, gates_ref, routes_ref, x_hbm, *refs):
    pieces = refs[:6]
    wide_ref, sums_hbm, x, sums, sem = refs[6:]
    group = info_ref[0]
    loads = [
        pltpu.make_async_copy(x_hbm.at[pl.ds(j * 256, 256), :], x.at[j], sem.at[j])
        for j in range(4)
    ]
    for load in loads:
        load.start()
    for e in range(NE):
        wide_ref[e] = jnp.broadcast_to(gates_ref[:, e : e + 1], (1024, 128))

    def block(j, carry):
        pltpu.make_async_copy(x.at[j], x.at[j], sem.at[j]).wait()
        rows = routes_ref.at[pl.ds(pl.multiple_of(j * 256, 256), 256), :]
        first, base = products(group, x.at[j], rows, pieces, EARLY, 0)
        sums[j, 2] = base
        second, base = products(group, x.at[j], rows, pieces, EARLY, 1)
        sums[j, 3] = base
        for k in range(TOPK):
            sums[j, k] = first[k] + second[k]
        pltpu.make_async_copy(sums.at[j], sums_hbm.at[j], sem.at[4 + j]).start()
        return carry

    lax.fori_loop(0, 4, block, 0)
    for j in range(4):
        pltpu.make_async_copy(sums.at[j], sums_hbm.at[j], sem.at[4 + j]).wait()


def project_early(info, gates, routes, x, pieces):
    return pl.pallas_call(
        early_kernel,
        out_shape=(
            jax.ShapeDtypeStruct((NE, 1024, 128), F32),
            jax.ShapeDtypeStruct((4, 4, 256, 256), F32),
        ),
        in_specs=[SCALARS, WHOLE, WHOLE, HBM] + [WHOLE] * 6,
        out_specs=(WHOLE, HBM),
        scratch_shapes=[
            pltpu.VMEM((4, 256, 2048), BF),
            pltpu.VMEM((4, 4, 256, 256), F32),
            pltpu.SemaphoreType.DMA((8,)),
        ],
        compiler_params=pltpu.CompilerParams(vmem_limit_bytes=24 * 2**20),
        cost_estimate=cost(15),
        name="project_early",
    )(info, gates, routes, x, *pieces)


def attend_kernel(info_ref, routes_ref, down_ref, x_hbm, sums_hbm, recv_hbm, *refs):
    pieces = refs[:4]
    out_ref, x, sums, up, cache, sem = refs[4:]
    group = info_ref[0]
    for j in range(4):
        slot = info_ref[1 + j]
        start = pl.multiple_of(ROW_UP + (slot % 4) * 16, 16)
        pltpu.make_async_copy(x_hbm.at[pl.ds(j * 256, 256), :], x.at[j], sem.at[0, j]).start()
        pltpu.make_async_copy(sums_hbm.at[j], sums.at[j], sem.at[1, j]).start()
        pltpu.make_async_copy(
            recv_hbm.at[slot // 4, pl.ds(start, 16), :], up.at[j], sem.at[2, j]
        ).start()
        pltpu.make_async_copy(
            recv_hbm.at[info_ref[5 + j], pl.ds(0, 64), :], cache.at[j], sem.at[3, j]
        ).start()

    def attend(j, carry):
        for i, ref in enumerate((x, sums, up, cache)):
            pltpu.make_async_copy(ref.at[j], ref.at[j], sem.at[i, j]).wait()
        rows = pl.ds(pl.multiple_of(j * 256, 256), 256)
        routes = routes_ref.at[rows, :]
        for half in range(2):
            chosen, base = products(group, x.at[j], routes, pieces, LATE, half)
            sums[j, 2 + half] += base
            for k in range(TOPK):
                sums[j, k] += chosen[k]
        down = jnp.concatenate([down_ref[e, j] for e in range(NE)], axis=1)
        low = lax.dot_general(
            x[j], down, (((1,), (1,)), ((), ())), preferred_element_type=F32
        ).astype(BF)
        cached_length = info_ref[9 + j]
        place = lax.broadcasted_iota(jnp.int32, (256, 320), 1)
        query_at = lax.broadcasted_iota(jnp.int32, (256, 320), 0)
        allowed = (place < cached_length) | ((place >= 64) & (place - 64 <= query_at))
        for h in range(2):
            cols = slice(h * HD, (h + 1) * HD)
            extra = jnp.dot(low, up[j, :, h * 256 : h * 256 + 256], preferred_element_type=F32)
            fresh = (sums[j, 2 + h] + adapter_scale * extra).astype(BF)
            keys = jnp.concatenate(
                [cache[j, :, h * 256 : h * 256 + HD], fresh[:, 0:HD]], axis=0
            )
            values = jnp.concatenate(
                [cache[j, :, h * 256 + HD : h * 256 + 2 * HD], fresh[:, HD : 2 * HD]], axis=0
            )
            attended = []
            for k in range(TOPK):
                scores = lax.dot_general(
                    sums[j, k, :, cols].astype(BF),
                    keys,
                    (((1,), (1,)), ((), ())),
                    preferred_element_type=F32,
                ) * (HD**-0.5)
                scores = jnp.where(allowed, scores, NEG)
                weights = jnp.exp(scores - jnp.max(scores, axis=-1, keepdims=True))
                total = jnp.sum(weights, axis=-1, keepdims=True)
                probability = (weights * (1.0 / total)).astype(BF)
                attended.append(jnp.dot(probability, values, preferred_element_type=F32))
            for e in range(NE):
                chosen = jnp.where(
                    routes[:, 0:1] == e,
                    attended[0],
                    jnp.where(routes[:, 1:2] == e, attended[1], 0.0),
                )
                out_ref[e, rows, cols] = chosen.astype(BF)
        return carry

    lax.fori_loop(0, 4, attend, 0)


def attention(info, routes, down, x, sums, recv, pieces):
    return pl.pallas_call(
        attend_kernel,
        out_shape=jax.ShapeDtypeStruct((NE, 1024, 256), BF),
        in_specs=[SCALARS, WHOLE, WHOLE, HBM, HBM, ANY] + [WHOLE] * 4,
        out_specs=WHOLE,
        scratch_shapes=[
            pltpu.VMEM((4, 256, 2048), BF),
            pltpu.VMEM((4, 4, 256, 256), F32),
            pltpu.VMEM((4, 16, 512), BF),
            pltpu.VMEM((4, 64, 512), BF),
            pltpu.SemaphoreType.DMA((4, 4)),
        ],
        compiler_params=pltpu.CompilerParams(vmem_limit_bytes=24 * 2**20),
        cost_estimate=cost(22),
        name="attention",
    )(info, routes, down, x, sums, recv, *pieces)


def project_out_kernel(blocks, place_ref, wide_ref, lhs_ref, w_hbm, out_ref, w, sem):
    y, core = place_ref[0], place_ref[1]
    for b, (mine, ahead) in enumerate(blocks):
        side = core if mine else 1 - core
        start = ((y + ahead) % 4 * 2 + side) * 2
        pltpu.make_async_copy(w_hbm.at[pl.ds(start, 2)], w.at[b], sem.at[b]).start()

    def block(b, carry):
        pltpu.make_async_copy(w.at[b], w.at[b], sem.at[b]).wait()

        def tile(i, inner):
            rows = pl.ds(pl.multiple_of(i * 256, 256), 256)
            total = None
            for e in range(NE):
                weight = jnp.concatenate([w[b, 0, e], w[b, 1, e]], axis=1)
                value = jnp.dot(lhs_ref[e, rows, :], weight, preferred_element_type=F32)
                gate = wide_ref[e, rows, :]
                value = value * jnp.concatenate([gate, gate], axis=1)
                total = value if total is None else total + value
            out_ref[b, rows, :] = total.astype(BF)
            return inner

        return lax.fori_loop(0, 4, tile, carry)

    lax.fori_loop(0, len(blocks), block, 0)


def project_out(blocks, place, wide, lhs, weight):
    return pl.pallas_call(
        functools.partial(project_out_kernel, blocks),
        out_shape=jax.ShapeDtypeStruct((len(blocks), 1024, 256), BF),
        in_specs=[SCALARS, WHOLE, WHOLE, HBM],
        out_specs=WHOLE,
        scratch_shapes=[
            pltpu.VMEM((len(blocks), 2, NE, 256, 128), BF),
            pltpu.SemaphoreType.DMA((len(blocks),)),
        ],
        compiler_params=pltpu.CompilerParams(vmem_limit_bytes=16 * 2**20),
        cost_estimate=cost(2.5 * len(blocks)),
        name="project_out_" + str(len(blocks)),
    )(place, wide, lhs, weight)


def exchange(value, step):
    if step == 0:
        return lax.ppermute(value, "exp", [(i, i ^ 1) for i in range(8)])
    return lax.ppermute(value, "exp", [(i, (i + 2 * step) % 8) for i in range(8)])


def rounded_sum(*values):
    total = values[0].astype(F32)
    for value in values[1:]:
        total = total + value.astype(F32)
    return total.astype(BF)


def body(
    tokens,
    routes,
    lengths,
    cached_prefix_length,
    prefix_cache_row,
    adapter_per_request,
    adapter_storage_slot,
    router_weight,
    key_value_weight,
    expert_query_weight,
    expert_output_weight,
    adapter_down_maps,
    adapter_up_maps,
    prefix_cache_store,
):
    group = lax.axis_index("req")
    part = lax.axis_index("exp")
    out_weight = lax.all_gather(expert_output_weight, "req", axis=0, tiled=True).reshape(
        16, NE, 256, 128
    )
    rows_by_group = prefix_cache_row.reshape(16, 4)
    held = (rows_by_group == group).astype(jnp.int32)
    wanted_by = jnp.sum(held * jnp.arange(4, dtype=jnp.int32)[None, :], axis=1)
    down_rows = (
        lax.dynamic_slice_in_dim(adapter_down_maps, part * 256, 256, 1)
        .transpose(0, 2, 1)
        .reshape(64, 256)
    )
    outgoing = pack(wanted_by, prefix_cache_store, adapter_up_maps.reshape(64, 512), down_rows)

    query_rows = expert_query_weight.transpose(1, 0, 2).reshape(NE * 128, 256)
    own = [
        jnp.concatenate(
            [
                query_rows[half * 512 : half * 512 + 512],
                key_value_weight[:, half * 256 : half * 256 + 256],
            ],
            axis=0,
        )
        for half in range(2)
    ]
    *own, outgoing = lax.optimization_barrier((*own, outgoing))
    received = lax.all_to_all(outgoing, "req", 0, 0, tiled=True)
    near = []
    for half in range(2):
        before, after = first_step(own[half], half)
        far = second_step(before, after, half)
        near.append(jnp.concatenate([own[half], before, after, *far], axis=0))

    adapter_hot = (
        adapter_per_request[:, None]
        == jnp.arange(adapter_storage_slot.shape[0], dtype=jnp.int32)[None, :]
    ).astype(jnp.int32)
    slots = jnp.sum(adapter_hot * adapter_storage_slot[None, :], axis=1)
    own_rows = lax.dynamic_slice_in_dim(prefix_cache_row, group * 4, 4, 0)
    info = jnp.concatenate([group[None].astype(jnp.int32), slots, own_rows, cached_prefix_length])

    logits = jnp.dot(tokens, router_weight, preferred_element_type=F32)
    expert = jnp.arange(NE, dtype=jnp.int32)
    route_hot = (routes[:, :, None] == expert[None, None, :]).astype(F32)
    chosen = jnp.sum(route_hot * logits[:, None, :], axis=-1)
    gate_values = jax.nn.sigmoid(chosen - chosen[:, ::-1])
    live = (jnp.arange(256, dtype=jnp.int32)[None, :] < lengths[:, None]).reshape(1024, 1)
    gates = jnp.sum(route_hot * gate_values[:, :, None], axis=1) * live.astype(F32)
    wide = jnp.broadcast_to(gates.T[:, :, None], (NE, 1024, 128))

    beside = [*first_step(near[0], 1), *first_step(near[1], 0)]
    down_part = pick_down(info, received)
    down = lax.all_to_all(
        jnp.broadcast_to(down_part[None], (NE, 4, 16, 256)), "exp", 0, 0, tiled=True
    )
    *beside, down = lax.optimization_barrier((*beside, down))
    late = [*second_step(*beside[:2], 1), *second_step(*beside[2:], 0)]
    wide, sums = project_early(
        info, gates, routes, tokens, [near[0], *beside[:2], near[1], *beside[2:]]
    )
    lhs = attention(info, routes, down, tokens, sums, received, late)

    place = jnp.stack([part // 2, part % 2]).astype(jnp.int32)
    far = project_out(((False, 2), (True, 2)), place, wide, lhs, out_weight)
    far_swapped = exchange(far[0], 0)
    place = lax.optimization_barrier((place, far))[0]
    theirs = project_out(((False, 1), (False, 3), (False, 0)), place, wide, lhs, out_weight)
    swapped = exchange(theirs, 0)
    both_far = rounded_sum(far[1], far_swapped)
    low = exchange(both_far[:512], 1)
    high = exchange(both_far[512:], -1)
    place = lax.optimization_barrier((place, theirs, both_far))[0]
    mine = project_out(((True, 1), (True, 3)), place, wide, lhs, out_weight)
    ahead = jnp.concatenate(
        [rounded_sum(mine[0, :512], swapped[0, :512], low), rounded_sum(mine[0, 512:], swapped[0, 512:])],
        axis=0,
    )
    behind = jnp.concatenate(
        [rounded_sum(mine[1, :512], swapped[1, :512]), rounded_sum(mine[1, 512:], swapped[1, 512:], high)],
        axis=0,
    )
    from_behind, from_ahead = exchange(ahead, 1), exchange(behind, -1)
    place = lax.optimization_barrier((place, ahead, behind))[0]
    own_block = project_out(((True, 0),), place, wide, lhs, out_weight)
    return rounded_sum(own_block[0], swapped[2], from_behind, from_ahead)


def solution(mesh):
    return jax.shard_map(
        body,
        mesh=mesh,
        in_specs=(
            P("req", None),
            P("req", None),
            P("req"),
            P("req"),
            P(),
            P("req"),
            P(),
            P(),
            P("req", "exp"),
            P("req", None, "exp"),
            P(None, "exp", "req"),
            P("req", None, None),
            P("req", None, "exp"),
            P("req", None, "exp"),
        ),
        out_specs=P("req", "exp"),
        check_vma=False,
    )
```

profile of v0, /device:TPU:6, one launch (start us, length us, event | category | flops | bytes accessed | tf_op | source)
XLA Modules:
  0.0 240.6 jit_solution(1811971397149792736)
XLA Ops:
  6.5 0.7 all-gather.2.cloned.1.call-update
  7.3 1.4 fusion.8
  10.1 0.9 pad_maximum_fusion.2
  11.0 2.7 %pack.1 = bf16[16,160,512]{2,1,0:T(8,128)(2,1)} custom-call(s32[16]{0:T(128)} %select_reduce_fusion.2.index_ref, bf16[4,64,512]{2,1,0:T(8,128)(2,1)} %store_ref.1, bf16[64,512]{1,0:T(8,128)(2,1)} %bitcast.50, bf16[64,256]{1,0:T(8,128)(2,1)} %bitcast.48), custom_call_target="tpu_custom_call" | custom-call | flops 3449999872 | bytes 1048576 | tf_op jit(solution)/shard_map/pack/pallas_call | solution.py:79
  14.1 1.6 collective-permute-start.1
  15.7 1.9 collective-permute-start.6
  17.7 2.1 collective-permute-start.7
  19.8 6.3 %all-to-all-start = ((bf16[16,160,512]{2,1,0:T(8,128)(2,1)}), bf16[16,160,512]{2,1,0:T(8,128)(2,1)S(1)}, u32[]{:S(2)}, u32[]{:S(2)}) async-start(bf16[16,160,512]{2,1,0:T(8,128)(2,1)} %pack.1), calls=%async_computation | async-start | bytes 5242880 | tf_op jit(solution)/shard_map/all_to_all | solution.py:385
  26.4 3.4 %fusion.10 = f32[1024,8]{0,1:T(8,128)S(1)} fusion(bf16[1024,2048]{1,0:T(8,128)(2,1)} %x_hbm.3, bf16[2048,8]{0,1:T(8,128)(2,1)S(1)} %copy-done.12), kind=kOutput, calls=%fused_computation.46 | convolution fusion | flops 33554432 | bytes 4259840 | tf_op jit(solution)/shard_map/dot_general | solution.py:400
  30.0 1.8 constant_dynamic-update-slice_fusion.4
  31.8 1.8 constant_dynamic-update-slice_fusion.9
  33.5 0.9 slice.110
  34.6 0.9 slice.111
  35.6 2.0 collective-permute-start.3
  37.6 0.9 slice.112
  38.5 1.6 collective-permute-start.8
  40.1 0.9 slice.113
  41.0 1.8 collective-permute-start.9
  42.8 1.7 constant_dynamic-update-slice_fusion.3
  44.5 1.7 constant_dynamic-update-slice_fusion.2
  46.2 1.7 constant_dynamic-update-slice_fusion.8
  48.0 1.8 constant_dynamic-update-slice_fusion.7
  49.7 14.9 %collective-permute-done.2 = bf16[320,256]{1,0:T(8,128)(2,1)S(1)} collective-permute-done((bf16[320,256]{1,0:T(8,128)(2,1)S(1)}, bf16[320,256]{1,0:T(8,128)(2,1)S(1)}, u32[]{:S(2)}, u32[]{:S(2)}) %collective-permute-start.2) | collective-permute-done | bytes 163872 | tf_op jit(solution)/shard_map/ppermute | solution.py:37
  64.7 0.7 constant_dynamic-update-slice_fusion.1
  65.7 0.7 constant_dynamic-update-slice_fusion.refs_0_
  66.4 3.4 %collective-permute-start.4 = (bf16[2560,256]{1,0:T(8,128)(2,1)}, bf16[2560,256]{1,0:T(8,128)(2,1)}, u32[]{:S(2)}, u32[]{:S(2)}) collective-permute-start(bf16[2560,256]{1,0:T(8,128)(2,1)} %constant_dynamic-update-slice_fusion.refs_0_), channel_id=1, source_target_pairs={{0,8},{8,16},{16,24},{24,0},{32,40},{40,48},{48,56},{56,32},{64,72... | collective-permute-start | bytes 3932168 | tf_op jit(solution)/shard_map/ppermute | solution.py:37
  69.7 0.7 constant_dynamic-update-slice_fusion.6
  70.4 0.7 constant_dynamic-update-slice_fusion.5.refs_3_
  71.1 3.4 %collective-permute-start.10 = (bf16[2560,256]{1,0:T(8,128)(2,1)}, bf16[2560,256]{1,0:T(8,128)(2,1)}, u32[]{:S(2)}, u32[]{:S(2)}) collective-permute-start(bf16[2560,256]{1,0:T(8,128)(2,1)} %constant_dynamic-update-slice_fusion.5.refs_3_), channel_id=1, source_target_pairs={{0,32},{8,40},{16,48},{24,56},{32,64},{40,72},{48,80},{56,88},{64,... | collective-permute-start | bytes 3932168 | tf_op jit(solution)/shard_map/ppermute | solution.py:37
  74.6 1.0 copy.38
  76.6 1.5 copy-done.7
  78.1 2.1 pick_down.1
  80.2 1.5 broadcast_in_dim.5
  81.7 4.7 %all-to-all-start.1 = ((bf16[8,4,16,256]{3,2,1,0:T(8,128)(2,1)}), bf16[8,4,16,256]{3,2,1,0:T(8,128)(2,1)S(1)}, u32[]{:S(2)}, u32[]{:S(2)}) async-start(bf16[8,4,16,256]{3,2,1,0:T(8,128)(2,1)} %broadcast_in_dim.5), calls=%async_computation.1 | async-start | bytes 524288 | tf_op jit(solution)/shard_map/all_to_all | solution.py:411
  86.4 1.3 broadcast_multiply_fusion.gates_ref
  87.6 33.1 %collective-permute-done.4.refs_1_ = bf16[2560,256]{1,0:T(8,128)(2,1)} collective-permute-done((bf16[2560,256]{1,0:T(8,128)(2,1)}, bf16[2560,256]{1,0:T(8,128)(2,1)}, u32[]{:S(2)}, u32[]{:S(2)}) %collective-permute-start.4) | collective-permute-done | bytes 1310752 | tf_op jit(solution)/shard_map/ppermute | solution.py:37
  120.7 2.7 %collective-permute-done.5.refs_2_ = bf16[2560,256]{1,0:T(8,128)(2,1)} collective-permute-done((bf16[2560,256]{1,0:T(8,128)(2,1)}, bf16[2560,256]{1,0:T(8,128)(2,1)}, u32[]{:S(2)}, u32[]{:S(2)}) %collective-permute-start.5) | collective-permute-done | bytes 1310752 | tf_op jit(solution)/shard_map/ppermute | solution.py:37
  123.4 6.8 %collective-permute-done.10.refs_4_ = bf16[2560,256]{1,0:T(8,128)(2,1)} collective-permute-done((bf16[2560,256]{1,0:T(8,128)(2,1)}, bf16[2560,256]{1,0:T(8,128)(2,1)}, u32[]{:S(2)}, u32[]{:S(2)}) %collective-permute-start.10) | collective-permute-done | bytes 1310752 | tf_op jit(solution)/shard_map/ppermute | solution.py:37
  130.2 4.8 %collective-permute-done.11.refs_5_ = bf16[2560,256]{1,0:T(8,128)(2,1)} collective-permute-done((bf16[2560,256]{1,0:T(8,128)(2,1)}, bf16[2560,256]{1,0:T(8,128)(2,1)}, u32[]{:S(2)}, u32[]{:S(2)}) %collective-permute-start.11) | collective-permute-done | bytes 1310752 | tf_op jit(solution)/shard_map/ppermute | solution.py:37
  135.0 1.3 slice.91
  136.3 1.2 slice.92
  137.6 3.2 %collective-permute-start.13 = (bf16[1280,256]{1,0:T(8,128)(2,1)S(1)}, bf16[1280,256]{1,0:T(8,128)(2,1)S(1)}, u32[]{:S(2)}, u32[]{:S(2)}) collective-permute-start(bf16[1280,256]{1,0:T(8,128)(2,1)S(1)} %slice.92), channel_id=1, source_target_pairs={{0,24},{8,0},{16,8},{24,16},{32,56},{40,32},{48,40},{56,48},{64,88... | collective-permute-start | bytes 1966088 | tf_op jit(solution)/shard_map/ppermute | solution.py:37
  140.8 1.1 slice.93
  142.0 1.1 slice.94
  143.1 2.3 collective-permute-start.15
  145.4 14.3 %project_early.1 = (f32[8,1024,128]{2,1,0:T(8,128)S(1)}, f32[4,4,256,256]{3,2,1,0:T(8,128)S(1)}) custom-call(s32[13]{0:T(128)S(1)} %copy-done.9, f32[1024,8]{1,0:T(8,128)S(1)} %broadcast_multiply_fusion.gates_ref, s32[1024,2]{1,0:T(8,128)S(1)} %copy.42.routes_ref, bf16[1024,2048]{1,0:T(8,128)(2,1)S(1)} %copy-done.2, ...), custom_call_target="tpu_custom_call" | custom-call | flops 17250000896 | bytes 1048576 | tf_op jit(solution)/shard_map/project_early/pallas_call | solution.py:179
  159.7 1.9 copy-done.3
  161.7 19.1 %attention.1.lhs_ref = bf16[8,1024,256]{2,1,0:T(8,128)(2,1)S(1)} custom-call(s32[13]{0:T(128)S(1)} %copy-done.9, s32[1024,2]{1,0:T(8,128)S(1)} %copy.42.routes_ref, bf16[8,4,16,256]{3,2,1,0:T(8,128)(2,1)S(1)} %all-to-all-done.1.down_ref, bf16[1024,2048]{1,0:T(8,128)(2,1)S(1)} %copy-done.2, f32[4,4,256,256]{3,2,1,0:T(8,128)S(1)} %get-tuple-element.27.sums_hbm, ...), custom_call_target="tpu_custom_call" | custom-call | flops 25300000768 | bytes 1048576 | tf_op jit(solution)/shard_map/attention/pallas_call | solution.py:268
  180.8 1.9 copy-done.5
  182.7 3.4 %copy-done.1 = bf16[128,256,128]{2,1,0:T(8,128)(2,1)S(1)} copy-done((bf16[128,256,128]{2,1,0:T(8,128)(2,1)S(1)}, bf16[128,256,128]{2,1,0:T(8,128)(2,1)}, u32[]{:S(2)}) %copy-start.1) | copy-done | bytes 8388632
  186.1 2.2 copy-done.4
  188.3 2.2 copy-done.6
  190.5 4.3 %project_out_2.2 = bf16[2,1024,256]{2,1,0:T(8,128)(2,1)S(1)} custom-call(s32[2]{0:T(128)S(1)} %pad_add_fusion.place_ref, f32[8,1024,128]{2,1,0:T(8,128)S(1)} %copy-done.4, bf16[8,1024,256]{2,1,0:T(8,128)(2,1)S(1)} %copy-done.6, bf16[16,8,256,128]{3,2,1,0:T(8,128)(2,1)S(1)} %bitcast.41), custom_call_target="tpu_custom_call" | custom-call | flops 5750000128 | bytes 1048576 | tf_op jit(solution)/shard_map/project_out_2/pallas_call | solution.py:314
  194.8 6.1 %project_out_3.1 = bf16[3,1024,256]{2,1,0:T(8,128)(2,1)S(1)} custom-call(s32[2]{0:T(128)S(1)} %pad_add_fusion.place_ref, f32[8,1024,128]{2,1,0:T(8,128)S(1)} %copy-done.4, bf16[8,1024,256]{2,1,0:T(8,128)(2,1)S(1)} %copy-done.6, bf16[16,8,256,128]{3,2,1,0:T(8,128)(2,1)S(1)} %bitcast.42), custom_call_target="tpu_custom_call" | custom-call | flops 8625000448 | bytes 1048576 | tf_op jit(solution)/shard_map/project_out_3/pallas_call | solution.py:314
  201.6 3.5 %collective-permute-done.16 = bf16[1024,256]{1,0:T(8,128)(2,1)S(1)} collective-permute-done((bf16[1024,256]{1,0:T(8,128)(2,1)S(1)}, bf16[1024,256]{1,0:T(8,128)(2,1)S(1)}, u32[]{:S(2)}, u32[]{:S(2)}) %collective-permute-start.16) | collective-permute-done | bytes 524320 | tf_op jit(solution)/shard_map/ppermute | solution.py:331
  205.3 1.7 collective-permute-start.18
  207.0 1.6 collective-permute-start.19
  208.6 4.3 %project_out_2.3 = bf16[2,1024,256]{2,1,0:T(8,128)(2,1)S(1)} custom-call(s32[2]{0:T(128)S(1)} %pad_add_fusion.place_ref, f32[8,1024,128]{2,1,0:T(8,128)S(1)} %copy-done.4, bf16[8,1024,256]{2,1,0:T(8,128)(2,1)S(1)} %copy-done.6, bf16[16,8,256,128]{3,2,1,0:T(8,128)(2,1)S(1)} %bitcast.43), custom_call_target="tpu_custom_call" | custom-call | flops 5750000128 | bytes 1048576 | tf_op jit(solution)/shard_map/project_out_2/pallas_call | solution.py:314
  213.0 2.1 collective-permute-done.18
  215.4 3.1 %collective-permute-start.21 = (bf16[1024,256]{1,0:T(8,128)(2,1)S(1)}, bf16[1024,256]{1,0:T(8,128)(2,1)S(1)}, u32[]{:S(2)}, u32[]{:S(2)}) collective-permute-start(bf16[1024,256]{1,0:T(8,128)(2,1)S(1)} %pad_maximum_fusion.1), channel_id=1, source_target_pairs={{0,6},{1,7},{2,0},{3,1},{4,2},{5,3},{6,4},{7,5},{8,14},{9,15},{10,... | collective-permute-start | bytes 1572872 | tf_op jit(solution)/shard_map/ppermute | solution.py:332
  218.6 2.4 %project_out_1.1 = bf16[1,1024,256]{2,1,0:T(8,128)(2,1)S(1)} custom-call(s32[2]{0:T(128)S(1)} %pad_add_fusion.place_ref, f32[8,1024,128]{2,1,0:T(8,128)S(1)} %copy-done.4, bf16[8,1024,256]{2,1,0:T(8,128)(2,1)S(1)} %copy-done.6, bf16[16,8,256,128]{3,2,1,0:T(8,128)(2,1)S(1)} %bitcast.44), custom_call_target="tpu_custom_call" | custom-call | flops 2875000064 | bytes 1048576 | tf_op jit(solution)/shard_map/project_out_1/pallas_call | solution.py:314
  221.0 8.1 %collective-permute-done.21 = bf16[1024,256]{1,0:T(8,128)(2,1)S(1)} collective-permute-done((bf16[1024,256]{1,0:T(8,128)(2,1)S(1)}, bf16[1024,256]{1,0:T(8,128)(2,1)S(1)}, u32[]{:S(2)}, u32[]{:S(2)}) %collective-permute-start.21) | collective-permute-done | bytes 524320 | tf_op jit(solution)/shard_map/ppermute | solution.py:332
  229.1 3.5 %collective-permute-done.20 = bf16[1024,256]{1,0:T(8,128)(2,1)S(1)} collective-permute-done((bf16[1024,256]{1,0:T(8,128)(2,1)S(1)}, bf16[1024,256]{1,0:T(8,128)(2,1)S(1)}, u32[]{:S(2)}, u32[]{:S(2)}) %collective-permute-start.20) | collective-permute-done | bytes 524320 | tf_op jit(solution)/shard_map/ppermute | solution.py:332
  232.7 1.1 fusion.2
  (81 shorter events, 5.5 us)
Async XLA Ops:
  6.5 3.0 %copy-start = (bf16[4,2048,16]{1,2,0:T(8,128)(2,1)S(1)}, bf16[4,2048,16]{1,2,0:T(8,128)(2,1)}, u32[]{:S(2)}) copy-start(bf16[4,2048,16]{1,2,0:T(8,128)(2,1)} %param.25) | copy-start | bytes 786436
  6.5 2.3 copy-start.15
  6.5 3.6 %copy-start.10 = (bf16[128,512]{1,0:T(8,128)(2,1)S(1)}, bf16[128,512]{1,0:T(8,128)(2,1)}, u32[]{:S(2)}) copy-start(bf16[128,512]{1,0:T(8,128)(2,1)} %param.22) | copy-start | bytes 393220
  6.5 176.2 %all-gather.2.cloned.1.call-start = ((), (), s32[]{:S(2)}) async-start(), calls=%async_computation.2 | async-start | bytes 8912896 | tf_op jit(solution)/shard_map/all_gather | solution.py:360
  13.7 12.4 %copy-start.11 = (s32[1024,2]{0,1:T(2,128)S(1)}, s32[1024,2]{0,1:T(2,128)}, u32[]{:S(2)}) copy-start(s32[1024,2]{0,1:T(2,128)} %param.15) | copy-start | bytes 24580
  13.7 12.6 %copy-start.12 = (bf16[2048,8]{0,1:T(8,128)(2,1)S(1)}, bf16[2048,8]{0,1:T(8,128)(2,1)}, u32[]{:S(2)}) copy-start(bf16[2048,8]{0,1:T(8,128)(2,1)} %param.21) | copy-start | bytes 98308
  13.7 19.8 %collective-permute-start = (bf16[640,256]{1,0:T(8,128)(2,1)}, bf16[640,256]{1,0:T(8,128)(2,1)}, u32[]{:S(2)}, u32[]{:S(2)}) collective-permute-start(bf16[640,256]{1,0:T(8,128)(2,1)} %get-tuple-element.18), channel_id=1, source_target_pairs={{0,32},{8,40},{16,48},{24,56},{32,64},{40,72},{48,80},{56,88},{64,... | collective-permute-start | bytes 983048 | tf_op jit(solution)/shard_map/ppermute | solution.py:37
  14.1 20.5 %collective-permute-start.1 = (bf16[640,256]{1,0:T(8,128)(2,1)}, bf16[640,256]{1,0:T(8,128)(2,1)}, u32[]{:S(2)}, u32[]{:S(2)}) collective-permute-start(bf16[640,256]{1,0:T(8,128)(2,1)} %get-tuple-element.18), channel_id=1, source_target_pairs={{0,96},{8,104},{16,112},{24,120},{32,0},{40,8},{48,16},{56,24},{64... | collective-permute-start | bytes 983048 | tf_op jit(solution)/shard_map/ppermute | solution.py:37
  15.7 21.8 %collective-permute-start.6 = (bf16[640,256]{1,0:T(8,128)(2,1)}, bf16[640,256]{1,0:T(8,128)(2,1)}, u32[]{:S(2)}, u32[]{:S(2)}) collective-permute-start(bf16[640,256]{1,0:T(8,128)(2,1)} %get-tuple-element.19), channel_id=1, source_target_pairs={{0,8},{8,16},{16,24},{24,0},{32,40},{40,48},{48,56},{56,32},{64,72... | collective-permute-start | bytes 983048 | tf_op jit(solution)/shard_map/ppermute | solution.py:37
  17.7 22.4 %collective-permute-start.7 = (bf16[640,256]{1,0:T(8,128)(2,1)}, bf16[640,256]{1,0:T(8,128)(2,1)}, u32[]{:S(2)}, u32[]{:S(2)}) collective-permute-start(bf16[640,256]{1,0:T(8,128)(2,1)} %get-tuple-element.19), channel_id=1, source_target_pairs={{0,24},{8,0},{16,8},{24,16},{32,56},{40,32},{48,40},{56,48},{64,88... | collective-permute-start | bytes 983048 | tf_op jit(solution)/shard_map/ppermute | solution.py:37
  19.8 56.8 %all-to-all-start = ((bf16[16,160,512]{2,1,0:T(8,128)(2,1)}), bf16[16,160,512]{2,1,0:T(8,128)(2,1)S(1)}, u32[]{:S(2)}, u32[]{:S(2)}) async-start(bf16[16,160,512]{2,1,0:T(8,128)(2,1)} %pack.1), calls=%async_computation | async-start | bytes 5242880 | tf_op jit(solution)/shard_map/all_to_all | solution.py:385
  34.5 30.2 %collective-permute-start.2 = (bf16[320,256]{1,0:T(8,128)(2,1)S(1)}, bf16[320,256]{1,0:T(8,128)(2,1)S(1)}, u32[]{:S(2)}, u32[]{:S(2)}) collective-permute-start(bf16[320,256]{1,0:T(8,128)(2,1)S(1)} %slice.110), channel_id=1, source_target_pairs={{0,32},{8,40},{16,48},{24,56},{32,64},{40,72},{48,80},{56,88},{64,... | collective-permute-start | bytes 491528 | tf_op jit(solution)/shard_map/ppermute | solution.py:37
  35.6 30.1 %collective-permute-start.3 = (bf16[320,256]{1,0:T(8,128)(2,1)S(1)}, bf16[320,256]{1,0:T(8,128)(2,1)S(1)}, u32[]{:S(2)}, u32[]{:S(2)}) collective-permute-start(bf16[320,256]{1,0:T(8,128)(2,1)S(1)} %slice.111), channel_id=1, source_target_pairs={{0,96},{8,104},{16,112},{24,120},{32,0},{40,8},{48,16},{56,24},{64... | collective-permute-start | bytes 491528 | tf_op jit(solution)/shard_map/ppermute | solution.py:37
  38.5 31.2 %collective-permute-start.8 = (bf16[320,256]{1,0:T(8,128)(2,1)S(1)}, bf16[320,256]{1,0:T(8,128)(2,1)S(1)}, u32[]{:S(2)}, u32[]{:S(2)}) collective-permute-start(bf16[320,256]{1,0:T(8,128)(2,1)S(1)} %slice.112), channel_id=1, source_target_pairs={{0,8},{8,16},{16,24},{24,0},{32,40},{40,48},{48,56},{56,32},{64,72... | collective-permute-start | bytes 491528 | tf_op jit(solution)/shard_map/ppermute | solution.py:37
  41.0 29.4 %collective-permute-start.9 = (bf16[320,256]{1,0:T(8,128)(2,1)S(1)}, bf16[320,256]{1,0:T(8,128)(2,1)S(1)}, u32[]{:S(2)}, u32[]{:S(2)}) collective-permute-start(bf16[320,256]{1,0:T(8,128)(2,1)S(1)} %slice.113), channel_id=1, source_target_pairs={{0,24},{8,0},{16,8},{24,16},{32,56},{40,32},{48,40},{56,48},{64,88... | collective-permute-start | bytes 491528 | tf_op jit(solution)/shard_map/ppermute | solution.py:37
  48.0 27.6 %copy-start.13 = (s32[4]{0:T(128)S(1)}, s32[4]{0:T(128)}, u32[]{:S(2)}) copy-start(s32[4]{0:T(128)} %param.16) | copy-start | bytes 52
  48.0 27.8 %copy-start.16 = (s32[64]{0:T(128)S(1)}, s32[64]{0:T(128)}, u32[]{:S(2)}) copy-start(s32[64]{0:T(128)} %param.20) | copy-start | bytes 772
  48.0 27.8 %copy-start.17 = (s32[4]{0:T(128)S(1)}, s32[4]{0:T(128)}, u32[]{:S(2)}) copy-start(s32[4]{0:T(128)} %param.19) | copy-start | bytes 52
  48.0 28.0 %copy-start.14 = (s32[4]{0:T(128)S(1)}, s32[4]{0:T(128)}, u32[]{:S(2)}) copy-start(s32[4]{0:T(128)} %param.17) | copy-start | bytes 52
  66.4 54.4 %collective-permute-start.4 = (bf16[2560,256]{1,0:T(8,128)(2,1)}, bf16[2560,256]{1,0:T(8,128)(2,1)}, u32[]{:S(2)}, u32[]{:S(2)}) collective-permute-start(bf16[2560,256]{1,0:T(8,128)(2,1)} %constant_dynamic-update-slice_fusion.refs_0_), channel_id=1, source_target_pairs={{0,8},{8,16},{16,24},{24,0},{32,40},{40,48},{48,56},{56,32},{64,72... | collective-permute-start | bytes 3932168 | tf_op jit(solution)/shard_map/ppermute | solution.py:37
  69.7 53.7 %collective-permute-start.5 = (bf16[2560,256]{1,0:T(8,128)(2,1)}, bf16[2560,256]{1,0:T(8,128)(2,1)}, u32[]{:S(2)}, u32[]{:S(2)}) collective-permute-start(bf16[2560,256]{1,0:T(8,128)(2,1)} %constant_dynamic-update-slice_fusion.refs_0_), channel_id=1, source_target_pairs={{0,24},{8,0},{16,8},{24,16},{32,56},{40,32},{48,40},{56,48},{64,88... | collective-permute-start | bytes 3932168 | tf_op jit(solution)/shard_map/ppermute | solution.py:37
  71.1 59.1 %collective-permute-start.10 = (bf16[2560,256]{1,0:T(8,128)(2,1)}, bf16[2560,256]{1,0:T(8,128)(2,1)}, u32[]{:S(2)}, u32[]{:S(2)}) collective-permute-start(bf16[2560,256]{1,0:T(8,128)(2,1)} %constant_dynamic-update-slice_fusion.5.refs_3_), channel_id=1, source_target_pairs={{0,32},{8,40},{16,48},{24,56},{32,64},{40,72},{48,80},{56,88},{64,... | collective-permute-start | bytes 3932168 | tf_op jit(solution)/shard_map/ppermute | solution.py:37
  74.6 60.4 %collective-permute-start.11 = (bf16[2560,256]{1,0:T(8,128)(2,1)}, bf16[2560,256]{1,0:T(8,128)(2,1)}, u32[]{:S(2)}, u32[]{:S(2)}) collective-permute-start(bf16[2560,256]{1,0:T(8,128)(2,1)} %constant_dynamic-update-slice_fusion.5.refs_3_), channel_id=1, source_target_pairs={{0,96},{8,104},{16,112},{24,120},{32,0},{40,8},{48,16},{56,24},{64... | collective-permute-start | bytes 3932168 | tf_op jit(solution)/shard_map/ppermute | solution.py:37
  76.6 1.5 copy-start.7
  81.7 53.3 %all-to-all-start.1 = ((bf16[8,4,16,256]{3,2,1,0:T(8,128)(2,1)}), bf16[8,4,16,256]{3,2,1,0:T(8,128)(2,1)S(1)}, u32[]{:S(2)}, u32[]{:S(2)}) async-start(bf16[8,4,16,256]{3,2,1,0:T(8,128)(2,1)} %broadcast_in_dim.5), calls=%async_computation.1 | async-start | bytes 524288 | tf_op jit(solution)/shard_map/all_to_all | solution.py:411
  135.0 10.4 %copy-start.2 = (bf16[1024,2048]{1,0:T(8,128)(2,1)S(1)}, bf16[1024,2048]{1,0:T(8,128)(2,1)}, u32[]{:S(2)}) copy-start(bf16[1024,2048]{1,0:T(8,128)(2,1)} %x_hbm.3) | copy-start | bytes 12582916
  136.3 25.4 %collective-permute-start.12 = (bf16[1280,256]{1,0:T(8,128)(2,1)S(1)}, bf16[1280,256]{1,0:T(8,128)(2,1)S(1)}, u32[]{:S(2)}, u32[]{:S(2)}) collective-permute-start(bf16[1280,256]{1,0:T(8,128)(2,1)S(1)} %slice.91), channel_id=1, source_target_pairs={{0,8},{8,16},{16,24},{24,0},{32,40},{40,48},{48,56},{56,32},{64,72... | collective-permute-start | bytes 1966088 | tf_op jit(solution)/shard_map/ppermute | solution.py:37
  137.6 7.8 %copy-start.9 = (s32[13]{0:T(128)S(1)}, s32[13]{0:T(128)}, u32[]{:S(2)}) copy-start(s32[13]{0:T(128)} %pad_add_fusion.1.info_ref) | copy-start | bytes 160
  137.6 24.1 %collective-permute-start.13 = (bf16[1280,256]{1,0:T(8,128)(2,1)S(1)}, bf16[1280,256]{1,0:T(8,128)(2,1)S(1)}, u32[]{:S(2)}, u32[]{:S(2)}) collective-permute-start(bf16[1280,256]{1,0:T(8,128)(2,1)S(1)} %slice.92), channel_id=1, source_target_pairs={{0,24},{8,0},{16,8},{24,16},{32,56},{40,32},{48,40},{56,48},{64,88... | collective-permute-start | bytes 1966088 | tf_op jit(solution)/shard_map/ppermute | solution.py:37
  141.9 19.7 %collective-permute-start.14 = (bf16[1280,256]{1,0:T(8,128)(2,1)S(1)}, bf16[1280,256]{1,0:T(8,128)(2,1)S(1)}, u32[]{:S(2)}, u32[]{:S(2)}) collective-permute-start(bf16[1280,256]{1,0:T(8,128)(2,1)S(1)} %slice.93), channel_id=1, source_target_pairs={{0,32},{8,40},{16,48},{24,56},{32,64},{40,72},{48,80},{56,88},{64,... | collective-permute-start | bytes 1966088 | tf_op jit(solution)/shard_map/ppermute | solution.py:37
  143.1 18.5 %copy-start.8 = (bf16[16,160,512]{2,1,0:T(8,128)(2,1)S(1)}, bf16[16,160,512]{2,1,0:T(8,128)(2,1)}, u32[]{:S(2)}) copy-start(bf16[16,160,512]{2,1,0:T(8,128)(2,1)} %copy-done.7) | copy-start | bytes 7864324
  143.1 18.5 %collective-permute-start.15 = (bf16[1280,256]{1,0:T(8,128)(2,1)S(1)}, bf16[1280,256]{1,0:T(8,128)(2,1)S(1)}, u32[]{:S(2)}, u32[]{:S(2)}) collective-permute-start(bf16[1280,256]{1,0:T(8,128)(2,1)S(1)} %slice.94), channel_id=1, source_target_pairs={{0,96},{8,104},{16,112},{24,120},{32,0},{40,8},{48,16},{56,24},{64... | collective-permute-start | bytes 1966088 | tf_op jit(solution)/shard_map/ppermute | solution.py:37
  159.7 1.9 copy-start.3
  180.8 1.9 copy-start.5
  182.7 3.4 %copy-start.1 = (bf16[128,256,128]{2,1,0:T(8,128)(2,1)S(1)}, bf16[128,256,128]{2,1,0:T(8,128)(2,1)}, u32[]{:S(2)}) copy-start(bf16[128,256,128]{2,1,0:T(8,128)(2,1)} %all-gather.2.cloned.1.call-done) | copy-start | bytes 25165828
  186.1 2.2 copy-start.4
  188.3 2.2 copy-start.6
  200.9 12.0 %collective-permute-start.17 = (bf16[3,1024,256]{2,1,0:T(8,128)(2,1)S(1)}, bf16[3,1024,256]{2,1,0:T(8,128)(2,1)S(1)}, u32[]{:S(2)}, u32[]{:S(2)}) collective-permute-start(bf16[3,1024,256]{2,1,0:T(8,128)(2,1)S(1)} %project_out_3.1), channel_id=1, source_target_pairs={{0,1},{1,0},{2,3},{3,2},{4,5},{5,4},{6,7},{7,6},{8,9},{9,8},{10,11... | collective-permute-start | bytes 4718600 | tf_op jit(solution)/shard_map/ppermute | solution.py:331
  201.0 4.1 %collective-permute-start.16 = (bf16[1024,256]{1,0:T(8,128)(2,1)S(1)}, bf16[1024,256]{1,0:T(8,128)(2,1)S(1)}, u32[]{:S(2)}, u32[]{:S(2)}) collective-permute-start(bf16[1024,256]{1,0:T(8,128)(2,1)S(1)} %slice_bitcast_fusion), channel_id=1, source_target_pairs={{0,1},{1,0},{2,3},{3,2},{4,5},{5,4},{6,7},{7,6},{8,9},{9,8},{10,11... | collective-permute-start | bytes 1572872 | tf_op jit(solution)/shard_map/ppermute | solution.py:331
  205.3 9.8 %collective-permute-start.18 = (bf16[512,256]{1,0:T(8,128)(2,1)S(1)}, bf16[512,256]{1,0:T(8,128)(2,1)S(1)}, u32[]{:S(2)}, u32[]{:S(2)}) collective-permute-start(bf16[512,256]{1,0:T(8,128)(2,1)S(1)} %get-tuple-element.35), channel_id=1, source_target_pairs={{0,2},{1,3},{2,4},{3,5},{4,6},{5,7},{6,0},{7,1},{8,10},{9,11},{10,... | collective-permute-start | bytes 786440 | tf_op jit(solution)/shard_map/ppermute | solution.py:332
  207.0 8.2 %collective-permute-start.19 = (bf16[512,256]{1,0:T(8,128)(2,1)S(1)}, bf16[512,256]{1,0:T(8,128)(2,1)S(1)}, u32[]{:S(2)}, u32[]{:S(2)}) collective-permute-start(bf16[512,256]{1,0:T(8,128)(2,1)S(1)} %get-tuple-element.36), channel_id=1, source_target_pairs={{0,6},{1,7},{2,0},{3,1},{4,2},{5,3},{6,4},{7,5},{8,14},{9,15},{10,... | collective-permute-start | bytes 786440 | tf_op jit(solution)/shard_map/ppermute | solution.py:332
  215.4 13.7 %collective-permute-start.21 = (bf16[1024,256]{1,0:T(8,128)(2,1)S(1)}, bf16[1024,256]{1,0:T(8,128)(2,1)S(1)}, u32[]{:S(2)}, u32[]{:S(2)}) collective-permute-start(bf16[1024,256]{1,0:T(8,128)(2,1)S(1)} %pad_maximum_fusion.1), channel_id=1, source_target_pairs={{0,6},{1,7},{2,0},{3,1},{4,2},{5,3},{6,4},{7,5},{8,14},{9,15},{10,... | collective-permute-start | bytes 1572872 | tf_op jit(solution)/shard_map/ppermute | solution.py:332
  218.5 14.1 %collective-permute-start.20 = (bf16[1024,256]{1,0:T(8,128)(2,1)S(1)}, bf16[1024,256]{1,0:T(8,128)(2,1)S(1)}, u32[]{:S(2)}, u32[]{:S(2)}) collective-permute-start(bf16[1024,256]{1,0:T(8,128)(2,1)S(1)} %pad_maximum_fusion), channel_id=1, source_target_pairs={{0,2},{1,3},{2,4},{3,5},{4,6},{5,7},{6,0},{7,1},{8,10},{9,11},{10,... | collective-permute-start | bytes 1572872 | tf_op jit(solution)/shard_map/ppermute | solution.py:332
Sparse Core Ops, SparseCore 0:
  9.5 129.4 all-gather.1
where the time goes:
time: 242 us; the launch traced here: 241 us
  waiting for transfers between devices  80.7 us (33%)
  Pallas kernels  55.2 us (23%)
  starting transfers between devices  42.1 us (17%)
  local copies, waits for them, and re-layouts  40.1 us (17%)
  between operations  13.8 us (6%)
  other arithmetic  5.37 us (2%)
  matrix products  3.37 us (1%)
    ppermute x16, waiting for transfers between devices, send(): lax.ppermute(value, 'req', torus(step, 0) if along == 0 else torus(0, step))  62.7 us
    unnamed x46, local copies, waits for them, and re-layouts  25.2 us
    ppermute x16, starting transfers between devices, send(): lax.ppermute(value, 'req', torus(step, 0) if along == 0 else torus(0, step))  24 us
    pallas_call x1, Pallas kernels, attention(): pl.pallas_call(attend_kernel, out_shape=jax.ShapeDtypeStruct((NE, 1024, 2...  19.1 us
    pallas_call x4, Pallas kernels, project_out(): pl.pallas_call(functools.partial(project_out_kernel, blocks), out_shape=j...  17.1 us
    pallas_call x1, Pallas kernels, project_early(): pl.pallas_call(early_kernel, out_shape=(jax.ShapeDtypeStruct((NE, 1024, 1...  14.3 us
    ppermute x4, waiting for transfers between devices, exchange(): lax.ppermute(value, 'exp', [(i, (i + 2 * step) % 8) for i in range(8)])  13.7 us
    slice x8, local copies, waits for them, and re-layouts, second_step(): return (send(before[:half], along, 1), send(after[half:], along, -1))  8.47 us
  transfers between devices with their start and end apart: 25, of which 10 were waited for; matrix products, arithmetic and copies ran while one was open for 14% of the time, Pallas kernels for 19%

commit v1 on v0

--- a/solution.py
+++ b/solution.py
@@ -18,6 +18,7 @@
 
 ROW_KV = 512
 SHARD_ROWS = 640
+OUT_ROWS = 512
 ROW_UP, ROW_DN, SENT_ROWS = 64, 128, 160
 PLACES = []
 for _piece, _off in ((0, 0), (1, -1), (2, 1)):
@@ -25,6 +26,7 @@
         PLACES.append((_piece, _i, _near, _off))
 EARLY = list(PLACES)
 LATE = [(0, 0, 0, 2), (0, 1, -1, 2), (1, 0, 1, 2), (1, 1, 2, 2)]
+PLACES += [(3 + piece, shard, first, second) for piece, shard, first, second in LATE]
 
 
 def torus(dx, dz):
@@ -57,7 +59,6 @@
 
 
 ANY = pl.BlockSpec(memory_space=pl.ANY)
-HBM = pl.BlockSpec(memory_space=pltpu.HBM)
 WHOLE = pl.BlockSpec(memory_space=pltpu.VMEM)
 SCALARS = pl.BlockSpec(memory_space=pltpu.SMEM)
 
@@ -145,34 +146,25 @@
     return chosen, product(ROW_KV)
 
 
-def early_kernel(info_ref, gates_ref, routes_ref, x_hbm, *refs):
+def early_kernel(info_ref, gates_ref, routes_ref, x_ref, *refs):
     pieces = refs[:6]
-    wide_ref, sums_hbm, x, sums, sem = refs[6:]
+    wide_ref, sums_ref = refs[6:]
     group = info_ref[0]
-    loads = [
-        pltpu.make_async_copy(x_hbm.at[pl.ds(j * 256, 256), :], x.at[j], sem.at[j])
-        for j in range(4)
-    ]
-    for load in loads:
-        load.start()
     for e in range(NE):
         wide_ref[e] = jnp.broadcast_to(gates_ref[:, e : e + 1], (1024, 128))
 
     def block(j, carry):
-        pltpu.make_async_copy(x.at[j], x.at[j], sem.at[j]).wait()
-        rows = routes_ref.at[pl.ds(pl.multiple_of(j * 256, 256), 256), :]
-        first, base = products(group, x.at[j], rows, pieces, EARLY, 0)
-        sums[j, 2] = base
-        second, base = products(group, x.at[j], rows, pieces, EARLY, 1)
-        sums[j, 3] = base
+        rows = pl.ds(pl.multiple_of(j * 256, 256), 256)
+        x, routes = x_ref.at[rows, :], routes_ref.at[rows, :]
+        first, base = products(group, x, routes, pieces, EARLY, 0)
+        sums_ref[j, 2] = base
+        second, base = products(group, x, routes, pieces, EARLY, 1)
+        sums_ref[j, 3] = base
         for k in range(TOPK):
-            sums[j, k] = first[k] + second[k]
-        pltpu.make_async_copy(sums.at[j], sums_hbm.at[j], sem.at[4 + j]).start()
+            sums_ref[j, k] = first[k] + second[k]
         return carry
 
     lax.fori_loop(0, 4, block, 0)
-    for j in range(4):
-        pltpu.make_async_copy(sums.at[j], sums_hbm.at[j], sem.at[4 + j]).wait()
 
 
 def project_early(info, gates, routes, x, pieces):
@@ -182,48 +174,42 @@
             jax.ShapeDtypeStruct((NE, 1024, 128), F32),
             jax.ShapeDtypeStruct((4, 4, 256, 256), F32),
         ),
-        in_specs=[SCALARS, WHOLE, WHOLE, HBM] + [WHOLE] * 6,
-        out_specs=(WHOLE, HBM),
-        scratch_shapes=[
-            pltpu.VMEM((4, 256, 2048), BF),
-            pltpu.VMEM((4, 4, 256, 256), F32),
-            pltpu.SemaphoreType.DMA((8,)),
-        ],
-        compiler_params=pltpu.CompilerParams(vmem_limit_bytes=24 * 2**20),
+        in_specs=[SCALARS] + [WHOLE] * 9,
+        out_specs=(WHOLE, WHOLE),
+        compiler_params=pltpu.CompilerParams(vmem_limit_bytes=10 * 2**20),
         cost_estimate=cost(15),
         name="project_early",
     )(info, gates, routes, x, *pieces)
 
 
-def attend_kernel(info_ref, routes_ref, down_ref, x_hbm, sums_hbm, recv_hbm, *refs):
+def attend_kernel(info_ref, routes_ref, down_ref, x_ref, sums_ref, recv_hbm, *refs):
     pieces = refs[:4]
-    out_ref, x, sums, up, cache, sem = refs[4:]
+    out_ref, sums, up, cache, sem = refs[4:]
     group = info_ref[0]
     for j in range(4):
         slot = info_ref[1 + j]
         start = pl.multiple_of(ROW_UP + (slot % 4) * 16, 16)
-        pltpu.make_async_copy(x_hbm.at[pl.ds(j * 256, 256), :], x.at[j], sem.at[0, j]).start()
-        pltpu.make_async_copy(sums_hbm.at[j], sums.at[j], sem.at[1, j]).start()
         pltpu.make_async_copy(
-            recv_hbm.at[slot // 4, pl.ds(start, 16), :], up.at[j], sem.at[2, j]
+            recv_hbm.at[slot // 4, pl.ds(start, 16), :], up.at[j], sem.at[0, j]
         ).start()
         pltpu.make_async_copy(
-            recv_hbm.at[info_ref[5 + j], pl.ds(0, 64), :], cache.at[j], sem.at[3, j]
+            recv_hbm.at[info_ref[5 + j], pl.ds(0, 64), :], cache.at[j], sem.at[1, j]
         ).start()
 
     def attend(j, carry):
-        for i, ref in enumerate((x, sums, up, cache)):
+        for i, ref in enumerate((up, cache)):
             pltpu.make_async_copy(ref.at[j], ref.at[j], sem.at[i, j]).wait()
         rows = pl.ds(pl.multiple_of(j * 256, 256), 256)
-        routes = routes_ref.at[rows, :]
+        x, routes = x_ref.at[rows, :], routes_ref.at[rows, :]
         for half in range(2):
-            chosen, base = products(group, x.at[j], routes, pieces, LATE, half)
-            sums[j, 2 + half] += base
+            chosen, base = products(group, x, routes, pieces, LATE, half)
+            sums[2 + half] = sums_ref[j, 2 + half] + base
             for k in range(TOPK):
-                sums[j, k] += chosen[k]
+                before = sums_ref[j, k] if half == 0 else sums[k]
+                sums[k] = before + chosen[k]
         down = jnp.concatenate([down_ref[e, j] for e in range(NE)], axis=1)
         low = lax.dot_general(
-            x[j], down, (((1,), (1,)), ((), ())), preferred_element_type=F32
+            x[...], down, (((1,), (1,)), ((), ())), preferred_element_type=F32
         ).astype(BF)
         cached_length = info_ref[9 + j]
         place = lax.broadcasted_iota(jnp.int32, (256, 320), 1)
@@ -232,7 +218,7 @@
         for h in range(2):
             cols = slice(h * HD, (h + 1) * HD)
             extra = jnp.dot(low, up[j, :, h * 256 : h * 256 + 256], preferred_element_type=F32)
-            fresh = (sums[j, 2 + h] + adapter_scale * extra).astype(BF)
+            fresh = (sums[2 + h] + adapter_scale * extra).astype(BF)
             keys = jnp.concatenate(
                 [cache[j, :, h * 256 : h * 256 + HD], fresh[:, 0:HD]], axis=0
             )
@@ -242,7 +228,7 @@
             attended = []
             for k in range(TOPK):
                 scores = lax.dot_general(
-                    sums[j, k, :, cols].astype(BF),
+                    sums[k, :, cols].astype(BF),
                     keys,
                     (((1,), (1,)), ((), ())),
                     preferred_element_type=F32,
@@ -268,27 +254,38 @@
     return pl.pallas_call(
         attend_kernel,
         out_shape=jax.ShapeDtypeStruct((NE, 1024, 256), BF),
-        in_specs=[SCALARS, WHOLE, WHOLE, HBM, HBM, ANY] + [WHOLE] * 4,
+        in_specs=[SCALARS] + [WHOLE] * 4 + [ANY] + [WHOLE] * 4,
         out_specs=WHOLE,
         scratch_shapes=[
-            pltpu.VMEM((4, 256, 2048), BF),
-            pltpu.VMEM((4, 4, 256, 256), F32),
+            pltpu.VMEM((4, 256, 256), F32),
             pltpu.VMEM((4, 16, 512), BF),
             pltpu.VMEM((4, 64, 512), BF),
-            pltpu.SemaphoreType.DMA((4, 4)),
+            pltpu.SemaphoreType.DMA((2, 4)),
         ],
-        compiler_params=pltpu.CompilerParams(vmem_limit_bytes=24 * 2**20),
+        compiler_params=pltpu.CompilerParams(vmem_limit_bytes=10 * 2**20),
         cost_estimate=cost(22),
         name="attention",
     )(info, routes, down, x, sums, recv, *pieces)
 
 
-def project_out_kernel(blocks, place_ref, wide_ref, lhs_ref, w_hbm, out_ref, w, sem):
-    y, core = place_ref[0], place_ref[1]
+def project_out_kernel(blocks, place_ref, wide_ref, lhs_ref, *refs):
+    pieces = refs[:10]
+    out_ref, w, sem = refs[10:]
+    group, y, core = place_ref[0], place_ref[1], place_ref[2]
     for b, (mine, ahead) in enumerate(blocks):
+        wanted_x = (y + ahead) % 4
         side = core if mine else 1 - core
-        start = ((y + ahead) % 4 * 2 + side) * 2
-        pltpu.make_async_copy(w_hbm.at[pl.ds(start, 2)], w.at[b], sem.at[b]).start()
+        for half in range(2):
+            for piece, shard, first, second in PLACES:
+                owner = source(group, half, first, second)
+
+                @pl.when((owner // 4 == wanted_x) & ((owner % 4) // 2 == side))
+                def _(b=b, half=half, piece=piece, shard=shard, owner=owner):
+                    pltpu.make_async_copy(
+                        pieces[half * 5 + piece].at[pl.ds(shard * OUT_ROWS, OUT_ROWS), :],
+                        w.at[b, half, owner % 2],
+                        sem.at[b],
+                    ).start()
 
     def block(b, carry):
         pltpu.make_async_copy(w.at[b], w.at[b], sem.at[b]).wait()
@@ -297,7 +294,11 @@
             rows = pl.ds(pl.multiple_of(i * 256, 256), 256)
             total = None
             for e in range(NE):
-                weight = jnp.concatenate([w[b, 0, e], w[b, 1, e]], axis=1)
+                half, pair, lane = e // 4, (e % 4) // 2, e % 2
+                place = (pl.ds(pair * 256, 256), pl.ds(lane * 128, 128))
+                weight = jnp.concatenate(
+                    [w[b, half, 0, place[0], place[1]], w[b, half, 1, place[0], place[1]]], axis=1
+                )
                 value = jnp.dot(lhs_ref[e, rows, :], weight, preferred_element_type=F32)
                 gate = wide_ref[e, rows, :]
                 value = value * jnp.concatenate([gate, gate], axis=1)
@@ -310,20 +311,20 @@
     lax.fori_loop(0, len(blocks), block, 0)
 
 
-def project_out(blocks, place, wide, lhs, weight):
+def project_out(blocks, place, wide, lhs, pieces):
     return pl.pallas_call(
         functools.partial(project_out_kernel, blocks),
         out_shape=jax.ShapeDtypeStruct((len(blocks), 1024, 256), BF),
-        in_specs=[SCALARS, WHOLE, WHOLE, HBM],
+        in_specs=[SCALARS, WHOLE, WHOLE] + [ANY] * 10,
         out_specs=WHOLE,
         scratch_shapes=[
-            pltpu.VMEM((len(blocks), 2, NE, 256, 128), BF),
+            pltpu.VMEM((len(blocks), 2, 2, OUT_ROWS, 256), BF),
             pltpu.SemaphoreType.DMA((len(blocks),)),
         ],
-        compiler_params=pltpu.CompilerParams(vmem_limit_bytes=16 * 2**20),
+        compiler_params=pltpu.CompilerParams(vmem_limit_bytes=8 * 2**20),
         cost_estimate=cost(2.5 * len(blocks)),
         name="project_out_" + str(len(blocks)),
-    )(place, wide, lhs, weight)
+    )(place, wide, lhs, *pieces)
 
 
 def exchange(value, step):
@@ -357,9 +358,6 @@
 ):
     group = lax.axis_index("req")
     part = lax.axis_index("exp")
-    out_weight = lax.all_gather(expert_output_weight, "req", axis=0, tiled=True).reshape(
-        16, NE, 256, 128
-    )
     rows_by_group = prefix_cache_row.reshape(16, 4)
     held = (rows_by_group == group).astype(jnp.int32)
     wanted_by = jnp.sum(held * jnp.arange(4, dtype=jnp.int32)[None, :], axis=1)
@@ -371,23 +369,51 @@
     outgoing = pack(wanted_by, prefix_cache_store, adapter_up_maps.reshape(64, 512), down_rows)
 
     query_rows = expert_query_weight.transpose(1, 0, 2).reshape(NE * 128, 256)
+    out_rows = (
+        expert_output_weight.reshape(4, 2, 256, 128).transpose(0, 2, 1, 3).reshape(1024, 256)
+    )
     own = [
         jnp.concatenate(
             [
                 query_rows[half * 512 : half * 512 + 512],
                 key_value_weight[:, half * 256 : half * 256 + 256],
+                out_rows[half * 512 : half * 512 + 512],
             ],
             axis=0,
         )
         for half in range(2)
     ]
-    *own, outgoing = lax.optimization_barrier((*own, outgoing))
+    neighbours = [*first_step(own[0], 0), *first_step(own[1], 1)]
+    *neighbours, outgoing = lax.optimization_barrier((*neighbours, outgoing))
     received = lax.all_to_all(outgoing, "req", 0, 0, tiled=True)
-    near = []
+    near, near_out = [], []
     for half in range(2):
-        before, after = first_step(own[half], half)
-        far = second_step(before, after, half)
-        near.append(jnp.concatenate([own[half], before, after, *far], axis=0))
+        before, after = neighbours[2 * half : 2 * half + 2]
+        far_low, far_high = second_step(before, after, half)
+        cut = SHARD_ROWS - far_low.shape[0]
+        near.append(
+            jnp.concatenate(
+                [
+                    own[half][:SHARD_ROWS],
+                    before[:SHARD_ROWS],
+                    after[:SHARD_ROWS],
+                    far_low,
+                    far_high[:cut],
+                ],
+                axis=0,
+            )
+        )
+        near_out.append(
+            jnp.concatenate(
+                [
+                    own[half][SHARD_ROWS:],
+                    before[SHARD_ROWS:],
+                    after[SHARD_ROWS:],
+                    far_high[cut:],
+                ],
+                axis=0,
+            )
+        )
 
     adapter_hot = (
         adapter_per_request[:, None]
@@ -416,19 +442,27 @@
     wide, sums = project_early(
         info, gates, routes, tokens, [near[0], *beside[:2], near[1], *beside[2:]]
     )
+    *late, near_out[0], near_out[1] = lax.optimization_barrier((*late, *near_out))
+    out_beside = [*first_step(near_out[0], 1), *first_step(near_out[1], 0)]
     lhs = attention(info, routes, down, tokens, sums, received, late)
-
-    place = jnp.stack([part // 2, part % 2]).astype(jnp.int32)
-    far = project_out(((False, 2), (True, 2)), place, wide, lhs, out_weight)
+    *out_beside, lhs = lax.optimization_barrier((*out_beside, lhs))
+    out_late = [*second_step(*out_beside[:2], 1), *second_step(*out_beside[2:], 0)]
+    out_pieces = []
+    for half in range(2):
+        two = slice(half * 2, half * 2 + 2)
+        out_pieces += [near_out[half], *out_beside[two], *out_late[two]]
+
+    place = jnp.stack([group, part // 2, part % 2]).astype(jnp.int32)
+    far = project_out(((False, 2), (True, 2)), place, wide, lhs, out_pieces)
     far_swapped = exchange(far[0], 0)
     place = lax.optimization_barrier((place, far))[0]
-    theirs = project_out(((False, 1), (False, 3), (False, 0)), place, wide, lhs, out_weight)
+    theirs = project_out(((False, 1), (False, 3), (False, 0)), place, wide, lhs, out_pieces)
     swapped = exchange(theirs, 0)
     both_far = rounded_sum(far[1], far_swapped)
     low = exchange(both_far[:512], 1)
     high = exchange(both_far[512:], -1)
     place = lax.optimization_barrier((place, theirs, both_far))[0]
-    mine = project_out(((True, 1), (True, 3)), place, wide, lhs, out_weight)
+    mine = project_out(((True, 1), (True, 3)), place, wide, lhs, out_pieces)
     ahead = jnp.concatenate(
         [rounded_sum(mine[0, :512], swapped[0, :512], low), rounded_sum(mine[0, 512:], swapped[0, 512:])],
         axis=0,
@@ -439,7 +473,7 @@
     )
     from_behind, from_ahead = exchange(ahead, 1), exchange(behind, -1)
     place = lax.optimization_barrier((place, ahead, behind))[0]
-    own_block = project_out(((True, 0),), place, wide, lhs, out_weight)
+    own_block = project_out(((True, 0),), place, wide, lhs, out_pieces)
     return rounded_sum(own_block[0], swapped[2], from_behind, from_ahead)
 
 

time: 242 us -> 234 us (0.967)
  between operations: 13.8 us -> 0.59 us
  waiting for transfers between devices: 80.7 us -> 69.2 us
  starting transfers between devices: 42.1 us -> 53.3 us
  Pallas kernels: 55.2 us -> 59.3 us
    ppermute x16 -> x24, starting transfers between devices: 24 us -> 34.4 us  [send(): lax.ppermute(value, 'req', torus(step, 0) if along == 0 else torus(0, step))]
    ppermute x16 -> x24, waiting for transfers between devices: 62.7 us -> 53.7 us  [send(): lax.ppermute(value, 'req', torus(step, 0) if along == 0 else torus(0, step))]
    pallas_call x4, Pallas kernels: 17.1 us -> 22.1 us  [project_out(): pl.pallas_call(functools.partial(project_out_kernel, blocks), out_shape=j...]
    unnamed x46 -> x82, local copies, waits for them, and re-layouts: 25.2 us -> 20.5 us
    slice x1 -> x9, local copies, waits for them, and re-layouts: 0.01 us -> 4.51 us  [the longest x3 1.73 us: body(): after[SHARD_ROWS:]]
    slice x8 -> x12, local copies, waits for them, and re-layouts: 8.47 us -> 9.31 us  [second_step(): return (send(before[:half], along, 1), send(after[half:], along, -1))]
  transfers between devices with their start and end apart: 25 -> 32, of which waited for: 10 -> 16; matrix products, arithmetic and copies ran while one was open for 14% -> 12% of each run, Pallas kernels for 19% -> 20%
where the time goes in v1:
time: 234 us; the launch traced here: 233 us
  waiting for transfers between devices  69.2 us (30%)
  Pallas kernels  59.3 us (25%)
  starting transfers between devices  53.3 us (23%)
  local copies, waits for them, and re-layouts  40.3 us (17%)
  other arithmetic  6.56 us (3%)
  matrix products  3.37 us (1%)
    ppermute x24, waiting for transfers between devices, send(): lax.ppermute(value, 'req', torus(step, 0) if along == 0 else torus(0, step))  53.7 us
    ppermute x24, starting transfers between devices, send(): lax.ppermute(value, 'req', torus(step, 0) if along == 0 else torus(0, step))  34.4 us
    pallas_call x4, Pallas kernels, project_out(): pl.pallas_call(functools.partial(project_out_kernel, blocks), out_shape=j...  22.1 us
    unnamed x82, local copies, waits for them, and re-layouts  20.5 us
    pallas_call x1, Pallas kernels, attention(): pl.pallas_call(attend_kernel, out_shape=jax.ShapeDtypeStruct((NE, 1024, 2...  18.9 us
    pallas_call x1, Pallas kernels, project_early(): pl.pallas_call(early_kernel, out_shape=(jax.ShapeDtypeStruct((NE, 1024, 1...  13.6 us
    ppermute x4, waiting for transfers between devices, exchange(): lax.ppermute(value, 'exp', [(i, (i + 2 * step) % 8) for i in range(8)])  12 us
    slice x12, local copies, waits for them, and re-layouts, second_step(): return (send(before[:half], along, 1), send(after[half:], along, -1))  9.31 us
  transfers between devices with their start and end apart: 32, of which 16 were waited for; matrix products, arithmetic and copies ran while one was open for 12% of the time, Pallas kernels for 20%

profile of v1, /device:TPU:6, one launch (start us, length us, event | category | flops | bytes accessed | tf_op | source)
XLA Modules:
  0.0 232.6 jit_solution(9667024358626484909)
XLA Ops:
  0.0 1.4 fusion.8
  5.9 1.6 collective-permute-start.1
  7.6 0.9 pad_maximum_fusion.3
  8.5 1.9 collective-permute-start.2
  10.4 2.1 collective-permute-start.3
  12.6 3.4 %fusion.10 = f32[1024,8]{0,1:T(8,128)S(1)} fusion(bf16[1024,2048]{1,0:T(8,128)(2,1)} %x_ref.3, bf16[2048,8]{0,1:T(8,128)(2,1)S(1)} %copy-done.29), kind=kOutput, calls=%fused_computation.53 | convolution fusion | flops 33554432 | bytes 4259840 | tf_op jit(solution)/shard_map/dot_general | solution.py:426
  17.9 2.7 %pack.1 = bf16[16,160,512]{2,1,0:T(8,128)(2,1)} custom-call(s32[16]{0:T(128)} %select_reduce_fusion.2.index_ref, bf16[4,64,512]{2,1,0:T(8,128)(2,1)} %store_ref.1, bf16[64,512]{1,0:T(8,128)(2,1)} %bitcast.69, bf16[64,256]{1,0:T(8,128)(2,1)} %bitcast.67), custom_call_target="tpu_custom_call" | custom-call | flops 3449999872 | bytes 1048576 | tf_op jit(solution)/shard_map/pack/pallas_call | solution.py:80
  20.8 1.2 collective-permute-done.1
  22.0 3.5 %collective-permute-done.2 = bf16[1152,256]{1,0:T(8,128)(2,1)S(1)} collective-permute-done((bf16[1152,256]{1,0:T(8,128)(2,1)}, bf16[1152,256]{1,0:T(8,128)(2,1)S(1)}, u32[]{:S(2)}, u32[]{:S(2)}) %collective-permute-start.2) | collective-permute-done | bytes 589856 | tf_op jit(solution)/shard_map/ppermute | solution.py:39
  25.5 7.3 %all-to-all-start = ((bf16[16,160,512]{2,1,0:T(8,128)(2,1)}), bf16[16,160,512]{2,1,0:T(8,128)(2,1)}, u32[]{:S(2)}, u32[]{:S(2)}) async-start(bf16[16,160,512]{2,1,0:T(8,128)(2,1)} %pack.1), calls=%async_computation | async-start | bytes 5242880 | tf_op jit(solution)/shard_map/all_to_all | solution.py:388
  33.3 0.9 slice_dynamic-update-slice_fusion.1
  35.0 1.9 collective-permute-start.5
  37.0 1.5 collective-permute-start.8
  38.4 1.0 slice.163
  39.4 1.8 collective-permute-start.9
  41.2 1.7 slice_dynamic-update-slice_fusion
  43.0 24.0 %collective-permute-done.4 = bf16[576,256]{1,0:T(8,128)(2,1)S(1)} collective-permute-done((bf16[576,256]{1,0:T(8,128)(2,1)S(1)}, bf16[576,256]{1,0:T(8,128)(2,1)S(1)}, u32[]{:S(2)}, u32[]{:S(2)}) %collective-permute-start.4) | collective-permute-done | bytes 294944 | tf_op jit(solution)/shard_map/ppermute | solution.py:39
  68.3 1.5 collective-permute-start.6
  69.8 1.8 collective-permute-start.7
  72.9 2.6 %collective-permute-start.10 = (bf16[2560,256]{1,0:T(8,128)(2,1)}, bf16[2560,256]{1,0:T(8,128)(2,1)}, u32[]{:S(2)}, u32[]{:S(2)}) collective-permute-start(bf16[2560,256]{1,0:T(8,128)(2,1)} %slice_dynamic-update-slice_fusion.4.refs_3_), channel_id=1, source_target_pairs={{0,32},{8,40},{16,48},{24,56},{32,64},{40,72},{48,80},{56,88},{64,... | collective-permute-start | bytes 3932168 | tf_op jit(solution)/shard_map/ppermute | solution.py:39
  76.6 1.7 slice.173
  78.3 1.7 slice.172
  80.8 2.1 pick_down.1
  82.9 1.5 broadcast_in_dim.2
  84.4 4.5 %all-to-all-start.1 = ((bf16[8,4,16,256]{3,2,1,0:T(8,128)(2,1)}), bf16[8,4,16,256]{3,2,1,0:T(8,128)(2,1)S(1)}, u32[]{:S(2)}, u32[]{:S(2)}) async-start(bf16[8,4,16,256]{3,2,1,0:T(8,128)(2,1)} %broadcast_in_dim.2), calls=%async_computation.1 | async-start | bytes 524288 | tf_op jit(solution)/shard_map/all_to_all | solution.py:437
  88.9 1.3 pad_maximum_fusion.1.refs_5_
  90.1 8.9 %collective-permute-done.6.refs_1_ = bf16[2560,256]{1,0:T(8,128)(2,1)} collective-permute-done((bf16[2560,256]{1,0:T(8,128)(2,1)}, bf16[2560,256]{1,0:T(8,128)(2,1)}, u32[]{:S(2)}, u32[]{:S(2)}) %collective-permute-start.6) | collective-permute-done | bytes 1310752 | tf_op jit(solution)/shard_map/ppermute | solution.py:39
  99.3 2.5 %collective-permute-done.10.refs_4_ = bf16[2560,256]{1,0:T(8,128)(2,1)} collective-permute-done((bf16[2560,256]{1,0:T(8,128)(2,1)}, bf16[2560,256]{1,0:T(8,128)(2,1)}, u32[]{:S(2)}, u32[]{:S(2)}) %collective-permute-start.10) | collective-permute-done | bytes 1310752 | tf_op jit(solution)/shard_map/ppermute | solution.py:39
  101.8 2.3 %collective-permute-done.11.refs_5_ = bf16[2560,256]{1,0:T(8,128)(2,1)} collective-permute-done((bf16[2560,256]{1,0:T(8,128)(2,1)}, bf16[2560,256]{1,0:T(8,128)(2,1)}, u32[]{:S(2)}, u32[]{:S(2)}) %collective-permute-start.11) | collective-permute-done | bytes 1310752 | tf_op jit(solution)/shard_map/ppermute | solution.py:39
  104.2 1.3 slice.165
  105.8 1.1 slice.166
  107.0 3.1 %collective-permute-start.13 = (bf16[1280,256]{1,0:T(8,128)(2,1)S(1)}, bf16[1280,256]{1,0:T(8,128)(2,1)S(1)}, u32[]{:S(2)}, u32[]{:S(2)}) collective-permute-start(bf16[1280,256]{1,0:T(8,128)(2,1)S(1)} %slice.166), channel_id=1, source_target_pairs={{0,24},{8,0},{16,8},{24,16},{32,56},{40,32},{48,40},{56,48},{64,88... | collective-permute-start | bytes 1966088 | tf_op jit(solution)/shard_map/ppermute | solution.py:39
  110.0 1.1 slice.167
  111.8 1.1 slice.168
  112.9 1.7 collective-permute-start.15
  114.6 13.6 %project_early.1 = (f32[8,1024,128]{2,1,0:T(8,128)S(1)}, f32[4,4,256,256]{3,2,1,0:T(8,128)S(1)}) custom-call(s32[13]{0:T(128)S(1)} %copy-done.20, f32[1024,8]{1,0:T(8,128)S(1)} %broadcast_multiply_fusion.gates_ref, s32[1024,2]{1,0:T(8,128)S(1)} %copy.40.routes_ref, bf16[1024,2048]{1,0:T(8,128)(2,1)S(1)} %copy-done.2, ...), custom_call_target="tpu_custom_call" | custom-call | flops 17250000896 | bytes 1048576 | tf_op jit(solution)/shard_map/project_early/pallas_call | solution.py:171
  128.2 2.0 copy-done.3
  130.3 3.2 %collective-permute-start.17 = (bf16[2048,256]{1,0:T(8,128)(2,1)S(1)}, bf16[2048,256]{1,0:T(8,128)(2,1)S(1)}, u32[]{:S(2)}, u32[]{:S(2)}) collective-permute-start(bf16[2048,256]{1,0:T(8,128)(2,1)S(1)} %pad_maximum_fusion.refs_0_), channel_id=1, source_target_pairs={{0,24},{8,0},{16,8},{24,16},{32,56},{40,32},{48,40},{56,48},{64,88... | collective-permute-start | bytes 3145736 | tf_op jit(solution)/shard_map/ppermute | solution.py:39
  133.5 1.8 collective-permute-start.18
  135.5 1.0 copy-done.17
  136.6 18.9 %attention.1.lhs_ref = bf16[8,1024,256]{2,1,0:T(8,128)(2,1)S(1)} custom-call(s32[13]{0:T(128)S(1)} %copy-done.20, s32[1024,2]{1,0:T(8,128)S(1)} %copy-done.17, bf16[8,4,16,256]{3,2,1,0:T(8,128)(2,1)S(1)} %copy-done.19, bf16[1024,2048]{1,0:T(8,128)(2,1)S(1)} %copy-done.2, f32[4,4,256,256]{3,2,1,0:T(8,128)S(1)} %get-tuple-element.44.sums_ref, ...), custom_call_target="tpu_custom_call" | custom-call | flops 25300000768 | bytes 1048576 | tf_op jit(solution)/shard_map/attention/pallas_call | solution.py:254
  155.5 2.0 copy-done.6
  158.4 1.0 slice.176
  159.4 3.0 %collective-permute-start.21 = (bf16[1024,256]{1,0:T(8,128)(2,1)}, bf16[1024,256]{1,0:T(8,128)(2,1)}, u32[]{:S(2)}, u32[]{:S(2)}) collective-permute-start(bf16[1024,256]{1,0:T(8,128)(2,1)} %slice.176), channel_id=1, source_target_pairs={{0,24},{8,0},{16,8},{24,16},{32,56},{40,32},{48,40},{56,48},{64,88... | collective-permute-start | bytes 1572872 | tf_op jit(solution)/shard_map/ppermute | solution.py:39
  163.4 3.0 %collective-permute-start.22 = (bf16[1024,256]{1,0:T(8,128)(2,1)}, bf16[1024,256]{1,0:T(8,128)(2,1)}, u32[]{:S(2)}, u32[]{:S(2)}) collective-permute-start(bf16[1024,256]{1,0:T(8,128)(2,1)} %slice.177), channel_id=1, source_target_pairs={{0,32},{8,40},{16,48},{24,56},{32,64},{40,72},{48,80},{56,88},{64,... | collective-permute-start | bytes 1572872 | tf_op jit(solution)/shard_map/ppermute | solution.py:39
  167.2 1.9 collective-permute-done.20.refs_3_
  169.5 3.8 %collective-permute-done.22.refs_8_ = bf16[1024,256]{1,0:T(8,128)(2,1)} collective-permute-done((bf16[1024,256]{1,0:T(8,128)(2,1)}, bf16[1024,256]{1,0:T(8,128)(2,1)}, u32[]{:S(2)}, u32[]{:S(2)}) %collective-permute-start.22) | collective-permute-done | bytes 524320 | tf_op jit(solution)/shard_map/ppermute | solution.py:39
  173.3 4.5 %collective-permute-done.23.refs_9_ = bf16[1024,256]{1,0:T(8,128)(2,1)} collective-permute-done((bf16[1024,256]{1,0:T(8,128)(2,1)}, bf16[1024,256]{1,0:T(8,128)(2,1)}, u32[]{:S(2)}, u32[]{:S(2)}) %collective-permute-start.23) | collective-permute-done | bytes 524320 | tf_op jit(solution)/shard_map/ppermute | solution.py:39
  177.8 2.2 copy-done.4
  180.0 2.2 copy-done.7
  182.2 1.2 copy-done.10
  183.5 1.2 copy-done.13
  184.7 1.2 copy-done.15
  185.9 5.4 %project_out_2.2 = bf16[2,1024,256]{2,1,0:T(8,128)(2,1)S(1)} custom-call(s32[3]{0:T(128)S(1)} %pad_add_fusion.place_ref, f32[8,1024,128]{2,1,0:T(8,128)S(1)} %copy-done.4, bf16[8,1024,256]{2,1,0:T(8,128)(2,1)S(1)} %copy-done.7, bf16[2048,256]{1,0:T(8,128)(2,1)S(1)} %pad_maximum_fusion.refs_0_, bf16[2048,256]{1,0:T(8,128)(2,1)S(1)} %collective-permute-done.16.refs_1_, ...), custom_call_target="tpu_custom_call" | custom-call | flops 5750000128 | bytes 1048576 | tf_op jit(solution)/shard_map/project_out_2/pallas_call | solution.py:315
  191.3 8.4 %project_out_3.1 = bf16[3,1024,256]{2,1,0:T(8,128)(2,1)S(1)} custom-call(s32[3]{0:T(128)S(1)} %pad_add_fusion.place_ref, f32[8,1024,128]{2,1,0:T(8,128)S(1)} %copy-done.4, bf16[8,1024,256]{2,1,0:T(8,128)(2,1)S(1)} %copy-done.7, bf16[2048,256]{1,0:T(8,128)(2,1)S(1)} %pad_maximum_fusion.refs_0_, bf16[2048,256]{1,0:T(8,128)(2,1)S(1)} %collective-permute-done.16.refs_1_, ...), custom_call_target="tpu_custom_call" | custom-call | flops 8625000448 | bytes 1048576 | tf_op jit(solution)/shard_map/project_out_3/pallas_call | solution.py:315
  200.4 3.5 %collective-permute-done.24 = bf16[1024,256]{1,0:T(8,128)(2,1)S(1)} collective-permute-done((bf16[1024,256]{1,0:T(8,128)(2,1)S(1)}, bf16[1024,256]{1,0:T(8,128)(2,1)S(1)}, u32[]{:S(2)}, u32[]{:S(2)}) %collective-permute-start.24) | collective-permute-done | bytes 524320 | tf_op jit(solution)/shard_map/ppermute | solution.py:332
  204.1 1.5 collective-permute-start.26
  205.7 1.8 collective-permute-start.27
  207.5 5.6 %project_out_2.3 = bf16[2,1024,256]{2,1,0:T(8,128)(2,1)S(1)} custom-call(s32[3]{0:T(128)S(1)} %pad_add_fusion.place_ref, f32[8,1024,128]{2,1,0:T(8,128)S(1)} %copy-done.5, bf16[8,1024,256]{2,1,0:T(8,128)(2,1)S(1)} %copy-done.8, bf16[2048,256]{1,0:T(8,128)(2,1)S(1)} %pad_maximum_fusion.refs_0_, bf16[2048,256]{1,0:T(8,128)(2,1)S(1)} %collective-permute-done.16.refs_1_, ...), custom_call_target="tpu_custom_call" | custom-call | flops 5750000128 | bytes 1048576 | tf_op jit(solution)/shard_map/project_out_2/pallas_call | solution.py:315
  214.2 3.1 %collective-permute-start.29 = (bf16[1024,256]{1,0:T(8,128)(2,1)S(1)}, bf16[1024,256]{1,0:T(8,128)(2,1)S(1)}, u32[]{:S(2)}, u32[]{:S(2)}) collective-permute-start(bf16[1024,256]{1,0:T(8,128)(2,1)S(1)} %pad_maximum_fusion.5), channel_id=1, source_target_pairs={{0,6},{1,7},{2,0},{3,1},{4,2},{5,3},{6,4},{7,5},{8,14},{9,15},{10,... | collective-permute-start | bytes 1572872 | tf_op jit(solution)/shard_map/ppermute | solution.py:333
  217.4 2.8 %project_out_1.1 = bf16[1,1024,256]{2,1,0:T(8,128)(2,1)S(1)} custom-call(s32[3]{0:T(128)S(1)} %pad_add_fusion.place_ref, f32[8,1024,128]{2,1,0:T(8,128)S(1)} %copy-done.5, bf16[8,1024,256]{2,1,0:T(8,128)(2,1)S(1)} %copy-done.8, bf16[2048,256]{1,0:T(8,128)(2,1)S(1)} %pad_maximum_fusion.refs_0_, bf16[2048,256]{1,0:T(8,128)(2,1)S(1)} %collective-permute-done.16.refs_1_, ...), custom_call_target="tpu_custom_call" | custom-call | flops 2875000064 | bytes 1048576 | tf_op jit(solution)/shard_map/project_out_1/pallas_call | solution.py:315
  220.3 7.7 %collective-permute-done.29 = bf16[1024,256]{1,0:T(8,128)(2,1)S(1)} collective-permute-done((bf16[1024,256]{1,0:T(8,128)(2,1)S(1)}, bf16[1024,256]{1,0:T(8,128)(2,1)S(1)}, u32[]{:S(2)}, u32[]{:S(2)}) %collective-permute-start.29) | collective-permute-done | bytes 524320 | tf_op jit(solution)/shard_map/ppermute | solution.py:333
  227.9 3.5 %collective-permute-done.28 = bf16[1024,256]{1,0:T(8,128)(2,1)S(1)} collective-permute-done((bf16[1024,256]{1,0:T(8,128)(2,1)S(1)}, bf16[1024,256]{1,0:T(8,128)(2,1)S(1)}, u32[]{:S(2)}, u32[]{:S(2)}) %collective-permute-start.28) | collective-permute-done | bytes 524320 | tf_op jit(solution)/shard_map/ppermute | solution.py:333
  231.5 1.1 fusion.2
  (146 shorter events, 19.2 us)
Async XLA Ops:
  0.0 16.1 %copy-start = (bf16[4,2048,16]{1,2,0:T(8,128)(2,1)S(1)}, bf16[4,2048,16]{1,2,0:T(8,128)(2,1)}, u32[]{:S(2)}) copy-start(bf16[4,2048,16]{1,2,0:T(8,128)(2,1)} %param.25) | copy-start | bytes 786436
  1.5 1.5 copy-start.26
  4.6 7.9 %copy-start.32 = (s32[64]{0:T(128)S(1)}, s32[64]{0:T(128)}, u32[]{:S(2)}) copy-start(s32[64]{0:T(128)} %param.18) | copy-start | bytes 772
  4.6 8.0 %copy-start.29 = (bf16[2048,8]{0,1:T(8,128)(2,1)S(1)}, bf16[2048,8]{0,1:T(8,128)(2,1)}, u32[]{:S(2)}) copy-start(bf16[2048,8]{0,1:T(8,128)(2,1)} %param.21) | copy-start | bytes 98308
  5.5 15.3 %collective-permute-start = (bf16[1152,256]{1,0:T(8,128)(2,1)}, bf16[1152,256]{1,0:T(8,128)(2,1)S(1)}, u32[]{:S(2)}, u32[]{:S(2)}) collective-permute-start(bf16[1152,256]{1,0:T(8,128)(2,1)} %pad_maximum_fusion.2), channel_id=1, source_target_pairs={{0,32},{8,40},{16,48},{24,56},{32,64},{40,72},{48,80},{56,88},{64,... | collective-permute-start | bytes 1769480 | tf_op jit(solution)/shard_map/ppermute | solution.py:39
  5.9 16.1 %collective-permute-start.1 = (bf16[1152,256]{1,0:T(8,128)(2,1)}, bf16[1152,256]{1,0:T(8,128)(2,1)S(1)}, u32[]{:S(2)}, u32[]{:S(2)}) collective-permute-start(bf16[1152,256]{1,0:T(8,128)(2,1)} %pad_maximum_fusion.2), channel_id=1, source_target_pairs={{0,96},{8,104},{16,112},{24,120},{32,0},{40,8},{48,16},{56,24},{64... | collective-permute-start | bytes 1769480 | tf_op jit(solution)/shard_map/ppermute | solution.py:39
  8.5 17.0 %collective-permute-start.2 = (bf16[1152,256]{1,0:T(8,128)(2,1)}, bf16[1152,256]{1,0:T(8,128)(2,1)S(1)}, u32[]{:S(2)}, u32[]{:S(2)}) collective-permute-start(bf16[1152,256]{1,0:T(8,128)(2,1)} %pad_maximum_fusion.3), channel_id=1, source_target_pairs={{0,8},{8,16},{16,24},{24,0},{32,40},{40,48},{48,56},{56,32},{64,72... | collective-permute-start | bytes 1769480 | tf_op jit(solution)/shard_map/ppermute | solution.py:39
  10.4 15.1 %collective-permute-start.3 = (bf16[1152,256]{1,0:T(8,128)(2,1)}, bf16[1152,256]{1,0:T(8,128)(2,1)}, u32[]{:S(2)}, u32[]{:S(2)}) collective-permute-start(bf16[1152,256]{1,0:T(8,128)(2,1)} %pad_maximum_fusion.3), channel_id=1, source_target_pairs={{0,24},{8,0},{16,8},{24,16},{32,56},{40,32},{48,40},{56,48},{64,88... | collective-permute-start | bytes 1769480 | tf_op jit(solution)/shard_map/ppermute | solution.py:39
  12.6 3.4 %copy-start.28 = (s32[1024,2]{0,1:T(2,128)S(1)}, s32[1024,2]{0,1:T(2,128)}, u32[]{:S(2)}) copy-start(s32[1024,2]{0,1:T(2,128)} %param.15) | copy-start | bytes 24580
  17.6 97.1 %copy-start.16 = (s32[1024,2]{1,0:T(8,128)}, s32[1024,2]{1,0:T(8,128)S(1)}, u32[]{:S(2)}) copy-start(s32[1024,2]{1,0:T(8,128)S(1)} %copy.40.routes_ref) | copy-start | bytes 24580
  20.8 55.8 %copy-start.22 = (bf16[1152,256]{1,0:T(8,128)(2,1)}, bf16[1152,256]{1,0:T(8,128)(2,1)S(1)}, u32[]{:S(2)}) copy-start(bf16[1152,256]{1,0:T(8,128)(2,1)S(1)} %collective-permute-done) | copy-start | bytes 1769476
  22.0 3.5 %copy-start.24 = (bf16[1152,256]{1,0:T(8,128)(2,1)}, bf16[1152,256]{1,0:T(8,128)(2,1)S(1)}, u32[]{:S(2)}) copy-start(bf16[1152,256]{1,0:T(8,128)(2,1)S(1)} %collective-permute-done.1) | copy-start | bytes 1769476
  25.5 9.4 %copy-start.23 = (bf16[1152,256]{1,0:T(8,128)(2,1)}, bf16[1152,256]{1,0:T(8,128)(2,1)S(1)}, u32[]{:S(2)}) copy-start(bf16[1152,256]{1,0:T(8,128)(2,1)S(1)} %collective-permute-done.2) | copy-start | bytes 1769476
  25.5 55.3 %all-to-all-start = ((bf16[16,160,512]{2,1,0:T(8,128)(2,1)}), bf16[16,160,512]{2,1,0:T(8,128)(2,1)}, u32[]{:S(2)}, u32[]{:S(2)}) async-start(bf16[16,160,512]{2,1,0:T(8,128)(2,1)} %pack.1), calls=%async_computation | async-start | bytes 5242880 | tf_op jit(solution)/shard_map/all_to_all | solution.py:388
  33.0 33.9 %collective-permute-start.4 = (bf16[576,256]{1,0:T(8,128)(2,1)S(1)}, bf16[576,256]{1,0:T(8,128)(2,1)S(1)}, u32[]{:S(2)}, u32[]{:S(2)}) collective-permute-start(bf16[576,256]{1,0:T(8,128)(2,1)S(1)} %slice.157), channel_id=1, source_target_pairs={{0,32},{8,40},{16,48},{24,56},{32,64},{40,72},{48,80},{56,88},{64,... | collective-permute-start | bytes 884744 | tf_op jit(solution)/shard_map/ppermute | solution.py:39
  35.0 40.6 %copy-start.30 = (s32[4]{0:T(128)S(1)}, s32[4]{0:T(128)}, u32[]{:S(2)}) copy-start(s32[4]{0:T(128)} %param.16) | copy-start | bytes 52
  35.0 40.6 %copy-start.33 = (s32[64]{0:T(128)S(1)}, s32[64]{0:T(128)}, u32[]{:S(2)}) copy-start(s32[64]{0:T(128)} %param.20) | copy-start | bytes 772
  35.0 40.6 %copy-start.34 = (s32[4]{0:T(128)S(1)}, s32[4]{0:T(128)}, u32[]{:S(2)}) copy-start(s32[4]{0:T(128)} %param.19) | copy-start | bytes 52
  35.0 40.8 %copy-start.31 = (s32[4]{0:T(128)S(1)}, s32[4]{0:T(128)}, u32[]{:S(2)}) copy-start(s32[4]{0:T(128)} %param.17) | copy-start | bytes 52
  35.0 32.7 %collective-permute-start.5 = (bf16[576,256]{1,0:T(8,128)(2,1)S(1)}, bf16[576,256]{1,0:T(8,128)(2,1)S(1)}, u32[]{:S(2)}, u32[]{:S(2)}) collective-permute-start(bf16[576,256]{1,0:T(8,128)(2,1)S(1)} %slice.158), channel_id=1, source_target_pairs={{0,96},{8,104},{16,112},{24,120},{32,0},{40,8},{48,16},{56,24},{64... | collective-permute-start | bytes 884744 | tf_op jit(solution)/shard_map/ppermute | solution.py:39
  37.0 34.6 %collective-permute-start.8 = (bf16[576,256]{1,0:T(8,128)(2,1)S(1)}, bf16[576,256]{1,0:T(8,128)(2,1)S(1)}, u32[]{:S(2)}, u32[]{:S(2)}) collective-permute-start(bf16[576,256]{1,0:T(8,128)(2,1)S(1)} %slice.162), channel_id=1, source_target_pairs={{0,8},{8,16},{16,24},{24,0},{32,40},{40,48},{48,56},{56,32},{64,72... | collective-permute-start | bytes 884744 | tf_op jit(solution)/shard_map/ppermute | solution.py:39
  39.4 32.9 %collective-permute-start.9 = (bf16[576,256]{1,0:T(8,128)(2,1)S(1)}, bf16[576,256]{1,0:T(8,128)(2,1)S(1)}, u32[]{:S(2)}, u32[]{:S(2)}) collective-permute-start(bf16[576,256]{1,0:T(8,128)(2,1)S(1)} %slice.163), channel_id=1, source_target_pairs={{0,24},{8,0},{16,8},{24,16},{32,56},{40,32},{48,40},{56,48},{64,88... | collective-permute-start | bytes 884744 | tf_op jit(solution)/shard_map/ppermute | solution.py:39
  68.3 30.7 %collective-permute-start.6 = (bf16[2560,256]{1,0:T(8,128)(2,1)}, bf16[2560,256]{1,0:T(8,128)(2,1)}, u32[]{:S(2)}, u32[]{:S(2)}) collective-permute-start(bf16[2560,256]{1,0:T(8,128)(2,1)} %slice_dynamic-update-slice_fusion.5.refs_0_), channel_id=1, source_target_pairs={{0,8},{8,16},{16,24},{24,0},{32,40},{40,48},{48,56},{56,32},{64,72... | collective-permute-start | bytes 3932168 | tf_op jit(solution)/shard_map/ppermute | solution.py:39
  69.8 29.6 %collective-permute-start.7 = (bf16[2560,256]{1,0:T(8,128)(2,1)}, bf16[2560,256]{1,0:T(8,128)(2,1)}, u32[]{:S(2)}, u32[]{:S(2)}) collective-permute-start(bf16[2560,256]{1,0:T(8,128)(2,1)} %slice_dynamic-update-slice_fusion.5.refs_0_), channel_id=1, source_target_pairs={{0,24},{8,0},{16,8},{24,16},{32,56},{40,32},{48,40},{56,48},{64,88... | collective-permute-start | bytes 3932168 | tf_op jit(solution)/shard_map/ppermute | solution.py:39
  72.9 28.9 %collective-permute-start.10 = (bf16[2560,256]{1,0:T(8,128)(2,1)}, bf16[2560,256]{1,0:T(8,128)(2,1)}, u32[]{:S(2)}, u32[]{:S(2)}) collective-permute-start(bf16[2560,256]{1,0:T(8,128)(2,1)} %slice_dynamic-update-slice_fusion.4.refs_3_), channel_id=1, source_target_pairs={{0,32},{8,40},{16,48},{24,56},{32,64},{40,72},{48,80},{56,88},{64,... | collective-permute-start | bytes 3932168 | tf_op jit(solution)/shard_map/ppermute | solution.py:39
  75.5 28.7 %collective-permute-start.11 = (bf16[2560,256]{1,0:T(8,128)(2,1)}, bf16[2560,256]{1,0:T(8,128)(2,1)}, u32[]{:S(2)}, u32[]{:S(2)}) collective-permute-start(bf16[2560,256]{1,0:T(8,128)(2,1)} %slice_dynamic-update-slice_fusion.4.refs_3_), channel_id=1, source_target_pairs={{0,96},{8,104},{16,112},{24,120},{32,0},{40,8},{48,16},{56,24},{64... | collective-permute-start | bytes 3932168 | tf_op jit(solution)/shard_map/ppermute | solution.py:39
  76.6 4.2 %slice-start.1 = ((bf16[1152,256]{1,0:T(8,128)(2,1)}), bf16[512,256]{1,0:T(8,128)(2,1)S(1)}, s32[]{:S(2)}) async-start(bf16[1152,256]{1,0:T(8,128)(2,1)} %copy-done.24), calls=%async_computation.3 | async-start | bytes 524288 | tf_op jit(solution)/shard_map/slice | solution.py:411
  76.6 4.2 %slice-start = ((bf16[1152,256]{1,0:T(8,128)(2,1)}), bf16[512,256]{1,0:T(8,128)(2,1)S(1)}, s32[]{:S(2)}) async-start(bf16[1152,256]{1,0:T(8,128)(2,1)} %copy-done.22), calls=%async_computation.2 | async-start | bytes 524288 | tf_op jit(solution)/shard_map/slice | solution.py:410
  84.4 19.8 %all-to-all-start.1 = ((bf16[8,4,16,256]{3,2,1,0:T(8,128)(2,1)}), bf16[8,4,16,256]{3,2,1,0:T(8,128)(2,1)S(1)}, u32[]{:S(2)}, u32[]{:S(2)}) async-start(bf16[8,4,16,256]{3,2,1,0:T(8,128)(2,1)} %broadcast_in_dim.2), calls=%async_computation.1 | async-start | bytes 524288 | tf_op jit(solution)/shard_map/all_to_all | solution.py:437
  104.2 2.7 %copy-start.18 = (bf16[8,4,16,256]{3,2,1,0:T(8,128)(2,1)}, bf16[8,4,16,256]{3,2,1,0:T(8,128)(2,1)S(1)}, u32[]{:S(2)}) copy-start(bf16[8,4,16,256]{3,2,1,0:T(8,128)(2,1)S(1)} %all-to-all-done.1.down_ref) | copy-start | bytes 786436
  104.2 10.4 %copy-start.2 = (bf16[1024,2048]{1,0:T(8,128)(2,1)S(1)}, bf16[1024,2048]{1,0:T(8,128)(2,1)}, u32[]{:S(2)}) copy-start(bf16[1024,2048]{1,0:T(8,128)(2,1)} %x_ref.3) | copy-start | bytes 12582916
  105.5 24.7 %collective-permute-start.12 = (bf16[1280,256]{1,0:T(8,128)(2,1)S(1)}, bf16[1280,256]{1,0:T(8,128)(2,1)S(1)}, u32[]{:S(2)}, u32[]{:S(2)}) collective-permute-start(bf16[1280,256]{1,0:T(8,128)(2,1)S(1)} %slice.165), channel_id=1, source_target_pairs={{0,8},{8,16},{16,24},{24,0},{32,40},{40,48},{48,56},{56,32},{64,72... | collective-permute-start | bytes 1966088 | tf_op jit(solution)/shard_map/ppermute | solution.py:39
  106.9 7.7 %copy-start.20 = (s32[13]{0:T(128)S(1)}, s32[13]{0:T(128)}, u32[]{:S(2)}) copy-start(s32[13]{0:T(128)} %pad_add_fusion.1.info_ref) | copy-start | bytes 160
  107.0 23.2 %collective-permute-start.13 = (bf16[1280,256]{1,0:T(8,128)(2,1)S(1)}, bf16[1280,256]{1,0:T(8,128)(2,1)S(1)}, u32[]{:S(2)}, u32[]{:S(2)}) collective-permute-start(bf16[1280,256]{1,0:T(8,128)(2,1)S(1)} %slice.166), channel_id=1, source_target_pairs={{0,24},{8,0},{16,8},{24,16},{32,56},{40,32},{48,40},{56,48},{64,88... | collective-permute-start | bytes 1966088 | tf_op jit(solution)/shard_map/ppermute | solution.py:39
  111.1 19.1 %collective-permute-start.14 = (bf16[1280,256]{1,0:T(8,128)(2,1)S(1)}, bf16[1280,256]{1,0:T(8,128)(2,1)S(1)}, u32[]{:S(2)}, u32[]{:S(2)}) collective-permute-start(bf16[1280,256]{1,0:T(8,128)(2,1)S(1)} %slice.167), channel_id=1, source_target_pairs={{0,32},{8,40},{16,48},{24,56},{32,64},{40,72},{48,80},{56,88},{64,... | collective-permute-start | bytes 1966088 | tf_op jit(solution)/shard_map/ppermute | solution.py:39
  112.9 22.6 %copy-start.19 = (bf16[8,4,16,256]{3,2,1,0:T(8,128)(2,1)S(1)}, bf16[8,4,16,256]{3,2,1,0:T(8,128)(2,1)}, u32[]{:S(2)}) copy-start(bf16[8,4,16,256]{3,2,1,0:T(8,128)(2,1)} %copy-done.18) | copy-start | bytes 786436
  112.9 17.3 %collective-permute-start.15 = (bf16[1280,256]{1,0:T(8,128)(2,1)S(1)}, bf16[1280,256]{1,0:T(8,128)(2,1)S(1)}, u32[]{:S(2)}, u32[]{:S(2)}) collective-permute-start(bf16[1280,256]{1,0:T(8,128)(2,1)S(1)} %slice.168), channel_id=1, source_target_pairs={{0,96},{8,104},{16,112},{24,120},{32,0},{40,8},{48,16},{56,24},{64... | collective-permute-start | bytes 1966088 | tf_op jit(solution)/shard_map/ppermute | solution.py:39
  128.2 2.0 copy-start.3
  130.2 27.3 %collective-permute-start.16 = (bf16[2048,256]{1,0:T(8,128)(2,1)S(1)}, bf16[2048,256]{1,0:T(8,128)(2,1)S(1)}, u32[]{:S(2)}, u32[]{:S(2)}) collective-permute-start(bf16[2048,256]{1,0:T(8,128)(2,1)S(1)} %pad_maximum_fusion.refs_0_), channel_id=1, source_target_pairs={{0,8},{8,16},{16,24},{24,0},{32,40},{40,48},{48,56},{56,32},{64,72... | collective-permute-start | bytes 3145736 | tf_op jit(solution)/shard_map/ppermute | solution.py:39
  130.3 27.2 %collective-permute-start.17 = (bf16[2048,256]{1,0:T(8,128)(2,1)S(1)}, bf16[2048,256]{1,0:T(8,128)(2,1)S(1)}, u32[]{:S(2)}, u32[]{:S(2)}) collective-permute-start(bf16[2048,256]{1,0:T(8,128)(2,1)S(1)} %pad_maximum_fusion.refs_0_), channel_id=1, source_target_pairs={{0,24},{8,0},{16,8},{24,16},{32,56},{40,32},{48,40},{56,48},{64,88... | collective-permute-start | bytes 3145736 | tf_op jit(solution)/shard_map/ppermute | solution.py:39
  133.5 24.0 %collective-permute-start.18 = (bf16[2048,256]{1,0:T(8,128)(2,1)S(1)}, bf16[2048,256]{1,0:T(8,128)(2,1)S(1)}, u32[]{:S(2)}, u32[]{:S(2)}) collective-permute-start(bf16[2048,256]{1,0:T(8,128)(2,1)S(1)} %pad_maximum_fusion.1.refs_5_), channel_id=1, source_target_pairs={{0,32},{8,40},{16,48},{24,56},{32,64},{40,72},{48,80},{56,88},{64,... | collective-permute-start | bytes 3145736 | tf_op jit(solution)/shard_map/ppermute | solution.py:39
  135.3 22.2 %collective-permute-start.19 = (bf16[2048,256]{1,0:T(8,128)(2,1)S(1)}, bf16[2048,256]{1,0:T(8,128)(2,1)S(1)}, u32[]{:S(2)}, u32[]{:S(2)}) collective-permute-start(bf16[2048,256]{1,0:T(8,128)(2,1)S(1)} %pad_maximum_fusion.1.refs_5_), channel_id=1, source_target_pairs={{0,96},{8,104},{16,112},{24,120},{32,0},{40,8},{48,16},{56,24},{64... | collective-permute-start | bytes 3145736 | tf_op jit(solution)/shard_map/ppermute | solution.py:39
  155.5 2.0 copy-start.6
  157.5 5.9 %copy-start.9 = (bf16[2048,256]{1,0:T(8,128)(2,1)}, bf16[2048,256]{1,0:T(8,128)(2,1)S(1)}, u32[]{:S(2)}) copy-start(bf16[2048,256]{1,0:T(8,128)(2,1)S(1)} %collective-permute-done.17.refs_2_) | copy-start | bytes 3145732
  157.5 5.9 %copy-start.12 = (bf16[2048,256]{1,0:T(8,128)(2,1)}, bf16[2048,256]{1,0:T(8,128)(2,1)S(1)}, u32[]{:S(2)}) copy-start(bf16[2048,256]{1,0:T(8,128)(2,1)S(1)} %collective-permute-done.18.refs_6_) | copy-start | bytes 3145732
  157.5 8.8 %copy-start.14 = (bf16[2048,256]{1,0:T(8,128)(2,1)}, bf16[2048,256]{1,0:T(8,128)(2,1)S(1)}, u32[]{:S(2)}) copy-start(bf16[2048,256]{1,0:T(8,128)(2,1)S(1)} %collective-permute-done.19.refs_7_) | copy-start | bytes 3145732
  158.4 10.7 %collective-permute-start.20 = (bf16[1024,256]{1,0:T(8,128)(2,1)}, bf16[1024,256]{1,0:T(8,128)(2,1)}, u32[]{:S(2)}, u32[]{:S(2)}) collective-permute-start(bf16[1024,256]{1,0:T(8,128)(2,1)} %slice.175), channel_id=1, source_target_pairs={{0,8},{8,16},{16,24},{24,0},{32,40},{40,48},{48,56},{56,32},{64,72... | collective-permute-start | bytes 1572872 | tf_op jit(solution)/shard_map/ppermute | solution.py:39
  159.4 10.1 %collective-permute-start.21 = (bf16[1024,256]{1,0:T(8,128)(2,1)}, bf16[1024,256]{1,0:T(8,128)(2,1)}, u32[]{:S(2)}, u32[]{:S(2)}) collective-permute-start(bf16[1024,256]{1,0:T(8,128)(2,1)} %slice.176), channel_id=1, source_target_pairs={{0,24},{8,0},{16,8},{24,16},{32,56},{40,32},{48,40},{56,48},{64,88... | collective-permute-start | bytes 1572872 | tf_op jit(solution)/shard_map/ppermute | solution.py:39
  163.4 10.0 %collective-permute-start.22 = (bf16[1024,256]{1,0:T(8,128)(2,1)}, bf16[1024,256]{1,0:T(8,128)(2,1)}, u32[]{:S(2)}, u32[]{:S(2)}) collective-permute-start(bf16[1024,256]{1,0:T(8,128)(2,1)} %slice.177), channel_id=1, source_target_pairs={{0,32},{8,40},{16,48},{24,56},{32,64},{40,72},{48,80},{56,88},{64,... | collective-permute-start | bytes 1572872 | tf_op jit(solution)/shard_map/ppermute | solution.py:39
  167.1 10.7 %collective-permute-start.23 = (bf16[1024,256]{1,0:T(8,128)(2,1)}, bf16[1024,256]{1,0:T(8,128)(2,1)}, u32[]{:S(2)}, u32[]{:S(2)}) collective-permute-start(bf16[1024,256]{1,0:T(8,128)(2,1)} %slice.178), channel_id=1, source_target_pairs={{0,96},{8,104},{16,112},{24,120},{32,0},{40,8},{48,16},{56,24},{64... | collective-permute-start | bytes 1572872 | tf_op jit(solution)/shard_map/ppermute | solution.py:39
  177.8 2.2 copy-start.4
  180.0 2.2 copy-start.7
  182.2 1.2 copy-start.10
  183.4 1.2 copy-start.13
  185.9 5.4 %copy-start.11 = (bf16[2048,256]{1,0:T(8,128)(2,1)S(1)}, bf16[2048,256]{1,0:T(8,128)(2,1)}, u32[]{:S(2)}) copy-start(bf16[2048,256]{1,0:T(8,128)(2,1)} %copy-done.9) | copy-start | bytes 3145732
  191.3 16.2 %copy-start.5 = (f32[8,1024,128]{2,1,0:T(8,128)S(1)}, f32[8,1024,128]{2,1,0:T(8,128)}, u32[]{:S(2)}) copy-start(f32[8,1024,128]{2,1,0:T(8,128)} %copy-done.3) | copy-start | bytes 12582916
  191.3 16.2 %copy-start.8 = (bf16[8,1024,256]{2,1,0:T(8,128)(2,1)S(1)}, bf16[8,1024,256]{2,1,0:T(8,128)(2,1)}, u32[]{:S(2)}) copy-start(bf16[8,1024,256]{2,1,0:T(8,128)(2,1)} %copy-done.6) | copy-start | bytes 12582916
  199.7 13.3 %collective-permute-start.25 = (bf16[3,1024,256]{2,1,0:T(8,128)(2,1)S(1)}, bf16[3,1024,256]{2,1,0:T(8,128)(2,1)S(1)}, u32[]{:S(2)}, u32[]{:S(2)}) collective-permute-start(bf16[3,1024,256]{2,1,0:T(8,128)(2,1)S(1)} %project_out_3.1), channel_id=1, source_target_pairs={{0,1},{1,0},{2,3},{3,2},{4,5},{5,4},{6,7},{7,6},{8,9},{9,8},{10,11... | collective-permute-start | bytes 4718600 | tf_op jit(solution)/shard_map/ppermute | solution.py:332
  199.8 4.1 %collective-permute-start.24 = (bf16[1024,256]{1,0:T(8,128)(2,1)S(1)}, bf16[1024,256]{1,0:T(8,128)(2,1)S(1)}, u32[]{:S(2)}, u32[]{:S(2)}) collective-permute-start(bf16[1024,256]{1,0:T(8,128)(2,1)S(1)} %slice_bitcast_fusion), channel_id=1, source_target_pairs={{0,1},{1,0},{2,3},{3,2},{4,5},{5,4},{6,7},{7,6},{8,9},{9,8},{10,11... | collective-permute-start | bytes 1572872 | tf_op jit(solution)/shard_map/ppermute | solution.py:332
  204.1 9.8 %collective-permute-start.26 = (bf16[512,256]{1,0:T(8,128)(2,1)S(1)}, bf16[512,256]{1,0:T(8,128)(2,1)S(1)}, u32[]{:S(2)}, u32[]{:S(2)}) collective-permute-start(bf16[512,256]{1,0:T(8,128)(2,1)S(1)} %get-tuple-element.61), channel_id=1, source_target_pairs={{0,2},{1,3},{2,4},{3,5},{4,6},{5,7},{6,0},{7,1},{8,10},{9,11},{10,... | collective-permute-start | bytes 786440 | tf_op jit(solution)/shard_map/ppermute | solution.py:333
  205.7 8.3 %collective-permute-start.27 = (bf16[512,256]{1,0:T(8,128)(2,1)S(1)}, bf16[512,256]{1,0:T(8,128)(2,1)S(1)}, u32[]{:S(2)}, u32[]{:S(2)}) collective-permute-start(bf16[512,256]{1,0:T(8,128)(2,1)S(1)} %get-tuple-element.62), channel_id=1, source_target_pairs={{0,6},{1,7},{2,0},{3,1},{4,2},{5,3},{6,4},{7,5},{8,14},{9,15},{10,... | collective-permute-start | bytes 786440 | tf_op jit(solution)/shard_map/ppermute | solution.py:333
  214.2 13.7 %collective-permute-start.29 = (bf16[1024,256]{1,0:T(8,128)(2,1)S(1)}, bf16[1024,256]{1,0:T(8,128)(2,1)S(1)}, u32[]{:S(2)}, u32[]{:S(2)}) collective-permute-start(bf16[1024,256]{1,0:T(8,128)(2,1)S(1)} %pad_maximum_fusion.5), channel_id=1, source_target_pairs={{0,6},{1,7},{2,0},{3,1},{4,2},{5,3},{6,4},{7,5},{8,14},{9,15},{10,... | collective-permute-start | bytes 1572872 | tf_op jit(solution)/shard_map/ppermute | solution.py:333
  217.4 14.1 %collective-permute-start.28 = (bf16[1024,256]{1,0:T(8,128)(2,1)S(1)}, bf16[1024,256]{1,0:T(8,128)(2,1)S(1)}, u32[]{:S(2)}, u32[]{:S(2)}) collective-permute-start(bf16[1024,256]{1,0:T(8,128)(2,1)S(1)} %pad_maximum_fusion.4), channel_id=1, source_target_pairs={{0,2},{1,3},{2,4},{3,5},{4,6},{5,7},{6,0},{7,1},{8,10},{9,11},{10,... | collective-permute-start | bytes 1572872 | tf_op jit(solution)/shard_map/ppermute | solution.py:333
  217.4 15.1 %copy-start.1 = (bf16[4,2048,16]{1,2,0:T(8,128)(2,1)S(1)}, bf16[4,2048,16]{1,2,0:T(8,128)(2,1)}, u32[]{:S(2)}) copy-start(bf16[4,2048,16]{1,2,0:T(8,128)(2,1)} %param.25) | copy-start | bytes 786436
  (5 other events, 5.3 us)

commit v2 on v1

--- a/solution.py
+++ b/solution.py
@@ -16,10 +16,10 @@
 NEG = -1e30
 adapter_scale = 0.5
 
-ROW_KV = 512
-SHARD_ROWS = 640
+ROW_KV, ROW_UP = 512, 640
+SHARD_ROWS = 704
 OUT_ROWS = 512
-ROW_UP, ROW_DN, SENT_ROWS = 64, 128, 160
+ROW_DN, SENT_ROWS = 64, 96
 PLACES = []
 for _piece, _off in ((0, 0), (1, -1), (2, 1)):
     for _i, _near in enumerate((0, -1, 1, 2)):
@@ -43,11 +43,6 @@
     return send(value, along, 1), send(value, along, -1)
 
 
-def second_step(before, after, along):
-    half = before.shape[0] // 2
-    return send(before[:half], along, 1), send(after[half:], along, -1)
-
-
 def source(group, half, first, second):
     x, z = group // SIDE, group % SIDE
     dx, dz = (first, second) if half == 0 else (second, first)
@@ -63,10 +58,9 @@
 SCALARS = pl.BlockSpec(memory_space=pltpu.SMEM)
 
 
-def pack_kernel(index_ref, store_ref, up_ref, down_ref, out_ref):
+def pack_kernel(index_ref, store_ref, down_ref, out_ref):
     def one(i, carry):
-        out_ref[i, 0:ROW_UP, :] = store_ref[index_ref[i]]
-        out_ref[i, ROW_UP:ROW_DN, :] = up_ref[...]
+        out_ref[i, 0:ROW_DN, :] = store_ref[index_ref[i]]
         for side in range(2):
             out_ref[i, ROW_DN:SENT_ROWS, side * 256 : side * 256 + 256] = down_ref[
                 side * 32 : side * 32 + 32, :
@@ -76,15 +70,15 @@
     lax.fori_loop(0, out_ref.shape[0], one, 0)
 
 
-def pack(index, store, up, down):
+def pack(index, store, down):
     return pl.pallas_call(
         pack_kernel,
         out_shape=jax.ShapeDtypeStruct((16, SENT_ROWS, 512), BF),
-        in_specs=[SCALARS] + [WHOLE] * 3,
+        in_specs=[SCALARS] + [WHOLE] * 2,
         out_specs=WHOLE,
         cost_estimate=cost(3),
         name="pack",
-    )(index, store, up, down)
+    )(index, store, down)
 
 
 def pick_down_kernel(info_ref, recv_ref, out_ref, sem):
@@ -146,12 +140,26 @@
     return chosen, product(ROW_KV)
 
 
-def early_kernel(info_ref, gates_ref, routes_ref, x_ref, *refs):
+def pick_up(info_ref, pieces, shards, up_ref):
+    count = len(pieces) // 2
+    for half in range(2):
+        for piece, shard, first, second in shards:
+            owner = source(info_ref[0], half, first, second)
+            for j in range(4):
+                slot = info_ref[1 + j]
+
+                @pl.when(slot // 4 == owner)
+                def _(half=half, piece=piece, shard=shard, j=j, slot=slot):
+                    start = pl.multiple_of(shard * SHARD_ROWS + ROW_UP + slot % 4 * 16, 16)
+                    up_ref[j, half] = pieces[half * count + piece][pl.ds(start, 16), :]
+
+
+def early_kernel(info_ref, routes_ref, x_ref, *refs):
     pieces = refs[:6]
-    wide_ref, sums_ref = refs[6:]
+    up_ref, sums_ref = refs[6:]
     group = info_ref[0]
-    for e in range(NE):
-        wide_ref[e] = jnp.broadcast_to(gates_ref[:, e : e + 1], (1024, 128))
+    up_ref[...] = jnp.zeros_like(up_ref)
+    pick_up(info_ref, pieces, EARLY, up_ref)
 
     def block(j, carry):
         rows = pl.ds(pl.multiple_of(j * 256, 256), 256)
@@ -167,38 +175,34 @@
     lax.fori_loop(0, 4, block, 0)
 
 
-def project_early(info, gates, routes, x, pieces):
+def project_early(info, routes, x, pieces):
     return pl.pallas_call(
         early_kernel,
         out_shape=(
-            jax.ShapeDtypeStruct((NE, 1024, 128), F32),
+            jax.ShapeDtypeStruct((4, 2, 16, 256), BF),
             jax.ShapeDtypeStruct((4, 4, 256, 256), F32),
         ),
-        in_specs=[SCALARS] + [WHOLE] * 9,
+        in_specs=[SCALARS] + [WHOLE] * 8,
         out_specs=(WHOLE, WHOLE),
-        compiler_params=pltpu.CompilerParams(vmem_limit_bytes=10 * 2**20),
+        compiler_params=pltpu.CompilerParams(vmem_limit_bytes=20 * 2**20),
         cost_estimate=cost(15),
         name="project_early",
-    )(info, gates, routes, x, *pieces)
-
-
-def attend_kernel(info_ref, routes_ref, down_ref, x_ref, sums_ref, recv_hbm, *refs):
+    )(info, routes, x, *pieces)
+
+
+def attend_kernel(info_ref, routes_ref, down_ref, x_ref, up_ref, sums_ref, recv_hbm, *refs):
     pieces = refs[:4]
     out_ref, sums, up, cache, sem = refs[4:]
     group = info_ref[0]
     for j in range(4):
-        slot = info_ref[1 + j]
-        start = pl.multiple_of(ROW_UP + (slot % 4) * 16, 16)
         pltpu.make_async_copy(
-            recv_hbm.at[slot // 4, pl.ds(start, 16), :], up.at[j], sem.at[0, j]
+            recv_hbm.at[info_ref[5 + j], pl.ds(0, 64), :], cache.at[j], sem.at[j]
         ).start()
-        pltpu.make_async_copy(
-            recv_hbm.at[info_ref[5 + j], pl.ds(0, 64), :], cache.at[j], sem.at[1, j]
-        ).start()
+    up[...] = up_ref[...]
+    pick_up(info_ref, pieces, LATE, up)
 
     def attend(j, carry):
-        for i, ref in enumerate((up, cache)):
-            pltpu.make_async_copy(ref.at[j], ref.at[j], sem.at[i, j]).wait()
+        pltpu.make_async_copy(cache.at[j], cache.at[j], sem.at[j]).wait()
         rows = pl.ds(pl.multiple_of(j * 256, 256), 256)
         x, routes = x_ref.at[rows, :], routes_ref.at[rows, :]
         for half in range(2):
@@ -217,7 +221,7 @@
         allowed = (place < cached_length) | ((place >= 64) & (place - 64 <= query_at))
         for h in range(2):
             cols = slice(h * HD, (h + 1) * HD)
-            extra = jnp.dot(low, up[j, :, h * 256 : h * 256 + 256], preferred_element_type=F32)
+            extra = jnp.dot(low, up[j, h], preferred_element_type=F32)
             fresh = (sums[2 + h] + adapter_scale * extra).astype(BF)
             keys = jnp.concatenate(
                 [cache[j, :, h * 256 : h * 256 + HD], fresh[:, 0:HD]], axis=0
@@ -250,27 +254,27 @@
     lax.fori_loop(0, 4, attend, 0)
 
 
-def attention(info, routes, down, x, sums, recv, pieces):
+def attention(info, routes, down, x, up, sums, recv, pieces):
     return pl.pallas_call(
         attend_kernel,
         out_shape=jax.ShapeDtypeStruct((NE, 1024, 256), BF),
-        in_specs=[SCALARS] + [WHOLE] * 4 + [ANY] + [WHOLE] * 4,
+        in_specs=[SCALARS] + [WHOLE] * 5 + [ANY] + [WHOLE] * 4,
         out_specs=WHOLE,
         scratch_shapes=[
             pltpu.VMEM((4, 256, 256), F32),
-            pltpu.VMEM((4, 16, 512), BF),
+            pltpu.VMEM((4, 2, 16, 256), BF),
             pltpu.VMEM((4, 64, 512), BF),
-            pltpu.SemaphoreType.DMA((2, 4)),
+            pltpu.SemaphoreType.DMA((4,)),
         ],
-        compiler_params=pltpu.CompilerParams(vmem_limit_bytes=10 * 2**20),
+        compiler_params=pltpu.CompilerParams(vmem_limit_bytes=20 * 2**20),
         cost_estimate=cost(22),
         name="attention",
-    )(info, routes, down, x, sums, recv, *pieces)
-
-
-def project_out_kernel(blocks, place_ref, wide_ref, lhs_ref, *refs):
+    )(info, routes, down, x, up, sums, recv, *pieces)
+
+
+def project_out_kernel(blocks, place_ref, gates_ref, lhs_ref, *refs):
     pieces = refs[:10]
-    out_ref, w, sem = refs[10:]
+    *outs, w, sem = refs[10:]
     group, y, core = place_ref[0], place_ref[1], place_ref[2]
     for b, (mine, ahead) in enumerate(blocks):
         wanted_x = (y + ahead) % 4
@@ -287,10 +291,10 @@
                         sem.at[b],
                     ).start()
 
-    def block(b, carry):
+    def block(b, out_ref):
         pltpu.make_async_copy(w.at[b], w.at[b], sem.at[b]).wait()
 
-        def tile(i, inner):
+        def tile(i, carry):
             rows = pl.ds(pl.multiple_of(i * 256, 256), 256)
             total = None
             for e in range(NE):
@@ -300,31 +304,94 @@
                     [w[b, half, 0, place[0], place[1]], w[b, half, 1, place[0], place[1]]], axis=1
                 )
                 value = jnp.dot(lhs_ref[e, rows, :], weight, preferred_element_type=F32)
-                gate = wide_ref[e, rows, :]
-                value = value * jnp.concatenate([gate, gate], axis=1)
+                value = value * gates_ref[rows, e : e + 1]
                 total = value if total is None else total + value
-            out_ref[b, rows, :] = total.astype(BF)
-            return inner
-
-        return lax.fori_loop(0, 4, tile, carry)
-
-    lax.fori_loop(0, len(blocks), block, 0)
-
-
-def project_out(blocks, place, wide, lhs, pieces):
+            out_ref[rows, :] = total.astype(BF)
+            return carry
+
+        lax.fori_loop(0, 4, tile, 0)
+
+    if len(outs) > 1:
+        for b, out_ref in enumerate(outs):
+            block(b, out_ref)
+    else:
+
+        def step(b, carry):
+            block(b, outs[0].at[b])
+            return carry
+
+        lax.fori_loop(0, len(blocks), step, 0)
+
+
+def project_out(blocks, place, gates, lhs, pieces, apart=False):
+    if apart:
+        shapes = [jax.ShapeDtypeStruct((1024, 256), BF)] * len(blocks)
+    else:
+        shapes = [jax.ShapeDtypeStruct((len(blocks), 1024, 256), BF)]
     return pl.pallas_call(
         functools.partial(project_out_kernel, blocks),
-        out_shape=jax.ShapeDtypeStruct((len(blocks), 1024, 256), BF),
+        out_shape=shapes,
         in_specs=[SCALARS, WHOLE, WHOLE] + [ANY] * 10,
-        out_specs=WHOLE,
+        out_specs=[WHOLE] * len(shapes),
         scratch_shapes=[
             pltpu.VMEM((len(blocks), 2, 2, OUT_ROWS, 256), BF),
             pltpu.SemaphoreType.DMA((len(blocks),)),
         ],
         compiler_params=pltpu.CompilerParams(vmem_limit_bytes=8 * 2**20),
-        cost_estimate=cost(2.5 * len(blocks)),
+        cost_estimate=cost(2.2 * len(blocks)),
         name="project_out_" + str(len(blocks)),
-    )(place, wide, lhs, *pieces)
+    )(place, gates, lhs, *pieces)
+
+
+def small_call(kernel, shapes, us, *operands):
+    return pl.pallas_call(
+        kernel,
+        out_shape=[jax.ShapeDtypeStruct(shape, BF) for shape in shapes],
+        in_specs=[WHOLE] * len(operands),
+        out_specs=[WHOLE] * len(shapes),
+        compiler_params=pltpu.CompilerParams(vmem_limit_bytes=8 * 2**20),
+        cost_estimate=cost(us),
+        name=kernel.__name__,
+    )(*operands)
+
+
+def forward_kernel(*refs):
+    for i in range(4):
+        source_ref, out_ref = refs[i], refs[4 + i]
+        half = out_ref.shape[0]
+        out_ref[...] = source_ref[pl.ds(i % 2 * half, half), :]
+
+
+def forwarded(values):
+    half = values[0].shape[0] // 2
+    return small_call(forward_kernel, [(half, 256)] * 4, 2, *values)
+
+
+def onward(values, along):
+    low0, high0, low1, high1 = forwarded(values)
+    return [
+        send(low0, along, 1),
+        send(high0, along, -1),
+        send(low1, 1 - along, 1),
+        send(high1, 1 - along, -1),
+    ]
+
+
+def far_sum_kernel(mine_ref, theirs_ref, low_ref, high_ref):
+    for i, out_ref in enumerate((low_ref, high_ref)):
+        rows = pl.ds(i * 512, 512)
+        out_ref[...] = (mine_ref[rows, :].astype(F32) + theirs_ref[rows, :].astype(F32)).astype(BF)
+
+
+def near_sum_kernel(mine_ref, theirs_ref, low_ref, high_ref, ahead_ref, behind_ref):
+    for i, out_ref in enumerate((ahead_ref, behind_ref)):
+        extra_ref = (low_ref, high_ref)[i]
+        for half in range(2):
+            rows = pl.ds(half * 512, 512)
+            total = mine_ref[i, rows, :].astype(F32) + theirs_ref[i, rows, :].astype(F32)
+            if half == i:
+                total = total + extra_ref[...].astype(F32)
+            out_ref[rows, :] = total.astype(BF)
 
 
 def exchange(value, step):
@@ -366,7 +433,8 @@
         .transpose(0, 2, 1)
         .reshape(64, 256)
     )
-    outgoing = pack(wanted_by, prefix_cache_store, adapter_up_maps.reshape(64, 512), down_rows)
+    outgoing = pack(wanted_by, prefix_cache_store, down_rows)
+    up_rows = adapter_up_maps.reshape(64, 512)
 
     query_rows = expert_query_weight.transpose(1, 0, 2).reshape(NE * 128, 256)
     out_rows = (
@@ -377,6 +445,7 @@
             [
                 query_rows[half * 512 : half * 512 + 512],
                 key_value_weight[:, half * 256 : half * 256 + 256],
+                up_rows[:, half * 256 : half * 256 + 256],
                 out_rows[half * 512 : half * 512 + 512],
             ],
             axis=0,
@@ -386,10 +455,11 @@
     neighbours = [*first_step(own[0], 0), *first_step(own[1], 1)]
     *neighbours, outgoing = lax.optimization_barrier((*neighbours, outgoing))
     received = lax.all_to_all(outgoing, "req", 0, 0, tiled=True)
+    passed = onward(neighbours, 0)
     near, near_out = [], []
     for half in range(2):
         before, after = neighbours[2 * half : 2 * half + 2]
-        far_low, far_high = second_step(before, after, half)
+        far_low, far_high = passed[2 * half : 2 * half + 2]
         cut = SHARD_ROWS - far_low.shape[0]
         near.append(
             jnp.concatenate(
@@ -430,50 +500,40 @@
     gate_values = jax.nn.sigmoid(chosen - chosen[:, ::-1])
     live = (jnp.arange(256, dtype=jnp.int32)[None, :] < lengths[:, None]).reshape(1024, 1)
     gates = jnp.sum(route_hot * gate_values[:, :, None], axis=1) * live.astype(F32)
-    wide = jnp.broadcast_to(gates.T[:, :, None], (NE, 1024, 128))
 
     beside = [*first_step(near[0], 1), *first_step(near[1], 0)]
     down_part = pick_down(info, received)
     down = lax.all_to_all(
         jnp.broadcast_to(down_part[None], (NE, 4, 16, 256)), "exp", 0, 0, tiled=True
     )
-    *beside, down = lax.optimization_barrier((*beside, down))
-    late = [*second_step(*beside[:2], 1), *second_step(*beside[2:], 0)]
-    wide, sums = project_early(
-        info, gates, routes, tokens, [near[0], *beside[:2], near[1], *beside[2:]]
-    )
+    *beside, down, gates = lax.optimization_barrier((*beside, down, gates))
+    late = onward(beside, 1)
+    up, sums = project_early(info, routes, tokens, [near[0], *beside[:2], near[1], *beside[2:]])
     *late, near_out[0], near_out[1] = lax.optimization_barrier((*late, *near_out))
     out_beside = [*first_step(near_out[0], 1), *first_step(near_out[1], 0)]
-    lhs = attention(info, routes, down, tokens, sums, received, late)
+    lhs = attention(info, routes, down, tokens, up, sums, received, late)
     *out_beside, lhs = lax.optimization_barrier((*out_beside, lhs))
-    out_late = [*second_step(*out_beside[:2], 1), *second_step(*out_beside[2:], 0)]
+    out_late = onward(out_beside, 1)
     out_pieces = []
     for half in range(2):
         two = slice(half * 2, half * 2 + 2)
         out_pieces += [near_out[half], *out_beside[two], *out_late[two]]
 
     place = jnp.stack([group, part // 2, part % 2]).astype(jnp.int32)
-    far = project_out(((False, 2), (True, 2)), place, wide, lhs, out_pieces)
-    far_swapped = exchange(far[0], 0)
-    place = lax.optimization_barrier((place, far))[0]
-    theirs = project_out(((False, 1), (False, 3), (False, 0)), place, wide, lhs, out_pieces)
+    operands = (gates, lhs, out_pieces)
+    far, far_mine = project_out(((False, 2), (True, 2)), place, *operands, apart=True)
+    far_swapped = exchange(far, 0)
+    place = lax.optimization_barrier((place, far_mine))[0]
+    (theirs,) = project_out(((False, 1), (False, 3), (False, 0)), place, *operands)
     swapped = exchange(theirs, 0)
-    both_far = rounded_sum(far[1], far_swapped)
-    low = exchange(both_far[:512], 1)
-    high = exchange(both_far[512:], -1)
-    place = lax.optimization_barrier((place, theirs, both_far))[0]
-    mine = project_out(((True, 1), (True, 3)), place, wide, lhs, out_pieces)
-    ahead = jnp.concatenate(
-        [rounded_sum(mine[0, :512], swapped[0, :512], low), rounded_sum(mine[0, 512:], swapped[0, 512:])],
-        axis=0,
-    )
-    behind = jnp.concatenate(
-        [rounded_sum(mine[1, :512], swapped[1, :512]), rounded_sum(mine[1, 512:], swapped[1, 512:], high)],
-        axis=0,
-    )
+    low, high = small_call(far_sum_kernel, [(512, 256)] * 2, 1, far_mine, far_swapped)
+    place = lax.optimization_barrier((place, theirs, low))[0]
+    low, high = exchange(low, 1), exchange(high, -1)
+    (mine,) = project_out(((True, 1), (True, 3)), place, *operands)
+    ahead, behind = small_call(near_sum_kernel, [(1024, 256)] * 2, 2, mine, swapped, low, high)
     from_behind, from_ahead = exchange(ahead, 1), exchange(behind, -1)
-    place = lax.optimization_barrier((place, ahead, behind))[0]
-    own_block = project_out(((True, 0),), place, wide, lhs, out_pieces)
+    place = lax.optimization_barrier((place, ahead))[0]
+    (own_block,) = project_out(((True, 0),), place, *operands)
     return rounded_sum(own_block[0], swapped[2], from_behind, from_ahead)
 
 

time: 234 us -> 225 us (0.962)
  local copies, waits for them, and re-layouts: 40.3 us -> 27.6 us
  Pallas kernels: 59.3 us -> 65.5 us
    slice x13 -> x0, local copies, waits for them, and re-layouts: 9.35 us -> none  [the longest x12 9.31 us: second_step(): return (send(before[:half], along, 1), send(after[half:], along, -1))]
    ppermute x24, waiting for transfers between devices: 53.7 us -> 45.4 us  [send(): lax.ppermute(value, 'req', torus(step, 0) if along == 0 else torus(0, step))]
    all_to_all x1, waiting for transfers between devices: 0.01 us -> 6.51 us  [body(): lax.all_to_all(jnp.broadcast_to(down_part[None], (NE, 4, 16, 256)), 'exp'...]
    pallas_call x5 -> x10, Pallas kernels: 35.7 us -> 41.7 us  [the longest x4 21.5 us: project_out(): pl.pallas_call(functools.partial(project_out_kernel, blocks), out_shape=s...]
    unnamed x82 -> x93, local copies, waits for them, and re-layouts: 20.5 us -> 19.8 us
  transfers between devices with their start and end apart: 32 -> 32, of which waited for: 16 -> 15; matrix products, arithmetic and copies ran while one was open for 12% -> 8% of each run, Pallas kernels for 20% -> 21%
where the time goes in v2:
time: 225 us; the launch traced here: 224 us
  waiting for transfers between devices  67.3 us (30%)
  Pallas kernels  65.5 us (29%)
  starting transfers between devices  52.8 us (23%)
  local copies, waits for them, and re-layouts  27.6 us (12%)
  other arithmetic  7 us (3%)
  matrix products  3.37 us (1%)
    ppermute x24, waiting for transfers between devices, send(): lax.ppermute(value, 'req', torus(step, 0) if along == 0 else torus(0, step))  45.4 us
    ppermute x24, starting transfers between devices, send(): lax.ppermute(value, 'req', torus(step, 0) if along == 0 else torus(0, step))  33.8 us
    pallas_call x4, Pallas kernels, project_out(): pl.pallas_call(functools.partial(project_out_kernel, blocks), out_shape=s...  21.5 us
    unnamed x93, local copies, waits for them, and re-layouts  19.8 us
    pallas_call x1, Pallas kernels, attention(): pl.pallas_call(attend_kernel, out_shape=jax.ShapeDtypeStruct((NE, 1024, 2...  19.3 us
    pallas_call x1, Pallas kernels, project_early(): pl.pallas_call(early_kernel, out_shape=(jax.ShapeDtypeStruct((4, 2, 16, 2...  14.5 us
    ppermute x4, waiting for transfers between devices, exchange(): lax.ppermute(value, 'exp', [(i, (i + 2 * step) % 8) for i in range(8)])  11.8 us
    all_to_all x1, starting transfers between devices, body(): received = lax.all_to_all(outgoing, 'req', 0, 0, tiled=True)  7.33 us
  transfers between devices with their start and end apart: 32, of which 15 were waited for; matrix products, arithmetic and copies ran while one was open for 8% of the time, Pallas kernels for 21%

profile of v2, /device:TPU:6, one launch (start us, length us, event | category | flops | bytes accessed | tf_op | source)
XLA Modules:
  0.0 224.2 jit_solution(4398777079536696546)
XLA Ops:
  0.0 1.7 copy.41
  2.4 0.8 constant_dynamic-update-slice_fusion.3
  4.5 0.9 pad_maximum_fusion.2
  5.4 0.8 collective-permute-start.1
  6.3 2.4 %collective-permute-start = (bf16[1216,256]{1,0:T(8,128)(2,1)}, bf16[1216,256]{1,0:T(8,128)(2,1)S(1)}, u32[]{:S(2)}, u32[]{:S(2)}) collective-permute-start(bf16[1216,256]{1,0:T(8,128)(2,1)} %pad_maximum_fusion.2), channel_id=1, source_target_pairs={{0,32},{8,40},{16,48},{24,56},{32,64},{40,72},{48,80},{56,88},{64,... | collective-permute-start | bytes 1867784 | tf_op jit(solution)/shard_map/ppermute | solution.py:39
  8.7 1.0 pad_maximum_fusion.3
  9.7 4.0 %collective-permute-start.3 = (bf16[1216,256]{1,0:T(8,128)(2,1)}, bf16[1216,256]{1,0:T(8,128)(2,1)S(1)}, u32[]{:S(2)}, u32[]{:S(2)}) collective-permute-start(bf16[1216,256]{1,0:T(8,128)(2,1)} %pad_maximum_fusion.3), channel_id=1, source_target_pairs={{0,24},{8,0},{16,8},{24,16},{32,56},{40,32},{48,40},{56,48},{64,88... | collective-permute-start | bytes 1867784 | tf_op jit(solution)/shard_map/ppermute | solution.py:39
  14.0 1.0 copy.34.routes_ref
  15.0 3.4 %fusion.4 = f32[1024,8]{0,1:T(8,128)S(1)} fusion(bf16[1024,2048]{1,0:T(8,128)(2,1)} %x_ref.3, bf16[2048,8]{0,1:T(8,128)(2,1)S(1)} %copy-done.34), kind=kOutput, calls=%fused_computation.40 | convolution fusion | flops 33554432 | bytes 4259840 | tf_op jit(solution)/shard_map/dot_general | solution.py:496
  19.9 2.3 %pack.1 = bf16[16,96,512]{2,1,0:T(8,128)(2,1)} custom-call(s32[16]{0:T(128)} %select_reduce_fusion.2.index_ref, bf16[4,64,512]{2,1,0:T(8,128)(2,1)} %store_ref.1, bf16[64,256]{1,0:T(8,128)(2,1)} %bitcast.49), custom_call_target="tpu_custom_call" | custom-call | flops 3449999872 | bytes 1048576 | tf_op jit(solution)/shard_map/pack/pallas_call | solution.py:74
  22.6 4.1 %collective-permute-done.3.refs_3_ = bf16[1216,256]{1,0:T(8,128)(2,1)S(1)} collective-permute-done((bf16[1216,256]{1,0:T(8,128)(2,1)}, bf16[1216,256]{1,0:T(8,128)(2,1)S(1)}, u32[]{:S(2)}, u32[]{:S(2)}) %collective-permute-start.3) | collective-permute-done | bytes 622624 | tf_op jit(solution)/shard_map/ppermute | solution.py:39
  26.8 3.3 %collective-permute-done.2.refs_2_ = bf16[1216,256]{1,0:T(8,128)(2,1)S(1)} collective-permute-done((bf16[1216,256]{1,0:T(8,128)(2,1)}, bf16[1216,256]{1,0:T(8,128)(2,1)S(1)}, u32[]{:S(2)}, u32[]{:S(2)}) %collective-permute-start.2) | collective-permute-done | bytes 622624 | tf_op jit(solution)/shard_map/ppermute | solution.py:39
  30.1 0.8 slice_dynamic-update-slice_fusion.3
  30.9 0.8 slice_dynamic-update-slice_fusion.2
  31.7 0.8 forward_kernel.3
  33.9 7.3 %all-to-all-start = ((bf16[16,96,512]{2,1,0:T(8,128)(2,1)}), bf16[16,96,512]{2,1,0:T(8,128)(2,1)}, u32[]{:S(2)}, u32[]{:S(2)}) async-start(bf16[16,96,512]{2,1,0:T(8,128)(2,1)} %pack.1), calls=%async_computation | async-start | bytes 3145728 | tf_op jit(solution)/shard_map/all_to_all | solution.py:457
  41.5 1.9 collective-permute-start.5
  43.4 2.7 %collective-permute-start.9 = (bf16[608,256]{1,0:T(8,128)(2,1)S(1)}, bf16[608,256]{1,0:T(8,128)(2,1)S(1)}, u32[]{:S(2)}, u32[]{:S(2)}) collective-permute-start(bf16[608,256]{1,0:T(8,128)(2,1)S(1)} %copy-done.23), channel_id=1, source_target_pairs={{0,24},{8,0},{16,8},{24,16},{32,56},{40,32},{48,40},{56,48},{64,88... | collective-permute-start | bytes 933896 | tf_op jit(solution)/shard_map/ppermute | solution.py:39
  46.8 1.7 constant_dynamic-update-slice_fusion.4
  48.5 16.0 %collective-permute-done.9 = bf16[608,256]{1,0:T(8,128)(2,1)S(1)} collective-permute-done((bf16[608,256]{1,0:T(8,128)(2,1)S(1)}, bf16[608,256]{1,0:T(8,128)(2,1)S(1)}, u32[]{:S(2)}, u32[]{:S(2)}) %collective-permute-start.9) | collective-permute-done | bytes 311328 | tf_op jit(solution)/shard_map/ppermute | solution.py:39
  65.2 0.8 collective-permute-start.11
  66.1 2.4 %collective-permute-start.10 = (bf16[2816,256]{1,0:T(8,128)(2,1)}, bf16[2816,256]{1,0:T(8,128)(2,1)}, u32[]{:S(2)}, u32[]{:S(2)}) collective-permute-start(bf16[2816,256]{1,0:T(8,128)(2,1)} %slice_dynamic-update-slice_fusion.4.refs_3_), channel_id=1, source_target_pairs={{0,32},{8,40},{16,48},{24,56},{32,64},{40,72},{48,80},{56,88},{64,... | collective-permute-start | bytes 4325384 | tf_op jit(solution)/shard_map/ppermute | solution.py:39
  69.9 2.6 %collective-permute-start.7 = (bf16[2816,256]{1,0:T(8,128)(2,1)}, bf16[2816,256]{1,0:T(8,128)(2,1)}, u32[]{:S(2)}, u32[]{:S(2)}) collective-permute-start(bf16[2816,256]{1,0:T(8,128)(2,1)} %slice_dynamic-update-slice_fusion.5.refs_0_), channel_id=1, source_target_pairs={{0,24},{8,0},{16,8},{24,16},{32,56},{40,32},{48,40},{56,48},{64,88... | collective-permute-start | bytes 4325384 | tf_op jit(solution)/shard_map/ppermute | solution.py:39
  72.6 1.0 copy.32
  74.4 1.2 broadcast_multiply_fusion.gates_ref
  75.7 0.9 copy-done.30
  77.4 2.2 pick_down.1
  79.6 1.5 broadcast_in_dim.2
  81.1 4.5 %all-to-all-start.1 = ((bf16[8,4,16,256]{3,2,1,0:T(8,128)(2,1)}), bf16[8,4,16,256]{3,2,1,0:T(8,128)(2,1)}, u32[]{:S(2)}, u32[]{:S(2)}) async-start(bf16[8,4,16,256]{3,2,1,0:T(8,128)(2,1)} %broadcast_in_dim.2), calls=%async_computation.1 | async-start | bytes 524288 | tf_op jit(solution)/shard_map/all_to_all | solution.py:506
  85.6 1.1 pad_maximum_fusion.1.refs_5_
  86.7 6.5 %all-to-all-done.1.down_ref = bf16[8,4,16,256]{3,2,1,0:T(8,128)(2,1)} async-done(((bf16[8,4,16,256]{3,2,1,0:T(8,128)(2,1)}), bf16[8,4,16,256]{3,2,1,0:T(8,128)(2,1)}, u32[]{:S(2)}, u32[]{:S(2)}) %all-to-all-start.1) | async-done | bytes 262176 | tf_op jit(solution)/shard_map/all_to_all | solution.py:506
  93.2 5.7 %collective-permute-done.11.refs_3_.refs_5_ = bf16[2816,256]{1,0:T(8,128)(2,1)} collective-permute-done((bf16[2816,256]{1,0:T(8,128)(2,1)}, bf16[2816,256]{1,0:T(8,128)(2,1)}, u32[]{:S(2)}, u32[]{:S(2)}) %collective-permute-start.11) | collective-permute-done | bytes 1441824 | tf_op jit(solution)/shard_map/ppermute | solution.py:39
  99.0 3.4 %collective-permute-done.7.refs_1_.refs_2_ = bf16[2816,256]{1,0:T(8,128)(2,1)} collective-permute-done((bf16[2816,256]{1,0:T(8,128)(2,1)}, bf16[2816,256]{1,0:T(8,128)(2,1)}, u32[]{:S(2)}, u32[]{:S(2)}) %collective-permute-start.7) | collective-permute-done | bytes 1441824 | tf_op jit(solution)/shard_map/ppermute | solution.py:39
  102.4 3.4 %collective-permute-done.6.refs_0_.refs_1_ = bf16[2816,256]{1,0:T(8,128)(2,1)} collective-permute-done((bf16[2816,256]{1,0:T(8,128)(2,1)}, bf16[2816,256]{1,0:T(8,128)(2,1)}, u32[]{:S(2)}, u32[]{:S(2)}) %collective-permute-start.6) | collective-permute-done | bytes 1441824 | tf_op jit(solution)/shard_map/ppermute | solution.py:39
  105.8 2.9 %forward_kernel.4 = (bf16[1408,256]{1,0:T(8,128)(2,1)S(1)}, bf16[1408,256]{1,0:T(8,128)(2,1)S(1)}, bf16[1408,256]{1,0:T(8,128)(2,1)S(1)}, bf16[1408,256]{1,0:T(8,128)(2,1)S(1)}) custom-call(bf16[2816,256]{1,0:T(8,128)(2,1)} %collective-permute-done.6.refs_0_.refs_1_, bf16[2816,256]{1,0:T(8,128)(2,1)} %collective-permute-done.7.refs_1_.refs_2_, ...), custom_call_target="tpu_custom_call" | custom-call | flops 2300000000 | bytes 1048576 | tf_op jit(solution)/shard_map/forward_kernel/pallas_call | solution.py:347
  108.7 3.2 %collective-permute-start.13 = (bf16[1408,256]{1,0:T(8,128)(2,1)S(1)}, bf16[1408,256]{1,0:T(8,128)(2,1)S(1)}, u32[]{:S(2)}, u32[]{:S(2)}) collective-permute-start(bf16[1408,256]{1,0:T(8,128)(2,1)S(1)} %get-tuple-element.65), channel_id=1, source_target_pairs={{0,24},{8,0},{16,8},{24,16},{32,56},{40,32},{48,40},{56,48},{64,88... | collective-permute-start | bytes 2162696 | tf_op jit(solution)/shard_map/ppermute | solution.py:39
  112.2 1.7 collective-permute-start.15
  114.0 14.5 %project_early.1 = (bf16[4,2,16,256]{3,2,1,0:T(8,128)(2,1)S(1)}, f32[4,4,256,256]{3,2,1,0:T(8,128)S(1)}) custom-call(s32[13]{0:T(128)S(1)} %copy-done.21, s32[1024,2]{1,0:T(8,128)S(1)} %copy-done.20, bf16[1024,2048]{1,0:T(8,128)(2,1)S(1)} %copy-done.1, bf16[2816,256]{1,0:T(8,128)(2,1)} %slice_dynamic-update-slice_fusion.5.refs_0_, ...), custom_call_target="tpu_custom_call" | custom-call | flops 17250000896 | bytes 1048576 | tf_op jit(solution)/shard_map/project_early/pallas_call | solution.py:179
  128.6 2.0 collective-permute-start.16
  130.6 3.2 %collective-permute-start.18 = (bf16[2048,256]{1,0:T(8,128)(2,1)S(1)}, bf16[2048,256]{1,0:T(8,128)(2,1)S(1)}, u32[]{:S(2)}, u32[]{:S(2)}) collective-permute-start(bf16[2048,256]{1,0:T(8,128)(2,1)S(1)} %pad_maximum_fusion.1.refs_5_), channel_id=1, source_target_pairs={{0,32},{8,40},{16,48},{24,56},{32,64},{40,72},{48,80},{56,88},{64,... | collective-permute-start | bytes 3145736 | tf_op jit(solution)/shard_map/ppermute | solution.py:39
  133.8 19.3 %attention.1.lhs_ref = bf16[8,1024,256]{2,1,0:T(8,128)(2,1)S(1)} custom-call(s32[13]{0:T(128)S(1)} %copy-done.21, s32[1024,2]{1,0:T(8,128)S(1)} %copy-done.20, bf16[8,4,16,256]{3,2,1,0:T(8,128)(2,1)} %all-to-all-done.1.down_ref, bf16[1024,2048]{1,0:T(8,128)(2,1)S(1)} %copy-done.1, bf16[4,2,16,256]{3,2,1,0:T(8,128)(2,1)S(1)} %get-tuple-element.71.up_ref, ...), custom_call_target="tpu_custom_call" | custom-call | flops 25300000768 | bytes 1048576 | tf_op jit(solution)/shard_map/attention/pallas_call | solution.py:258
  153.2 1.6 forward_kernel.5
  154.9 0.9 copy-done.2
  157.1 3.2 %collective-permute-start.21 = (bf16[1024,256]{1,0:T(8,128)(2,1)}, bf16[1024,256]{1,0:T(8,128)(2,1)}, u32[]{:S(2)}, u32[]{:S(2)}) collective-permute-start(bf16[1024,256]{1,0:T(8,128)(2,1)} %get-tuple-element.83), channel_id=1, source_target_pairs={{0,24},{8,0},{16,8},{24,16},{32,56},{40,32},{48,40},{56,48},{64,88... | collective-permute-start | bytes 1572872 | tf_op jit(solution)/shard_map/ppermute | solution.py:39
  160.7 1.7 collective-permute-start.23
  162.4 5.3 %collective-permute-done.20.refs_3_ = bf16[1024,256]{1,0:T(8,128)(2,1)S(1)} collective-permute-done((bf16[1024,256]{1,0:T(8,128)(2,1)}, bf16[1024,256]{1,0:T(8,128)(2,1)S(1)}, u32[]{:S(2)}, u32[]{:S(2)}) %collective-permute-start.20) | collective-permute-done | bytes 524320 | tf_op jit(solution)/shard_map/ppermute | solution.py:39
  167.7 2.1 collective-permute-done.22.refs_8_
  169.8 1.6 collective-permute-done.23.refs_9_
  171.4 2.2 copy-done.3
  173.6 1.2 copy-done.6
  174.8 1.2 copy-done.9
  176.0 1.2 copy-done.12
  177.2 1.2 copy-done.15
  178.5 5.2 %project_out_2.2 = (bf16[1024,256]{1,0:T(8,128)(2,1)S(1)}, bf16[1024,256]{1,0:T(8,128)(2,1)S(1)}) custom-call(s32[3]{0:T(128)S(1)} %pad_add_fusion.place_ref, f32[1024,8]{1,0:T(8,128)S(1)} %broadcast_multiply_fusion.gates_ref, bf16[8,1024,256]{2,1,0:T(8,128)(2,1)S(1)} %copy-done.3, bf16[2048,256]{1,0:T(8,128)(2,1)S(1)} %pad_maximum_fusion.refs_0_, ...), custom_call_target="tpu_custom_call" | custom-call | flops 5059999744 | bytes 1048576 | tf_op jit(solution)/shard_map/project_out_2/pallas_call | solution.py:331
  183.7 7.5 %project_out_3.1 = bf16[3,1024,256]{2,1,0:T(8,128)(2,1)S(1)} custom-call(s32[3]{0:T(128)S(1)} %pad_add_fusion.place_ref, f32[1024,8]{1,0:T(8,128)S(1)} %broadcast_multiply_fusion.gates_ref, bf16[8,1024,256]{2,1,0:T(8,128)(2,1)S(1)} %copy-done.3, bf16[2048,256]{1,0:T(8,128)(2,1)S(1)} %pad_maximum_fusion.refs_0_, bf16[2048,256]{1,0:T(8,128)(2,1)S(1)} %copy-done.10, ...), custom_call_target="tpu_custom_call" | custom-call | flops 7590000128 | bytes 1048576 | tf_op jit(solution)/shard_map/project_out_3/pallas_call | solution.py:331
  191.8 3.6 %collective-permute-done.24.theirs_ref = bf16[1024,256]{1,0:T(8,128)(2,1)S(1)} collective-permute-done((bf16[1024,256]{1,0:T(8,128)(2,1)S(1)}, bf16[1024,256]{1,0:T(8,128)(2,1)S(1)}, u32[]{:S(2)}, u32[]{:S(2)}) %collective-permute-start.24) | collective-permute-done | bytes 524320 | tf_op jit(solution)/shard_map/ppermute | solution.py:399
  195.6 1.2 collective-permute-start.26
  196.8 2.3 %collective-permute-start.27 = (bf16[512,256]{1,0:T(8,128)(2,1)S(1)}, bf16[512,256]{1,0:T(8,128)(2,1)S(1)}, u32[]{:S(2)}, u32[]{:S(2)}) collective-permute-start(bf16[512,256]{1,0:T(8,128)(2,1)S(1)} %get-tuple-element.91), channel_id=1, source_target_pairs={{0,6},{1,7},{2,0},{3,1},{4,2},{5,3},{6,4},{7,5},{8,14},{9,15},{10,... | collective-permute-start | bytes 786440 | tf_op jit(solution)/shard_map/ppermute | solution.py:400
  199.1 5.9 %project_out_2.3.mine_ref = bf16[2,1024,256]{2,1,0:T(8,128)(2,1)S(1)} custom-call(s32[3]{0:T(128)S(1)} %pad_add_fusion.place_ref, f32[1024,8]{1,0:T(8,128)S(1)} %broadcast_multiply_fusion.gates_ref, bf16[8,1024,256]{2,1,0:T(8,128)(2,1)S(1)} %copy-done.4, bf16[2048,256]{1,0:T(8,128)(2,1)S(1)} %pad_maximum_fusion.refs_0_, bf16[2048,256]{1,0:T(8,128)(2,1)S(1)} %copy-done.10, ...), custom_call_target="tpu_custom_call" | custom-call | flops 5059999744 | bytes 1048576 | tf_op jit(solution)/shard_map/project_out_2/pallas_call | solution.py:331
  205.9 3.1 %collective-permute-start.29 = (bf16[1024,256]{1,0:T(8,128)(2,1)S(1)}, bf16[1024,256]{1,0:T(8,128)(2,1)S(1)}, u32[]{:S(2)}, u32[]{:S(2)}) collective-permute-start(bf16[1024,256]{1,0:T(8,128)(2,1)S(1)} %get-tuple-element.94), channel_id=1, source_target_pairs={{0,6},{1,7},{2,0},{3,1},{4,2},{5,3},{6,4},{7,5},{8,14},{9,15},{10,... | collective-permute-start | bytes 1572872 | tf_op jit(solution)/shard_map/ppermute | solution.py:400
  209.0 2.9 %project_out_1.1 = bf16[1,1024,256]{2,1,0:T(8,128)(2,1)S(1)} custom-call(s32[3]{0:T(128)S(1)} %pad_add_fusion.place_ref, f32[1024,8]{1,0:T(8,128)S(1)} %broadcast_multiply_fusion.gates_ref, bf16[8,1024,256]{2,1,0:T(8,128)(2,1)S(1)} %copy-done.4, bf16[2048,256]{1,0:T(8,128)(2,1)S(1)} %pad_maximum_fusion.refs_0_, bf16[2048,256]{1,0:T(8,128)(2,1)S(1)} %copy-done.10, ...), custom_call_target="tpu_custom_call" | custom-call | flops 2529999872 | bytes 1048576 | tf_op jit(solution)/shard_map/project_out_1/pallas_call | solution.py:331
  212.0 7.7 %collective-permute-done.29 = bf16[1024,256]{1,0:T(8,128)(2,1)S(1)} collective-permute-done((bf16[1024,256]{1,0:T(8,128)(2,1)S(1)}, bf16[1024,256]{1,0:T(8,128)(2,1)S(1)}, u32[]{:S(2)}, u32[]{:S(2)}) %collective-permute-start.29) | collective-permute-done | bytes 524320 | tf_op jit(solution)/shard_map/ppermute | solution.py:400
  219.7 3.4 %collective-permute-done.28 = bf16[1024,256]{1,0:T(8,128)(2,1)S(1)} collective-permute-done((bf16[1024,256]{1,0:T(8,128)(2,1)S(1)}, bf16[1024,256]{1,0:T(8,128)(2,1)S(1)}, u32[]{:S(2)}, u32[]{:S(2)}) %collective-permute-start.28) | collective-permute-done | bytes 524320 | tf_op jit(solution)/shard_map/ppermute | solution.py:400
  223.1 1.1 fusion.1
  (146 shorter events, 14.3 us)
Async XLA Ops:
  0.0 19.3 %copy-start = (bf16[4,2048,16]{1,2,0:T(8,128)(2,1)S(1)}, bf16[4,2048,16]{1,2,0:T(8,128)(2,1)}, u32[]{:S(2)}) copy-start(bf16[4,2048,16]{1,2,0:T(8,128)(2,1)} %param.25) | copy-start | bytes 786436
  0.0 2.1 copy-start.28
  2.1 2.4 %copy-start.24 = (bf16[64,8,2,128]{3,1,2,0:T(8,128)(2,1)}, bf16[64,8,2,128]{3,1,2,0:T(8,128)(2,1)S(1)}, u32[]{:S(2)}) copy-start(bf16[64,8,2,128]{3,1,2,0:T(8,128)(2,1)S(1)} %copy.43) | copy-start | bytes 786436
  4.5 9.2 %copy-start.37 = (s32[64]{0:T(128)S(1)}, s32[64]{0:T(128)}, u32[]{:S(2)}) copy-start(s32[64]{0:T(128)} %param.18) | copy-start | bytes 772
  4.5 9.4 %copy-start.35 = (s32[4]{0:T(128)S(1)}, s32[4]{0:T(128)}, u32[]{:S(2)}) copy-start(s32[4]{0:T(128)} %param.16) | copy-start | bytes 52
  4.5 9.5 %copy-start.32 = (s32[1024,2]{0,1:T(2,128)S(1)}, s32[1024,2]{0,1:T(2,128)}, u32[]{:S(2)}) copy-start(s32[1024,2]{0,1:T(2,128)} %param.15) | copy-start | bytes 24580
  5.4 9.6 %copy-start.34 = (bf16[2048,8]{0,1:T(8,128)(2,1)S(1)}, bf16[2048,8]{0,1:T(8,128)(2,1)}, u32[]{:S(2)}) copy-start(bf16[2048,8]{0,1:T(8,128)(2,1)} %param.21) | copy-start | bytes 98308
  5.4 17.2 %collective-permute-start.1 = (bf16[1216,256]{1,0:T(8,128)(2,1)}, bf16[1216,256]{1,0:T(8,128)(2,1)S(1)}, u32[]{:S(2)}, u32[]{:S(2)}) collective-permute-start(bf16[1216,256]{1,0:T(8,128)(2,1)} %pad_maximum_fusion.2), channel_id=1, source_target_pairs={{0,96},{8,104},{16,112},{24,120},{32,0},{40,8},{48,16},{56,24},{64... | collective-permute-start | bytes 1867784 | tf_op jit(solution)/shard_map/ppermute | solution.py:39
  6.3 16.4 %collective-permute-start = (bf16[1216,256]{1,0:T(8,128)(2,1)}, bf16[1216,256]{1,0:T(8,128)(2,1)S(1)}, u32[]{:S(2)}, u32[]{:S(2)}) collective-permute-start(bf16[1216,256]{1,0:T(8,128)(2,1)} %pad_maximum_fusion.2), channel_id=1, source_target_pairs={{0,32},{8,40},{16,48},{24,56},{32,64},{40,72},{48,80},{56,88},{64,... | collective-permute-start | bytes 1867784 | tf_op jit(solution)/shard_map/ppermute | solution.py:39
  9.7 17.1 %collective-permute-start.3 = (bf16[1216,256]{1,0:T(8,128)(2,1)}, bf16[1216,256]{1,0:T(8,128)(2,1)S(1)}, u32[]{:S(2)}, u32[]{:S(2)}) collective-permute-start(bf16[1216,256]{1,0:T(8,128)(2,1)} %pad_maximum_fusion.3), channel_id=1, source_target_pairs={{0,24},{8,0},{16,8},{24,16},{32,56},{40,32},{48,40},{56,48},{64,88... | collective-permute-start | bytes 1867784 | tf_op jit(solution)/shard_map/ppermute | solution.py:39
  13.7 16.4 %collective-permute-start.2 = (bf16[1216,256]{1,0:T(8,128)(2,1)}, bf16[1216,256]{1,0:T(8,128)(2,1)S(1)}, u32[]{:S(2)}, u32[]{:S(2)}) collective-permute-start(bf16[1216,256]{1,0:T(8,128)(2,1)} %pad_maximum_fusion.3), channel_id=1, source_target_pairs={{0,8},{8,16},{16,24},{24,0},{32,40},{40,48},{48,56},{56,32},{64,72... | collective-permute-start | bytes 1867784 | tf_op jit(solution)/shard_map/ppermute | solution.py:39
  22.6 53.0 %copy-start.16 = (bf16[1216,256]{1,0:T(8,128)(2,1)}, bf16[1216,256]{1,0:T(8,128)(2,1)S(1)}, u32[]{:S(2)}) copy-start(bf16[1216,256]{1,0:T(8,128)(2,1)S(1)} %collective-permute-done.1.refs_1_) | copy-start | bytes 1867780
  22.6 53.0 %copy-start.17 = (bf16[1216,256]{1,0:T(8,128)(2,1)}, bf16[1216,256]{1,0:T(8,128)(2,1)S(1)}, u32[]{:S(2)}) copy-start(bf16[1216,256]{1,0:T(8,128)(2,1)S(1)} %collective-permute-done.refs_0_) | copy-start | bytes 1867780
  26.8 48.9 %copy-start.18 = (bf16[1216,256]{1,0:T(8,128)(2,1)}, bf16[1216,256]{1,0:T(8,128)(2,1)S(1)}, u32[]{:S(2)}) copy-start(bf16[1216,256]{1,0:T(8,128)(2,1)S(1)} %collective-permute-done.3.refs_3_) | copy-start | bytes 1867780
  30.1 3.1 %copy-start.19 = (bf16[1216,256]{1,0:T(8,128)(2,1)}, bf16[1216,256]{1,0:T(8,128)(2,1)S(1)}, u32[]{:S(2)}) copy-start(bf16[1216,256]{1,0:T(8,128)(2,1)S(1)} %collective-permute-done.2.refs_2_) | copy-start | bytes 1867780
  33.2 13.7 %collective-permute-start.8 = (bf16[608,256]{1,0:T(8,128)(2,1)}, bf16[608,256]{1,0:T(8,128)(2,1)}, u32[]{:S(2)}, u32[]{:S(2)}) collective-permute-start(bf16[608,256]{1,0:T(8,128)(2,1)} %get-tuple-element.56), channel_id=1, source_target_pairs={{0,8},{8,16},{16,24},{24,0},{32,40},{40,48},{48,56},{56,32},{64,72... | collective-permute-start | bytes 933896 | tf_op jit(solution)/shard_map/ppermute | solution.py:39
  33.9 9.5 %copy-start.23 = (bf16[608,256]{1,0:T(8,128)(2,1)S(1)}, bf16[608,256]{1,0:T(8,128)(2,1)}, u32[]{:S(2)}) copy-start(bf16[608,256]{1,0:T(8,128)(2,1)} %copy-done.22) | copy-start | bytes 933892
  33.9 43.5 %all-to-all-start = ((bf16[16,96,512]{2,1,0:T(8,128)(2,1)}), bf16[16,96,512]{2,1,0:T(8,128)(2,1)}, u32[]{:S(2)}, u32[]{:S(2)}) async-start(bf16[16,96,512]{2,1,0:T(8,128)(2,1)} %pack.1), calls=%async_computation | async-start | bytes 3145728 | tf_op jit(solution)/shard_map/all_to_all | solution.py:457
  41.3 32.3 %copy-start.38 = (s32[64]{0:T(128)S(1)}, s32[64]{0:T(128)}, u32[]{:S(2)}) copy-start(s32[64]{0:T(128)} %param.20) | copy-start | bytes 772
  41.3 32.3 %copy-start.39 = (s32[4]{0:T(128)S(1)}, s32[4]{0:T(128)}, u32[]{:S(2)}) copy-start(s32[4]{0:T(128)} %param.19) | copy-start | bytes 52
  41.3 32.5 %copy-start.36 = (s32[4]{0:T(128)S(1)}, s32[4]{0:T(128)}, u32[]{:S(2)}) copy-start(s32[4]{0:T(128)} %param.17) | copy-start | bytes 52
  41.3 27.2 %collective-permute-start.4 = (bf16[608,256]{1,0:T(8,128)(2,1)S(1)}, bf16[608,256]{1,0:T(8,128)(2,1)S(1)}, u32[]{:S(2)}, u32[]{:S(2)}) collective-permute-start(bf16[608,256]{1,0:T(8,128)(2,1)S(1)} %get-tuple-element.54), channel_id=1, source_target_pairs={{0,32},{8,40},{16,48},{24,56},{32,64},{40,72},{48,80},{56,88},{64,... | collective-permute-start | bytes 933896 | tf_op jit(solution)/shard_map/ppermute | solution.py:39
  41.5 27.7 %collective-permute-start.5 = (bf16[608,256]{1,0:T(8,128)(2,1)S(1)}, bf16[608,256]{1,0:T(8,128)(2,1)S(1)}, u32[]{:S(2)}, u32[]{:S(2)}) collective-permute-start(bf16[608,256]{1,0:T(8,128)(2,1)S(1)} %get-tuple-element.55), channel_id=1, source_target_pairs={{0,96},{8,104},{16,112},{24,120},{32,0},{40,8},{48,16},{56,24},{64... | collective-permute-start | bytes 933896 | tf_op jit(solution)/shard_map/ppermute | solution.py:39
  43.4 21.2 %collective-permute-start.9 = (bf16[608,256]{1,0:T(8,128)(2,1)S(1)}, bf16[608,256]{1,0:T(8,128)(2,1)S(1)}, u32[]{:S(2)}, u32[]{:S(2)}) collective-permute-start(bf16[608,256]{1,0:T(8,128)(2,1)S(1)} %copy-done.23), channel_id=1, source_target_pairs={{0,24},{8,0},{16,8},{24,16},{32,56},{40,32},{48,40},{56,48},{64,88... | collective-permute-start | bytes 933896 | tf_op jit(solution)/shard_map/ppermute | solution.py:39
  64.6 4.6 %copy-start.29 = (bf16[608,256]{1,0:T(8,128)(2,1)}, bf16[608,256]{1,0:T(8,128)(2,1)S(1)}, u32[]{:S(2)}) copy-start(bf16[608,256]{1,0:T(8,128)(2,1)S(1)} %collective-permute-done.9) | copy-start | bytes 933892
  65.2 33.7 %collective-permute-start.11 = (bf16[2816,256]{1,0:T(8,128)(2,1)}, bf16[2816,256]{1,0:T(8,128)(2,1)}, u32[]{:S(2)}, u32[]{:S(2)}) collective-permute-start(bf16[2816,256]{1,0:T(8,128)(2,1)} %slice_dynamic-update-slice_fusion.4.refs_3_), channel_id=1, source_target_pairs={{0,96},{8,104},{16,112},{24,120},{32,0},{40,8},{48,16},{56,24},{64... | collective-permute-start | bytes 4325384 | tf_op jit(solution)/shard_map/ppermute | solution.py:39
  66.1 32.9 %collective-permute-start.10 = (bf16[2816,256]{1,0:T(8,128)(2,1)}, bf16[2816,256]{1,0:T(8,128)(2,1)}, u32[]{:S(2)}, u32[]{:S(2)}) collective-permute-start(bf16[2816,256]{1,0:T(8,128)(2,1)} %slice_dynamic-update-slice_fusion.4.refs_3_), channel_id=1, source_target_pairs={{0,32},{8,40},{16,48},{24,56},{32,64},{40,72},{48,80},{56,88},{64,... | collective-permute-start | bytes 4325384 | tf_op jit(solution)/shard_map/ppermute | solution.py:39
  69.2 5.1 %copy-start.27 = (bf16[608,256]{1,0:T(8,128)(2,1)}, bf16[608,256]{1,0:T(8,128)(2,1)S(1)}, u32[]{:S(2)}) copy-start(bf16[608,256]{1,0:T(8,128)(2,1)S(1)} %collective-permute-done.5) | copy-start | bytes 933892
  69.9 32.5 %collective-permute-start.7 = (bf16[2816,256]{1,0:T(8,128)(2,1)}, bf16[2816,256]{1,0:T(8,128)(2,1)}, u32[]{:S(2)}, u32[]{:S(2)}) collective-permute-start(bf16[2816,256]{1,0:T(8,128)(2,1)} %slice_dynamic-update-slice_fusion.5.refs_0_), channel_id=1, source_target_pairs={{0,24},{8,0},{16,8},{24,16},{32,56},{40,32},{48,40},{56,48},{64,88... | collective-permute-start | bytes 4325384 | tf_op jit(solution)/shard_map/ppermute | solution.py:39
  72.5 33.3 %collective-permute-start.6 = (bf16[2816,256]{1,0:T(8,128)(2,1)}, bf16[2816,256]{1,0:T(8,128)(2,1)}, u32[]{:S(2)}, u32[]{:S(2)}) collective-permute-start(bf16[2816,256]{1,0:T(8,128)(2,1)} %slice_dynamic-update-slice_fusion.5.refs_0_), channel_id=1, source_target_pairs={{0,8},{8,16},{16,24},{24,0},{32,40},{40,48},{48,56},{56,32},{64,72... | collective-permute-start | bytes 4325384 | tf_op jit(solution)/shard_map/ppermute | solution.py:39
  77.4 8.2 %slice-start.2 = ((bf16[1216,256]{1,0:T(8,128)(2,1)}), bf16[512,256]{1,0:T(8,128)(2,1)S(1)}, s32[]{:S(2)}) async-start(bf16[1216,256]{1,0:T(8,128)(2,1)} %copy-done.18), calls=%async_computation.4 | async-start | bytes 524288 | tf_op jit(solution)/shard_map/slice | solution.py:481
  77.4 8.2 %slice-start.3 = ((bf16[1216,256]{1,0:T(8,128)(2,1)}), bf16[512,256]{1,0:T(8,128)(2,1)S(1)}, s32[]{:S(2)}) async-start(bf16[1216,256]{1,0:T(8,128)(2,1)} %copy-done.19), calls=%async_computation.5 | async-start | bytes 524288 | tf_op jit(solution)/shard_map/slice | solution.py:480
  81.1 12.1 %all-to-all-start.1 = ((bf16[8,4,16,256]{3,2,1,0:T(8,128)(2,1)}), bf16[8,4,16,256]{3,2,1,0:T(8,128)(2,1)}, u32[]{:S(2)}, u32[]{:S(2)}) async-start(bf16[8,4,16,256]{3,2,1,0:T(8,128)(2,1)} %broadcast_in_dim.2), calls=%async_computation.1 | async-start | bytes 524288 | tf_op jit(solution)/shard_map/all_to_all | solution.py:506
  86.7 27.3 %copy-start.20 = (s32[1024,2]{1,0:T(8,128)S(1)}, s32[1024,2]{1,0:T(8,128)}, u32[]{:S(2)}) copy-start(s32[1024,2]{1,0:T(8,128)} %copy.34.routes_ref) | copy-start | bytes 24580
  86.7 27.3 %copy-start.21 = (s32[13]{0:T(128)S(1)}, s32[13]{0:T(128)}, u32[]{:S(2)}) copy-start(s32[13]{0:T(128)} %pad_add_fusion.1.info_ref) | copy-start | bytes 160
  93.2 20.7 %copy-start.1 = (bf16[1024,2048]{1,0:T(8,128)(2,1)S(1)}, bf16[1024,2048]{1,0:T(8,128)(2,1)}, u32[]{:S(2)}) copy-start(bf16[1024,2048]{1,0:T(8,128)(2,1)} %x_ref.3) | copy-start | bytes 12582916
  108.7 19.8 %collective-permute-start.12 = (bf16[1408,256]{1,0:T(8,128)(2,1)S(1)}, bf16[1408,256]{1,0:T(8,128)(2,1)S(1)}, u32[]{:S(2)}, u32[]{:S(2)}) collective-permute-start(bf16[1408,256]{1,0:T(8,128)(2,1)S(1)} %get-tuple-element.64), channel_id=1, source_target_pairs={{0,8},{8,16},{16,24},{24,0},{32,40},{40,48},{48,56},{56,32},{64,72... | collective-permute-start | bytes 2162696 | tf_op jit(solution)/shard_map/ppermute | solution.py:39
  108.7 19.8 %collective-permute-start.13 = (bf16[1408,256]{1,0:T(8,128)(2,1)S(1)}, bf16[1408,256]{1,0:T(8,128)(2,1)S(1)}, u32[]{:S(2)}, u32[]{:S(2)}) collective-permute-start(bf16[1408,256]{1,0:T(8,128)(2,1)S(1)} %get-tuple-element.65), channel_id=1, source_target_pairs={{0,24},{8,0},{16,8},{24,16},{32,56},{40,32},{48,40},{56,48},{64,88... | collective-permute-start | bytes 2162696 | tf_op jit(solution)/shard_map/ppermute | solution.py:39
  112.0 16.5 %collective-permute-start.14 = (bf16[1408,256]{1,0:T(8,128)(2,1)S(1)}, bf16[1408,256]{1,0:T(8,128)(2,1)S(1)}, u32[]{:S(2)}, u32[]{:S(2)}) collective-permute-start(bf16[1408,256]{1,0:T(8,128)(2,1)S(1)} %get-tuple-element.66), channel_id=1, source_target_pairs={{0,32},{8,40},{16,48},{24,56},{32,64},{40,72},{48,80},{56,88},{64,... | collective-permute-start | bytes 2162696 | tf_op jit(solution)/shard_map/ppermute | solution.py:39
  112.2 16.3 %collective-permute-start.15 = (bf16[1408,256]{1,0:T(8,128)(2,1)S(1)}, bf16[1408,256]{1,0:T(8,128)(2,1)S(1)}, u32[]{:S(2)}, u32[]{:S(2)}) collective-permute-start(bf16[1408,256]{1,0:T(8,128)(2,1)S(1)} %get-tuple-element.67), channel_id=1, source_target_pairs={{0,96},{8,104},{16,112},{24,120},{32,0},{40,8},{48,16},{56,24},{64... | collective-permute-start | bytes 2162696 | tf_op jit(solution)/shard_map/ppermute | solution.py:39
  128.5 24.6 %collective-permute-start.17 = (bf16[2048,256]{1,0:T(8,128)(2,1)S(1)}, bf16[2048,256]{1,0:T(8,128)(2,1)S(1)}, u32[]{:S(2)}, u32[]{:S(2)}) collective-permute-start(bf16[2048,256]{1,0:T(8,128)(2,1)S(1)} %pad_maximum_fusion.refs_0_), channel_id=1, source_target_pairs={{0,24},{8,0},{16,8},{24,16},{32,56},{40,32},{48,40},{56,48},{64,88... | collective-permute-start | bytes 3145736 | tf_op jit(solution)/shard_map/ppermute | solution.py:39
  128.6 24.6 %collective-permute-start.16 = (bf16[2048,256]{1,0:T(8,128)(2,1)S(1)}, bf16[2048,256]{1,0:T(8,128)(2,1)S(1)}, u32[]{:S(2)}, u32[]{:S(2)}) collective-permute-start(bf16[2048,256]{1,0:T(8,128)(2,1)S(1)} %pad_maximum_fusion.refs_0_), channel_id=1, source_target_pairs={{0,8},{8,16},{16,24},{24,0},{32,40},{40,48},{48,56},{56,32},{64,72... | collective-permute-start | bytes 3145736 | tf_op jit(solution)/shard_map/ppermute | solution.py:39
  130.6 22.6 %collective-permute-start.19 = (bf16[2048,256]{1,0:T(8,128)(2,1)S(1)}, bf16[2048,256]{1,0:T(8,128)(2,1)S(1)}, u32[]{:S(2)}, u32[]{:S(2)}) collective-permute-start(bf16[2048,256]{1,0:T(8,128)(2,1)S(1)} %pad_maximum_fusion.1.refs_5_), channel_id=1, source_target_pairs={{0,96},{8,104},{16,112},{24,120},{32,0},{40,8},{48,16},{56,24},{64... | collective-permute-start | bytes 3145736 | tf_op jit(solution)/shard_map/ppermute | solution.py:39
  130.6 22.6 %collective-permute-start.18 = (bf16[2048,256]{1,0:T(8,128)(2,1)S(1)}, bf16[2048,256]{1,0:T(8,128)(2,1)S(1)}, u32[]{:S(2)}, u32[]{:S(2)}) collective-permute-start(bf16[2048,256]{1,0:T(8,128)(2,1)S(1)} %pad_maximum_fusion.1.refs_5_), channel_id=1, source_target_pairs={{0,32},{8,40},{16,48},{24,56},{32,64},{40,72},{48,80},{56,88},{64,... | collective-permute-start | bytes 3145736 | tf_op jit(solution)/shard_map/ppermute | solution.py:39
  153.1 2.7 %copy-start.2 = (bf16[8,1024,256]{2,1,0:T(8,128)(2,1)}, bf16[8,1024,256]{2,1,0:T(8,128)(2,1)S(1)}, u32[]{:S(2)}) copy-start(bf16[8,1024,256]{2,1,0:T(8,128)(2,1)S(1)} %attention.1.lhs_ref) | copy-start | bytes 12582916
  153.2 2.9 %copy-start.5 = (bf16[2048,256]{1,0:T(8,128)(2,1)}, bf16[2048,256]{1,0:T(8,128)(2,1)S(1)}, u32[]{:S(2)}) copy-start(bf16[2048,256]{1,0:T(8,128)(2,1)S(1)} %collective-permute-done.17.refs_1_.refs_2_) | copy-start | bytes 3145732
  153.2 3.2 %copy-start.8 = (bf16[2048,256]{1,0:T(8,128)(2,1)}, bf16[2048,256]{1,0:T(8,128)(2,1)S(1)}, u32[]{:S(2)}) copy-start(bf16[2048,256]{1,0:T(8,128)(2,1)S(1)} %collective-permute-done.16.refs_0_.refs_1_) | copy-start | bytes 3145732
  153.2 3.5 %copy-start.11 = (bf16[2048,256]{1,0:T(8,128)(2,1)}, bf16[2048,256]{1,0:T(8,128)(2,1)S(1)}, u32[]{:S(2)}) copy-start(bf16[2048,256]{1,0:T(8,128)(2,1)S(1)} %collective-permute-done.19.refs_3_.refs_7_) | copy-start | bytes 3145732
  153.2 3.8 %copy-start.14 = (bf16[2048,256]{1,0:T(8,128)(2,1)}, bf16[2048,256]{1,0:T(8,128)(2,1)S(1)}, u32[]{:S(2)}) copy-start(bf16[2048,256]{1,0:T(8,128)(2,1)S(1)} %collective-permute-done.18.refs_2_.refs_6_) | copy-start | bytes 3145732
  157.1 10.6 %collective-permute-start.20 = (bf16[1024,256]{1,0:T(8,128)(2,1)}, bf16[1024,256]{1,0:T(8,128)(2,1)S(1)}, u32[]{:S(2)}, u32[]{:S(2)}) collective-permute-start(bf16[1024,256]{1,0:T(8,128)(2,1)} %get-tuple-element.82), channel_id=1, source_target_pairs={{0,8},{8,16},{16,24},{24,0},{32,40},{40,48},{48,56},{56,32},{64,72... | collective-permute-start | bytes 1572872 | tf_op jit(solution)/shard_map/ppermute | solution.py:39
  157.1 10.6 %collective-permute-start.21 = (bf16[1024,256]{1,0:T(8,128)(2,1)}, bf16[1024,256]{1,0:T(8,128)(2,1)}, u32[]{:S(2)}, u32[]{:S(2)}) collective-permute-start(bf16[1024,256]{1,0:T(8,128)(2,1)} %get-tuple-element.83), channel_id=1, source_target_pairs={{0,24},{8,0},{16,8},{24,16},{32,56},{40,32},{48,40},{56,48},{64,88... | collective-permute-start | bytes 1572872 | tf_op jit(solution)/shard_map/ppermute | solution.py:39
  160.3 9.5 %collective-permute-start.22 = (bf16[1024,256]{1,0:T(8,128)(2,1)}, bf16[1024,256]{1,0:T(8,128)(2,1)}, u32[]{:S(2)}, u32[]{:S(2)}) collective-permute-start(bf16[1024,256]{1,0:T(8,128)(2,1)} %get-tuple-element.84), channel_id=1, source_target_pairs={{0,32},{8,40},{16,48},{24,56},{32,64},{40,72},{48,80},{56,88},{64,... | collective-permute-start | bytes 1572872 | tf_op jit(solution)/shard_map/ppermute | solution.py:39
  160.7 10.7 %collective-permute-start.23 = (bf16[1024,256]{1,0:T(8,128)(2,1)}, bf16[1024,256]{1,0:T(8,128)(2,1)}, u32[]{:S(2)}, u32[]{:S(2)}) collective-permute-start(bf16[1024,256]{1,0:T(8,128)(2,1)} %get-tuple-element.85), channel_id=1, source_target_pairs={{0,96},{8,104},{16,112},{24,120},{32,0},{40,8},{48,16},{56,24},{64... | collective-permute-start | bytes 1572872 | tf_op jit(solution)/shard_map/ppermute | solution.py:39
  171.4 2.2 copy-start.3
  178.5 5.2 %copy-start.7 = (bf16[2048,256]{1,0:T(8,128)(2,1)S(1)}, bf16[2048,256]{1,0:T(8,128)(2,1)}, u32[]{:S(2)}) copy-start(bf16[2048,256]{1,0:T(8,128)(2,1)} %copy-done.5) | copy-start | bytes 3145732
  178.5 5.2 %copy-start.10 = (bf16[2048,256]{1,0:T(8,128)(2,1)S(1)}, bf16[2048,256]{1,0:T(8,128)(2,1)}, u32[]{:S(2)}) copy-start(bf16[2048,256]{1,0:T(8,128)(2,1)} %copy-done.8) | copy-start | bytes 3145732
  178.5 5.2 %copy-start.13 = (bf16[2048,256]{1,0:T(8,128)(2,1)S(1)}, bf16[2048,256]{1,0:T(8,128)(2,1)}, u32[]{:S(2)}) copy-start(bf16[2048,256]{1,0:T(8,128)(2,1)} %copy-done.11) | copy-start | bytes 3145732
  191.2 14.4 %collective-permute-start.25 = (bf16[3,1024,256]{2,1,0:T(8,128)(2,1)S(1)}, bf16[3,1024,256]{2,1,0:T(8,128)(2,1)S(1)}, u32[]{:S(2)}, u32[]{:S(2)}) collective-permute-start(bf16[3,1024,256]{2,1,0:T(8,128)(2,1)S(1)} %project_out_3.1), channel_id=1, source_target_pairs={{0,1},{1,0},{2,3},{3,2},{4,5},{5,4},{6,7},{7,6},{8,9},{9,8},{10,11... | collective-permute-start | bytes 4718600 | tf_op jit(solution)/shard_map/ppermute | solution.py:399
  191.3 7.7 %copy-start.4 = (bf16[8,1024,256]{2,1,0:T(8,128)(2,1)S(1)}, bf16[8,1024,256]{2,1,0:T(8,128)(2,1)}, u32[]{:S(2)}) copy-start(bf16[8,1024,256]{2,1,0:T(8,128)(2,1)} %copy-done.2) | copy-start | bytes 12582916
  191.3 4.1 %collective-permute-start.24 = (bf16[1024,256]{1,0:T(8,128)(2,1)S(1)}, bf16[1024,256]{1,0:T(8,128)(2,1)S(1)}, u32[]{:S(2)}, u32[]{:S(2)}) collective-permute-start(bf16[1024,256]{1,0:T(8,128)(2,1)S(1)} %get-tuple-element.88), channel_id=1, source_target_pairs={{0,1},{1,0},{2,3},{3,2},{4,5},{5,4},{6,7},{7,6},{8,9},{9,8},{10,11... | collective-permute-start | bytes 1572872 | tf_op jit(solution)/shard_map/ppermute | solution.py:399
  195.6 10.0 %collective-permute-start.26 = (bf16[512,256]{1,0:T(8,128)(2,1)S(1)}, bf16[512,256]{1,0:T(8,128)(2,1)S(1)}, u32[]{:S(2)}, u32[]{:S(2)}) collective-permute-start(bf16[512,256]{1,0:T(8,128)(2,1)S(1)} %get-tuple-element.89), channel_id=1, source_target_pairs={{0,2},{1,3},{2,4},{3,5},{4,6},{5,7},{6,0},{7,1},{8,10},{9,11},{10,... | collective-permute-start | bytes 786440 | tf_op jit(solution)/shard_map/ppermute | solution.py:400
  196.8 8.3 %collective-permute-start.27 = (bf16[512,256]{1,0:T(8,128)(2,1)S(1)}, bf16[512,256]{1,0:T(8,128)(2,1)S(1)}, u32[]{:S(2)}, u32[]{:S(2)}) collective-permute-start(bf16[512,256]{1,0:T(8,128)(2,1)S(1)} %get-tuple-element.91), channel_id=1, source_target_pairs={{0,6},{1,7},{2,0},{3,1},{4,2},{5,3},{6,4},{7,5},{8,14},{9,15},{10,... | collective-permute-start | bytes 786440 | tf_op jit(solution)/shard_map/ppermute | solution.py:400
  205.9 13.8 %collective-permute-start.29 = (bf16[1024,256]{1,0:T(8,128)(2,1)S(1)}, bf16[1024,256]{1,0:T(8,128)(2,1)S(1)}, u32[]{:S(2)}, u32[]{:S(2)}) collective-permute-start(bf16[1024,256]{1,0:T(8,128)(2,1)S(1)} %get-tuple-element.94), channel_id=1, source_target_pairs={{0,6},{1,7},{2,0},{3,1},{4,2},{5,3},{6,4},{7,5},{8,14},{9,15},{10,... | collective-permute-start | bytes 1572872 | tf_op jit(solution)/shard_map/ppermute | solution.py:400
  209.0 14.1 %collective-permute-start.28 = (bf16[1024,256]{1,0:T(8,128)(2,1)S(1)}, bf16[1024,256]{1,0:T(8,128)(2,1)S(1)}, u32[]{:S(2)}, u32[]{:S(2)}) collective-permute-start(bf16[1024,256]{1,0:T(8,128)(2,1)S(1)} %get-tuple-element.92), channel_id=1, source_target_pairs={{0,2},{1,3},{2,4},{3,5},{4,6},{5,7},{6,0},{7,1},{8,10},{9,11},{10,... | collective-permute-start | bytes 1572872 | tf_op jit(solution)/shard_map/ppermute | solution.py:400
  (13 other events, 16.9 us)

commit v3 on v2

--- a/solution.py
+++ b/solution.py
@@ -452,9 +452,17 @@
         )
         for half in range(2)
     ]
+    adapter_hot = (
+        adapter_per_request[:, None]
+        == jnp.arange(adapter_storage_slot.shape[0], dtype=jnp.int32)[None, :]
+    ).astype(jnp.int32)
+    slots = jnp.sum(adapter_hot * adapter_storage_slot[None, :], axis=1)
+    own_rows = lax.dynamic_slice_in_dim(prefix_cache_row, group * 4, 4, 0)
+    info = jnp.concatenate([group[None].astype(jnp.int32), slots, own_rows, cached_prefix_length])
+    place = jnp.stack([group, lax.div(part, 2), lax.rem(part, 2)]).astype(jnp.int32)
     neighbours = [*first_step(own[0], 0), *first_step(own[1], 1)]
-    *neighbours, outgoing = lax.optimization_barrier((*neighbours, outgoing))
     received = lax.all_to_all(outgoing, "req", 0, 0, tiled=True)
+    *neighbours, info, place, _ = lax.optimization_barrier((*neighbours, info, place, outgoing))
     passed = onward(neighbours, 0)
     near, near_out = [], []
     for half in range(2):
@@ -485,14 +493,6 @@
             )
         )
 
-    adapter_hot = (
-        adapter_per_request[:, None]
-        == jnp.arange(adapter_storage_slot.shape[0], dtype=jnp.int32)[None, :]
-    ).astype(jnp.int32)
-    slots = jnp.sum(adapter_hot * adapter_storage_slot[None, :], axis=1)
-    own_rows = lax.dynamic_slice_in_dim(prefix_cache_row, group * 4, 4, 0)
-    info = jnp.concatenate([group[None].astype(jnp.int32), slots, own_rows, cached_prefix_length])
-
     logits = jnp.dot(tokens, router_weight, preferred_element_type=F32)
     expert = jnp.arange(NE, dtype=jnp.int32)
     route_hot = (routes[:, :, None] == expert[None, None, :]).astype(F32)
@@ -519,7 +519,6 @@
         two = slice(half * 2, half * 2 + 2)
         out_pieces += [near_out[half], *out_beside[two], *out_late[two]]
 
-    place = jnp.stack([group, part // 2, part % 2]).astype(jnp.int32)
     operands = (gates, lhs, out_pieces)
     far, far_mine = project_out(((False, 2), (True, 2)), place, *operands, apart=True)
     far_swapped = exchange(far, 0)

time: 225 us -> 205 us (0.911)
  local copies, waits for them, and re-layouts: 27.6 us -> 16.7 us
  waiting for transfers between devices: 67.3 us -> 59.4 us
  Pallas kernels: 65.5 us -> 62.3 us
  starting transfers between devices: 52.8 us -> 55.2 us
    unnamed x93 -> x61, local copies, waits for them, and re-layouts: 19.8 us -> 8.88 us
    ppermute x24, waiting for transfers between devices: 45.4 us -> 37.1 us  [send(): lax.ppermute(value, 'req', torus(step, 0) if along == 0 else torus(0, step))]
    ppermute x24, starting transfers between devices: 33.8 us -> 36.4 us  [send(): lax.ppermute(value, 'req', torus(step, 0) if along == 0 else torus(0, step))]
  transfers between devices with their start and end apart: 32 -> 32, of which waited for: 15 -> 17; matrix products, arithmetic and copies ran while one was open for 8% -> 10% of each run, Pallas kernels for 21% -> 23%
where the time goes in v3:
time: 205 us; the launch traced here: 204 us
  Pallas kernels  62.3 us (30%)
  waiting for transfers between devices  59.4 us (29%)
  starting transfers between devices  55.2 us (27%)
  local copies, waits for them, and re-layouts  16.7 us (8%)
  other arithmetic  6.99 us (3%)
  matrix products  3.37 us (2%)
    ppermute x24, waiting for transfers between devices, send(): lax.ppermute(value, 'req', torus(step, 0) if along == 0 else torus(0, step))  37.1 us
    ppermute x24, starting transfers between devices, send(): lax.ppermute(value, 'req', torus(step, 0) if along == 0 else torus(0, step))  36.4 us
    pallas_call x4, Pallas kernels, project_out(): pl.pallas_call(functools.partial(project_out_kernel, blocks), out_shape=s...  20.4 us
    pallas_call x1, Pallas kernels, attention(): pl.pallas_call(attend_kernel, out_shape=jax.ShapeDtypeStruct((NE, 1024, 2...  19.3 us
    pallas_call x1, Pallas kernels, project_early(): pl.pallas_call(early_kernel, out_shape=(jax.ShapeDtypeStruct((4, 2, 16, 2...  14.5 us
    ppermute x4, waiting for transfers between devices, exchange(): lax.ppermute(value, 'exp', [(i, (i + 2 * step) % 8) for i in range(8)])  12.1 us
    unnamed x61, local copies, waits for them, and re-layouts  8.88 us
    all_to_all x1, starting transfers between devices, body(): received = lax.all_to_all(outgoing, 'req', 0, 0, tiled=True)  7.34 us
  transfers between devices with their start and end apart: 32, of which 17 were waited for; matrix products, arithmetic and copies ran while one was open for 10% of the time, Pallas kernels for 23%

profile of v3, /device:TPU:6, one launch (start us, length us, event | category | flops | bytes accessed | tf_op | source)
XLA Modules:
  0.0 204.5 jit_solution(1284998220425196093)
XLA Ops:
  0.0 1.7 copy.41
  2.4 0.8 constant_dynamic-update-slice_fusion.3
  3.2 0.7 constant_dynamic-update-slice_fusion.6
  4.6 0.9 pad_maximum_fusion.2
  5.4 0.8 collective-permute-start.1
  6.3 2.4 %collective-permute-start = (bf16[1216,256]{1,0:T(8,128)(2,1)}, bf16[1216,256]{1,0:T(8,128)(2,1)S(1)}, u32[]{:S(2)}, u32[]{:S(2)}) collective-permute-start(bf16[1216,256]{1,0:T(8,128)(2,1)} %pad_maximum_fusion.2), channel_id=1, source_target_pairs={{0,32},{8,40},{16,48},{24,56},{32,64},{40,72},{48,80},{56,88},{64,... | collective-permute-start | bytes 1867784 | tf_op jit(solution)/shard_map/ppermute | solution.py:39
  8.7 1.0 pad_maximum_fusion.3
  9.7 4.0 %collective-permute-start.3 = (bf16[1216,256]{1,0:T(8,128)(2,1)}, bf16[1216,256]{1,0:T(8,128)(2,1)S(1)}, u32[]{:S(2)}, u32[]{:S(2)}) collective-permute-start(bf16[1216,256]{1,0:T(8,128)(2,1)} %pad_maximum_fusion.3), channel_id=1, source_target_pairs={{0,24},{8,0},{16,8},{24,16},{32,56},{40,32},{48,40},{56,48},{64,88... | collective-permute-start | bytes 1867784 | tf_op jit(solution)/shard_map/ppermute | solution.py:39
  13.8 0.7 select_reduce_fusion.2.index_ref
  15.1 2.3 %pack.1 = bf16[16,96,512]{2,1,0:T(8,128)(2,1)} custom-call(s32[16]{0:T(128)} %select_reduce_fusion.2.index_ref, bf16[4,64,512]{2,1,0:T(8,128)(2,1)} %store_ref.1, bf16[64,256]{1,0:T(8,128)(2,1)} %bitcast.49), custom_call_target="tpu_custom_call" | custom-call | flops 3449999872 | bytes 1048576 | tf_op jit(solution)/shard_map/pack/pallas_call | solution.py:74
  17.4 7.3 %all-to-all-start = ((bf16[16,96,512]{2,1,0:T(8,128)(2,1)}), bf16[16,96,512]{2,1,0:T(8,128)(2,1)}, u32[]{:S(2)}, u32[]{:S(2)}) async-start(bf16[16,96,512]{2,1,0:T(8,128)(2,1)} %pack.1), calls=%async_computation | async-start | bytes 3145728 | tf_op jit(solution)/shard_map/all_to_all | solution.py:464
  25.7 3.4 %fusion.4 = f32[1024,8]{0,1:T(8,128)S(1)} fusion(bf16[1024,2048]{1,0:T(8,128)(2,1)} %x_ref.3, bf16[2048,8]{0,1:T(8,128)(2,1)S(1)} %copy-done.18), kind=kOutput, calls=%fused_computation.40 | convolution fusion | flops 33554432 | bytes 4259840 | tf_op jit(solution)/shard_map/dot_general | solution.py:496
  29.2 13.4 %collective-permute-done.3.refs_3_ = bf16[1216,256]{1,0:T(8,128)(2,1)S(1)} collective-permute-done((bf16[1216,256]{1,0:T(8,128)(2,1)}, bf16[1216,256]{1,0:T(8,128)(2,1)S(1)}, u32[]{:S(2)}, u32[]{:S(2)}) %collective-permute-start.3) | collective-permute-done | bytes 622624 | tf_op jit(solution)/shard_map/ppermute | solution.py:39
  42.6 4.3 %collective-permute-done.2.refs_2_ = bf16[1216,256]{1,0:T(8,128)(2,1)S(1)} collective-permute-done((bf16[1216,256]{1,0:T(8,128)(2,1)}, bf16[1216,256]{1,0:T(8,128)(2,1)S(1)}, u32[]{:S(2)}, u32[]{:S(2)}) %collective-permute-start.2) | collective-permute-done | bytes 622624 | tf_op jit(solution)/shard_map/ppermute | solution.py:39
  46.9 0.8 slice_dynamic-update-slice_fusion.3
  47.7 0.8 slice_dynamic-update-slice_fusion.2
  48.6 0.8 slice_dynamic-update-slice_fusion.1
  49.4 2.0 collective-permute-start.5
  51.4 3.2 %collective-permute-start.9 = (bf16[608,256]{1,0:T(8,128)(2,1)S(1)}, bf16[608,256]{1,0:T(8,128)(2,1)S(1)}, u32[]{:S(2)}, u32[]{:S(2)}) collective-permute-start(bf16[608,256]{1,0:T(8,128)(2,1)S(1)} %get-tuple-element.59), channel_id=1, source_target_pairs={{0,24},{8,0},{16,8},{24,16},{32,56},{40,32},{48,40},{56,48},{64,88... | collective-permute-start | bytes 933896 | tf_op jit(solution)/shard_map/ppermute | solution.py:39
  54.6 0.7 slice_dynamic-update-slice_fusion
  55.4 1.3 collective-permute-done.8
  56.7 0.7 constant_dynamic-update-slice_fusion.4
  57.4 4.5 %collective-permute-done.9 = bf16[608,256]{1,0:T(8,128)(2,1)S(1)} collective-permute-done((bf16[608,256]{1,0:T(8,128)(2,1)S(1)}, bf16[608,256]{1,0:T(8,128)(2,1)S(1)}, u32[]{:S(2)}, u32[]{:S(2)}) %collective-permute-start.9) | collective-permute-done | bytes 311328 | tf_op jit(solution)/shard_map/ppermute | solution.py:39
  63.0 2.9 %collective-permute-start.10 = (bf16[2816,256]{1,0:T(8,128)(2,1)}, bf16[2816,256]{1,0:T(8,128)(2,1)}, u32[]{:S(2)}, u32[]{:S(2)}) collective-permute-start(bf16[2816,256]{1,0:T(8,128)(2,1)} %slice_dynamic-update-slice_fusion.4.refs_3_), channel_id=1, source_target_pairs={{0,32},{8,40},{16,48},{24,56},{32,64},{40,72},{48,80},{56,88},{64,... | collective-permute-start | bytes 4325384 | tf_op jit(solution)/shard_map/ppermute | solution.py:39
  65.9 0.7 constant_dynamic-update-slice_fusion
  66.6 0.7 slice_dynamic-update-slice_fusion.5.refs_0_
  67.3 3.7 %collective-permute-start.7 = (bf16[2816,256]{1,0:T(8,128)(2,1)}, bf16[2816,256]{1,0:T(8,128)(2,1)}, u32[]{:S(2)}, u32[]{:S(2)}) collective-permute-start(bf16[2816,256]{1,0:T(8,128)(2,1)} %slice_dynamic-update-slice_fusion.5.refs_0_), channel_id=1, source_target_pairs={{0,24},{8,0},{16,8},{24,16},{32,56},{40,32},{48,40},{56,48},{64,88... | collective-permute-start | bytes 4325384 | tf_op jit(solution)/shard_map/ppermute | solution.py:39
  71.1 1.1 copy.34.routes_ref
  72.5 1.0 copy.32
  73.5 1.2 broadcast_multiply_fusion.gates_ref
  74.8 0.9 copy-done.14
  75.7 0.7 slice.113
  76.5 2.2 %pick_down.1 = bf16[4,16,256]{2,1,0:T(8,128)(2,1)} custom-call(s32[13]{0:T(128)} %pad_add_fusion.info_ref, bf16[16,96,512]{2,1,0:T(8,128)(2,1)} %all-to-all-done.recv_ref.recv_hbm), custom_call_target="tpu_custom_call" | custom-call | flops 2300000000 | bytes 1048576 | tf_op jit(solution)/shard_map/pick_down/pallas_call | solution.py:104
  78.8 1.5 broadcast_in_dim.5
  80.2 4.5 %all-to-all-start.1 = ((bf16[8,4,16,256]{3,2,1,0:T(8,128)(2,1)}), bf16[8,4,16,256]{3,2,1,0:T(8,128)(2,1)}, u32[]{:S(2)}, u32[]{:S(2)}) async-start(bf16[8,4,16,256]{3,2,1,0:T(8,128)(2,1)} %broadcast_in_dim.5), calls=%async_computation.1 | async-start | bytes 524288 | tf_op jit(solution)/shard_map/all_to_all | solution.py:506
  84.7 1.1 pad_maximum_fusion.1.refs_5_
  85.8 6.5 %all-to-all-done.1.down_ref = bf16[8,4,16,256]{3,2,1,0:T(8,128)(2,1)} async-done(((bf16[8,4,16,256]{3,2,1,0:T(8,128)(2,1)}), bf16[8,4,16,256]{3,2,1,0:T(8,128)(2,1)}, u32[]{:S(2)}, u32[]{:S(2)}) %all-to-all-start.1) | async-done | bytes 262176 | tf_op jit(solution)/shard_map/all_to_all | solution.py:506
  92.4 3.0 %forward_kernel.4 = (bf16[1408,256]{1,0:T(8,128)(2,1)S(1)}, bf16[1408,256]{1,0:T(8,128)(2,1)S(1)}, bf16[1408,256]{1,0:T(8,128)(2,1)S(1)}, bf16[1408,256]{1,0:T(8,128)(2,1)S(1)}) custom-call(bf16[2816,256]{1,0:T(8,128)(2,1)} %collective-permute-done.6.refs_0_.refs_1_, bf16[2816,256]{1,0:T(8,128)(2,1)} %collective-permute-done.7.refs_1_.refs_2_, ...), custom_call_target="tpu_custom_call" | custom-call | flops 2300000000 | bytes 1048576 | tf_op jit(solution)/shard_map/forward_kernel/pallas_call | solution.py:347
  95.5 3.3 %collective-permute-start.13 = (bf16[1408,256]{1,0:T(8,128)(2,1)S(1)}, bf16[1408,256]{1,0:T(8,128)(2,1)S(1)}, u32[]{:S(2)}, u32[]{:S(2)}) collective-permute-start(bf16[1408,256]{1,0:T(8,128)(2,1)S(1)} %get-tuple-element.67), channel_id=1, source_target_pairs={{0,24},{8,0},{16,8},{24,16},{32,56},{40,32},{48,40},{56,48},{64,88... | collective-permute-start | bytes 2162696 | tf_op jit(solution)/shard_map/ppermute | solution.py:39
  99.1 1.7 collective-permute-start.15
  100.8 14.5 %project_early.1 = (bf16[4,2,16,256]{3,2,1,0:T(8,128)(2,1)S(1)}, f32[4,4,256,256]{3,2,1,0:T(8,128)S(1)}) custom-call(s32[13]{0:T(128)S(1)} %copy-done.7, s32[1024,2]{1,0:T(8,128)S(1)} %copy-done.6, bf16[1024,2048]{1,0:T(8,128)(2,1)S(1)} %copy-done.1, bf16[2816,256]{1,0:T(8,128)(2,1)} %slice_dynamic-update-slice_fusion.5.refs_0_, ...), custom_call_target="tpu_custom_call" | custom-call | flops 17250000896 | bytes 1048576 | tf_op jit(solution)/shard_map/project_early/pallas_call | solution.py:179
  115.3 0.7 collective-permute-done.14.refs_2_
  116.0 1.3 collective-permute-done.15.refs_3_
  117.3 1.7 collective-permute-start.17
  119.8 2.8 %collective-permute-start.18 = (bf16[2048,256]{1,0:T(8,128)(2,1)S(1)}, bf16[2048,256]{1,0:T(8,128)(2,1)S(1)}, u32[]{:S(2)}, u32[]{:S(2)}) collective-permute-start(bf16[2048,256]{1,0:T(8,128)(2,1)S(1)} %pad_maximum_fusion.1.refs_5_), channel_id=1, source_target_pairs={{0,32},{8,40},{16,48},{24,56},{32,64},{40,72},{48,80},{56,88},{64,... | collective-permute-start | bytes 3145736 | tf_op jit(solution)/shard_map/ppermute | solution.py:39
  122.5 19.3 %attention.1.lhs_ref = bf16[8,1024,256]{2,1,0:T(8,128)(2,1)S(1)} custom-call(s32[13]{0:T(128)S(1)} %copy-done.7, s32[1024,2]{1,0:T(8,128)S(1)} %copy-done.6, bf16[8,4,16,256]{3,2,1,0:T(8,128)(2,1)} %all-to-all-done.1.down_ref, bf16[1024,2048]{1,0:T(8,128)(2,1)S(1)} %copy-done.1, bf16[4,2,16,256]{3,2,1,0:T(8,128)(2,1)S(1)} %get-tuple-element.73.up_ref, ...), custom_call_target="tpu_custom_call" | custom-call | flops 25300000768 | bytes 1048576 | tf_op jit(solution)/shard_map/attention/pallas_call | solution.py:258
  141.8 0.8 collective-permute-done.16.refs_0_.refs_1_
  143.5 3.0 %collective-permute-start.21 = (bf16[1024,256]{1,0:T(8,128)(2,1)S(1)}, bf16[1024,256]{1,0:T(8,128)(2,1)S(1)}, u32[]{:S(2)}, u32[]{:S(2)}) collective-permute-start(bf16[1024,256]{1,0:T(8,128)(2,1)S(1)} %get-tuple-element.85), channel_id=1, source_target_pairs={{0,24},{8,0},{16,8},{24,16},{32,56},{40,32},{48,40},{56,48},{64,88... | collective-permute-start | bytes 1572872 | tf_op jit(solution)/shard_map/ppermute | solution.py:39
  146.4 3.0 %collective-permute-start.22 = (bf16[1024,256]{1,0:T(8,128)(2,1)S(1)}, bf16[1024,256]{1,0:T(8,128)(2,1)S(1)}, u32[]{:S(2)}, u32[]{:S(2)}) collective-permute-start(bf16[1024,256]{1,0:T(8,128)(2,1)S(1)} %get-tuple-element.86), channel_id=1, source_target_pairs={{0,32},{8,40},{16,48},{24,56},{32,64},{40,72},{48,80},{56,88},{64,... | collective-permute-start | bytes 1572872 | tf_op jit(solution)/shard_map/ppermute | solution.py:39
  149.4 5.4 %collective-permute-done.20.refs_3_ = bf16[1024,256]{1,0:T(8,128)(2,1)S(1)} collective-permute-done((bf16[1024,256]{1,0:T(8,128)(2,1)S(1)}, bf16[1024,256]{1,0:T(8,128)(2,1)S(1)}, u32[]{:S(2)}, u32[]{:S(2)}) %collective-permute-start.20) | collective-permute-done | bytes 524320 | tf_op jit(solution)/shard_map/ppermute | solution.py:39
  154.8 1.7 collective-permute-done.22.refs_8_
  156.4 3.4 %collective-permute-done.23.refs_9_ = bf16[1024,256]{1,0:T(8,128)(2,1)S(1)} collective-permute-done((bf16[1024,256]{1,0:T(8,128)(2,1)S(1)}, bf16[1024,256]{1,0:T(8,128)(2,1)S(1)}, u32[]{:S(2)}, u32[]{:S(2)}) %collective-permute-start.23) | collective-permute-done | bytes 524320 | tf_op jit(solution)/shard_map/ppermute | solution.py:39
  159.8 5.3 %project_out_2.2 = (bf16[1024,256]{1,0:T(8,128)(2,1)S(1)}, bf16[1024,256]{1,0:T(8,128)(2,1)S(1)}) custom-call(s32[3]{0:T(128)S(1)} %pad_add_fusion.1.place_ref, f32[1024,8]{1,0:T(8,128)S(1)} %broadcast_multiply_fusion.gates_ref, bf16[8,1024,256]{2,1,0:T(8,128)(2,1)S(1)} %attention.1.lhs_ref, bf16[2048,256]{1,0:T(8,128)(2,1)S(1)} %pad_maximum_fusion.refs_0_, ...), custom_call_target="tpu_custom_call" | custom-call | flops 5059999744 | bytes 1048576 | tf_op jit(solution)/shard_map/project_out_2/pallas_call | solution.py:331
  165.1 7.2 %project_out_3.1 = bf16[3,1024,256]{2,1,0:T(8,128)(2,1)S(1)} custom-call(s32[3]{0:T(128)S(1)} %pad_add_fusion.1.place_ref, f32[1024,8]{1,0:T(8,128)S(1)} %broadcast_multiply_fusion.gates_ref, bf16[8,1024,256]{2,1,0:T(8,128)(2,1)S(1)} %attention.1.lhs_ref, bf16[2048,256]{1,0:T(8,128)(2,1)S(1)} %pad_maximum_fusion.refs_0_, ...), custom_call_target="tpu_custom_call" | custom-call | flops 7590000128 | bytes 1048576 | tf_op jit(solution)/shard_map/project_out_3/pallas_call | solution.py:331
  172.9 3.6 %collective-permute-done.24.theirs_ref = bf16[1024,256]{1,0:T(8,128)(2,1)S(1)} collective-permute-done((bf16[1024,256]{1,0:T(8,128)(2,1)S(1)}, bf16[1024,256]{1,0:T(8,128)(2,1)S(1)}, u32[]{:S(2)}, u32[]{:S(2)}) %collective-permute-start.24) | collective-permute-done | bytes 524320 | tf_op jit(solution)/shard_map/ppermute | solution.py:399
  176.7 1.2 collective-permute-start.26
  177.9 2.1 %collective-permute-start.27 = (bf16[512,256]{1,0:T(8,128)(2,1)S(1)}, bf16[512,256]{1,0:T(8,128)(2,1)S(1)}, u32[]{:S(2)}, u32[]{:S(2)}) collective-permute-start(bf16[512,256]{1,0:T(8,128)(2,1)S(1)} %get-tuple-element.93), channel_id=1, source_target_pairs={{0,6},{1,7},{2,0},{3,1},{4,2},{5,3},{6,4},{7,5},{8,14},{9,15},{10,... | collective-permute-start | bytes 786440 | tf_op jit(solution)/shard_map/ppermute | solution.py:400
  180.0 5.0 %project_out_2.3.mine_ref = bf16[2,1024,256]{2,1,0:T(8,128)(2,1)S(1)} custom-call(s32[3]{0:T(128)S(1)} %pad_add_fusion.1.place_ref, f32[1024,8]{1,0:T(8,128)S(1)} %broadcast_multiply_fusion.gates_ref, bf16[8,1024,256]{2,1,0:T(8,128)(2,1)S(1)} %attention.1.lhs_ref, bf16[2048,256]{1,0:T(8,128)(2,1)S(1)} %pad_maximum_fusion.refs_0_, ...), custom_call_target="tpu_custom_call" | custom-call | flops 5059999744 | bytes 1048576 | tf_op jit(solution)/shard_map/project_out_2/pallas_call | solution.py:331
  185.1 0.9 collective-permute-done.27.high_ref
  186.6 3.0 %collective-permute-start.29 = (bf16[1024,256]{1,0:T(8,128)(2,1)S(1)}, bf16[1024,256]{1,0:T(8,128)(2,1)S(1)}, u32[]{:S(2)}, u32[]{:S(2)}) collective-permute-start(bf16[1024,256]{1,0:T(8,128)(2,1)S(1)} %get-tuple-element.96), channel_id=1, source_target_pairs={{0,6},{1,7},{2,0},{3,1},{4,2},{5,3},{6,4},{7,5},{8,14},{9,15},{10,... | collective-permute-start | bytes 1572872 | tf_op jit(solution)/shard_map/ppermute | solution.py:400
  189.7 2.9 %project_out_1.1 = bf16[1,1024,256]{2,1,0:T(8,128)(2,1)S(1)} custom-call(s32[3]{0:T(128)S(1)} %pad_add_fusion.1.place_ref, f32[1024,8]{1,0:T(8,128)S(1)} %broadcast_multiply_fusion.gates_ref, bf16[8,1024,256]{2,1,0:T(8,128)(2,1)S(1)} %attention.1.lhs_ref, bf16[2048,256]{1,0:T(8,128)(2,1)S(1)} %pad_maximum_fusion.refs_0_, ...), custom_call_target="tpu_custom_call" | custom-call | flops 2529999872 | bytes 1048576 | tf_op jit(solution)/shard_map/project_out_1/pallas_call | solution.py:331
  192.6 7.4 %collective-permute-done.29 = bf16[1024,256]{1,0:T(8,128)(2,1)S(1)} collective-permute-done((bf16[1024,256]{1,0:T(8,128)(2,1)S(1)}, bf16[1024,256]{1,0:T(8,128)(2,1)S(1)}, u32[]{:S(2)}, u32[]{:S(2)}) %collective-permute-start.29) | collective-permute-done | bytes 524320 | tf_op jit(solution)/shard_map/ppermute | solution.py:400
  200.0 3.4 %collective-permute-done.28 = bf16[1024,256]{1,0:T(8,128)(2,1)S(1)} collective-permute-done((bf16[1024,256]{1,0:T(8,128)(2,1)S(1)}, bf16[1024,256]{1,0:T(8,128)(2,1)S(1)}, u32[]{:S(2)}, u32[]{:S(2)}) %collective-permute-start.28) | collective-permute-done | bytes 524320 | tf_op jit(solution)/shard_map/ppermute | solution.py:400
  203.4 1.1 fusion.1
  (114 shorter events, 8.2 us)
Async XLA Ops:
  0.0 14.5 %copy-start = (bf16[4,2048,16]{1,2,0:T(8,128)(2,1)S(1)}, bf16[4,2048,16]{1,2,0:T(8,128)(2,1)}, u32[]{:S(2)}) copy-start(bf16[4,2048,16]{1,2,0:T(8,128)(2,1)} %param.25) | copy-start | bytes 786436
  0.0 2.1 %copy-start.12 = (bf16[128,8,256]{2,1,0:T(8,128)(2,1)S(1)}, bf16[128,8,256]{2,1,0:T(8,128)(2,1)}, u32[]{:S(2)}) copy-start(bf16[128,8,256]{2,1,0:T(8,128)(2,1)} %param.23) | copy-start | bytes 1572868
  2.1 2.5 %copy-start.8 = (bf16[64,8,2,128]{3,1,2,0:T(8,128)(2,1)}, bf16[64,8,2,128]{3,1,2,0:T(8,128)(2,1)S(1)}, u32[]{:S(2)}) copy-start(bf16[64,8,2,128]{3,1,2,0:T(8,128)(2,1)S(1)} %copy.43) | copy-start | bytes 786436
  2.1 1.1 copy-start.15
  2.3 1.6 copy-start.17
  4.5 9.2 %copy-start.21 = (s32[64]{0:T(128)S(1)}, s32[64]{0:T(128)}, u32[]{:S(2)}) copy-start(s32[64]{0:T(128)} %param.18) | copy-start | bytes 772
  5.4 23.7 %collective-permute-start.1 = (bf16[1216,256]{1,0:T(8,128)(2,1)}, bf16[1216,256]{1,0:T(8,128)(2,1)S(1)}, u32[]{:S(2)}, u32[]{:S(2)}) collective-permute-start(bf16[1216,256]{1,0:T(8,128)(2,1)} %pad_maximum_fusion.2), channel_id=1, source_target_pairs={{0,96},{8,104},{16,112},{24,120},{32,0},{40,8},{48,16},{56,24},{64... | collective-permute-start | bytes 1867784 | tf_op jit(solution)/shard_map/ppermute | solution.py:39
  6.3 22.9 %collective-permute-start = (bf16[1216,256]{1,0:T(8,128)(2,1)}, bf16[1216,256]{1,0:T(8,128)(2,1)S(1)}, u32[]{:S(2)}, u32[]{:S(2)}) collective-permute-start(bf16[1216,256]{1,0:T(8,128)(2,1)} %pad_maximum_fusion.2), channel_id=1, source_target_pairs={{0,32},{8,40},{16,48},{24,56},{32,64},{40,72},{48,80},{56,88},{64,... | collective-permute-start | bytes 1867784 | tf_op jit(solution)/shard_map/ppermute | solution.py:39
  8.7 1.0 copy-start.10
  9.7 32.9 %collective-permute-start.3 = (bf16[1216,256]{1,0:T(8,128)(2,1)}, bf16[1216,256]{1,0:T(8,128)(2,1)S(1)}, u32[]{:S(2)}, u32[]{:S(2)}) collective-permute-start(bf16[1216,256]{1,0:T(8,128)(2,1)} %pad_maximum_fusion.3), channel_id=1, source_target_pairs={{0,24},{8,0},{16,8},{24,16},{32,56},{40,32},{48,40},{56,48},{64,88... | collective-permute-start | bytes 1867784 | tf_op jit(solution)/shard_map/ppermute | solution.py:39
  13.7 33.1 %collective-permute-start.2 = (bf16[1216,256]{1,0:T(8,128)(2,1)}, bf16[1216,256]{1,0:T(8,128)(2,1)S(1)}, u32[]{:S(2)}, u32[]{:S(2)}) collective-permute-start(bf16[1216,256]{1,0:T(8,128)(2,1)} %pad_maximum_fusion.3), channel_id=1, source_target_pairs={{0,8},{8,16},{16,24},{24,0},{32,40},{40,48},{48,56},{56,32},{64,72... | collective-permute-start | bytes 1867784 | tf_op jit(solution)/shard_map/ppermute | solution.py:39
  17.4 7.5 %copy-start.22 = (s32[64]{0:T(128)S(1)}, s32[64]{0:T(128)}, u32[]{:S(2)}) copy-start(s32[64]{0:T(128)} %param.20) | copy-start | bytes 772
  17.4 7.5 %copy-start.23 = (s32[4]{0:T(128)S(1)}, s32[4]{0:T(128)}, u32[]{:S(2)}) copy-start(s32[4]{0:T(128)} %param.19) | copy-start | bytes 52
  17.4 7.7 %copy-start.19 = (s32[4]{0:T(128)S(1)}, s32[4]{0:T(128)}, u32[]{:S(2)}) copy-start(s32[4]{0:T(128)} %param.17) | copy-start | bytes 52
  17.4 8.3 %copy-start.18 = (bf16[2048,8]{0,1:T(8,128)(2,1)S(1)}, bf16[2048,8]{0,1:T(8,128)(2,1)}, u32[]{:S(2)}) copy-start(bf16[2048,8]{0,1:T(8,128)(2,1)} %param.21) | copy-start | bytes 98308
  17.4 59.1 %all-to-all-start = ((bf16[16,96,512]{2,1,0:T(8,128)(2,1)}), bf16[16,96,512]{2,1,0:T(8,128)(2,1)}, u32[]{:S(2)}, u32[]{:S(2)}) async-start(bf16[16,96,512]{2,1,0:T(8,128)(2,1)} %pack.1), calls=%async_computation | async-start | bytes 3145728 | tf_op jit(solution)/shard_map/all_to_all | solution.py:464
  29.1 45.6 %copy-start.2 = (bf16[1216,256]{1,0:T(8,128)(2,1)}, bf16[1216,256]{1,0:T(8,128)(2,1)S(1)}, u32[]{:S(2)}) copy-start(bf16[1216,256]{1,0:T(8,128)(2,1)S(1)} %collective-permute-done.1.refs_1_) | copy-start | bytes 1867780
  29.1 45.6 %copy-start.3 = (bf16[1216,256]{1,0:T(8,128)(2,1)}, bf16[1216,256]{1,0:T(8,128)(2,1)S(1)}, u32[]{:S(2)}) copy-start(bf16[1216,256]{1,0:T(8,128)(2,1)S(1)} %collective-permute-done.refs_0_) | copy-start | bytes 1867780
  42.6 32.2 %copy-start.4 = (bf16[1216,256]{1,0:T(8,128)(2,1)}, bf16[1216,256]{1,0:T(8,128)(2,1)S(1)}, u32[]{:S(2)}) copy-start(bf16[1216,256]{1,0:T(8,128)(2,1)S(1)} %collective-permute-done.3.refs_3_) | copy-start | bytes 1867780
  46.9 1.8 copy-start.5
  48.5 8.2 %collective-permute-start.8 = (bf16[608,256]{1,0:T(8,128)(2,1)S(1)}, bf16[608,256]{1,0:T(8,128)(2,1)S(1)}, u32[]{:S(2)}, u32[]{:S(2)}) collective-permute-start(bf16[608,256]{1,0:T(8,128)(2,1)S(1)} %get-tuple-element.58), channel_id=1, source_target_pairs={{0,8},{8,16},{16,24},{24,0},{32,40},{40,48},{48,56},{56,32},{64,72... | collective-permute-start | bytes 933896 | tf_op jit(solution)/shard_map/ppermute | solution.py:39
  48.6 22.4 %copy-start.20 = (s32[4]{0:T(128)S(1)}, s32[4]{0:T(128)}, u32[]{:S(2)}) copy-start(s32[4]{0:T(128)} %param.16) | copy-start | bytes 52
  48.6 22.4 %copy-start.16 = (s32[1024,2]{0,1:T(2,128)S(1)}, s32[1024,2]{0,1:T(2,128)}, u32[]{:S(2)}) copy-start(s32[1024,2]{0,1:T(2,128)} %param.15) | copy-start | bytes 24580
  49.4 16.5 %collective-permute-start.4 = (bf16[608,256]{1,0:T(8,128)(2,1)S(1)}, bf16[608,256]{1,0:T(8,128)(2,1)S(1)}, u32[]{:S(2)}, u32[]{:S(2)}) collective-permute-start(bf16[608,256]{1,0:T(8,128)(2,1)S(1)} %get-tuple-element.56), channel_id=1, source_target_pairs={{0,32},{8,40},{16,48},{24,56},{32,64},{40,72},{48,80},{56,88},{64,... | collective-permute-start | bytes 933896 | tf_op jit(solution)/shard_map/ppermute | solution.py:39
  49.4 17.2 %collective-permute-start.5 = (bf16[608,256]{1,0:T(8,128)(2,1)S(1)}, bf16[608,256]{1,0:T(8,128)(2,1)S(1)}, u32[]{:S(2)}, u32[]{:S(2)}) collective-permute-start(bf16[608,256]{1,0:T(8,128)(2,1)S(1)} %get-tuple-element.57), channel_id=1, source_target_pairs={{0,96},{8,104},{16,112},{24,120},{32,0},{40,8},{48,16},{56,24},{64... | collective-permute-start | bytes 933896 | tf_op jit(solution)/shard_map/ppermute | solution.py:39
  51.4 10.5 %collective-permute-start.9 = (bf16[608,256]{1,0:T(8,128)(2,1)S(1)}, bf16[608,256]{1,0:T(8,128)(2,1)S(1)}, u32[]{:S(2)}, u32[]{:S(2)}) collective-permute-start(bf16[608,256]{1,0:T(8,128)(2,1)S(1)} %get-tuple-element.59), channel_id=1, source_target_pairs={{0,24},{8,0},{16,8},{24,16},{32,56},{40,32},{48,40},{56,48},{64,88... | collective-permute-start | bytes 933896 | tf_op jit(solution)/shard_map/ppermute | solution.py:39
  62.0 11.5 %copy-start.13 = (bf16[608,256]{1,0:T(8,128)(2,1)}, bf16[608,256]{1,0:T(8,128)(2,1)S(1)}, u32[]{:S(2)}) copy-start(bf16[608,256]{1,0:T(8,128)(2,1)S(1)} %collective-permute-done.9) | copy-start | bytes 933892
  62.6 29.7 %collective-permute-start.11 = (bf16[2816,256]{1,0:T(8,128)(2,1)}, bf16[2816,256]{1,0:T(8,128)(2,1)}, u32[]{:S(2)}, u32[]{:S(2)}) collective-permute-start(bf16[2816,256]{1,0:T(8,128)(2,1)} %slice_dynamic-update-slice_fusion.4.refs_3_), channel_id=1, source_target_pairs={{0,96},{8,104},{16,112},{24,120},{32,0},{40,8},{48,16},{56,24},{64... | collective-permute-start | bytes 4325384 | tf_op jit(solution)/shard_map/ppermute | solution.py:39
  63.0 29.4 %collective-permute-start.10 = (bf16[2816,256]{1,0:T(8,128)(2,1)}, bf16[2816,256]{1,0:T(8,128)(2,1)}, u32[]{:S(2)}, u32[]{:S(2)}) collective-permute-start(bf16[2816,256]{1,0:T(8,128)(2,1)} %slice_dynamic-update-slice_fusion.4.refs_3_), channel_id=1, source_target_pairs={{0,32},{8,40},{16,48},{24,56},{32,64},{40,72},{48,80},{56,88},{64,... | collective-permute-start | bytes 4325384 | tf_op jit(solution)/shard_map/ppermute | solution.py:39
  66.6 8.1 %copy-start.11 = (bf16[608,256]{1,0:T(8,128)(2,1)}, bf16[608,256]{1,0:T(8,128)(2,1)S(1)}, u32[]{:S(2)}) copy-start(bf16[608,256]{1,0:T(8,128)(2,1)S(1)} %collective-permute-done.5) | copy-start | bytes 933892
  67.3 25.1 %collective-permute-start.7 = (bf16[2816,256]{1,0:T(8,128)(2,1)}, bf16[2816,256]{1,0:T(8,128)(2,1)}, u32[]{:S(2)}, u32[]{:S(2)}) collective-permute-start(bf16[2816,256]{1,0:T(8,128)(2,1)} %slice_dynamic-update-slice_fusion.5.refs_0_), channel_id=1, source_target_pairs={{0,24},{8,0},{16,8},{24,16},{32,56},{40,32},{48,40},{56,48},{64,88... | collective-permute-start | bytes 4325384 | tf_op jit(solution)/shard_map/ppermute | solution.py:39
  71.0 21.4 %collective-permute-start.6 = (bf16[2816,256]{1,0:T(8,128)(2,1)}, bf16[2816,256]{1,0:T(8,128)(2,1)}, u32[]{:S(2)}, u32[]{:S(2)}) collective-permute-start(bf16[2816,256]{1,0:T(8,128)(2,1)} %slice_dynamic-update-slice_fusion.5.refs_0_), channel_id=1, source_target_pairs={{0,8},{8,16},{16,24},{24,0},{32,40},{40,48},{48,56},{56,32},{64,72... | collective-permute-start | bytes 4325384 | tf_op jit(solution)/shard_map/ppermute | solution.py:39
  74.7 1.0 copy-start.14
  74.7 1.7 slice-start.1
  74.8 1.7 copy-start.9
  74.8 1.7 slice-start.4
  74.8 1.6 slice-start
  76.5 8.2 %slice-start.2 = ((bf16[1216,256]{1,0:T(8,128)(2,1)}), bf16[512,256]{1,0:T(8,128)(2,1)S(1)}, s32[]{:S(2)}) async-start(bf16[1216,256]{1,0:T(8,128)(2,1)} %copy-done.4), calls=%async_computation.4 | async-start | bytes 524288 | tf_op jit(solution)/shard_map/slice | solution.py:489
  76.5 8.2 %slice-start.3 = ((bf16[1216,256]{1,0:T(8,128)(2,1)}), bf16[512,256]{1,0:T(8,128)(2,1)S(1)}, s32[]{:S(2)}) async-start(bf16[1216,256]{1,0:T(8,128)(2,1)} %copy-done.5), calls=%async_computation.5 | async-start | bytes 524288 | tf_op jit(solution)/shard_map/slice | solution.py:488
  80.2 12.1 %all-to-all-start.1 = ((bf16[8,4,16,256]{3,2,1,0:T(8,128)(2,1)}), bf16[8,4,16,256]{3,2,1,0:T(8,128)(2,1)}, u32[]{:S(2)}, u32[]{:S(2)}) async-start(bf16[8,4,16,256]{3,2,1,0:T(8,128)(2,1)} %broadcast_in_dim.5), calls=%async_computation.1 | async-start | bytes 524288 | tf_op jit(solution)/shard_map/all_to_all | solution.py:506
  85.8 15.0 %copy-start.6 = (s32[1024,2]{1,0:T(8,128)S(1)}, s32[1024,2]{1,0:T(8,128)}, u32[]{:S(2)}) copy-start(s32[1024,2]{1,0:T(8,128)} %copy.34.routes_ref) | copy-start | bytes 24580
  85.8 15.0 %copy-start.7 = (s32[13]{0:T(128)S(1)}, s32[13]{0:T(128)}, u32[]{:S(2)}) copy-start(s32[13]{0:T(128)} %pad_add_fusion.info_ref) | copy-start | bytes 160
  92.3 8.5 %copy-start.1 = (bf16[1024,2048]{1,0:T(8,128)(2,1)S(1)}, bf16[1024,2048]{1,0:T(8,128)(2,1)}, u32[]{:S(2)}) copy-start(bf16[1024,2048]{1,0:T(8,128)(2,1)} %x_ref.3) | copy-start | bytes 12582916
  95.4 19.9 %collective-permute-start.12 = (bf16[1408,256]{1,0:T(8,128)(2,1)S(1)}, bf16[1408,256]{1,0:T(8,128)(2,1)S(1)}, u32[]{:S(2)}, u32[]{:S(2)}) collective-permute-start(bf16[1408,256]{1,0:T(8,128)(2,1)S(1)} %get-tuple-element.66), channel_id=1, source_target_pairs={{0,8},{8,16},{16,24},{24,0},{32,40},{40,48},{48,56},{56,32},{64,72... | collective-permute-start | bytes 2162696 | tf_op jit(solution)/shard_map/ppermute | solution.py:39
  95.5 19.8 %collective-permute-start.13 = (bf16[1408,256]{1,0:T(8,128)(2,1)S(1)}, bf16[1408,256]{1,0:T(8,128)(2,1)S(1)}, u32[]{:S(2)}, u32[]{:S(2)}) collective-permute-start(bf16[1408,256]{1,0:T(8,128)(2,1)S(1)} %get-tuple-element.67), channel_id=1, source_target_pairs={{0,24},{8,0},{16,8},{24,16},{32,56},{40,32},{48,40},{56,48},{64,88... | collective-permute-start | bytes 2162696 | tf_op jit(solution)/shard_map/ppermute | solution.py:39
  98.8 17.2 %collective-permute-start.14 = (bf16[1408,256]{1,0:T(8,128)(2,1)S(1)}, bf16[1408,256]{1,0:T(8,128)(2,1)S(1)}, u32[]{:S(2)}, u32[]{:S(2)}) collective-permute-start(bf16[1408,256]{1,0:T(8,128)(2,1)S(1)} %get-tuple-element.68), channel_id=1, source_target_pairs={{0,32},{8,40},{16,48},{24,56},{32,64},{40,72},{48,80},{56,88},{64,... | collective-permute-start | bytes 2162696 | tf_op jit(solution)/shard_map/ppermute | solution.py:39
  99.1 18.2 %collective-permute-start.15 = (bf16[1408,256]{1,0:T(8,128)(2,1)S(1)}, bf16[1408,256]{1,0:T(8,128)(2,1)S(1)}, u32[]{:S(2)}, u32[]{:S(2)}) collective-permute-start(bf16[1408,256]{1,0:T(8,128)(2,1)S(1)} %get-tuple-element.69), channel_id=1, source_target_pairs={{0,96},{8,104},{16,112},{24,120},{32,0},{40,8},{48,16},{56,24},{64... | collective-permute-start | bytes 2162696 | tf_op jit(solution)/shard_map/ppermute | solution.py:39
  117.3 24.6 %collective-permute-start.17 = (bf16[2048,256]{1,0:T(8,128)(2,1)S(1)}, bf16[2048,256]{1,0:T(8,128)(2,1)S(1)}, u32[]{:S(2)}, u32[]{:S(2)}) collective-permute-start(bf16[2048,256]{1,0:T(8,128)(2,1)S(1)} %pad_maximum_fusion.refs_0_), channel_id=1, source_target_pairs={{0,24},{8,0},{16,8},{24,16},{32,56},{40,32},{48,40},{56,48},{64,88... | collective-permute-start | bytes 3145736 | tf_op jit(solution)/shard_map/ppermute | solution.py:39
  118.9 23.7 %collective-permute-start.16 = (bf16[2048,256]{1,0:T(8,128)(2,1)S(1)}, bf16[2048,256]{1,0:T(8,128)(2,1)S(1)}, u32[]{:S(2)}, u32[]{:S(2)}) collective-permute-start(bf16[2048,256]{1,0:T(8,128)(2,1)S(1)} %pad_maximum_fusion.refs_0_), channel_id=1, source_target_pairs={{0,8},{8,16},{16,24},{24,0},{32,40},{40,48},{48,56},{56,32},{64,72... | collective-permute-start | bytes 3145736 | tf_op jit(solution)/shard_map/ppermute | solution.py:39
  119.3 23.7 %collective-permute-start.19 = (bf16[2048,256]{1,0:T(8,128)(2,1)S(1)}, bf16[2048,256]{1,0:T(8,128)(2,1)S(1)}, u32[]{:S(2)}, u32[]{:S(2)}) collective-permute-start(bf16[2048,256]{1,0:T(8,128)(2,1)S(1)} %pad_maximum_fusion.1.refs_5_), channel_id=1, source_target_pairs={{0,96},{8,104},{16,112},{24,120},{32,0},{40,8},{48,16},{56,24},{64... | collective-permute-start | bytes 3145736 | tf_op jit(solution)/shard_map/ppermute | solution.py:39
  119.8 23.2 %collective-permute-start.18 = (bf16[2048,256]{1,0:T(8,128)(2,1)S(1)}, bf16[2048,256]{1,0:T(8,128)(2,1)S(1)}, u32[]{:S(2)}, u32[]{:S(2)}) collective-permute-start(bf16[2048,256]{1,0:T(8,128)(2,1)S(1)} %pad_maximum_fusion.1.refs_5_), channel_id=1, source_target_pairs={{0,32},{8,40},{16,48},{24,56},{32,64},{40,72},{48,80},{56,88},{64,... | collective-permute-start | bytes 3145736 | tf_op jit(solution)/shard_map/ppermute | solution.py:39
  143.1 11.6 %collective-permute-start.20 = (bf16[1024,256]{1,0:T(8,128)(2,1)S(1)}, bf16[1024,256]{1,0:T(8,128)(2,1)S(1)}, u32[]{:S(2)}, u32[]{:S(2)}) collective-permute-start(bf16[1024,256]{1,0:T(8,128)(2,1)S(1)} %get-tuple-element.84), channel_id=1, source_target_pairs={{0,8},{8,16},{16,24},{24,0},{32,40},{40,48},{48,56},{56,32},{64,72... | collective-permute-start | bytes 1572872 | tf_op jit(solution)/shard_map/ppermute | solution.py:39
  143.5 11.3 %collective-permute-start.21 = (bf16[1024,256]{1,0:T(8,128)(2,1)S(1)}, bf16[1024,256]{1,0:T(8,128)(2,1)S(1)}, u32[]{:S(2)}, u32[]{:S(2)}) collective-permute-start(bf16[1024,256]{1,0:T(8,128)(2,1)S(1)} %get-tuple-element.85), channel_id=1, source_target_pairs={{0,24},{8,0},{16,8},{24,16},{32,56},{40,32},{48,40},{56,48},{64,88... | collective-permute-start | bytes 1572872 | tf_op jit(solution)/shard_map/ppermute | solution.py:39
  146.4 10.0 %collective-permute-start.22 = (bf16[1024,256]{1,0:T(8,128)(2,1)S(1)}, bf16[1024,256]{1,0:T(8,128)(2,1)S(1)}, u32[]{:S(2)}, u32[]{:S(2)}) collective-permute-start(bf16[1024,256]{1,0:T(8,128)(2,1)S(1)} %get-tuple-element.86), channel_id=1, source_target_pairs={{0,32},{8,40},{16,48},{24,56},{32,64},{40,72},{48,80},{56,88},{64,... | collective-permute-start | bytes 1572872 | tf_op jit(solution)/shard_map/ppermute | solution.py:39
  149.4 10.4 %collective-permute-start.23 = (bf16[1024,256]{1,0:T(8,128)(2,1)S(1)}, bf16[1024,256]{1,0:T(8,128)(2,1)S(1)}, u32[]{:S(2)}, u32[]{:S(2)}) collective-permute-start(bf16[1024,256]{1,0:T(8,128)(2,1)S(1)} %get-tuple-element.87), channel_id=1, source_target_pairs={{0,96},{8,104},{16,112},{24,120},{32,0},{40,8},{48,16},{56,24},{64... | collective-permute-start | bytes 1572872 | tf_op jit(solution)/shard_map/ppermute | solution.py:39
  172.3 14.0 %collective-permute-start.25 = (bf16[3,1024,256]{2,1,0:T(8,128)(2,1)S(1)}, bf16[3,1024,256]{2,1,0:T(8,128)(2,1)S(1)}, u32[]{:S(2)}, u32[]{:S(2)}) collective-permute-start(bf16[3,1024,256]{2,1,0:T(8,128)(2,1)S(1)} %project_out_3.1), channel_id=1, source_target_pairs={{0,1},{1,0},{2,3},{3,2},{4,5},{5,4},{6,7},{7,6},{8,9},{9,8},{10,11... | collective-permute-start | bytes 4718600 | tf_op jit(solution)/shard_map/ppermute | solution.py:399
  172.4 4.1 %collective-permute-start.24 = (bf16[1024,256]{1,0:T(8,128)(2,1)S(1)}, bf16[1024,256]{1,0:T(8,128)(2,1)S(1)}, u32[]{:S(2)}, u32[]{:S(2)}) collective-permute-start(bf16[1024,256]{1,0:T(8,128)(2,1)S(1)} %get-tuple-element.90), channel_id=1, source_target_pairs={{0,1},{1,0},{2,3},{3,2},{4,5},{5,4},{6,7},{7,6},{8,9},{9,8},{10,11... | collective-permute-start | bytes 1572872 | tf_op jit(solution)/shard_map/ppermute | solution.py:399
  176.7 9.6 %collective-permute-start.26 = (bf16[512,256]{1,0:T(8,128)(2,1)S(1)}, bf16[512,256]{1,0:T(8,128)(2,1)S(1)}, u32[]{:S(2)}, u32[]{:S(2)}) collective-permute-start(bf16[512,256]{1,0:T(8,128)(2,1)S(1)} %get-tuple-element.91), channel_id=1, source_target_pairs={{0,2},{1,3},{2,4},{3,5},{4,6},{5,7},{6,0},{7,1},{8,10},{9,11},{10,... | collective-permute-start | bytes 786440 | tf_op jit(solution)/shard_map/ppermute | solution.py:400
  177.9 8.1 %collective-permute-start.27 = (bf16[512,256]{1,0:T(8,128)(2,1)S(1)}, bf16[512,256]{1,0:T(8,128)(2,1)S(1)}, u32[]{:S(2)}, u32[]{:S(2)}) collective-permute-start(bf16[512,256]{1,0:T(8,128)(2,1)S(1)} %get-tuple-element.93), channel_id=1, source_target_pairs={{0,6},{1,7},{2,0},{3,1},{4,2},{5,3},{6,4},{7,5},{8,14},{9,15},{10,... | collective-permute-start | bytes 786440 | tf_op jit(solution)/shard_map/ppermute | solution.py:400
  186.6 13.4 %collective-permute-start.29 = (bf16[1024,256]{1,0:T(8,128)(2,1)S(1)}, bf16[1024,256]{1,0:T(8,128)(2,1)S(1)}, u32[]{:S(2)}, u32[]{:S(2)}) collective-permute-start(bf16[1024,256]{1,0:T(8,128)(2,1)S(1)} %get-tuple-element.96), channel_id=1, source_target_pairs={{0,6},{1,7},{2,0},{3,1},{4,2},{5,3},{6,4},{7,5},{8,14},{9,15},{10,... | collective-permute-start | bytes 1572872 | tf_op jit(solution)/shard_map/ppermute | solution.py:400
  189.7 13.7 %collective-permute-start.28 = (bf16[1024,256]{1,0:T(8,128)(2,1)S(1)}, bf16[1024,256]{1,0:T(8,128)(2,1)S(1)}, u32[]{:S(2)}, u32[]{:S(2)}) collective-permute-start(bf16[1024,256]{1,0:T(8,128)(2,1)S(1)} %get-tuple-element.94), channel_id=1, source_target_pairs={{0,2},{1,3},{2,4},{3,5},{4,6},{5,7},{6,0},{7,1},{8,10},{9,11},{10,... | collective-permute-start | bytes 1572872 | tf_op jit(solution)/shard_map/ppermute | solution.py:400

commit v4 on v3

--- a/solution.py
+++ b/solution.py
@@ -503,10 +503,9 @@
 
     beside = [*first_step(near[0], 1), *first_step(near[1], 0)]
     down_part = pick_down(info, received)
-    down = lax.all_to_all(
-        jnp.broadcast_to(down_part[None], (NE, 4, 16, 256)), "exp", 0, 0, tiled=True
-    )
-    *beside, down, gates = lax.optimization_barrier((*beside, down, gates))
+    down_sent = jnp.broadcast_to(down_part[None], (NE, 4, 16, 256))
+    down = lax.all_to_all(down_sent, "exp", 0, 0, tiled=True)
+    *beside, gates, _ = lax.optimization_barrier((*beside, gates, down_sent))
     late = onward(beside, 1)
     up, sums = project_early(info, routes, tokens, [near[0], *beside[:2], near[1], *beside[2:]])
     *late, near_out[0], near_out[1] = lax.optimization_barrier((*late, *near_out))
@@ -523,7 +522,7 @@
     far, far_mine = project_out(((False, 2), (True, 2)), place, *operands, apart=True)
     far_swapped = exchange(far, 0)
     place = lax.optimization_barrier((place, far_mine))[0]
-    (theirs,) = project_out(((False, 1), (False, 3), (False, 0)), place, *operands)
+    (theirs,) = project_out(((False, 1), (False, 3)), place, *operands)
     swapped = exchange(theirs, 0)
     low, high = small_call(far_sum_kernel, [(512, 256)] * 2, 1, far_mine, far_swapped)
     place = lax.optimization_barrier((place, theirs, low))[0]
@@ -532,8 +531,11 @@
     ahead, behind = small_call(near_sum_kernel, [(1024, 256)] * 2, 2, mine, swapped, low, high)
     from_behind, from_ahead = exchange(ahead, 1), exchange(behind, -1)
     place = lax.optimization_barrier((place, ahead))[0]
+    (near_block,) = project_out(((False, 0),), place, *operands)
+    near_swapped = exchange(near_block, 0)
+    place = lax.optimization_barrier((place, near_block))[0]
     (own_block,) = project_out(((True, 0),), place, *operands)
-    return rounded_sum(own_block[0], swapped[2], from_behind, from_ahead)
+    return rounded_sum(own_block[0], near_swapped[0], from_behind, from_ahead)
 
 
 def solution(mesh):

time: 205 us -> 217 us (1.059)
  local copies, waits for them, and re-layouts: 16.7 us -> 30.6 us
  Pallas kernels: 62.3 us -> 67.4 us
  waiting for transfers between devices: 59.4 us -> 54.7 us
    unnamed x61 -> x83, local copies, waits for them, and re-layouts: 8.88 us -> 23.2 us
    all_to_all x1, waiting for transfers between devices: 6.51 us -> 0.01 us  [body(): down = lax.all_to_all(down_sent, 'exp', 0, 0, tiled=True)]
    ppermute x24, waiting for transfers between devices: 37.1 us -> 42.4 us  [send(): lax.ppermute(value, 'req', torus(step, 0) if along == 0 else torus(0, step))]
    ppermute x2 -> x3, waiting for transfers between devices: 3.65 us -> 0.01 us  [exchange(): return lax.ppermute(value, 'exp', [(i, i ^ 1) for i in range(8)])]
    pallas_call x4 -> x5, Pallas kernels: 20.4 us -> 23.9 us  [project_out(): pl.pallas_call(functools.partial(project_out_kernel, blocks), out_shape=s...]
  transfers between devices with their start and end apart: 32 -> 33, of which waited for: 17 -> 14; matrix products, arithmetic and copies ran while one was open for 10% -> 7% of each run, Pallas kernels for 23% -> 26%
where the time goes in v4:
time: 217 us; the launch traced here: 216 us
  Pallas kernels  67.4 us (31%)
  waiting for transfers between devices  54.7 us (25%)
  starting transfers between devices  54.4 us (25%)
  local copies, waits for them, and re-layouts  30.6 us (14%)
  other arithmetic  4.95 us (2%)
  matrix products  3.37 us (2%)
    ppermute x24, waiting for transfers between devices, send(): lax.ppermute(value, 'req', torus(step, 0) if along == 0 else torus(0, step))  42.4 us
    ppermute x24, starting transfers between devices, send(): lax.ppermute(value, 'req', torus(step, 0) if along == 0 else torus(0, step))  35.4 us
    pallas_call x5, Pallas kernels, project_out(): pl.pallas_call(functools.partial(project_out_kernel, blocks), out_shape=s...  23.9 us
    unnamed x83, local copies, waits for them, and re-layouts  23.2 us
    pallas_call x1, Pallas kernels, attention(): pl.pallas_call(attend_kernel, out_shape=jax.ShapeDtypeStruct((NE, 1024, 2...  19.1 us
    pallas_call x1, Pallas kernels, project_early(): pl.pallas_call(early_kernel, out_shape=(jax.ShapeDtypeStruct((4, 2, 16, 2...  14.5 us
    ppermute x4, waiting for transfers between devices, exchange(): lax.ppermute(value, 'exp', [(i, (i + 2 * step) % 8) for i in range(8)])  12.3 us
    all_to_all x1, starting transfers between devices, body(): received = lax.all_to_all(outgoing, 'req', 0, 0, tiled=True)  7.34 us
  transfers between devices with their start and end apart: 33, of which 14 were waited for; matrix products, arithmetic and copies ran while one was open for 7% of the time, Pallas kernels for 26%

profile of v4, /device:TPU:6, one launch (start us, length us, event | category | flops | bytes accessed | tf_op | source)
XLA Modules:
  0.0 216.0 jit_solution(9245800942047280491)
XLA Ops:
  0.0 1.7 copy.41
  2.4 0.8 constant_dynamic-update-slice_fusion.3
  4.5 0.9 pad_maximum_fusion.2
  5.4 0.8 collective-permute-start.1
  6.3 2.4 %collective-permute-start = (bf16[1216,256]{1,0:T(8,128)(2,1)}, bf16[1216,256]{1,0:T(8,128)(2,1)S(1)}, u32[]{:S(2)}, u32[]{:S(2)}) collective-permute-start(bf16[1216,256]{1,0:T(8,128)(2,1)} %pad_maximum_fusion.2), channel_id=1, source_target_pairs={{0,32},{8,40},{16,48},{24,56},{32,64},{40,72},{48,80},{56,88},{64,... | collective-permute-start | bytes 1867784 | tf_op jit(solution)/shard_map/ppermute | solution.py:39
  9.4 0.9 pad_maximum_fusion.3
  10.3 4.0 %collective-permute-start.3 = (bf16[1216,256]{1,0:T(8,128)(2,1)}, bf16[1216,256]{1,0:T(8,128)(2,1)S(1)}, u32[]{:S(2)}, u32[]{:S(2)}) collective-permute-start(bf16[1216,256]{1,0:T(8,128)(2,1)} %pad_maximum_fusion.3), channel_id=1, source_target_pairs={{0,24},{8,0},{16,8},{24,16},{32,56},{40,32},{48,40},{56,48},{64,88... | collective-permute-start | bytes 1867784 | tf_op jit(solution)/shard_map/ppermute | solution.py:39
  15.8 2.3 %pack.1 = bf16[16,96,512]{2,1,0:T(8,128)(2,1)} custom-call(s32[16]{0:T(128)} %select_reduce_fusion.2.index_ref, bf16[4,64,512]{2,1,0:T(8,128)(2,1)} %store_ref.1, bf16[64,256]{1,0:T(8,128)(2,1)} %bitcast.49), custom_call_target="tpu_custom_call" | custom-call | flops 3449999872 | bytes 1048576 | tf_op jit(solution)/shard_map/pack/pallas_call | solution.py:74
  18.1 7.3 %all-to-all-start = ((bf16[16,96,512]{2,1,0:T(8,128)(2,1)}), bf16[16,96,512]{2,1,0:T(8,128)(2,1)}, u32[]{:S(2)}, u32[]{:S(2)}) async-start(bf16[16,96,512]{2,1,0:T(8,128)(2,1)} %pack.1), calls=%async_computation | async-start | bytes 3145728 | tf_op jit(solution)/shard_map/all_to_all | solution.py:464
  26.4 3.4 %fusion.4 = f32[1024,8]{0,1:T(8,128)S(1)} fusion(bf16[1024,2048]{1,0:T(8,128)(2,1)} %x_ref.3, bf16[2048,8]{0,1:T(8,128)(2,1)S(1)} %copy-done.29), kind=kOutput, calls=%fused_computation.40 | convolution fusion | flops 33554432 | bytes 4259840 | tf_op jit(solution)/shard_map/dot_general | solution.py:496
  29.8 13.4 %collective-permute-done.3.refs_3_ = bf16[1216,256]{1,0:T(8,128)(2,1)S(1)} collective-permute-done((bf16[1216,256]{1,0:T(8,128)(2,1)}, bf16[1216,256]{1,0:T(8,128)(2,1)S(1)}, u32[]{:S(2)}, u32[]{:S(2)}) %collective-permute-start.3) | collective-permute-done | bytes 622624 | tf_op jit(solution)/shard_map/ppermute | solution.py:39
  43.3 4.3 %collective-permute-done.2.refs_2_ = bf16[1216,256]{1,0:T(8,128)(2,1)S(1)} collective-permute-done((bf16[1216,256]{1,0:T(8,128)(2,1)}, bf16[1216,256]{1,0:T(8,128)(2,1)S(1)}, u32[]{:S(2)}, u32[]{:S(2)}) %collective-permute-start.2) | collective-permute-done | bytes 622624 | tf_op jit(solution)/shard_map/ppermute | solution.py:39
  47.5 0.8 slice_dynamic-update-slice_fusion.3
  48.3 0.8 slice_dynamic-update-slice_fusion.2
  49.3 0.8 slice_dynamic-update-slice_fusion.1
  50.1 2.0 collective-permute-start.5
  52.1 3.2 %collective-permute-start.9 = (bf16[608,256]{1,0:T(8,128)(2,1)S(1)}, bf16[608,256]{1,0:T(8,128)(2,1)S(1)}, u32[]{:S(2)}, u32[]{:S(2)}) collective-permute-start(bf16[608,256]{1,0:T(8,128)(2,1)S(1)} %get-tuple-element.59), channel_id=1, source_target_pairs={{0,24},{8,0},{16,8},{24,16},{32,56},{40,32},{48,40},{56,48},{64,88... | collective-permute-start | bytes 933896 | tf_op jit(solution)/shard_map/ppermute | solution.py:39
  56.1 1.3 collective-permute-done.8
  58.1 4.6 %collective-permute-done.9 = bf16[608,256]{1,0:T(8,128)(2,1)S(1)} collective-permute-done((bf16[608,256]{1,0:T(8,128)(2,1)S(1)}, bf16[608,256]{1,0:T(8,128)(2,1)S(1)}, u32[]{:S(2)}, u32[]{:S(2)}) %collective-permute-start.9) | collective-permute-done | bytes 311328 | tf_op jit(solution)/shard_map/ppermute | solution.py:39
  63.6 3.0 %collective-permute-start.10 = (bf16[2816,256]{1,0:T(8,128)(2,1)}, bf16[2816,256]{1,0:T(8,128)(2,1)}, u32[]{:S(2)}, u32[]{:S(2)}) collective-permute-start(bf16[2816,256]{1,0:T(8,128)(2,1)} %slice_dynamic-update-slice_fusion.4.refs_3_), channel_id=1, source_target_pairs={{0,32},{8,40},{16,48},{24,56},{32,64},{40,72},{48,80},{56,88},{64,... | collective-permute-start | bytes 4325384 | tf_op jit(solution)/shard_map/ppermute | solution.py:39
  68.0 3.7 %collective-permute-start.7 = (bf16[2816,256]{1,0:T(8,128)(2,1)}, bf16[2816,256]{1,0:T(8,128)(2,1)}, u32[]{:S(2)}, u32[]{:S(2)}) collective-permute-start(bf16[2816,256]{1,0:T(8,128)(2,1)} %slice_dynamic-update-slice_fusion.5.refs_0_), channel_id=1, source_target_pairs={{0,24},{8,0},{16,8},{24,16},{32,56},{40,32},{48,40},{56,48},{64,88... | collective-permute-start | bytes 4325384 | tf_op jit(solution)/shard_map/ppermute | solution.py:39
  71.7 1.0 copy.34.routes_ref
  73.6 0.9 slice-done.1
  75.1 2.1 pick_down.1
  77.2 1.5 broadcast_in_dim.5
  78.7 4.5 %all-to-all-start.1 = ((bf16[8,4,16,256]{3,2,1,0:T(8,128)(2,1)}), bf16[8,4,16,256]{3,2,1,0:T(8,128)(2,1)}, u32[]{:S(2)}, u32[]{:S(2)}) async-start(bf16[8,4,16,256]{3,2,1,0:T(8,128)(2,1)} %broadcast_in_dim.5), calls=%async_computation.1 | async-start | bytes 524288 | tf_op jit(solution)/shard_map/all_to_all | solution.py:507
  83.2 6.0 %collective-permute-done.11.refs_3_.refs_5_ = bf16[2816,256]{1,0:T(8,128)(2,1)} collective-permute-done((bf16[2816,256]{1,0:T(8,128)(2,1)}, bf16[2816,256]{1,0:T(8,128)(2,1)}, u32[]{:S(2)}, u32[]{:S(2)}) %collective-permute-start.11) | collective-permute-done | bytes 1441824 | tf_op jit(solution)/shard_map/ppermute | solution.py:39
  89.2 1.8 collective-permute-done.7.refs_1_.refs_2_
  91.0 2.3 %collective-permute-done.6.refs_0_.refs_1_ = bf16[2816,256]{1,0:T(8,128)(2,1)} collective-permute-done((bf16[2816,256]{1,0:T(8,128)(2,1)}, bf16[2816,256]{1,0:T(8,128)(2,1)}, u32[]{:S(2)}, u32[]{:S(2)}) %collective-permute-start.6) | collective-permute-done | bytes 1441824 | tf_op jit(solution)/shard_map/ppermute | solution.py:39
  93.3 2.9 %forward_kernel.4 = (bf16[1408,256]{1,0:T(8,128)(2,1)S(1)}, bf16[1408,256]{1,0:T(8,128)(2,1)S(1)}, bf16[1408,256]{1,0:T(8,128)(2,1)S(1)}, bf16[1408,256]{1,0:T(8,128)(2,1)S(1)}) custom-call(bf16[2816,256]{1,0:T(8,128)(2,1)} %collective-permute-done.6.refs_0_.refs_1_, bf16[2816,256]{1,0:T(8,128)(2,1)} %collective-permute-done.7.refs_1_.refs_2_, ...), custom_call_target="tpu_custom_call" | custom-call | flops 2300000000 | bytes 1048576 | tf_op jit(solution)/shard_map/forward_kernel/pallas_call | solution.py:347
  96.6 2.9 %collective-permute-start.13 = (bf16[1408,256]{1,0:T(8,128)(2,1)S(1)}, bf16[1408,256]{1,0:T(8,128)(2,1)S(1)}, u32[]{:S(2)}, u32[]{:S(2)}) collective-permute-start(bf16[1408,256]{1,0:T(8,128)(2,1)S(1)} %get-tuple-element.67), channel_id=1, source_target_pairs={{0,24},{8,0},{16,8},{24,16},{32,56},{40,32},{48,40},{56,48},{64,88... | collective-permute-start | bytes 2162696 | tf_op jit(solution)/shard_map/ppermute | solution.py:39
  99.8 1.7 collective-permute-start.15
  101.5 14.5 %project_early.1 = (bf16[4,2,16,256]{3,2,1,0:T(8,128)(2,1)S(1)}, f32[4,4,256,256]{3,2,1,0:T(8,128)S(1)}) custom-call(s32[13]{0:T(128)S(1)} %copy-done.8, s32[1024,2]{1,0:T(8,128)S(1)} %copy-done.7, bf16[1024,2048]{1,0:T(8,128)(2,1)S(1)} %copy-done.1, bf16[2816,256]{1,0:T(8,128)(2,1)} %slice_dynamic-update-slice_fusion.5.refs_0_, ...), custom_call_target="tpu_custom_call" | custom-call | flops 17250000896 | bytes 1048576 | tf_op jit(solution)/shard_map/project_early/pallas_call | solution.py:179
  116.0 2.0 copy-done.17
  118.0 0.9 copy-done.9
  118.9 0.9 copy-done.11
  119.8 0.9 copy-done.13
  120.7 0.9 copy-done.15
  121.7 1.9 collective-permute-start.16
  123.6 3.2 %collective-permute-start.18 = (bf16[2048,256]{1,0:T(8,128)(2,1)S(1)}, bf16[2048,256]{1,0:T(8,128)(2,1)}, u32[]{:S(2)}, u32[]{:S(2)}) collective-permute-start(bf16[2048,256]{1,0:T(8,128)(2,1)S(1)} %pad_maximum_fusion.1.refs_5_), channel_id=1, source_target_pairs={{0,32},{8,40},{16,48},{24,56},{32,64},{40,72},{48,80},{56,88},{64,... | collective-permute-start | bytes 3145736 | tf_op jit(solution)/shard_map/ppermute | solution.py:39
  126.8 2.2 %copy-done.2 = bf16[1024,2048]{1,0:T(8,128)(2,1)S(1)} copy-done((bf16[1024,2048]{1,0:T(8,128)(2,1)S(1)}, bf16[1024,2048]{1,0:T(8,128)(2,1)}, u32[]{:S(2)}) %copy-start.2) | copy-done | bytes 4194328
  129.0 1.1 copy-done.10
  130.1 1.1 copy-done.12
  131.2 1.1 copy-done.14
  132.3 1.1 copy-done.16
  133.5 2.2 %copy-done.18 = f32[4,4,256,256]{3,2,1,0:T(8,128)S(1)} copy-done((f32[4,4,256,256]{3,2,1,0:T(8,128)S(1)}, f32[4,4,256,256]{3,2,1,0:T(8,128)}, u32[]{:S(2)}) %copy-start.18) | copy-done | bytes 4194328
  135.6 19.1 %attention.1.lhs_ref = bf16[8,1024,256]{2,1,0:T(8,128)(2,1)S(1)} custom-call(s32[13]{0:T(128)S(1)} %copy-done.8, s32[1024,2]{1,0:T(8,128)S(1)} %copy-done.7, bf16[8,4,16,256]{3,2,1,0:T(8,128)(2,1)} %all-to-all-done.1.down_ref, bf16[1024,2048]{1,0:T(8,128)(2,1)S(1)} %copy-done.2, bf16[4,2,16,256]{3,2,1,0:T(8,128)(2,1)S(1)} %get-tuple-element.72.up_ref, ...), custom_call_target="tpu_custom_call" | custom-call | flops 25300000768 | bytes 1048576 | tf_op jit(solution)/shard_map/attention/pallas_call | solution.py:258
  154.8 2.3 %forward_kernel.5 = (bf16[1024,256]{1,0:T(8,128)(2,1)S(1)}, bf16[1024,256]{1,0:T(8,128)(2,1)S(1)}, bf16[1024,256]{1,0:T(8,128)(2,1)S(1)}, bf16[1024,256]{1,0:T(8,128)(2,1)S(1)}) custom-call(bf16[2048,256]{1,0:T(8,128)(2,1)} %collective-permute-done.16.refs_0_.refs_1_, bf16[2048,256]{1,0:T(8,128)(2,1)} %collective-permute-done.17.refs_1_.refs_2_, ...), custom_call_target="tpu_custom_call" | custom-call | flops 2300000000 | bytes 1048576 | tf_op jit(solution)/shard_map/forward_kernel/pallas_call | solution.py:347
  157.2 3.2 %collective-permute-start.21 = (bf16[1024,256]{1,0:T(8,128)(2,1)S(1)}, bf16[1024,256]{1,0:T(8,128)(2,1)S(1)}, u32[]{:S(2)}, u32[]{:S(2)}) collective-permute-start(bf16[1024,256]{1,0:T(8,128)(2,1)S(1)} %get-tuple-element.84), channel_id=1, source_target_pairs={{0,24},{8,0},{16,8},{24,16},{32,56},{40,32},{48,40},{56,48},{64,88... | collective-permute-start | bytes 1572872 | tf_op jit(solution)/shard_map/ppermute | solution.py:39
  160.7 1.7 collective-permute-start.23
  162.4 5.1 %collective-permute-done.20.refs_3_ = bf16[1024,256]{1,0:T(8,128)(2,1)S(1)} collective-permute-done((bf16[1024,256]{1,0:T(8,128)(2,1)S(1)}, bf16[1024,256]{1,0:T(8,128)(2,1)S(1)}, u32[]{:S(2)}, u32[]{:S(2)}) %collective-permute-start.20) | collective-permute-done | bytes 524320 | tf_op jit(solution)/shard_map/ppermute | solution.py:39
  167.5 2.0 collective-permute-done.22.refs_8_
  169.6 1.5 collective-permute-done.23.refs_9_
  171.1 5.6 %project_out_2.3 = (bf16[1024,256]{1,0:T(8,128)(2,1)S(1)}, bf16[1024,256]{1,0:T(8,128)(2,1)S(1)}) custom-call(s32[3]{0:T(128)S(1)} %pad_add_fusion.1.place_ref, f32[1024,8]{1,0:T(8,128)S(1)} %broadcast_multiply_fusion.gates_ref, bf16[8,1024,256]{2,1,0:T(8,128)(2,1)S(1)} %attention.1.lhs_ref, bf16[2048,256]{1,0:T(8,128)(2,1)S(1)} %pad_maximum_fusion.refs_0_, ...), custom_call_target="tpu_custom_call" | custom-call | flops 5059999744 | bytes 1048576 | tf_op jit(solution)/shard_map/project_out_2/pallas_call | solution.py:331
  177.0 5.3 %project_out_2.4 = bf16[2,1024,256]{2,1,0:T(8,128)(2,1)S(1)} custom-call(s32[3]{0:T(128)S(1)} %pad_add_fusion.1.place_ref, f32[1024,8]{1,0:T(8,128)S(1)} %broadcast_multiply_fusion.gates_ref, bf16[8,1024,256]{2,1,0:T(8,128)(2,1)S(1)} %attention.1.lhs_ref, bf16[2048,256]{1,0:T(8,128)(2,1)S(1)} %pad_maximum_fusion.refs_0_, ...), custom_call_target="tpu_custom_call" | custom-call | flops 5059999744 | bytes 1048576 | tf_op jit(solution)/shard_map/project_out_2/pallas_call | solution.py:331
  183.1 1.4 collective-permute-start.26
  184.5 1.9 collective-permute-start.27
  186.4 5.4 %project_out_2.5.mine_ref = bf16[2,1024,256]{2,1,0:T(8,128)(2,1)S(1)} custom-call(s32[3]{0:T(128)S(1)} %pad_add_fusion.1.place_ref, f32[1024,8]{1,0:T(8,128)S(1)} %broadcast_multiply_fusion.gates_ref, bf16[8,1024,256]{2,1,0:T(8,128)(2,1)S(1)} %attention.1.lhs_ref, bf16[2048,256]{1,0:T(8,128)(2,1)S(1)} %pad_maximum_fusion.refs_0_, ...), custom_call_target="tpu_custom_call" | custom-call | flops 5059999744 | bytes 1048576 | tf_op jit(solution)/shard_map/project_out_2/pallas_call | solution.py:331
  193.1 3.8 %project_out_1.2 = bf16[1,1024,256]{2,1,0:T(8,128)(2,1)S(1)} custom-call(s32[3]{0:T(128)S(1)} %pad_add_fusion.1.place_ref, f32[1024,8]{1,0:T(8,128)S(1)} %broadcast_multiply_fusion.gates_ref, bf16[8,1024,256]{2,1,0:T(8,128)(2,1)S(1)} %attention.1.lhs_ref, bf16[2048,256]{1,0:T(8,128)(2,1)S(1)} %pad_maximum_fusion.refs_0_, ...), custom_call_target="tpu_custom_call" | custom-call | flops 2529999872 | bytes 1048576 | tf_op jit(solution)/shard_map/project_out_1/pallas_call | solution.py:331
  196.9 2.8 %collective-permute-start.30 = (bf16[1024,256]{1,0:T(8,128)(2,1)S(1)}, bf16[1024,256]{1,0:T(8,128)(2,1)S(1)}, u32[]{:S(2)}, u32[]{:S(2)}) collective-permute-start(bf16[1024,256]{1,0:T(8,128)(2,1)S(1)} %get-tuple-element.96), channel_id=1, source_target_pairs={{0,6},{1,7},{2,0},{3,1},{4,2},{5,3},{6,4},{7,5},{8,14},{9,15},{10,... | collective-permute-start | bytes 1572872 | tf_op jit(solution)/shard_map/ppermute | solution.py:400
  199.7 3.8 %project_out_1.3 = bf16[1,1024,256]{2,1,0:T(8,128)(2,1)S(1)} custom-call(s32[3]{0:T(128)S(1)} %pad_add_fusion.1.place_ref, f32[1024,8]{1,0:T(8,128)S(1)} %broadcast_multiply_fusion.gates_ref, bf16[8,1024,256]{2,1,0:T(8,128)(2,1)S(1)} %attention.1.lhs_ref, bf16[2048,256]{1,0:T(8,128)(2,1)S(1)} %pad_maximum_fusion.refs_0_, ...), custom_call_target="tpu_custom_call" | custom-call | flops 2529999872 | bytes 1048576 | tf_op jit(solution)/shard_map/project_out_1/pallas_call | solution.py:331
  203.5 8.0 %collective-permute-done.30 = bf16[1024,256]{1,0:T(8,128)(2,1)S(1)} collective-permute-done((bf16[1024,256]{1,0:T(8,128)(2,1)S(1)}, bf16[1024,256]{1,0:T(8,128)(2,1)S(1)}, u32[]{:S(2)}, u32[]{:S(2)}) %collective-permute-start.30) | collective-permute-done | bytes 524320 | tf_op jit(solution)/shard_map/ppermute | solution.py:400
  211.5 3.4 %collective-permute-done.29 = bf16[1024,256]{1,0:T(8,128)(2,1)S(1)} collective-permute-done((bf16[1024,256]{1,0:T(8,128)(2,1)S(1)}, bf16[1024,256]{1,0:T(8,128)(2,1)S(1)}, u32[]{:S(2)}, u32[]{:S(2)}) %collective-permute-start.29) | collective-permute-done | bytes 524320 | tf_op jit(solution)/shard_map/ppermute | solution.py:400
  214.9 1.1 fusion.1
  (140 shorter events, 14.4 us)
Async XLA Ops:
  0.0 15.2 %copy-start = (bf16[4,2048,16]{1,2,0:T(8,128)(2,1)S(1)}, bf16[4,2048,16]{1,2,0:T(8,128)(2,1)}, u32[]{:S(2)}) copy-start(bf16[4,2048,16]{1,2,0:T(8,128)(2,1)} %param.25) | copy-start | bytes 786436
  0.0 2.1 copy-start.25
  2.1 2.5 %copy-start.19 = (bf16[64,8,2,128]{3,1,2,0:T(8,128)(2,1)}, bf16[64,8,2,128]{3,1,2,0:T(8,128)(2,1)S(1)}, u32[]{:S(2)}) copy-start(bf16[64,8,2,128]{3,1,2,0:T(8,128)(2,1)S(1)} %copy.43) | copy-start | bytes 786436
  2.1 1.1 copy-start.26
  2.3 1.6 copy-start.28
  4.5 9.8 %copy-start.32 = (s32[64]{0:T(128)S(1)}, s32[64]{0:T(128)}, u32[]{:S(2)}) copy-start(s32[64]{0:T(128)} %param.18) | copy-start | bytes 772
  5.4 24.4 %collective-permute-start.1 = (bf16[1216,256]{1,0:T(8,128)(2,1)}, bf16[1216,256]{1,0:T(8,128)(2,1)S(1)}, u32[]{:S(2)}, u32[]{:S(2)}) collective-permute-start(bf16[1216,256]{1,0:T(8,128)(2,1)} %pad_maximum_fusion.2), channel_id=1, source_target_pairs={{0,96},{8,104},{16,112},{24,120},{32,0},{40,8},{48,16},{56,24},{64... | collective-permute-start | bytes 1867784 | tf_op jit(solution)/shard_map/ppermute | solution.py:39
  6.3 23.5 %collective-permute-start = (bf16[1216,256]{1,0:T(8,128)(2,1)}, bf16[1216,256]{1,0:T(8,128)(2,1)S(1)}, u32[]{:S(2)}, u32[]{:S(2)}) collective-permute-start(bf16[1216,256]{1,0:T(8,128)(2,1)} %pad_maximum_fusion.2), channel_id=1, source_target_pairs={{0,32},{8,40},{16,48},{24,56},{32,64},{40,72},{48,80},{56,88},{64,... | collective-permute-start | bytes 1867784 | tf_op jit(solution)/shard_map/ppermute | solution.py:39
  10.3 32.9 %collective-permute-start.3 = (bf16[1216,256]{1,0:T(8,128)(2,1)}, bf16[1216,256]{1,0:T(8,128)(2,1)S(1)}, u32[]{:S(2)}, u32[]{:S(2)}) collective-permute-start(bf16[1216,256]{1,0:T(8,128)(2,1)} %pad_maximum_fusion.3), channel_id=1, source_target_pairs={{0,24},{8,0},{16,8},{24,16},{32,56},{40,32},{48,40},{56,48},{64,88... | collective-permute-start | bytes 1867784 | tf_op jit(solution)/shard_map/ppermute | solution.py:39
  14.4 33.1 %collective-permute-start.2 = (bf16[1216,256]{1,0:T(8,128)(2,1)}, bf16[1216,256]{1,0:T(8,128)(2,1)S(1)}, u32[]{:S(2)}, u32[]{:S(2)}) collective-permute-start(bf16[1216,256]{1,0:T(8,128)(2,1)} %pad_maximum_fusion.3), channel_id=1, source_target_pairs={{0,8},{8,16},{16,24},{24,0},{32,40},{40,48},{48,56},{56,32},{64,72... | collective-permute-start | bytes 1867784 | tf_op jit(solution)/shard_map/ppermute | solution.py:39
  18.1 7.5 %copy-start.33 = (s32[64]{0:T(128)S(1)}, s32[64]{0:T(128)}, u32[]{:S(2)}) copy-start(s32[64]{0:T(128)} %param.20) | copy-start | bytes 772
  18.1 7.5 %copy-start.34 = (s32[4]{0:T(128)S(1)}, s32[4]{0:T(128)}, u32[]{:S(2)}) copy-start(s32[4]{0:T(128)} %param.19) | copy-start | bytes 52
  18.1 7.7 %copy-start.30 = (s32[4]{0:T(128)S(1)}, s32[4]{0:T(128)}, u32[]{:S(2)}) copy-start(s32[4]{0:T(128)} %param.17) | copy-start | bytes 52
  18.1 8.4 %copy-start.29 = (bf16[2048,8]{0,1:T(8,128)(2,1)S(1)}, bf16[2048,8]{0,1:T(8,128)(2,1)}, u32[]{:S(2)}) copy-start(bf16[2048,8]{0,1:T(8,128)(2,1)} %param.21) | copy-start | bytes 98308
  18.1 57.0 %all-to-all-start = ((bf16[16,96,512]{2,1,0:T(8,128)(2,1)}), bf16[16,96,512]{2,1,0:T(8,128)(2,1)}, u32[]{:S(2)}, u32[]{:S(2)}) async-start(bf16[16,96,512]{2,1,0:T(8,128)(2,1)} %pack.1), calls=%async_computation | async-start | bytes 3145728 | tf_op jit(solution)/shard_map/all_to_all | solution.py:464
  29.8 43.7 %copy-start.3 = (bf16[1216,256]{1,0:T(8,128)(2,1)}, bf16[1216,256]{1,0:T(8,128)(2,1)S(1)}, u32[]{:S(2)}) copy-start(bf16[1216,256]{1,0:T(8,128)(2,1)S(1)} %collective-permute-done.1.refs_1_) | copy-start | bytes 1867780
  29.8 43.7 %copy-start.4 = (bf16[1216,256]{1,0:T(8,128)(2,1)}, bf16[1216,256]{1,0:T(8,128)(2,1)S(1)}, u32[]{:S(2)}) copy-start(bf16[1216,256]{1,0:T(8,128)(2,1)S(1)} %collective-permute-done.refs_0_) | copy-start | bytes 1867780
  43.2 30.3 %copy-start.5 = (bf16[1216,256]{1,0:T(8,128)(2,1)}, bf16[1216,256]{1,0:T(8,128)(2,1)S(1)}, u32[]{:S(2)}) copy-start(bf16[1216,256]{1,0:T(8,128)(2,1)S(1)} %collective-permute-done.3.refs_3_) | copy-start | bytes 1867780
  47.5 1.7 copy-start.6
  49.2 8.2 %collective-permute-start.8 = (bf16[608,256]{1,0:T(8,128)(2,1)S(1)}, bf16[608,256]{1,0:T(8,128)(2,1)S(1)}, u32[]{:S(2)}, u32[]{:S(2)}) collective-permute-start(bf16[608,256]{1,0:T(8,128)(2,1)S(1)} %get-tuple-element.58), channel_id=1, source_target_pairs={{0,8},{8,16},{16,24},{24,0},{32,40},{40,48},{48,56},{56,32},{64,72... | collective-permute-start | bytes 933896 | tf_op jit(solution)/shard_map/ppermute | solution.py:39
  49.3 22.4 %copy-start.31 = (s32[4]{0:T(128)S(1)}, s32[4]{0:T(128)}, u32[]{:S(2)}) copy-start(s32[4]{0:T(128)} %param.16) | copy-start | bytes 52
  49.3 22.5 %copy-start.27 = (s32[1024,2]{0,1:T(2,128)S(1)}, s32[1024,2]{0,1:T(2,128)}, u32[]{:S(2)}) copy-start(s32[1024,2]{0,1:T(2,128)} %param.15) | copy-start | bytes 24580
  50.1 16.5 %collective-permute-start.4 = (bf16[608,256]{1,0:T(8,128)(2,1)S(1)}, bf16[608,256]{1,0:T(8,128)(2,1)S(1)}, u32[]{:S(2)}, u32[]{:S(2)}) collective-permute-start(bf16[608,256]{1,0:T(8,128)(2,1)S(1)} %get-tuple-element.56), channel_id=1, source_target_pairs={{0,32},{8,40},{16,48},{24,56},{32,64},{40,72},{48,80},{56,88},{64,... | collective-permute-start | bytes 933896 | tf_op jit(solution)/shard_map/ppermute | solution.py:39
  50.1 17.2 %collective-permute-start.5 = (bf16[608,256]{1,0:T(8,128)(2,1)S(1)}, bf16[608,256]{1,0:T(8,128)(2,1)S(1)}, u32[]{:S(2)}, u32[]{:S(2)}) collective-permute-start(bf16[608,256]{1,0:T(8,128)(2,1)S(1)} %get-tuple-element.57), channel_id=1, source_target_pairs={{0,96},{8,104},{16,112},{24,120},{32,0},{40,8},{48,16},{56,24},{64... | collective-permute-start | bytes 933896 | tf_op jit(solution)/shard_map/ppermute | solution.py:39
  52.1 10.6 %collective-permute-start.9 = (bf16[608,256]{1,0:T(8,128)(2,1)S(1)}, bf16[608,256]{1,0:T(8,128)(2,1)S(1)}, u32[]{:S(2)}, u32[]{:S(2)}) collective-permute-start(bf16[608,256]{1,0:T(8,128)(2,1)S(1)} %get-tuple-element.59), channel_id=1, source_target_pairs={{0,24},{8,0},{16,8},{24,16},{32,56},{40,32},{48,40},{56,48},{64,88... | collective-permute-start | bytes 933896 | tf_op jit(solution)/shard_map/ppermute | solution.py:39
  62.7 10.4 %copy-start.23 = (bf16[608,256]{1,0:T(8,128)(2,1)}, bf16[608,256]{1,0:T(8,128)(2,1)S(1)}, u32[]{:S(2)}) copy-start(bf16[608,256]{1,0:T(8,128)(2,1)S(1)} %collective-permute-done.9) | copy-start | bytes 933892
  63.3 25.8 %collective-permute-start.11 = (bf16[2816,256]{1,0:T(8,128)(2,1)}, bf16[2816,256]{1,0:T(8,128)(2,1)}, u32[]{:S(2)}, u32[]{:S(2)}) collective-permute-start(bf16[2816,256]{1,0:T(8,128)(2,1)} %slice_dynamic-update-slice_fusion.4.refs_3_), channel_id=1, source_target_pairs={{0,96},{8,104},{16,112},{24,120},{32,0},{40,8},{48,16},{56,24},{64... | collective-permute-start | bytes 4325384 | tf_op jit(solution)/shard_map/ppermute | solution.py:39
  63.6 25.6 %collective-permute-start.10 = (bf16[2816,256]{1,0:T(8,128)(2,1)}, bf16[2816,256]{1,0:T(8,128)(2,1)}, u32[]{:S(2)}, u32[]{:S(2)}) collective-permute-start(bf16[2816,256]{1,0:T(8,128)(2,1)} %slice_dynamic-update-slice_fusion.4.refs_3_), channel_id=1, source_target_pairs={{0,32},{8,40},{16,48},{24,56},{32,64},{40,72},{48,80},{56,88},{64,... | collective-permute-start | bytes 4325384 | tf_op jit(solution)/shard_map/ppermute | solution.py:39
  67.3 5.8 %copy-start.24 = (bf16[608,256]{1,0:T(8,128)(2,1)}, bf16[608,256]{1,0:T(8,128)(2,1)S(1)}, u32[]{:S(2)}) copy-start(bf16[608,256]{1,0:T(8,128)(2,1)S(1)} %collective-permute-done.5) | copy-start | bytes 933892
  68.0 23.0 %collective-permute-start.7 = (bf16[2816,256]{1,0:T(8,128)(2,1)}, bf16[2816,256]{1,0:T(8,128)(2,1)}, u32[]{:S(2)}, u32[]{:S(2)}) collective-permute-start(bf16[2816,256]{1,0:T(8,128)(2,1)} %slice_dynamic-update-slice_fusion.5.refs_0_), channel_id=1, source_target_pairs={{0,24},{8,0},{16,8},{24,16},{32,56},{40,32},{48,40},{56,48},{64,88... | collective-permute-start | bytes 4325384 | tf_op jit(solution)/shard_map/ppermute | solution.py:39
  71.7 21.7 %collective-permute-start.6 = (bf16[2816,256]{1,0:T(8,128)(2,1)}, bf16[2816,256]{1,0:T(8,128)(2,1)}, u32[]{:S(2)}, u32[]{:S(2)}) collective-permute-start(bf16[2816,256]{1,0:T(8,128)(2,1)} %slice_dynamic-update-slice_fusion.5.refs_0_), channel_id=1, source_target_pairs={{0,8},{8,16},{16,24},{24,0},{32,40},{40,48},{48,56},{56,32},{64,72... | collective-permute-start | bytes 4325384 | tf_op jit(solution)/shard_map/ppermute | solution.py:39
  73.6 1.2 slice-start
  73.6 1.2 slice-start.2
  73.6 1.3 slice-start.3
  73.6 1.4 copy-start.22
  73.6 1.4 slice-start.4
  78.7 48.1 %all-to-all-start.1 = ((bf16[8,4,16,256]{3,2,1,0:T(8,128)(2,1)}), bf16[8,4,16,256]{3,2,1,0:T(8,128)(2,1)}, u32[]{:S(2)}, u32[]{:S(2)}) async-start(bf16[8,4,16,256]{3,2,1,0:T(8,128)(2,1)} %broadcast_in_dim.5), calls=%async_computation.1 | async-start | bytes 524288 | tf_op jit(solution)/shard_map/all_to_all | solution.py:507
  83.2 18.3 %copy-start.1 = (bf16[1024,2048]{1,0:T(8,128)(2,1)S(1)}, bf16[1024,2048]{1,0:T(8,128)(2,1)}, u32[]{:S(2)}) copy-start(bf16[1024,2048]{1,0:T(8,128)(2,1)} %x_ref.3) | copy-start | bytes 12582916
  83.2 18.3 %copy-start.7 = (s32[1024,2]{1,0:T(8,128)S(1)}, s32[1024,2]{1,0:T(8,128)}, u32[]{:S(2)}) copy-start(s32[1024,2]{1,0:T(8,128)} %copy.34.routes_ref) | copy-start | bytes 24580
  83.2 18.3 %copy-start.8 = (s32[13]{0:T(128)S(1)}, s32[13]{0:T(128)}, u32[]{:S(2)}) copy-start(s32[13]{0:T(128)} %pad_add_fusion.info_ref) | copy-start | bytes 160
  96.2 21.8 %collective-permute-start.12 = (bf16[1408,256]{1,0:T(8,128)(2,1)S(1)}, bf16[1408,256]{1,0:T(8,128)(2,1)S(1)}, u32[]{:S(2)}, u32[]{:S(2)}) collective-permute-start(bf16[1408,256]{1,0:T(8,128)(2,1)S(1)} %get-tuple-element.66), channel_id=1, source_target_pairs={{0,8},{8,16},{16,24},{24,0},{32,40},{40,48},{48,56},{56,32},{64,72... | collective-permute-start | bytes 2162696 | tf_op jit(solution)/shard_map/ppermute | solution.py:39
  96.6 22.3 %collective-permute-start.13 = (bf16[1408,256]{1,0:T(8,128)(2,1)S(1)}, bf16[1408,256]{1,0:T(8,128)(2,1)S(1)}, u32[]{:S(2)}, u32[]{:S(2)}) collective-permute-start(bf16[1408,256]{1,0:T(8,128)(2,1)S(1)} %get-tuple-element.67), channel_id=1, source_target_pairs={{0,24},{8,0},{16,8},{24,16},{32,56},{40,32},{48,40},{56,48},{64,88... | collective-permute-start | bytes 2162696 | tf_op jit(solution)/shard_map/ppermute | solution.py:39
  99.5 20.3 %collective-permute-start.14 = (bf16[1408,256]{1,0:T(8,128)(2,1)S(1)}, bf16[1408,256]{1,0:T(8,128)(2,1)S(1)}, u32[]{:S(2)}, u32[]{:S(2)}) collective-permute-start(bf16[1408,256]{1,0:T(8,128)(2,1)S(1)} %get-tuple-element.68), channel_id=1, source_target_pairs={{0,32},{8,40},{16,48},{24,56},{32,64},{40,72},{48,80},{56,88},{64,... | collective-permute-start | bytes 2162696 | tf_op jit(solution)/shard_map/ppermute | solution.py:39
  99.8 20.9 %collective-permute-start.15 = (bf16[1408,256]{1,0:T(8,128)(2,1)S(1)}, bf16[1408,256]{1,0:T(8,128)(2,1)S(1)}, u32[]{:S(2)}, u32[]{:S(2)}) collective-permute-start(bf16[1408,256]{1,0:T(8,128)(2,1)S(1)} %get-tuple-element.69), channel_id=1, source_target_pairs={{0,96},{8,104},{16,112},{24,120},{32,0},{40,8},{48,16},{56,24},{64... | collective-permute-start | bytes 2162696 | tf_op jit(solution)/shard_map/ppermute | solution.py:39
  116.0 2.0 copy-start.17
  121.6 33.2 %collective-permute-start.17 = (bf16[2048,256]{1,0:T(8,128)(2,1)S(1)}, bf16[2048,256]{1,0:T(8,128)(2,1)}, u32[]{:S(2)}, u32[]{:S(2)}) collective-permute-start(bf16[2048,256]{1,0:T(8,128)(2,1)S(1)} %pad_maximum_fusion.refs_0_), channel_id=1, source_target_pairs={{0,24},{8,0},{16,8},{24,16},{32,56},{40,32},{48,40},{56,48},{64,88... | collective-permute-start | bytes 3145736 | tf_op jit(solution)/shard_map/ppermute | solution.py:39
  121.7 33.0 %collective-permute-start.16 = (bf16[2048,256]{1,0:T(8,128)(2,1)S(1)}, bf16[2048,256]{1,0:T(8,128)(2,1)}, u32[]{:S(2)}, u32[]{:S(2)}) collective-permute-start(bf16[2048,256]{1,0:T(8,128)(2,1)S(1)} %pad_maximum_fusion.refs_0_), channel_id=1, source_target_pairs={{0,8},{8,16},{16,24},{24,0},{32,40},{40,48},{48,56},{56,32},{64,72... | collective-permute-start | bytes 3145736 | tf_op jit(solution)/shard_map/ppermute | solution.py:39
  123.6 31.2 %collective-permute-start.19 = (bf16[2048,256]{1,0:T(8,128)(2,1)S(1)}, bf16[2048,256]{1,0:T(8,128)(2,1)}, u32[]{:S(2)}, u32[]{:S(2)}) collective-permute-start(bf16[2048,256]{1,0:T(8,128)(2,1)S(1)} %pad_maximum_fusion.1.refs_5_), channel_id=1, source_target_pairs={{0,96},{8,104},{16,112},{24,120},{32,0},{40,8},{48,16},{56,24},{64... | collective-permute-start | bytes 3145736 | tf_op jit(solution)/shard_map/ppermute | solution.py:39
  123.6 31.1 %collective-permute-start.18 = (bf16[2048,256]{1,0:T(8,128)(2,1)S(1)}, bf16[2048,256]{1,0:T(8,128)(2,1)}, u32[]{:S(2)}, u32[]{:S(2)}) collective-permute-start(bf16[2048,256]{1,0:T(8,128)(2,1)S(1)} %pad_maximum_fusion.1.refs_5_), channel_id=1, source_target_pairs={{0,32},{8,40},{16,48},{24,56},{32,64},{40,72},{48,80},{56,88},{64,... | collective-permute-start | bytes 3145736 | tf_op jit(solution)/shard_map/ppermute | solution.py:39
  126.8 2.2 %copy-start.2 = (bf16[1024,2048]{1,0:T(8,128)(2,1)S(1)}, bf16[1024,2048]{1,0:T(8,128)(2,1)}, u32[]{:S(2)}) copy-start(bf16[1024,2048]{1,0:T(8,128)(2,1)} %x_ref.3) | copy-start | bytes 12582916
  129.0 1.1 copy-start.10
  130.1 1.1 copy-start.12
  133.5 2.2 %copy-start.18 = (f32[4,4,256,256]{3,2,1,0:T(8,128)S(1)}, f32[4,4,256,256]{3,2,1,0:T(8,128)}, u32[]{:S(2)}) copy-start(f32[4,4,256,256]{3,2,1,0:T(8,128)} %copy-done.17) | copy-start | bytes 12582916
  157.1 10.5 %collective-permute-start.20 = (bf16[1024,256]{1,0:T(8,128)(2,1)S(1)}, bf16[1024,256]{1,0:T(8,128)(2,1)S(1)}, u32[]{:S(2)}, u32[]{:S(2)}) collective-permute-start(bf16[1024,256]{1,0:T(8,128)(2,1)S(1)} %get-tuple-element.83), channel_id=1, source_target_pairs={{0,8},{8,16},{16,24},{24,0},{32,40},{40,48},{48,56},{56,32},{64,72... | collective-permute-start | bytes 1572872 | tf_op jit(solution)/shard_map/ppermute | solution.py:39
  157.2 10.3 %collective-permute-start.21 = (bf16[1024,256]{1,0:T(8,128)(2,1)S(1)}, bf16[1024,256]{1,0:T(8,128)(2,1)S(1)}, u32[]{:S(2)}, u32[]{:S(2)}) collective-permute-start(bf16[1024,256]{1,0:T(8,128)(2,1)S(1)} %get-tuple-element.84), channel_id=1, source_target_pairs={{0,24},{8,0},{16,8},{24,16},{32,56},{40,32},{48,40},{56,48},{64,88... | collective-permute-start | bytes 1572872 | tf_op jit(solution)/shard_map/ppermute | solution.py:39
  160.4 9.2 %collective-permute-start.22 = (bf16[1024,256]{1,0:T(8,128)(2,1)S(1)}, bf16[1024,256]{1,0:T(8,128)(2,1)S(1)}, u32[]{:S(2)}, u32[]{:S(2)}) collective-permute-start(bf16[1024,256]{1,0:T(8,128)(2,1)S(1)} %get-tuple-element.85), channel_id=1, source_target_pairs={{0,32},{8,40},{16,48},{24,56},{32,64},{40,72},{48,80},{56,88},{64,... | collective-permute-start | bytes 1572872 | tf_op jit(solution)/shard_map/ppermute | solution.py:39
  160.7 10.4 %collective-permute-start.23 = (bf16[1024,256]{1,0:T(8,128)(2,1)S(1)}, bf16[1024,256]{1,0:T(8,128)(2,1)S(1)}, u32[]{:S(2)}, u32[]{:S(2)}) collective-permute-start(bf16[1024,256]{1,0:T(8,128)(2,1)S(1)} %get-tuple-element.86), channel_id=1, source_target_pairs={{0,96},{8,104},{16,112},{24,120},{32,0},{40,8},{48,16},{56,24},{64... | collective-permute-start | bytes 1572872 | tf_op jit(solution)/shard_map/ppermute | solution.py:39
  176.7 6.3 %collective-permute-start.24 = (bf16[1024,256]{1,0:T(8,128)(2,1)S(1)}, bf16[1024,256]{1,0:T(8,128)(2,1)S(1)}, u32[]{:S(2)}, u32[]{:S(2)}) collective-permute-start(bf16[1024,256]{1,0:T(8,128)(2,1)S(1)} %get-tuple-element.89), channel_id=1, source_target_pairs={{0,1},{1,0},{2,3},{3,2},{4,5},{5,4},{6,7},{7,6},{8,9},{9,8},{10,11... | collective-permute-start | bytes 1572872 | tf_op jit(solution)/shard_map/ppermute | solution.py:399
  182.4 10.4 %collective-permute-start.25 = (bf16[2,1024,256]{2,1,0:T(8,128)(2,1)S(1)}, bf16[2,1024,256]{2,1,0:T(8,128)(2,1)S(1)}, u32[]{:S(2)}, u32[]{:S(2)}) collective-permute-start(bf16[2,1024,256]{2,1,0:T(8,128)(2,1)S(1)} %project_out_2.4), channel_id=1, source_target_pairs={{0,1},{1,0},{2,3},{3,2},{4,5},{5,4},{6,7},{7,6},{8,9},{9,8},{10,11... | collective-permute-start | bytes 3145736 | tf_op jit(solution)/shard_map/ppermute | solution.py:399
  183.1 9.6 %collective-permute-start.26 = (bf16[512,256]{1,0:T(8,128)(2,1)S(1)}, bf16[512,256]{1,0:T(8,128)(2,1)S(1)}, u32[]{:S(2)}, u32[]{:S(2)}) collective-permute-start(bf16[512,256]{1,0:T(8,128)(2,1)S(1)} %get-tuple-element.90), channel_id=1, source_target_pairs={{0,2},{1,3},{2,4},{3,5},{4,6},{5,7},{6,0},{7,1},{8,10},{9,11},{10,... | collective-permute-start | bytes 786440 | tf_op jit(solution)/shard_map/ppermute | solution.py:400
  184.5 8.0 %collective-permute-start.27 = (bf16[512,256]{1,0:T(8,128)(2,1)S(1)}, bf16[512,256]{1,0:T(8,128)(2,1)S(1)}, u32[]{:S(2)}, u32[]{:S(2)}) collective-permute-start(bf16[512,256]{1,0:T(8,128)(2,1)S(1)} %get-tuple-element.92), channel_id=1, source_target_pairs={{0,6},{1,7},{2,0},{3,1},{4,2},{5,3},{6,4},{7,5},{8,14},{9,15},{10,... | collective-permute-start | bytes 786440 | tf_op jit(solution)/shard_map/ppermute | solution.py:400
  196.9 6.7 %collective-permute-start.28 = (bf16[1,1024,256]{2,1,0:T(8,128)(2,1)S(1)}, bf16[1,1024,256]{2,1,0:T(8,128)(2,1)S(1)}, u32[]{:S(2)}, u32[]{:S(2)}) collective-permute-start(bf16[1,1024,256]{2,1,0:T(8,128)(2,1)S(1)} %project_out_1.2), channel_id=1, source_target_pairs={{0,1},{1,0},{2,3},{3,2},{4,5},{5,4},{6,7},{7,6},{8,9},{9,8},{10,11... | collective-permute-start | bytes 1572872 | tf_op jit(solution)/shard_map/ppermute | solution.py:399
  196.9 14.6 %collective-permute-start.30 = (bf16[1024,256]{1,0:T(8,128)(2,1)S(1)}, bf16[1024,256]{1,0:T(8,128)(2,1)S(1)}, u32[]{:S(2)}, u32[]{:S(2)}) collective-permute-start(bf16[1024,256]{1,0:T(8,128)(2,1)S(1)} %get-tuple-element.96), channel_id=1, source_target_pairs={{0,6},{1,7},{2,0},{3,1},{4,2},{5,3},{6,4},{7,5},{8,14},{9,15},{10,... | collective-permute-start | bytes 1572872 | tf_op jit(solution)/shard_map/ppermute | solution.py:400
  199.7 15.2 %collective-permute-start.29 = (bf16[1024,256]{1,0:T(8,128)(2,1)S(1)}, bf16[1024,256]{1,0:T(8,128)(2,1)S(1)}, u32[]{:S(2)}, u32[]{:S(2)}) collective-permute-start(bf16[1024,256]{1,0:T(8,128)(2,1)S(1)} %get-tuple-element.93), channel_id=1, source_target_pairs={{0,2},{1,3},{2,4},{3,5},{4,6},{5,7},{6,0},{7,1},{8,10},{9,11},{10,... | collective-permute-start | bytes 1572872 | tf_op jit(solution)/shard_map/ppermute | solution.py:400
  (10 other events, 9.5 us)

commit v5 on v3

--- a/solution.py
+++ b/solution.py
@@ -291,10 +291,10 @@
                         sem.at[b],
                     ).start()
 
-    def block(b, out_ref):
+    def block(b, carry):
         pltpu.make_async_copy(w.at[b], w.at[b], sem.at[b]).wait()
 
-        def tile(i, carry):
+        def tile(i, inner):
             rows = pl.ds(pl.multiple_of(i * 256, 256), 256)
             total = None
             for e in range(NE):
@@ -306,21 +306,21 @@
                 value = jnp.dot(lhs_ref[e, rows, :], weight, preferred_element_type=F32)
                 value = value * gates_ref[rows, e : e + 1]
                 total = value if total is None else total + value
-            out_ref[rows, :] = total.astype(BF)
-            return carry
-
-        lax.fori_loop(0, 4, tile, 0)
-
-    if len(outs) > 1:
-        for b, out_ref in enumerate(outs):
-            block(b, out_ref)
-    else:
-
-        def step(b, carry):
-            block(b, outs[0].at[b])
-            return carry
-
-        lax.fori_loop(0, len(blocks), step, 0)
+            total = total.astype(BF)
+            if len(outs) == 1:
+                outs[0][b, rows, :] = total
+            else:
+                for at, out_ref in enumerate(outs):
+
+                    @pl.when(b == at)
+                    def _(out_ref=out_ref):
+                        out_ref[rows, :] = total
+
+            return inner
+
+        return lax.fori_loop(0, 4, tile, carry)
+
+    lax.fori_loop(0, len(blocks), block, 0)
 
 
 def project_out(blocks, place, gates, lhs, pieces, apart=False):
@@ -520,11 +520,14 @@
         out_pieces += [near_out[half], *out_beside[two], *out_late[two]]
 
     operands = (gates, lhs, out_pieces)
-    far, far_mine = project_out(((False, 2), (True, 2)), place, *operands, apart=True)
+    far, far_mine, near_theirs = project_out(
+        ((False, 2), (True, 2), (False, 0)), place, *operands, apart=True
+    )
     far_swapped = exchange(far, 0)
     place = lax.optimization_barrier((place, far_mine))[0]
-    (theirs,) = project_out(((False, 1), (False, 3), (False, 0)), place, *operands)
+    (theirs,) = project_out(((False, 1), (False, 3)), place, *operands)
     swapped = exchange(theirs, 0)
+    near_swapped = exchange(near_theirs, 0)
     low, high = small_call(far_sum_kernel, [(512, 256)] * 2, 1, far_mine, far_swapped)
     place = lax.optimization_barrier((place, theirs, low))[0]
     low, high = exchange(low, 1), exchange(high, -1)
@@ -533,7 +536,7 @@
     from_behind, from_ahead = exchange(ahead, 1), exchange(behind, -1)
     place = lax.optimization_barrier((place, ahead))[0]
     (own_block,) = project_out(((True, 0),), place, *operands)
-    return rounded_sum(own_block[0], swapped[2], from_behind, from_ahead)
+    return rounded_sum(own_block[0], near_swapped, from_behind, from_ahead)
 
 
 def solution(mesh):

time: 205 us -> 203 us (level)
  waiting for transfers between devices: 59.4 us -> 56.3 us
    ppermute x2 -> x3, waiting for transfers between devices: 3.65 us -> 0.01 us  [exchange(): return lax.ppermute(value, 'exp', [(i, i ^ 1) for i in range(8)])]
  transfers between devices with their start and end apart: 32 -> 33, of which waited for: 17 -> 16; matrix products, arithmetic and copies ran while one was open for 10% -> 10% of each run, Pallas kernels for 23% -> 26%
where the time goes in v5:
time: 203 us; the launch traced here: 202 us
  Pallas kernels  62.5 us (31%)
  waiting for transfers between devices  56.3 us (28%)
  starting transfers between devices  55.4 us (27%)
  local copies, waits for them, and re-layouts  16.7 us (8%)
  other arithmetic  7.1 us (3%)
  matrix products  3.37 us (2%)
    ppermute x24, waiting for transfers between devices, send(): lax.ppermute(value, 'req', torus(step, 0) if along == 0 else torus(0, step))  37 us
    ppermute x24, starting transfers between devices, send(): lax.ppermute(value, 'req', torus(step, 0) if along == 0 else torus(0, step))  36.5 us
    pallas_call x4, Pallas kernels, project_out(): pl.pallas_call(functools.partial(project_out_kernel, blocks), out_shape=s...  20.6 us
    pallas_call x1, Pallas kernels, attention(): pl.pallas_call(attend_kernel, out_shape=jax.ShapeDtypeStruct((NE, 1024, 2...  19.3 us
    pallas_call x1, Pallas kernels, project_early(): pl.pallas_call(early_kernel, out_shape=(jax.ShapeDtypeStruct((4, 2, 16, 2...  14.5 us
    ppermute x4, waiting for transfers between devices, exchange(): lax.ppermute(value, 'exp', [(i, (i + 2 * step) % 8) for i in range(8)])  12.7 us
    unnamed x61, local copies, waits for them, and re-layouts  8.86 us
    all_to_all x1, starting transfers between devices, body(): received = lax.all_to_all(outgoing, 'req', 0, 0, tiled=True)  7.34 us
  transfers between devices with their start and end apart: 33, of which 16 were waited for; matrix products, arithmetic and copies ran while one was open for 10% of the time, Pallas kernels for 26%

profile of v5, /device:TPU:6, one launch (start us, length us, event | category | flops | bytes accessed | tf_op | source)
XLA Modules:
  0.0 201.9 jit_solution(17287856524705041507)
XLA Ops:
  0.0 1.7 copy.41
  2.4 0.8 constant_dynamic-update-slice_fusion.3
  3.2 0.7 constant_dynamic-update-slice_fusion.6
  4.5 0.9 pad_maximum_fusion.2
  5.4 0.8 collective-permute-start.1
  6.2 2.4 %collective-permute-start = (bf16[1216,256]{1,0:T(8,128)(2,1)}, bf16[1216,256]{1,0:T(8,128)(2,1)S(1)}, u32[]{:S(2)}, u32[]{:S(2)}) collective-permute-start(bf16[1216,256]{1,0:T(8,128)(2,1)} %pad_maximum_fusion.2), channel_id=1, source_target_pairs={{0,32},{8,40},{16,48},{24,56},{32,64},{40,72},{48,80},{56,88},{64,... | collective-permute-start | bytes 1867784 | tf_op jit(solution)/shard_map/ppermute | solution.py:39
  8.7 1.0 pad_maximum_fusion.3
  9.7 4.0 %collective-permute-start.3 = (bf16[1216,256]{1,0:T(8,128)(2,1)}, bf16[1216,256]{1,0:T(8,128)(2,1)S(1)}, u32[]{:S(2)}, u32[]{:S(2)}) collective-permute-start(bf16[1216,256]{1,0:T(8,128)(2,1)} %pad_maximum_fusion.3), channel_id=1, source_target_pairs={{0,24},{8,0},{16,8},{24,16},{32,56},{40,32},{48,40},{56,48},{64,88... | collective-permute-start | bytes 1867784 | tf_op jit(solution)/shard_map/ppermute | solution.py:39
  13.8 0.7 select_reduce_fusion.2.index_ref
  15.1 2.3 %pack.1 = bf16[16,96,512]{2,1,0:T(8,128)(2,1)} custom-call(s32[16]{0:T(128)} %select_reduce_fusion.2.index_ref, bf16[4,64,512]{2,1,0:T(8,128)(2,1)} %store_ref.1, bf16[64,256]{1,0:T(8,128)(2,1)} %bitcast.46), custom_call_target="tpu_custom_call" | custom-call | flops 3449999872 | bytes 1048576 | tf_op jit(solution)/shard_map/pack/pallas_call | solution.py:74
  17.5 7.3 %all-to-all-start = ((bf16[16,96,512]{2,1,0:T(8,128)(2,1)}), bf16[16,96,512]{2,1,0:T(8,128)(2,1)}, u32[]{:S(2)}, u32[]{:S(2)}) async-start(bf16[16,96,512]{2,1,0:T(8,128)(2,1)} %pack.1), calls=%async_computation | async-start | bytes 3145728 | tf_op jit(solution)/shard_map/all_to_all | solution.py:464
  25.1 0.7 pad_add_fusion.info_ref
  25.8 3.4 %fusion.5 = f32[1024,8]{0,1:T(8,128)S(1)} fusion(bf16[1024,2048]{1,0:T(8,128)(2,1)} %x_ref.3, bf16[2048,8]{0,1:T(8,128)(2,1)S(1)} %copy-done.18), kind=kOutput, calls=%fused_computation.41 | convolution fusion | flops 33554432 | bytes 4259840 | tf_op jit(solution)/shard_map/dot_general | solution.py:496
  29.2 13.4 %collective-permute-done.3.refs_3_ = bf16[1216,256]{1,0:T(8,128)(2,1)S(1)} collective-permute-done((bf16[1216,256]{1,0:T(8,128)(2,1)}, bf16[1216,256]{1,0:T(8,128)(2,1)S(1)}, u32[]{:S(2)}, u32[]{:S(2)}) %collective-permute-start.3) | collective-permute-done | bytes 622624 | tf_op jit(solution)/shard_map/ppermute | solution.py:39
  42.6 4.3 %collective-permute-done.2.refs_2_ = bf16[1216,256]{1,0:T(8,128)(2,1)S(1)} collective-permute-done((bf16[1216,256]{1,0:T(8,128)(2,1)}, bf16[1216,256]{1,0:T(8,128)(2,1)S(1)}, u32[]{:S(2)}, u32[]{:S(2)}) %collective-permute-start.2) | collective-permute-done | bytes 622624 | tf_op jit(solution)/shard_map/ppermute | solution.py:39
  46.8 0.8 slice_dynamic-update-slice_fusion.3
  47.7 0.8 slice_dynamic-update-slice_fusion.2
  48.6 0.8 slice_dynamic-update-slice_fusion.1
  49.4 2.0 %collective-permute-start.5 = (bf16[608,256]{1,0:T(8,128)(2,1)S(1)}, bf16[608,256]{1,0:T(8,128)(2,1)S(1)}, u32[]{:S(2)}, u32[]{:S(2)}) collective-permute-start(bf16[608,256]{1,0:T(8,128)(2,1)S(1)} %get-tuple-element.58), channel_id=1, source_target_pairs={{0,96},{8,104},{16,112},{24,120},{32,0},{40,8},{48,16},{56,24},{64... | collective-permute-start | bytes 933896 | tf_op jit(solution)/shard_map/ppermute | solution.py:39
  51.4 3.2 %collective-permute-start.9 = (bf16[608,256]{1,0:T(8,128)(2,1)S(1)}, bf16[608,256]{1,0:T(8,128)(2,1)S(1)}, u32[]{:S(2)}, u32[]{:S(2)}) collective-permute-start(bf16[608,256]{1,0:T(8,128)(2,1)S(1)} %get-tuple-element.60), channel_id=1, source_target_pairs={{0,24},{8,0},{16,8},{24,16},{32,56},{40,32},{48,40},{56,48},{64,88... | collective-permute-start | bytes 933896 | tf_op jit(solution)/shard_map/ppermute | solution.py:39
  54.6 0.8 slice_dynamic-update-slice_fusion
  55.4 1.3 collective-permute-done.8
  56.7 0.7 constant_dynamic-update-slice_fusion.4
  57.4 4.6 %collective-permute-done.9 = bf16[608,256]{1,0:T(8,128)(2,1)S(1)} collective-permute-done((bf16[608,256]{1,0:T(8,128)(2,1)S(1)}, bf16[608,256]{1,0:T(8,128)(2,1)S(1)}, u32[]{:S(2)}, u32[]{:S(2)}) %collective-permute-start.9) | collective-permute-done | bytes 311328 | tf_op jit(solution)/shard_map/ppermute | solution.py:39
  62.0 0.7 slice_dynamic-update-slice_fusion.4.refs_3_
  62.9 2.9 %collective-permute-start.10 = (bf16[2816,256]{1,0:T(8,128)(2,1)}, bf16[2816,256]{1,0:T(8,128)(2,1)}, u32[]{:S(2)}, u32[]{:S(2)}) collective-permute-start(bf16[2816,256]{1,0:T(8,128)(2,1)} %slice_dynamic-update-slice_fusion.4.refs_3_), channel_id=1, source_target_pairs={{0,32},{8,40},{16,48},{24,56},{32,64},{40,72},{48,80},{56,88},{64,... | collective-permute-start | bytes 4325384 | tf_op jit(solution)/shard_map/ppermute | solution.py:39
  65.9 0.7 constant_dynamic-update-slice_fusion
  67.3 3.7 %collective-permute-start.7 = (bf16[2816,256]{1,0:T(8,128)(2,1)}, bf16[2816,256]{1,0:T(8,128)(2,1)}, u32[]{:S(2)}, u32[]{:S(2)}) collective-permute-start(bf16[2816,256]{1,0:T(8,128)(2,1)} %slice_dynamic-update-slice_fusion.5.refs_0_), channel_id=1, source_target_pairs={{0,24},{8,0},{16,8},{24,16},{32,56},{40,32},{48,40},{56,48},{64,88... | collective-permute-start | bytes 4325384 | tf_op jit(solution)/shard_map/ppermute | solution.py:39
  71.1 1.1 copy.34.routes_ref
  72.4 1.0 copy.32
  73.4 1.2 broadcast_multiply_fusion.gates_ref
  74.8 0.9 copy-done.14
  75.7 0.7 slice.109
  76.5 2.2 %pick_down.1 = bf16[4,16,256]{2,1,0:T(8,128)(2,1)} custom-call(s32[13]{0:T(128)} %pad_add_fusion.info_ref, bf16[16,96,512]{2,1,0:T(8,128)(2,1)} %all-to-all-done.recv_ref.recv_hbm), custom_call_target="tpu_custom_call" | custom-call | flops 2300000000 | bytes 1048576 | tf_op jit(solution)/shard_map/pick_down/pallas_call | solution.py:104
  78.7 1.5 broadcast_in_dim.5
  80.2 4.5 %all-to-all-start.1 = ((bf16[8,4,16,256]{3,2,1,0:T(8,128)(2,1)}), bf16[8,4,16,256]{3,2,1,0:T(8,128)(2,1)}, u32[]{:S(2)}, u32[]{:S(2)}) async-start(bf16[8,4,16,256]{3,2,1,0:T(8,128)(2,1)} %broadcast_in_dim.5), calls=%async_computation.1 | async-start | bytes 524288 | tf_op jit(solution)/shard_map/all_to_all | solution.py:506
  84.7 1.1 pad_maximum_fusion.1.refs_5_
  85.8 6.5 %all-to-all-done.1.down_ref = bf16[8,4,16,256]{3,2,1,0:T(8,128)(2,1)} async-done(((bf16[8,4,16,256]{3,2,1,0:T(8,128)(2,1)}), bf16[8,4,16,256]{3,2,1,0:T(8,128)(2,1)}, u32[]{:S(2)}, u32[]{:S(2)}) %all-to-all-start.1) | async-done | bytes 262176 | tf_op jit(solution)/shard_map/all_to_all | solution.py:506
  92.4 3.0 %forward_kernel.4 = (bf16[1408,256]{1,0:T(8,128)(2,1)S(1)}, bf16[1408,256]{1,0:T(8,128)(2,1)S(1)}, bf16[1408,256]{1,0:T(8,128)(2,1)S(1)}, bf16[1408,256]{1,0:T(8,128)(2,1)S(1)}) custom-call(bf16[2816,256]{1,0:T(8,128)(2,1)} %collective-permute-done.6.refs_0_.refs_1_, bf16[2816,256]{1,0:T(8,128)(2,1)} %collective-permute-done.7.refs_1_.refs_2_, ...), custom_call_target="tpu_custom_call" | custom-call | flops 2300000000 | bytes 1048576 | tf_op jit(solution)/shard_map/forward_kernel/pallas_call | solution.py:347
  95.4 3.3 %collective-permute-start.13 = (bf16[1408,256]{1,0:T(8,128)(2,1)S(1)}, bf16[1408,256]{1,0:T(8,128)(2,1)S(1)}, u32[]{:S(2)}, u32[]{:S(2)}) collective-permute-start(bf16[1408,256]{1,0:T(8,128)(2,1)S(1)} %get-tuple-element.68), channel_id=1, source_target_pairs={{0,24},{8,0},{16,8},{24,16},{32,56},{40,32},{48,40},{56,48},{64,88... | collective-permute-start | bytes 2162696 | tf_op jit(solution)/shard_map/ppermute | solution.py:39
  99.1 1.7 collective-permute-start.15
  100.8 14.5 %project_early.1 = (bf16[4,2,16,256]{3,2,1,0:T(8,128)(2,1)S(1)}, f32[4,4,256,256]{3,2,1,0:T(8,128)S(1)}) custom-call(s32[13]{0:T(128)S(1)} %copy-done.7, s32[1024,2]{1,0:T(8,128)S(1)} %copy-done.6, bf16[1024,2048]{1,0:T(8,128)(2,1)S(1)} %copy-done.1, bf16[2816,256]{1,0:T(8,128)(2,1)} %slice_dynamic-update-slice_fusion.5.refs_0_, ...), custom_call_target="tpu_custom_call" | custom-call | flops 17250000896 | bytes 1048576 | tf_op jit(solution)/shard_map/project_early/pallas_call | solution.py:179
  115.3 0.7 collective-permute-done.14.refs_2_
  116.0 1.2 collective-permute-done.15.refs_3_
  117.3 1.7 collective-permute-start.17
  119.8 2.7 %collective-permute-start.18 = (bf16[2048,256]{1,0:T(8,128)(2,1)S(1)}, bf16[2048,256]{1,0:T(8,128)(2,1)S(1)}, u32[]{:S(2)}, u32[]{:S(2)}) collective-permute-start(bf16[2048,256]{1,0:T(8,128)(2,1)S(1)} %pad_maximum_fusion.1.refs_5_), channel_id=1, source_target_pairs={{0,32},{8,40},{16,48},{24,56},{32,64},{40,72},{48,80},{56,88},{64,... | collective-permute-start | bytes 3145736 | tf_op jit(solution)/shard_map/ppermute | solution.py:39
  122.5 19.3 %attention.1.lhs_ref = bf16[8,1024,256]{2,1,0:T(8,128)(2,1)S(1)} custom-call(s32[13]{0:T(128)S(1)} %copy-done.7, s32[1024,2]{1,0:T(8,128)S(1)} %copy-done.6, bf16[8,4,16,256]{3,2,1,0:T(8,128)(2,1)} %all-to-all-done.1.down_ref, bf16[1024,2048]{1,0:T(8,128)(2,1)S(1)} %copy-done.1, bf16[4,2,16,256]{3,2,1,0:T(8,128)(2,1)S(1)} %get-tuple-element.74.up_ref, ...), custom_call_target="tpu_custom_call" | custom-call | flops 25300000768 | bytes 1048576 | tf_op jit(solution)/shard_map/attention/pallas_call | solution.py:258
  141.8 0.8 collective-permute-done.16.refs_0_.refs_1_
  143.5 3.0 %collective-permute-start.21 = (bf16[1024,256]{1,0:T(8,128)(2,1)S(1)}, bf16[1024,256]{1,0:T(8,128)(2,1)S(1)}, u32[]{:S(2)}, u32[]{:S(2)}) collective-permute-start(bf16[1024,256]{1,0:T(8,128)(2,1)S(1)} %get-tuple-element.86), channel_id=1, source_target_pairs={{0,24},{8,0},{16,8},{24,16},{32,56},{40,32},{48,40},{56,48},{64,88... | collective-permute-start | bytes 1572872 | tf_op jit(solution)/shard_map/ppermute | solution.py:39
  146.4 3.0 %collective-permute-start.22 = (bf16[1024,256]{1,0:T(8,128)(2,1)S(1)}, bf16[1024,256]{1,0:T(8,128)(2,1)S(1)}, u32[]{:S(2)}, u32[]{:S(2)}) collective-permute-start(bf16[1024,256]{1,0:T(8,128)(2,1)S(1)} %get-tuple-element.87), channel_id=1, source_target_pairs={{0,32},{8,40},{16,48},{24,56},{32,64},{40,72},{48,80},{56,88},{64,... | collective-permute-start | bytes 1572872 | tf_op jit(solution)/shard_map/ppermute | solution.py:39
  149.4 5.4 %collective-permute-done.20.refs_3_ = bf16[1024,256]{1,0:T(8,128)(2,1)S(1)} collective-permute-done((bf16[1024,256]{1,0:T(8,128)(2,1)S(1)}, bf16[1024,256]{1,0:T(8,128)(2,1)S(1)}, u32[]{:S(2)}, u32[]{:S(2)}) %collective-permute-start.20) | collective-permute-done | bytes 524320 | tf_op jit(solution)/shard_map/ppermute | solution.py:39
  154.8 1.7 collective-permute-done.22.refs_8_
  156.4 3.4 %collective-permute-done.23.refs_9_ = bf16[1024,256]{1,0:T(8,128)(2,1)S(1)} collective-permute-done((bf16[1024,256]{1,0:T(8,128)(2,1)S(1)}, bf16[1024,256]{1,0:T(8,128)(2,1)S(1)}, u32[]{:S(2)}, u32[]{:S(2)}) %collective-permute-start.23) | collective-permute-done | bytes 524320 | tf_op jit(solution)/shard_map/ppermute | solution.py:39
  159.8 7.7 %project_out_3.1 = (bf16[1024,256]{1,0:T(8,128)(2,1)S(1)}, bf16[1024,256]{1,0:T(8,128)(2,1)S(1)}, bf16[1024,256]{1,0:T(8,128)(2,1)S(1)}) custom-call(s32[3]{0:T(128)S(1)} %pad_add_fusion.1.place_ref, f32[1024,8]{1,0:T(8,128)S(1)} %broadcast_multiply_fusion.gates_ref, bf16[8,1024,256]{2,1,0:T(8,128)(2,1)S(1)} %attention.1.lhs_ref, ...), custom_call_target="tpu_custom_call" | custom-call | flops 7590000128 | bytes 1048576 | tf_op jit(solution)/shard_map/project_out_3/pallas_call | solution.py:331
  167.6 5.1 %project_out_2.2 = bf16[2,1024,256]{2,1,0:T(8,128)(2,1)S(1)} custom-call(s32[3]{0:T(128)S(1)} %pad_add_fusion.1.place_ref, f32[1024,8]{1,0:T(8,128)S(1)} %broadcast_multiply_fusion.gates_ref, bf16[8,1024,256]{2,1,0:T(8,128)(2,1)S(1)} %attention.1.lhs_ref, bf16[2048,256]{1,0:T(8,128)(2,1)S(1)} %pad_maximum_fusion.refs_0_, ...), custom_call_target="tpu_custom_call" | custom-call | flops 5059999744 | bytes 1048576 | tf_op jit(solution)/shard_map/project_out_2/pallas_call | solution.py:331
  173.4 1.2 collective-permute-start.26
  174.6 2.1 %collective-permute-start.27 = (bf16[512,256]{1,0:T(8,128)(2,1)S(1)}, bf16[512,256]{1,0:T(8,128)(2,1)S(1)}, u32[]{:S(2)}, u32[]{:S(2)}) collective-permute-start(bf16[512,256]{1,0:T(8,128)(2,1)S(1)} %get-tuple-element.94), channel_id=1, source_target_pairs={{0,6},{1,7},{2,0},{3,1},{4,2},{5,3},{6,4},{7,5},{8,14},{9,15},{10,... | collective-permute-start | bytes 786440 | tf_op jit(solution)/shard_map/ppermute | solution.py:400
  176.7 5.0 %project_out_2.3.mine_ref = bf16[2,1024,256]{2,1,0:T(8,128)(2,1)S(1)} custom-call(s32[3]{0:T(128)S(1)} %pad_add_fusion.1.place_ref, f32[1024,8]{1,0:T(8,128)S(1)} %broadcast_multiply_fusion.gates_ref, bf16[8,1024,256]{2,1,0:T(8,128)(2,1)S(1)} %attention.1.lhs_ref, bf16[2048,256]{1,0:T(8,128)(2,1)S(1)} %pad_maximum_fusion.refs_0_, ...), custom_call_target="tpu_custom_call" | custom-call | flops 5059999744 | bytes 1048576 | tf_op jit(solution)/shard_map/project_out_2/pallas_call | solution.py:331
  181.8 1.2 collective-permute-done.27.high_ref
  183.7 3.0 %collective-permute-start.30 = (bf16[1024,256]{1,0:T(8,128)(2,1)S(1)}, bf16[1024,256]{1,0:T(8,128)(2,1)S(1)}, u32[]{:S(2)}, u32[]{:S(2)}) collective-permute-start(bf16[1024,256]{1,0:T(8,128)(2,1)S(1)} %get-tuple-element.98), channel_id=1, source_target_pairs={{0,6},{1,7},{2,0},{3,1},{4,2},{5,3},{6,4},{7,5},{8,14},{9,15},{10,... | collective-permute-start | bytes 1572872 | tf_op jit(solution)/shard_map/ppermute | solution.py:400
  186.7 2.9 %project_out_1.1 = bf16[1,1024,256]{2,1,0:T(8,128)(2,1)S(1)} custom-call(s32[3]{0:T(128)S(1)} %pad_add_fusion.1.place_ref, f32[1024,8]{1,0:T(8,128)S(1)} %broadcast_multiply_fusion.gates_ref, bf16[8,1024,256]{2,1,0:T(8,128)(2,1)S(1)} %attention.1.lhs_ref, bf16[2048,256]{1,0:T(8,128)(2,1)S(1)} %pad_maximum_fusion.refs_0_, ...), custom_call_target="tpu_custom_call" | custom-call | flops 2529999872 | bytes 1048576 | tf_op jit(solution)/shard_map/project_out_1/pallas_call | solution.py:331
  189.6 7.8 %collective-permute-done.30 = bf16[1024,256]{1,0:T(8,128)(2,1)S(1)} collective-permute-done((bf16[1024,256]{1,0:T(8,128)(2,1)S(1)}, bf16[1024,256]{1,0:T(8,128)(2,1)S(1)}, u32[]{:S(2)}, u32[]{:S(2)}) %collective-permute-start.30) | collective-permute-done | bytes 524320 | tf_op jit(solution)/shard_map/ppermute | solution.py:400
  197.4 3.4 %collective-permute-done.29 = bf16[1024,256]{1,0:T(8,128)(2,1)S(1)} collective-permute-done((bf16[1024,256]{1,0:T(8,128)(2,1)S(1)}, bf16[1024,256]{1,0:T(8,128)(2,1)S(1)}, u32[]{:S(2)}, u32[]{:S(2)}) %collective-permute-start.29) | collective-permute-done | bytes 524320 | tf_op jit(solution)/shard_map/ppermute | solution.py:400
  200.8 1.1 fusion.2
  (116 shorter events, 7.7 us)
Async XLA Ops:
  0.0 14.5 %copy-start = (bf16[4,2048,16]{1,2,0:T(8,128)(2,1)S(1)}, bf16[4,2048,16]{1,2,0:T(8,128)(2,1)}, u32[]{:S(2)}) copy-start(bf16[4,2048,16]{1,2,0:T(8,128)(2,1)} %param.25) | copy-start | bytes 786436
  0.0 2.1 %copy-start.12 = (bf16[128,8,256]{2,1,0:T(8,128)(2,1)S(1)}, bf16[128,8,256]{2,1,0:T(8,128)(2,1)}, u32[]{:S(2)}) copy-start(bf16[128,8,256]{2,1,0:T(8,128)(2,1)} %param.23) | copy-start | bytes 1572868
  2.1 2.4 %copy-start.8 = (bf16[64,8,2,128]{3,1,2,0:T(8,128)(2,1)}, bf16[64,8,2,128]{3,1,2,0:T(8,128)(2,1)S(1)}, u32[]{:S(2)}) copy-start(bf16[64,8,2,128]{3,1,2,0:T(8,128)(2,1)S(1)} %copy.43) | copy-start | bytes 786436
  2.1 1.1 copy-start.15
  2.3 1.6 copy-start.17
  4.5 9.2 %copy-start.21 = (s32[64]{0:T(128)S(1)}, s32[64]{0:T(128)}, u32[]{:S(2)}) copy-start(s32[64]{0:T(128)} %param.18) | copy-start | bytes 772
  5.4 23.8 %collective-permute-start.1 = (bf16[1216,256]{1,0:T(8,128)(2,1)}, bf16[1216,256]{1,0:T(8,128)(2,1)S(1)}, u32[]{:S(2)}, u32[]{:S(2)}) collective-permute-start(bf16[1216,256]{1,0:T(8,128)(2,1)} %pad_maximum_fusion.2), channel_id=1, source_target_pairs={{0,96},{8,104},{16,112},{24,120},{32,0},{40,8},{48,16},{56,24},{64... | collective-permute-start | bytes 1867784 | tf_op jit(solution)/shard_map/ppermute | solution.py:39
  6.2 23.0 %collective-permute-start = (bf16[1216,256]{1,0:T(8,128)(2,1)}, bf16[1216,256]{1,0:T(8,128)(2,1)S(1)}, u32[]{:S(2)}, u32[]{:S(2)}) collective-permute-start(bf16[1216,256]{1,0:T(8,128)(2,1)} %pad_maximum_fusion.2), channel_id=1, source_target_pairs={{0,32},{8,40},{16,48},{24,56},{32,64},{40,72},{48,80},{56,88},{64,... | collective-permute-start | bytes 1867784 | tf_op jit(solution)/shard_map/ppermute | solution.py:39
  8.7 1.0 copy-start.10
  9.7 32.9 %collective-permute-start.3 = (bf16[1216,256]{1,0:T(8,128)(2,1)}, bf16[1216,256]{1,0:T(8,128)(2,1)S(1)}, u32[]{:S(2)}, u32[]{:S(2)}) collective-permute-start(bf16[1216,256]{1,0:T(8,128)(2,1)} %pad_maximum_fusion.3), channel_id=1, source_target_pairs={{0,24},{8,0},{16,8},{24,16},{32,56},{40,32},{48,40},{56,48},{64,88... | collective-permute-start | bytes 1867784 | tf_op jit(solution)/shard_map/ppermute | solution.py:39
  13.7 33.1 %collective-permute-start.2 = (bf16[1216,256]{1,0:T(8,128)(2,1)}, bf16[1216,256]{1,0:T(8,128)(2,1)S(1)}, u32[]{:S(2)}, u32[]{:S(2)}) collective-permute-start(bf16[1216,256]{1,0:T(8,128)(2,1)} %pad_maximum_fusion.3), channel_id=1, source_target_pairs={{0,8},{8,16},{16,24},{24,0},{32,40},{40,48},{48,56},{56,32},{64,72... | collective-permute-start | bytes 1867784 | tf_op jit(solution)/shard_map/ppermute | solution.py:39
  17.4 7.5 %copy-start.22 = (s32[64]{0:T(128)S(1)}, s32[64]{0:T(128)}, u32[]{:S(2)}) copy-start(s32[64]{0:T(128)} %param.20) | copy-start | bytes 772
  17.4 7.5 %copy-start.23 = (s32[4]{0:T(128)S(1)}, s32[4]{0:T(128)}, u32[]{:S(2)}) copy-start(s32[4]{0:T(128)} %param.19) | copy-start | bytes 52
  17.4 7.7 %copy-start.19 = (s32[4]{0:T(128)S(1)}, s32[4]{0:T(128)}, u32[]{:S(2)}) copy-start(s32[4]{0:T(128)} %param.17) | copy-start | bytes 52
  17.4 8.4 %copy-start.18 = (bf16[2048,8]{0,1:T(8,128)(2,1)S(1)}, bf16[2048,8]{0,1:T(8,128)(2,1)}, u32[]{:S(2)}) copy-start(bf16[2048,8]{0,1:T(8,128)(2,1)} %param.21) | copy-start | bytes 98308
  17.5 59.1 %all-to-all-start = ((bf16[16,96,512]{2,1,0:T(8,128)(2,1)}), bf16[16,96,512]{2,1,0:T(8,128)(2,1)}, u32[]{:S(2)}, u32[]{:S(2)}) async-start(bf16[16,96,512]{2,1,0:T(8,128)(2,1)} %pack.1), calls=%async_computation | async-start | bytes 3145728 | tf_op jit(solution)/shard_map/all_to_all | solution.py:464
  29.2 45.5 %copy-start.2 = (bf16[1216,256]{1,0:T(8,128)(2,1)}, bf16[1216,256]{1,0:T(8,128)(2,1)S(1)}, u32[]{:S(2)}) copy-start(bf16[1216,256]{1,0:T(8,128)(2,1)S(1)} %collective-permute-done.1.refs_1_) | copy-start | bytes 1867780
  29.2 45.5 %copy-start.3 = (bf16[1216,256]{1,0:T(8,128)(2,1)}, bf16[1216,256]{1,0:T(8,128)(2,1)S(1)}, u32[]{:S(2)}) copy-start(bf16[1216,256]{1,0:T(8,128)(2,1)S(1)} %collective-permute-done.refs_0_) | copy-start | bytes 1867780
  42.6 32.2 %copy-start.4 = (bf16[1216,256]{1,0:T(8,128)(2,1)}, bf16[1216,256]{1,0:T(8,128)(2,1)S(1)}, u32[]{:S(2)}) copy-start(bf16[1216,256]{1,0:T(8,128)(2,1)S(1)} %collective-permute-done.3.refs_3_) | copy-start | bytes 1867780
  46.8 1.7 copy-start.5
  48.5 8.2 %collective-permute-start.8 = (bf16[608,256]{1,0:T(8,128)(2,1)S(1)}, bf16[608,256]{1,0:T(8,128)(2,1)S(1)}, u32[]{:S(2)}, u32[]{:S(2)}) collective-permute-start(bf16[608,256]{1,0:T(8,128)(2,1)S(1)} %get-tuple-element.59), channel_id=1, source_target_pairs={{0,8},{8,16},{16,24},{24,0},{32,40},{40,48},{48,56},{56,32},{64,72... | collective-permute-start | bytes 933896 | tf_op jit(solution)/shard_map/ppermute | solution.py:39
  48.6 22.4 %copy-start.20 = (s32[4]{0:T(128)S(1)}, s32[4]{0:T(128)}, u32[]{:S(2)}) copy-start(s32[4]{0:T(128)} %param.16) | copy-start | bytes 52
  48.6 22.5 %copy-start.16 = (s32[1024,2]{0,1:T(2,128)S(1)}, s32[1024,2]{0,1:T(2,128)}, u32[]{:S(2)}) copy-start(s32[1024,2]{0,1:T(2,128)} %param.15) | copy-start | bytes 24580
  49.4 16.5 %collective-permute-start.4 = (bf16[608,256]{1,0:T(8,128)(2,1)S(1)}, bf16[608,256]{1,0:T(8,128)(2,1)S(1)}, u32[]{:S(2)}, u32[]{:S(2)}) collective-permute-start(bf16[608,256]{1,0:T(8,128)(2,1)S(1)} %get-tuple-element.57), channel_id=1, source_target_pairs={{0,32},{8,40},{16,48},{24,56},{32,64},{40,72},{48,80},{56,88},{64,... | collective-permute-start | bytes 933896 | tf_op jit(solution)/shard_map/ppermute | solution.py:39
  49.4 17.2 %collective-permute-start.5 = (bf16[608,256]{1,0:T(8,128)(2,1)S(1)}, bf16[608,256]{1,0:T(8,128)(2,1)S(1)}, u32[]{:S(2)}, u32[]{:S(2)}) collective-permute-start(bf16[608,256]{1,0:T(8,128)(2,1)S(1)} %get-tuple-element.58), channel_id=1, source_target_pairs={{0,96},{8,104},{16,112},{24,120},{32,0},{40,8},{48,16},{56,24},{64... | collective-permute-start | bytes 933896 | tf_op jit(solution)/shard_map/ppermute | solution.py:39
  51.4 10.6 %collective-permute-start.9 = (bf16[608,256]{1,0:T(8,128)(2,1)S(1)}, bf16[608,256]{1,0:T(8,128)(2,1)S(1)}, u32[]{:S(2)}, u32[]{:S(2)}) collective-permute-start(bf16[608,256]{1,0:T(8,128)(2,1)S(1)} %get-tuple-element.60), channel_id=1, source_target_pairs={{0,24},{8,0},{16,8},{24,16},{32,56},{40,32},{48,40},{56,48},{64,88... | collective-permute-start | bytes 933896 | tf_op jit(solution)/shard_map/ppermute | solution.py:39
  62.0 11.5 %copy-start.13 = (bf16[608,256]{1,0:T(8,128)(2,1)}, bf16[608,256]{1,0:T(8,128)(2,1)S(1)}, u32[]{:S(2)}) copy-start(bf16[608,256]{1,0:T(8,128)(2,1)S(1)} %collective-permute-done.9) | copy-start | bytes 933892
  62.6 29.7 %collective-permute-start.11 = (bf16[2816,256]{1,0:T(8,128)(2,1)}, bf16[2816,256]{1,0:T(8,128)(2,1)}, u32[]{:S(2)}, u32[]{:S(2)}) collective-permute-start(bf16[2816,256]{1,0:T(8,128)(2,1)} %slice_dynamic-update-slice_fusion.4.refs_3_), channel_id=1, source_target_pairs={{0,96},{8,104},{16,112},{24,120},{32,0},{40,8},{48,16},{56,24},{64... | collective-permute-start | bytes 4325384 | tf_op jit(solution)/shard_map/ppermute | solution.py:39
  62.9 29.4 %collective-permute-start.10 = (bf16[2816,256]{1,0:T(8,128)(2,1)}, bf16[2816,256]{1,0:T(8,128)(2,1)}, u32[]{:S(2)}, u32[]{:S(2)}) collective-permute-start(bf16[2816,256]{1,0:T(8,128)(2,1)} %slice_dynamic-update-slice_fusion.4.refs_3_), channel_id=1, source_target_pairs={{0,32},{8,40},{16,48},{24,56},{32,64},{40,72},{48,80},{56,88},{64,... | collective-permute-start | bytes 4325384 | tf_op jit(solution)/shard_map/ppermute | solution.py:39
  66.6 8.1 %copy-start.11 = (bf16[608,256]{1,0:T(8,128)(2,1)}, bf16[608,256]{1,0:T(8,128)(2,1)S(1)}, u32[]{:S(2)}) copy-start(bf16[608,256]{1,0:T(8,128)(2,1)S(1)} %collective-permute-done.5) | copy-start | bytes 933892
  67.3 25.1 %collective-permute-start.7 = (bf16[2816,256]{1,0:T(8,128)(2,1)}, bf16[2816,256]{1,0:T(8,128)(2,1)}, u32[]{:S(2)}, u32[]{:S(2)}) collective-permute-start(bf16[2816,256]{1,0:T(8,128)(2,1)} %slice_dynamic-update-slice_fusion.5.refs_0_), channel_id=1, source_target_pairs={{0,24},{8,0},{16,8},{24,16},{32,56},{40,32},{48,40},{56,48},{64,88... | collective-permute-start | bytes 4325384 | tf_op jit(solution)/shard_map/ppermute | solution.py:39
  71.0 21.4 %collective-permute-start.6 = (bf16[2816,256]{1,0:T(8,128)(2,1)}, bf16[2816,256]{1,0:T(8,128)(2,1)}, u32[]{:S(2)}, u32[]{:S(2)}) collective-permute-start(bf16[2816,256]{1,0:T(8,128)(2,1)} %slice_dynamic-update-slice_fusion.5.refs_0_), channel_id=1, source_target_pairs={{0,8},{8,16},{16,24},{24,0},{32,40},{40,48},{48,56},{56,32},{64,72... | collective-permute-start | bytes 4325384 | tf_op jit(solution)/shard_map/ppermute | solution.py:39
  74.7 1.0 copy-start.14
  74.7 1.7 slice-start.1
  74.7 1.7 copy-start.9
  74.7 1.7 slice-start.4
  74.8 1.6 slice-start
  76.5 8.2 %slice-start.2 = ((bf16[1216,256]{1,0:T(8,128)(2,1)}), bf16[512,256]{1,0:T(8,128)(2,1)S(1)}, s32[]{:S(2)}) async-start(bf16[1216,256]{1,0:T(8,128)(2,1)} %copy-done.4), calls=%async_computation.4 | async-start | bytes 524288 | tf_op jit(solution)/shard_map/slice | solution.py:489
  76.5 8.2 %slice-start.3 = ((bf16[1216,256]{1,0:T(8,128)(2,1)}), bf16[512,256]{1,0:T(8,128)(2,1)S(1)}, s32[]{:S(2)}) async-start(bf16[1216,256]{1,0:T(8,128)(2,1)} %copy-done.5), calls=%async_computation.5 | async-start | bytes 524288 | tf_op jit(solution)/shard_map/slice | solution.py:488
  80.2 12.1 %all-to-all-start.1 = ((bf16[8,4,16,256]{3,2,1,0:T(8,128)(2,1)}), bf16[8,4,16,256]{3,2,1,0:T(8,128)(2,1)}, u32[]{:S(2)}, u32[]{:S(2)}) async-start(bf16[8,4,16,256]{3,2,1,0:T(8,128)(2,1)} %broadcast_in_dim.5), calls=%async_computation.1 | async-start | bytes 524288 | tf_op jit(solution)/shard_map/all_to_all | solution.py:506
  85.8 15.0 %copy-start.6 = (s32[1024,2]{1,0:T(8,128)S(1)}, s32[1024,2]{1,0:T(8,128)}, u32[]{:S(2)}) copy-start(s32[1024,2]{1,0:T(8,128)} %copy.34.routes_ref) | copy-start | bytes 24580
  85.8 15.0 %copy-start.7 = (s32[13]{0:T(128)S(1)}, s32[13]{0:T(128)}, u32[]{:S(2)}) copy-start(s32[13]{0:T(128)} %pad_add_fusion.info_ref) | copy-start | bytes 160
  92.3 8.5 %copy-start.1 = (bf16[1024,2048]{1,0:T(8,128)(2,1)S(1)}, bf16[1024,2048]{1,0:T(8,128)(2,1)}, u32[]{:S(2)}) copy-start(bf16[1024,2048]{1,0:T(8,128)(2,1)} %x_ref.3) | copy-start | bytes 12582916
  95.4 19.9 %collective-permute-start.12 = (bf16[1408,256]{1,0:T(8,128)(2,1)S(1)}, bf16[1408,256]{1,0:T(8,128)(2,1)S(1)}, u32[]{:S(2)}, u32[]{:S(2)}) collective-permute-start(bf16[1408,256]{1,0:T(8,128)(2,1)S(1)} %get-tuple-element.67), channel_id=1, source_target_pairs={{0,8},{8,16},{16,24},{24,0},{32,40},{40,48},{48,56},{56,32},{64,72... | collective-permute-start | bytes 2162696 | tf_op jit(solution)/shard_map/ppermute | solution.py:39
  95.4 19.9 %collective-permute-start.13 = (bf16[1408,256]{1,0:T(8,128)(2,1)S(1)}, bf16[1408,256]{1,0:T(8,128)(2,1)S(1)}, u32[]{:S(2)}, u32[]{:S(2)}) collective-permute-start(bf16[1408,256]{1,0:T(8,128)(2,1)S(1)} %get-tuple-element.68), channel_id=1, source_target_pairs={{0,24},{8,0},{16,8},{24,16},{32,56},{40,32},{48,40},{56,48},{64,88... | collective-permute-start | bytes 2162696 | tf_op jit(solution)/shard_map/ppermute | solution.py:39
  98.8 17.2 %collective-permute-start.14 = (bf16[1408,256]{1,0:T(8,128)(2,1)S(1)}, bf16[1408,256]{1,0:T(8,128)(2,1)S(1)}, u32[]{:S(2)}, u32[]{:S(2)}) collective-permute-start(bf16[1408,256]{1,0:T(8,128)(2,1)S(1)} %get-tuple-element.69), channel_id=1, source_target_pairs={{0,32},{8,40},{16,48},{24,56},{32,64},{40,72},{48,80},{56,88},{64,... | collective-permute-start | bytes 2162696 | tf_op jit(solution)/shard_map/ppermute | solution.py:39
  99.1 18.2 %collective-permute-start.15 = (bf16[1408,256]{1,0:T(8,128)(2,1)S(1)}, bf16[1408,256]{1,0:T(8,128)(2,1)S(1)}, u32[]{:S(2)}, u32[]{:S(2)}) collective-permute-start(bf16[1408,256]{1,0:T(8,128)(2,1)S(1)} %get-tuple-element.70), channel_id=1, source_target_pairs={{0,96},{8,104},{16,112},{24,120},{32,0},{40,8},{48,16},{56,24},{64... | collective-permute-start | bytes 2162696 | tf_op jit(solution)/shard_map/ppermute | solution.py:39
  117.3 24.6 %collective-permute-start.17 = (bf16[2048,256]{1,0:T(8,128)(2,1)S(1)}, bf16[2048,256]{1,0:T(8,128)(2,1)S(1)}, u32[]{:S(2)}, u32[]{:S(2)}) collective-permute-start(bf16[2048,256]{1,0:T(8,128)(2,1)S(1)} %pad_maximum_fusion.refs_0_), channel_id=1, source_target_pairs={{0,24},{8,0},{16,8},{24,16},{32,56},{40,32},{48,40},{56,48},{64,88... | collective-permute-start | bytes 3145736 | tf_op jit(solution)/shard_map/ppermute | solution.py:39
  118.9 23.7 %collective-permute-start.16 = (bf16[2048,256]{1,0:T(8,128)(2,1)S(1)}, bf16[2048,256]{1,0:T(8,128)(2,1)S(1)}, u32[]{:S(2)}, u32[]{:S(2)}) collective-permute-start(bf16[2048,256]{1,0:T(8,128)(2,1)S(1)} %pad_maximum_fusion.refs_0_), channel_id=1, source_target_pairs={{0,8},{8,16},{16,24},{24,0},{32,40},{40,48},{48,56},{56,32},{64,72... | collective-permute-start | bytes 3145736 | tf_op jit(solution)/shard_map/ppermute | solution.py:39
  119.3 23.7 %collective-permute-start.19 = (bf16[2048,256]{1,0:T(8,128)(2,1)S(1)}, bf16[2048,256]{1,0:T(8,128)(2,1)S(1)}, u32[]{:S(2)}, u32[]{:S(2)}) collective-permute-start(bf16[2048,256]{1,0:T(8,128)(2,1)S(1)} %pad_maximum_fusion.1.refs_5_), channel_id=1, source_target_pairs={{0,96},{8,104},{16,112},{24,120},{32,0},{40,8},{48,16},{56,24},{64... | collective-permute-start | bytes 3145736 | tf_op jit(solution)/shard_map/ppermute | solution.py:39
  119.8 23.2 %collective-permute-start.18 = (bf16[2048,256]{1,0:T(8,128)(2,1)S(1)}, bf16[2048,256]{1,0:T(8,128)(2,1)S(1)}, u32[]{:S(2)}, u32[]{:S(2)}) collective-permute-start(bf16[2048,256]{1,0:T(8,128)(2,1)S(1)} %pad_maximum_fusion.1.refs_5_), channel_id=1, source_target_pairs={{0,32},{8,40},{16,48},{24,56},{32,64},{40,72},{48,80},{56,88},{64,... | collective-permute-start | bytes 3145736 | tf_op jit(solution)/shard_map/ppermute | solution.py:39
  143.1 11.6 %collective-permute-start.20 = (bf16[1024,256]{1,0:T(8,128)(2,1)S(1)}, bf16[1024,256]{1,0:T(8,128)(2,1)S(1)}, u32[]{:S(2)}, u32[]{:S(2)}) collective-permute-start(bf16[1024,256]{1,0:T(8,128)(2,1)S(1)} %get-tuple-element.85), channel_id=1, source_target_pairs={{0,8},{8,16},{16,24},{24,0},{32,40},{40,48},{48,56},{56,32},{64,72... | collective-permute-start | bytes 1572872 | tf_op jit(solution)/shard_map/ppermute | solution.py:39
  143.5 11.3 %collective-permute-start.21 = (bf16[1024,256]{1,0:T(8,128)(2,1)S(1)}, bf16[1024,256]{1,0:T(8,128)(2,1)S(1)}, u32[]{:S(2)}, u32[]{:S(2)}) collective-permute-start(bf16[1024,256]{1,0:T(8,128)(2,1)S(1)} %get-tuple-element.86), channel_id=1, source_target_pairs={{0,24},{8,0},{16,8},{24,16},{32,56},{40,32},{48,40},{56,48},{64,88... | collective-permute-start | bytes 1572872 | tf_op jit(solution)/shard_map/ppermute | solution.py:39
  146.4 10.0 %collective-permute-start.22 = (bf16[1024,256]{1,0:T(8,128)(2,1)S(1)}, bf16[1024,256]{1,0:T(8,128)(2,1)S(1)}, u32[]{:S(2)}, u32[]{:S(2)}) collective-permute-start(bf16[1024,256]{1,0:T(8,128)(2,1)S(1)} %get-tuple-element.87), channel_id=1, source_target_pairs={{0,32},{8,40},{16,48},{24,56},{32,64},{40,72},{48,80},{56,88},{64,... | collective-permute-start | bytes 1572872 | tf_op jit(solution)/shard_map/ppermute | solution.py:39
  149.4 10.4 %collective-permute-start.23 = (bf16[1024,256]{1,0:T(8,128)(2,1)S(1)}, bf16[1024,256]{1,0:T(8,128)(2,1)S(1)}, u32[]{:S(2)}, u32[]{:S(2)}) collective-permute-start(bf16[1024,256]{1,0:T(8,128)(2,1)S(1)} %get-tuple-element.88), channel_id=1, source_target_pairs={{0,96},{8,104},{16,112},{24,120},{32,0},{40,8},{48,16},{56,24},{64... | collective-permute-start | bytes 1572872 | tf_op jit(solution)/shard_map/ppermute | solution.py:39
  167.5 5.8 %collective-permute-start.24 = (bf16[1024,256]{1,0:T(8,128)(2,1)S(1)}, bf16[1024,256]{1,0:T(8,128)(2,1)S(1)}, u32[]{:S(2)}, u32[]{:S(2)}) collective-permute-start(bf16[1024,256]{1,0:T(8,128)(2,1)S(1)} %get-tuple-element.91), channel_id=1, source_target_pairs={{0,1},{1,0},{2,3},{3,2},{4,5},{5,4},{6,7},{7,6},{8,9},{9,8},{10,11... | collective-permute-start | bytes 1572872 | tf_op jit(solution)/shard_map/ppermute | solution.py:399
  172.6 10.7 %collective-permute-start.25 = (bf16[2,1024,256]{2,1,0:T(8,128)(2,1)S(1)}, bf16[2,1024,256]{2,1,0:T(8,128)(2,1)S(1)}, u32[]{:S(2)}, u32[]{:S(2)}) collective-permute-start(bf16[2,1024,256]{2,1,0:T(8,128)(2,1)S(1)} %project_out_2.2), channel_id=1, source_target_pairs={{0,1},{1,0},{2,3},{3,2},{4,5},{5,4},{6,7},{7,6},{8,9},{9,8},{10,11... | collective-permute-start | bytes 3145736 | tf_op jit(solution)/shard_map/ppermute | solution.py:399
  173.2 16.4 %collective-permute-start.28 = (bf16[1024,256]{1,0:T(8,128)(2,1)S(1)}, bf16[1024,256]{1,0:T(8,128)(2,1)S(1)}, u32[]{:S(2)}, u32[]{:S(2)}) collective-permute-start(bf16[1024,256]{1,0:T(8,128)(2,1)S(1)} %get-tuple-element.97), channel_id=1, source_target_pairs={{0,1},{1,0},{2,3},{3,2},{4,5},{5,4},{6,7},{7,6},{8,9},{9,8},{10,11... | collective-permute-start | bytes 1572872 | tf_op jit(solution)/shard_map/ppermute | solution.py:399
  173.4 9.9 %collective-permute-start.26 = (bf16[512,256]{1,0:T(8,128)(2,1)S(1)}, bf16[512,256]{1,0:T(8,128)(2,1)S(1)}, u32[]{:S(2)}, u32[]{:S(2)}) collective-permute-start(bf16[512,256]{1,0:T(8,128)(2,1)S(1)} %get-tuple-element.92), channel_id=1, source_target_pairs={{0,2},{1,3},{2,4},{3,5},{4,6},{5,7},{6,0},{7,1},{8,10},{9,11},{10,... | collective-permute-start | bytes 786440 | tf_op jit(solution)/shard_map/ppermute | solution.py:400
  174.6 8.4 %collective-permute-start.27 = (bf16[512,256]{1,0:T(8,128)(2,1)S(1)}, bf16[512,256]{1,0:T(8,128)(2,1)S(1)}, u32[]{:S(2)}, u32[]{:S(2)}) collective-permute-start(bf16[512,256]{1,0:T(8,128)(2,1)S(1)} %get-tuple-element.94), channel_id=1, source_target_pairs={{0,6},{1,7},{2,0},{3,1},{4,2},{5,3},{6,4},{7,5},{8,14},{9,15},{10,... | collective-permute-start | bytes 786440 | tf_op jit(solution)/shard_map/ppermute | solution.py:400
  183.7 13.7 %collective-permute-start.30 = (bf16[1024,256]{1,0:T(8,128)(2,1)S(1)}, bf16[1024,256]{1,0:T(8,128)(2,1)S(1)}, u32[]{:S(2)}, u32[]{:S(2)}) collective-permute-start(bf16[1024,256]{1,0:T(8,128)(2,1)S(1)} %get-tuple-element.98), channel_id=1, source_target_pairs={{0,6},{1,7},{2,0},{3,1},{4,2},{5,3},{6,4},{7,5},{8,14},{9,15},{10,... | collective-permute-start | bytes 1572872 | tf_op jit(solution)/shard_map/ppermute | solution.py:400
  186.7 14.1 %collective-permute-start.29 = (bf16[1024,256]{1,0:T(8,128)(2,1)S(1)}, bf16[1024,256]{1,0:T(8,128)(2,1)S(1)}, u32[]{:S(2)}, u32[]{:S(2)}) collective-permute-start(bf16[1024,256]{1,0:T(8,128)(2,1)S(1)} %get-tuple-element.95), channel_id=1, source_target_pairs={{0,2},{1,3},{2,4},{3,5},{4,6},{5,7},{6,0},{7,1},{8,10},{9,11},{10,... | collective-permute-start | bytes 1572872 | tf_op jit(solution)/shard_map/ppermute | solution.py:400

commit v6 on v5

--- a/solution.py
+++ b/solution.py
@@ -356,10 +356,17 @@
 
 
 def forward_kernel(*refs):
-    for i in range(4):
-        source_ref, out_ref = refs[i], refs[4 + i]
-        half = out_ref.shape[0]
-        out_ref[...] = source_ref[pl.ds(i % 2 * half, half), :]
+    half = refs[4].shape[0]
+    steps = 8 if half % 128 == 0 else 2
+    chunk = half // steps
+
+    def copy(step, carry):
+        start = pl.multiple_of(step * chunk, chunk)
+        for i in range(4):
+            refs[4 + i][pl.ds(start, chunk), :] = refs[i][pl.ds(i % 2 * half + start, chunk), :]
+        return carry
+
+    lax.fori_loop(0, steps, copy, 0)
 
 
 def forwarded(values):

time: 203 us -> 203 us (level)
  no operation moved by 1% of the time
where the time goes in v6:
time: 203 us; the launch traced here: 202 us
  Pallas kernels  62.6 us (31%)
  waiting for transfers between devices  56.3 us (28%)
  starting transfers between devices  55.4 us (27%)
  local copies, waits for them, and re-layouts  16.7 us (8%)
  other arithmetic  7.1 us (3%)
  matrix products  3.37 us (2%)
    ppermute x24, waiting for transfers between devices, send(): lax.ppermute(value, 'req', torus(step, 0) if along == 0 else torus(0, step))  37.1 us
    ppermute x24, starting transfers between devices, send(): lax.ppermute(value, 'req', torus(step, 0) if along == 0 else torus(0, step))  36.5 us
    pallas_call x4, Pallas kernels, project_out(): pl.pallas_call(functools.partial(project_out_kernel, blocks), out_shape=s...  20.6 us
    pallas_call x1, Pallas kernels, attention(): pl.pallas_call(attend_kernel, out_shape=jax.ShapeDtypeStruct((NE, 1024, 2...  19.3 us
    pallas_call x1, Pallas kernels, project_early(): pl.pallas_call(early_kernel, out_shape=(jax.ShapeDtypeStruct((4, 2, 16, 2...  14.5 us
    ppermute x4, waiting for transfers between devices, exchange(): lax.ppermute(value, 'exp', [(i, (i + 2 * step) % 8) for i in range(8)])  12.7 us
    unnamed x61, local copies, waits for them, and re-layouts  8.86 us
    all_to_all x1, starting transfers between devices, body(): received = lax.all_to_all(outgoing, 'req', 0, 0, tiled=True)  7.34 us
  transfers between devices with their start and end apart: 33, of which 16 were waited for; matrix products, arithmetic and copies ran while one was open for 10% of the time, Pallas kernels for 26%

profile of v6, /device:TPU:6, one launch (start us, length us, event | category | flops | bytes accessed | tf_op | source)
XLA Modules:
  0.0 201.9 jit_solution(2446743874292557850)
XLA Ops:
  0.0 1.7 copy.41
  2.4 0.8 constant_dynamic-update-slice_fusion.3
  3.2 0.7 constant_dynamic-update-slice_fusion.6
  4.5 0.9 pad_maximum_fusion.2
  5.4 0.8 collective-permute-start.1
  6.2 2.4 %collective-permute-start = (bf16[1216,256]{1,0:T(8,128)(2,1)}, bf16[1216,256]{1,0:T(8,128)(2,1)S(1)}, u32[]{:S(2)}, u32[]{:S(2)}) collective-permute-start(bf16[1216,256]{1,0:T(8,128)(2,1)} %pad_maximum_fusion.2), channel_id=1, source_target_pairs={{0,32},{8,40},{16,48},{24,56},{32,64},{40,72},{48,80},{56,88},{64,... | collective-permute-start | bytes 1867784 | tf_op jit(solution)/shard_map/ppermute | solution.py:39
  8.7 1.0 pad_maximum_fusion.3
  9.7 4.0 %collective-permute-start.3 = (bf16[1216,256]{1,0:T(8,128)(2,1)}, bf16[1216,256]{1,0:T(8,128)(2,1)S(1)}, u32[]{:S(2)}, u32[]{:S(2)}) collective-permute-start(bf16[1216,256]{1,0:T(8,128)(2,1)} %pad_maximum_fusion.3), channel_id=1, source_target_pairs={{0,24},{8,0},{16,8},{24,16},{32,56},{40,32},{48,40},{56,48},{64,88... | collective-permute-start | bytes 1867784 | tf_op jit(solution)/shard_map/ppermute | solution.py:39
  13.8 0.7 select_reduce_fusion.2.index_ref
  15.1 2.3 %pack.1 = bf16[16,96,512]{2,1,0:T(8,128)(2,1)} custom-call(s32[16]{0:T(128)} %select_reduce_fusion.2.index_ref, bf16[4,64,512]{2,1,0:T(8,128)(2,1)} %store_ref.1, bf16[64,256]{1,0:T(8,128)(2,1)} %bitcast.46), custom_call_target="tpu_custom_call" | custom-call | flops 3449999872 | bytes 1048576 | tf_op jit(solution)/shard_map/pack/pallas_call | solution.py:74
  17.5 7.3 %all-to-all-start = ((bf16[16,96,512]{2,1,0:T(8,128)(2,1)}), bf16[16,96,512]{2,1,0:T(8,128)(2,1)}, u32[]{:S(2)}, u32[]{:S(2)}) async-start(bf16[16,96,512]{2,1,0:T(8,128)(2,1)} %pack.1), calls=%async_computation | async-start | bytes 3145728 | tf_op jit(solution)/shard_map/all_to_all | solution.py:471
  25.1 0.7 pad_add_fusion.info_ref
  25.8 3.4 %fusion.5 = f32[1024,8]{0,1:T(8,128)S(1)} fusion(bf16[1024,2048]{1,0:T(8,128)(2,1)} %x_ref.3, bf16[2048,8]{0,1:T(8,128)(2,1)S(1)} %copy-done.18), kind=kOutput, calls=%fused_computation.41 | convolution fusion | flops 33554432 | bytes 4259840 | tf_op jit(solution)/shard_map/dot_general | solution.py:503
  29.2 13.4 %collective-permute-done.3.refs_3_ = bf16[1216,256]{1,0:T(8,128)(2,1)S(1)} collective-permute-done((bf16[1216,256]{1,0:T(8,128)(2,1)}, bf16[1216,256]{1,0:T(8,128)(2,1)S(1)}, u32[]{:S(2)}, u32[]{:S(2)}) %collective-permute-start.3) | collective-permute-done | bytes 622624 | tf_op jit(solution)/shard_map/ppermute | solution.py:39
  42.6 4.3 %collective-permute-done.2.refs_2_ = bf16[1216,256]{1,0:T(8,128)(2,1)S(1)} collective-permute-done((bf16[1216,256]{1,0:T(8,128)(2,1)}, bf16[1216,256]{1,0:T(8,128)(2,1)S(1)}, u32[]{:S(2)}, u32[]{:S(2)}) %collective-permute-start.2) | collective-permute-done | bytes 622624 | tf_op jit(solution)/shard_map/ppermute | solution.py:39
  46.8 0.8 slice_dynamic-update-slice_fusion.3
  47.7 0.8 slice_dynamic-update-slice_fusion.2
  48.6 0.8 slice_dynamic-update-slice_fusion.1
  49.4 2.0 %collective-permute-start.5 = (bf16[608,256]{1,0:T(8,128)(2,1)S(1)}, bf16[608,256]{1,0:T(8,128)(2,1)S(1)}, u32[]{:S(2)}, u32[]{:S(2)}) collective-permute-start(bf16[608,256]{1,0:T(8,128)(2,1)S(1)} %get-tuple-element.58), channel_id=1, source_target_pairs={{0,96},{8,104},{16,112},{24,120},{32,0},{40,8},{48,16},{56,24},{64... | collective-permute-start | bytes 933896 | tf_op jit(solution)/shard_map/ppermute | solution.py:39
  51.4 3.2 %collective-permute-start.9 = (bf16[608,256]{1,0:T(8,128)(2,1)S(1)}, bf16[608,256]{1,0:T(8,128)(2,1)S(1)}, u32[]{:S(2)}, u32[]{:S(2)}) collective-permute-start(bf16[608,256]{1,0:T(8,128)(2,1)S(1)} %get-tuple-element.60), channel_id=1, source_target_pairs={{0,24},{8,0},{16,8},{24,16},{32,56},{40,32},{48,40},{56,48},{64,88... | collective-permute-start | bytes 933896 | tf_op jit(solution)/shard_map/ppermute | solution.py:39
  54.6 0.8 slice_dynamic-update-slice_fusion
  55.4 1.3 collective-permute-done.8
  56.7 0.7 constant_dynamic-update-slice_fusion.4
  57.4 4.6 %collective-permute-done.9 = bf16[608,256]{1,0:T(8,128)(2,1)S(1)} collective-permute-done((bf16[608,256]{1,0:T(8,128)(2,1)S(1)}, bf16[608,256]{1,0:T(8,128)(2,1)S(1)}, u32[]{:S(2)}, u32[]{:S(2)}) %collective-permute-start.9) | collective-permute-done | bytes 311328 | tf_op jit(solution)/shard_map/ppermute | solution.py:39
  62.9 2.9 %collective-permute-start.10 = (bf16[2816,256]{1,0:T(8,128)(2,1)}, bf16[2816,256]{1,0:T(8,128)(2,1)}, u32[]{:S(2)}, u32[]{:S(2)}) collective-permute-start(bf16[2816,256]{1,0:T(8,128)(2,1)} %slice_dynamic-update-slice_fusion.4.refs_3_), channel_id=1, source_target_pairs={{0,32},{8,40},{16,48},{24,56},{32,64},{40,72},{48,80},{56,88},{64,... | collective-permute-start | bytes 4325384 | tf_op jit(solution)/shard_map/ppermute | solution.py:39
  65.9 0.7 constant_dynamic-update-slice_fusion
  66.6 0.7 slice_dynamic-update-slice_fusion.5.refs_0_
  67.3 3.7 %collective-permute-start.7 = (bf16[2816,256]{1,0:T(8,128)(2,1)}, bf16[2816,256]{1,0:T(8,128)(2,1)}, u32[]{:S(2)}, u32[]{:S(2)}) collective-permute-start(bf16[2816,256]{1,0:T(8,128)(2,1)} %slice_dynamic-update-slice_fusion.5.refs_0_), channel_id=1, source_target_pairs={{0,24},{8,0},{16,8},{24,16},{32,56},{40,32},{48,40},{56,48},{64,88... | collective-permute-start | bytes 4325384 | tf_op jit(solution)/shard_map/ppermute | solution.py:39
  71.1 1.1 copy.34.routes_ref
  72.4 1.0 copy.32
  73.4 1.2 broadcast_multiply_fusion.gates_ref
  74.8 0.9 copy-done.14
  75.7 0.7 slice.109
  76.5 2.2 %pick_down.1 = bf16[4,16,256]{2,1,0:T(8,128)(2,1)} custom-call(s32[13]{0:T(128)} %pad_add_fusion.info_ref, bf16[16,96,512]{2,1,0:T(8,128)(2,1)} %all-to-all-done.recv_ref.recv_hbm), custom_call_target="tpu_custom_call" | custom-call | flops 2300000000 | bytes 1048576 | tf_op jit(solution)/shard_map/pick_down/pallas_call | solution.py:104
  78.7 1.5 broadcast_in_dim.5
  80.2 4.5 %all-to-all-start.1 = ((bf16[8,4,16,256]{3,2,1,0:T(8,128)(2,1)}), bf16[8,4,16,256]{3,2,1,0:T(8,128)(2,1)}, u32[]{:S(2)}, u32[]{:S(2)}) async-start(bf16[8,4,16,256]{3,2,1,0:T(8,128)(2,1)} %broadcast_in_dim.5), calls=%async_computation.1 | async-start | bytes 524288 | tf_op jit(solution)/shard_map/all_to_all | solution.py:513
  84.7 1.1 pad_maximum_fusion.1.refs_5_
  85.8 6.5 %all-to-all-done.1.down_ref = bf16[8,4,16,256]{3,2,1,0:T(8,128)(2,1)} async-done(((bf16[8,4,16,256]{3,2,1,0:T(8,128)(2,1)}), bf16[8,4,16,256]{3,2,1,0:T(8,128)(2,1)}, u32[]{:S(2)}, u32[]{:S(2)}) %all-to-all-start.1) | async-done | bytes 262176 | tf_op jit(solution)/shard_map/all_to_all | solution.py:513
  92.4 3.0 %forward_kernel.4 = (bf16[1408,256]{1,0:T(8,128)(2,1)S(1)}, bf16[1408,256]{1,0:T(8,128)(2,1)S(1)}, bf16[1408,256]{1,0:T(8,128)(2,1)S(1)}, bf16[1408,256]{1,0:T(8,128)(2,1)S(1)}) custom-call(bf16[2816,256]{1,0:T(8,128)(2,1)} %collective-permute-done.6.refs_0_.refs_1_, bf16[2816,256]{1,0:T(8,128)(2,1)} %collective-permute-done.7.refs_1_.refs_2_, ...), custom_call_target="tpu_custom_call" | custom-call | flops 2300000000 | bytes 1048576 | tf_op jit(solution)/shard_map/forward_kernel/pallas_call | solution.py:347
  95.5 3.3 %collective-permute-start.13 = (bf16[1408,256]{1,0:T(8,128)(2,1)S(1)}, bf16[1408,256]{1,0:T(8,128)(2,1)S(1)}, u32[]{:S(2)}, u32[]{:S(2)}) collective-permute-start(bf16[1408,256]{1,0:T(8,128)(2,1)S(1)} %get-tuple-element.68), channel_id=1, source_target_pairs={{0,24},{8,0},{16,8},{24,16},{32,56},{40,32},{48,40},{56,48},{64,88... | collective-permute-start | bytes 2162696 | tf_op jit(solution)/shard_map/ppermute | solution.py:39
  99.1 1.8 collective-permute-start.15
  100.8 14.5 %project_early.1 = (bf16[4,2,16,256]{3,2,1,0:T(8,128)(2,1)S(1)}, f32[4,4,256,256]{3,2,1,0:T(8,128)S(1)}) custom-call(s32[13]{0:T(128)S(1)} %copy-done.7, s32[1024,2]{1,0:T(8,128)S(1)} %copy-done.6, bf16[1024,2048]{1,0:T(8,128)(2,1)S(1)} %copy-done.1, bf16[2816,256]{1,0:T(8,128)(2,1)} %slice_dynamic-update-slice_fusion.5.refs_0_, ...), custom_call_target="tpu_custom_call" | custom-call | flops 17250000896 | bytes 1048576 | tf_op jit(solution)/shard_map/project_early/pallas_call | solution.py:179
  115.3 0.7 collective-permute-done.14.refs_2_
  116.0 1.2 collective-permute-done.15.refs_3_
  117.2 1.7 collective-permute-start.17
  119.8 2.7 %collective-permute-start.18 = (bf16[2048,256]{1,0:T(8,128)(2,1)S(1)}, bf16[2048,256]{1,0:T(8,128)(2,1)S(1)}, u32[]{:S(2)}, u32[]{:S(2)}) collective-permute-start(bf16[2048,256]{1,0:T(8,128)(2,1)S(1)} %pad_maximum_fusion.1.refs_5_), channel_id=1, source_target_pairs={{0,32},{8,40},{16,48},{24,56},{32,64},{40,72},{48,80},{56,88},{64,... | collective-permute-start | bytes 3145736 | tf_op jit(solution)/shard_map/ppermute | solution.py:39
  122.5 19.3 %attention.1.lhs_ref = bf16[8,1024,256]{2,1,0:T(8,128)(2,1)S(1)} custom-call(s32[13]{0:T(128)S(1)} %copy-done.7, s32[1024,2]{1,0:T(8,128)S(1)} %copy-done.6, bf16[8,4,16,256]{3,2,1,0:T(8,128)(2,1)} %all-to-all-done.1.down_ref, bf16[1024,2048]{1,0:T(8,128)(2,1)S(1)} %copy-done.1, bf16[4,2,16,256]{3,2,1,0:T(8,128)(2,1)S(1)} %get-tuple-element.74.up_ref, ...), custom_call_target="tpu_custom_call" | custom-call | flops 25300000768 | bytes 1048576 | tf_op jit(solution)/shard_map/attention/pallas_call | solution.py:258
  141.8 0.8 collective-permute-done.16.refs_0_.refs_1_
  143.5 3.0 %collective-permute-start.21 = (bf16[1024,256]{1,0:T(8,128)(2,1)S(1)}, bf16[1024,256]{1,0:T(8,128)(2,1)S(1)}, u32[]{:S(2)}, u32[]{:S(2)}) collective-permute-start(bf16[1024,256]{1,0:T(8,128)(2,1)S(1)} %get-tuple-element.86), channel_id=1, source_target_pairs={{0,24},{8,0},{16,8},{24,16},{32,56},{40,32},{48,40},{56,48},{64,88... | collective-permute-start | bytes 1572872 | tf_op jit(solution)/shard_map/ppermute | solution.py:39
  146.4 3.0 %collective-permute-start.22 = (bf16[1024,256]{1,0:T(8,128)(2,1)S(1)}, bf16[1024,256]{1,0:T(8,128)(2,1)S(1)}, u32[]{:S(2)}, u32[]{:S(2)}) collective-permute-start(bf16[1024,256]{1,0:T(8,128)(2,1)S(1)} %get-tuple-element.87), channel_id=1, source_target_pairs={{0,32},{8,40},{16,48},{24,56},{32,64},{40,72},{48,80},{56,88},{64,... | collective-permute-start | bytes 1572872 | tf_op jit(solution)/shard_map/ppermute | solution.py:39
  149.4 5.4 %collective-permute-done.20.refs_3_ = bf16[1024,256]{1,0:T(8,128)(2,1)S(1)} collective-permute-done((bf16[1024,256]{1,0:T(8,128)(2,1)S(1)}, bf16[1024,256]{1,0:T(8,128)(2,1)S(1)}, u32[]{:S(2)}, u32[]{:S(2)}) %collective-permute-start.20) | collective-permute-done | bytes 524320 | tf_op jit(solution)/shard_map/ppermute | solution.py:39
  154.8 1.7 collective-permute-done.22.refs_8_
  156.4 3.4 %collective-permute-done.23.refs_9_ = bf16[1024,256]{1,0:T(8,128)(2,1)S(1)} collective-permute-done((bf16[1024,256]{1,0:T(8,128)(2,1)S(1)}, bf16[1024,256]{1,0:T(8,128)(2,1)S(1)}, u32[]{:S(2)}, u32[]{:S(2)}) %collective-permute-start.23) | collective-permute-done | bytes 524320 | tf_op jit(solution)/shard_map/ppermute | solution.py:39
  159.8 7.7 %project_out_3.1 = (bf16[1024,256]{1,0:T(8,128)(2,1)S(1)}, bf16[1024,256]{1,0:T(8,128)(2,1)S(1)}, bf16[1024,256]{1,0:T(8,128)(2,1)S(1)}) custom-call(s32[3]{0:T(128)S(1)} %pad_add_fusion.1.place_ref, f32[1024,8]{1,0:T(8,128)S(1)} %broadcast_multiply_fusion.gates_ref, bf16[8,1024,256]{2,1,0:T(8,128)(2,1)S(1)} %attention.1.lhs_ref, ...), custom_call_target="tpu_custom_call" | custom-call | flops 7590000128 | bytes 1048576 | tf_op jit(solution)/shard_map/project_out_3/pallas_call | solution.py:331
  167.6 5.1 %project_out_2.2 = bf16[2,1024,256]{2,1,0:T(8,128)(2,1)S(1)} custom-call(s32[3]{0:T(128)S(1)} %pad_add_fusion.1.place_ref, f32[1024,8]{1,0:T(8,128)S(1)} %broadcast_multiply_fusion.gates_ref, bf16[8,1024,256]{2,1,0:T(8,128)(2,1)S(1)} %attention.1.lhs_ref, bf16[2048,256]{1,0:T(8,128)(2,1)S(1)} %pad_maximum_fusion.refs_0_, ...), custom_call_target="tpu_custom_call" | custom-call | flops 5059999744 | bytes 1048576 | tf_op jit(solution)/shard_map/project_out_2/pallas_call | solution.py:331
  173.4 1.2 collective-permute-start.26
  174.6 2.1 %collective-permute-start.27 = (bf16[512,256]{1,0:T(8,128)(2,1)S(1)}, bf16[512,256]{1,0:T(8,128)(2,1)S(1)}, u32[]{:S(2)}, u32[]{:S(2)}) collective-permute-start(bf16[512,256]{1,0:T(8,128)(2,1)S(1)} %get-tuple-element.94), channel_id=1, source_target_pairs={{0,6},{1,7},{2,0},{3,1},{4,2},{5,3},{6,4},{7,5},{8,14},{9,15},{10,... | collective-permute-start | bytes 786440 | tf_op jit(solution)/shard_map/ppermute | solution.py:407
  176.7 5.0 %project_out_2.3.mine_ref = bf16[2,1024,256]{2,1,0:T(8,128)(2,1)S(1)} custom-call(s32[3]{0:T(128)S(1)} %pad_add_fusion.1.place_ref, f32[1024,8]{1,0:T(8,128)S(1)} %broadcast_multiply_fusion.gates_ref, bf16[8,1024,256]{2,1,0:T(8,128)(2,1)S(1)} %attention.1.lhs_ref, bf16[2048,256]{1,0:T(8,128)(2,1)S(1)} %pad_maximum_fusion.refs_0_, ...), custom_call_target="tpu_custom_call" | custom-call | flops 5059999744 | bytes 1048576 | tf_op jit(solution)/shard_map/project_out_2/pallas_call | solution.py:331
  181.8 1.2 collective-permute-done.27.high_ref
  183.7 3.0 %collective-permute-start.30 = (bf16[1024,256]{1,0:T(8,128)(2,1)S(1)}, bf16[1024,256]{1,0:T(8,128)(2,1)S(1)}, u32[]{:S(2)}, u32[]{:S(2)}) collective-permute-start(bf16[1024,256]{1,0:T(8,128)(2,1)S(1)} %get-tuple-element.98), channel_id=1, source_target_pairs={{0,6},{1,7},{2,0},{3,1},{4,2},{5,3},{6,4},{7,5},{8,14},{9,15},{10,... | collective-permute-start | bytes 1572872 | tf_op jit(solution)/shard_map/ppermute | solution.py:407
  186.7 2.9 %project_out_1.1 = bf16[1,1024,256]{2,1,0:T(8,128)(2,1)S(1)} custom-call(s32[3]{0:T(128)S(1)} %pad_add_fusion.1.place_ref, f32[1024,8]{1,0:T(8,128)S(1)} %broadcast_multiply_fusion.gates_ref, bf16[8,1024,256]{2,1,0:T(8,128)(2,1)S(1)} %attention.1.lhs_ref, bf16[2048,256]{1,0:T(8,128)(2,1)S(1)} %pad_maximum_fusion.refs_0_, ...), custom_call_target="tpu_custom_call" | custom-call | flops 2529999872 | bytes 1048576 | tf_op jit(solution)/shard_map/project_out_1/pallas_call | solution.py:331
  189.6 7.8 %collective-permute-done.30 = bf16[1024,256]{1,0:T(8,128)(2,1)S(1)} collective-permute-done((bf16[1024,256]{1,0:T(8,128)(2,1)S(1)}, bf16[1024,256]{1,0:T(8,128)(2,1)S(1)}, u32[]{:S(2)}, u32[]{:S(2)}) %collective-permute-start.30) | collective-permute-done | bytes 524320 | tf_op jit(solution)/shard_map/ppermute | solution.py:407
  197.4 3.4 %collective-permute-done.29 = bf16[1024,256]{1,0:T(8,128)(2,1)S(1)} collective-permute-done((bf16[1024,256]{1,0:T(8,128)(2,1)S(1)}, bf16[1024,256]{1,0:T(8,128)(2,1)S(1)}, u32[]{:S(2)}, u32[]{:S(2)}) %collective-permute-start.29) | collective-permute-done | bytes 524320 | tf_op jit(solution)/shard_map/ppermute | solution.py:407
  200.8 1.1 fusion.2
  (116 shorter events, 7.7 us)
Async XLA Ops:
  0.0 14.5 %copy-start = (bf16[4,2048,16]{1,2,0:T(8,128)(2,1)S(1)}, bf16[4,2048,16]{1,2,0:T(8,128)(2,1)}, u32[]{:S(2)}) copy-start(bf16[4,2048,16]{1,2,0:T(8,128)(2,1)} %param.25) | copy-start | bytes 786436
  0.0 2.1 %copy-start.12 = (bf16[128,8,256]{2,1,0:T(8,128)(2,1)S(1)}, bf16[128,8,256]{2,1,0:T(8,128)(2,1)}, u32[]{:S(2)}) copy-start(bf16[128,8,256]{2,1,0:T(8,128)(2,1)} %param.23) | copy-start | bytes 1572868
  2.1 2.4 %copy-start.8 = (bf16[64,8,2,128]{3,1,2,0:T(8,128)(2,1)}, bf16[64,8,2,128]{3,1,2,0:T(8,128)(2,1)S(1)}, u32[]{:S(2)}) copy-start(bf16[64,8,2,128]{3,1,2,0:T(8,128)(2,1)S(1)} %copy.43) | copy-start | bytes 786436
  2.1 1.1 copy-start.15
  2.3 1.6 copy-start.17
  4.5 9.2 %copy-start.21 = (s32[64]{0:T(128)S(1)}, s32[64]{0:T(128)}, u32[]{:S(2)}) copy-start(s32[64]{0:T(128)} %param.18) | copy-start | bytes 772
  5.4 23.8 %collective-permute-start.1 = (bf16[1216,256]{1,0:T(8,128)(2,1)}, bf16[1216,256]{1,0:T(8,128)(2,1)S(1)}, u32[]{:S(2)}, u32[]{:S(2)}) collective-permute-start(bf16[1216,256]{1,0:T(8,128)(2,1)} %pad_maximum_fusion.2), channel_id=1, source_target_pairs={{0,96},{8,104},{16,112},{24,120},{32,0},{40,8},{48,16},{56,24},{64... | collective-permute-start | bytes 1867784 | tf_op jit(solution)/shard_map/ppermute | solution.py:39
  6.2 23.0 %collective-permute-start = (bf16[1216,256]{1,0:T(8,128)(2,1)}, bf16[1216,256]{1,0:T(8,128)(2,1)S(1)}, u32[]{:S(2)}, u32[]{:S(2)}) collective-permute-start(bf16[1216,256]{1,0:T(8,128)(2,1)} %pad_maximum_fusion.2), channel_id=1, source_target_pairs={{0,32},{8,40},{16,48},{24,56},{32,64},{40,72},{48,80},{56,88},{64,... | collective-permute-start | bytes 1867784 | tf_op jit(solution)/shard_map/ppermute | solution.py:39
  8.7 1.0 copy-start.10
  9.7 32.9 %collective-permute-start.3 = (bf16[1216,256]{1,0:T(8,128)(2,1)}, bf16[1216,256]{1,0:T(8,128)(2,1)S(1)}, u32[]{:S(2)}, u32[]{:S(2)}) collective-permute-start(bf16[1216,256]{1,0:T(8,128)(2,1)} %pad_maximum_fusion.3), channel_id=1, source_target_pairs={{0,24},{8,0},{16,8},{24,16},{32,56},{40,32},{48,40},{56,48},{64,88... | collective-permute-start | bytes 1867784 | tf_op jit(solution)/shard_map/ppermute | solution.py:39
  13.7 33.1 %collective-permute-start.2 = (bf16[1216,256]{1,0:T(8,128)(2,1)}, bf16[1216,256]{1,0:T(8,128)(2,1)S(1)}, u32[]{:S(2)}, u32[]{:S(2)}) collective-permute-start(bf16[1216,256]{1,0:T(8,128)(2,1)} %pad_maximum_fusion.3), channel_id=1, source_target_pairs={{0,8},{8,16},{16,24},{24,0},{32,40},{40,48},{48,56},{56,32},{64,72... | collective-permute-start | bytes 1867784 | tf_op jit(solution)/shard_map/ppermute | solution.py:39
  17.4 7.5 %copy-start.22 = (s32[64]{0:T(128)S(1)}, s32[64]{0:T(128)}, u32[]{:S(2)}) copy-start(s32[64]{0:T(128)} %param.20) | copy-start | bytes 772
  17.4 7.5 %copy-start.23 = (s32[4]{0:T(128)S(1)}, s32[4]{0:T(128)}, u32[]{:S(2)}) copy-start(s32[4]{0:T(128)} %param.19) | copy-start | bytes 52
  17.4 7.7 %copy-start.19 = (s32[4]{0:T(128)S(1)}, s32[4]{0:T(128)}, u32[]{:S(2)}) copy-start(s32[4]{0:T(128)} %param.17) | copy-start | bytes 52
  17.4 8.4 %copy-start.18 = (bf16[2048,8]{0,1:T(8,128)(2,1)S(1)}, bf16[2048,8]{0,1:T(8,128)(2,1)}, u32[]{:S(2)}) copy-start(bf16[2048,8]{0,1:T(8,128)(2,1)} %param.21) | copy-start | bytes 98308
  17.5 59.1 %all-to-all-start = ((bf16[16,96,512]{2,1,0:T(8,128)(2,1)}), bf16[16,96,512]{2,1,0:T(8,128)(2,1)}, u32[]{:S(2)}, u32[]{:S(2)}) async-start(bf16[16,96,512]{2,1,0:T(8,128)(2,1)} %pack.1), calls=%async_computation | async-start | bytes 3145728 | tf_op jit(solution)/shard_map/all_to_all | solution.py:471
  29.2 45.5 %copy-start.2 = (bf16[1216,256]{1,0:T(8,128)(2,1)}, bf16[1216,256]{1,0:T(8,128)(2,1)S(1)}, u32[]{:S(2)}) copy-start(bf16[1216,256]{1,0:T(8,128)(2,1)S(1)} %collective-permute-done.1.refs_1_) | copy-start | bytes 1867780
  29.2 45.5 %copy-start.3 = (bf16[1216,256]{1,0:T(8,128)(2,1)}, bf16[1216,256]{1,0:T(8,128)(2,1)S(1)}, u32[]{:S(2)}) copy-start(bf16[1216,256]{1,0:T(8,128)(2,1)S(1)} %collective-permute-done.refs_0_) | copy-start | bytes 1867780
  42.6 32.2 %copy-start.4 = (bf16[1216,256]{1,0:T(8,128)(2,1)}, bf16[1216,256]{1,0:T(8,128)(2,1)S(1)}, u32[]{:S(2)}) copy-start(bf16[1216,256]{1,0:T(8,128)(2,1)S(1)} %collective-permute-done.3.refs_3_) | copy-start | bytes 1867780
  46.8 1.7 copy-start.5
  48.5 8.2 %collective-permute-start.8 = (bf16[608,256]{1,0:T(8,128)(2,1)S(1)}, bf16[608,256]{1,0:T(8,128)(2,1)S(1)}, u32[]{:S(2)}, u32[]{:S(2)}) collective-permute-start(bf16[608,256]{1,0:T(8,128)(2,1)S(1)} %get-tuple-element.59), channel_id=1, source_target_pairs={{0,8},{8,16},{16,24},{24,0},{32,40},{40,48},{48,56},{56,32},{64,72... | collective-permute-start | bytes 933896 | tf_op jit(solution)/shard_map/ppermute | solution.py:39
  48.6 22.4 %copy-start.20 = (s32[4]{0:T(128)S(1)}, s32[4]{0:T(128)}, u32[]{:S(2)}) copy-start(s32[4]{0:T(128)} %param.16) | copy-start | bytes 52
  48.6 22.5 %copy-start.16 = (s32[1024,2]{0,1:T(2,128)S(1)}, s32[1024,2]{0,1:T(2,128)}, u32[]{:S(2)}) copy-start(s32[1024,2]{0,1:T(2,128)} %param.15) | copy-start | bytes 24580
  49.4 16.5 %collective-permute-start.4 = (bf16[608,256]{1,0:T(8,128)(2,1)S(1)}, bf16[608,256]{1,0:T(8,128)(2,1)S(1)}, u32[]{:S(2)}, u32[]{:S(2)}) collective-permute-start(bf16[608,256]{1,0:T(8,128)(2,1)S(1)} %get-tuple-element.57), channel_id=1, source_target_pairs={{0,32},{8,40},{16,48},{24,56},{32,64},{40,72},{48,80},{56,88},{64,... | collective-permute-start | bytes 933896 | tf_op jit(solution)/shard_map/ppermute | solution.py:39
  49.4 17.2 %collective-permute-start.5 = (bf16[608,256]{1,0:T(8,128)(2,1)S(1)}, bf16[608,256]{1,0:T(8,128)(2,1)S(1)}, u32[]{:S(2)}, u32[]{:S(2)}) collective-permute-start(bf16[608,256]{1,0:T(8,128)(2,1)S(1)} %get-tuple-element.58), channel_id=1, source_target_pairs={{0,96},{8,104},{16,112},{24,120},{32,0},{40,8},{48,16},{56,24},{64... | collective-permute-start | bytes 933896 | tf_op jit(solution)/shard_map/ppermute | solution.py:39
  51.4 10.6 %collective-permute-start.9 = (bf16[608,256]{1,0:T(8,128)(2,1)S(1)}, bf16[608,256]{1,0:T(8,128)(2,1)S(1)}, u32[]{:S(2)}, u32[]{:S(2)}) collective-permute-start(bf16[608,256]{1,0:T(8,128)(2,1)S(1)} %get-tuple-element.60), channel_id=1, source_target_pairs={{0,24},{8,0},{16,8},{24,16},{32,56},{40,32},{48,40},{56,48},{64,88... | collective-permute-start | bytes 933896 | tf_op jit(solution)/shard_map/ppermute | solution.py:39
  62.0 11.5 %copy-start.13 = (bf16[608,256]{1,0:T(8,128)(2,1)}, bf16[608,256]{1,0:T(8,128)(2,1)S(1)}, u32[]{:S(2)}) copy-start(bf16[608,256]{1,0:T(8,128)(2,1)S(1)} %collective-permute-done.9) | copy-start | bytes 933892
  62.6 29.7 %collective-permute-start.11 = (bf16[2816,256]{1,0:T(8,128)(2,1)}, bf16[2816,256]{1,0:T(8,128)(2,1)}, u32[]{:S(2)}, u32[]{:S(2)}) collective-permute-start(bf16[2816,256]{1,0:T(8,128)(2,1)} %slice_dynamic-update-slice_fusion.4.refs_3_), channel_id=1, source_target_pairs={{0,96},{8,104},{16,112},{24,120},{32,0},{40,8},{48,16},{56,24},{64... | collective-permute-start | bytes 4325384 | tf_op jit(solution)/shard_map/ppermute | solution.py:39
  62.9 29.4 %collective-permute-start.10 = (bf16[2816,256]{1,0:T(8,128)(2,1)}, bf16[2816,256]{1,0:T(8,128)(2,1)}, u32[]{:S(2)}, u32[]{:S(2)}) collective-permute-start(bf16[2816,256]{1,0:T(8,128)(2,1)} %slice_dynamic-update-slice_fusion.4.refs_3_), channel_id=1, source_target_pairs={{0,32},{8,40},{16,48},{24,56},{32,64},{40,72},{48,80},{56,88},{64,... | collective-permute-start | bytes 4325384 | tf_op jit(solution)/shard_map/ppermute | solution.py:39
  66.6 8.1 %copy-start.11 = (bf16[608,256]{1,0:T(8,128)(2,1)}, bf16[608,256]{1,0:T(8,128)(2,1)S(1)}, u32[]{:S(2)}) copy-start(bf16[608,256]{1,0:T(8,128)(2,1)S(1)} %collective-permute-done.5) | copy-start | bytes 933892
  67.3 25.1 %collective-permute-start.7 = (bf16[2816,256]{1,0:T(8,128)(2,1)}, bf16[2816,256]{1,0:T(8,128)(2,1)}, u32[]{:S(2)}, u32[]{:S(2)}) collective-permute-start(bf16[2816,256]{1,0:T(8,128)(2,1)} %slice_dynamic-update-slice_fusion.5.refs_0_), channel_id=1, source_target_pairs={{0,24},{8,0},{16,8},{24,16},{32,56},{40,32},{48,40},{56,48},{64,88... | collective-permute-start | bytes 4325384 | tf_op jit(solution)/shard_map/ppermute | solution.py:39
  71.0 21.4 %collective-permute-start.6 = (bf16[2816,256]{1,0:T(8,128)(2,1)}, bf16[2816,256]{1,0:T(8,128)(2,1)}, u32[]{:S(2)}, u32[]{:S(2)}) collective-permute-start(bf16[2816,256]{1,0:T(8,128)(2,1)} %slice_dynamic-update-slice_fusion.5.refs_0_), channel_id=1, source_target_pairs={{0,8},{8,16},{16,24},{24,0},{32,40},{40,48},{48,56},{56,32},{64,72... | collective-permute-start | bytes 4325384 | tf_op jit(solution)/shard_map/ppermute | solution.py:39
  74.7 1.0 copy-start.14
  74.7 1.7 slice-start.1
  74.7 1.7 copy-start.9
  74.7 1.7 slice-start.4
  74.8 1.6 slice-start
  76.5 8.2 %slice-start.2 = ((bf16[1216,256]{1,0:T(8,128)(2,1)}), bf16[512,256]{1,0:T(8,128)(2,1)S(1)}, s32[]{:S(2)}) async-start(bf16[1216,256]{1,0:T(8,128)(2,1)} %copy-done.4), calls=%async_computation.4 | async-start | bytes 524288 | tf_op jit(solution)/shard_map/slice | solution.py:496
  76.5 8.2 %slice-start.3 = ((bf16[1216,256]{1,0:T(8,128)(2,1)}), bf16[512,256]{1,0:T(8,128)(2,1)S(1)}, s32[]{:S(2)}) async-start(bf16[1216,256]{1,0:T(8,128)(2,1)} %copy-done.5), calls=%async_computation.5 | async-start | bytes 524288 | tf_op jit(solution)/shard_map/slice | solution.py:495
  80.2 12.1 %all-to-all-start.1 = ((bf16[8,4,16,256]{3,2,1,0:T(8,128)(2,1)}), bf16[8,4,16,256]{3,2,1,0:T(8,128)(2,1)}, u32[]{:S(2)}, u32[]{:S(2)}) async-start(bf16[8,4,16,256]{3,2,1,0:T(8,128)(2,1)} %broadcast_in_dim.5), calls=%async_computation.1 | async-start | bytes 524288 | tf_op jit(solution)/shard_map/all_to_all | solution.py:513
  85.8 15.0 %copy-start.6 = (s32[1024,2]{1,0:T(8,128)S(1)}, s32[1024,2]{1,0:T(8,128)}, u32[]{:S(2)}) copy-start(s32[1024,2]{1,0:T(8,128)} %copy.34.routes_ref) | copy-start | bytes 24580
  85.8 15.0 %copy-start.7 = (s32[13]{0:T(128)S(1)}, s32[13]{0:T(128)}, u32[]{:S(2)}) copy-start(s32[13]{0:T(128)} %pad_add_fusion.info_ref) | copy-start | bytes 160
  92.3 8.5 %copy-start.1 = (bf16[1024,2048]{1,0:T(8,128)(2,1)S(1)}, bf16[1024,2048]{1,0:T(8,128)(2,1)}, u32[]{:S(2)}) copy-start(bf16[1024,2048]{1,0:T(8,128)(2,1)} %x_ref.3) | copy-start | bytes 12582916
  95.4 19.9 %collective-permute-start.12 = (bf16[1408,256]{1,0:T(8,128)(2,1)S(1)}, bf16[1408,256]{1,0:T(8,128)(2,1)S(1)}, u32[]{:S(2)}, u32[]{:S(2)}) collective-permute-start(bf16[1408,256]{1,0:T(8,128)(2,1)S(1)} %get-tuple-element.67), channel_id=1, source_target_pairs={{0,8},{8,16},{16,24},{24,0},{32,40},{40,48},{48,56},{56,32},{64,72... | collective-permute-start | bytes 2162696 | tf_op jit(solution)/shard_map/ppermute | solution.py:39
  95.5 19.8 %collective-permute-start.13 = (bf16[1408,256]{1,0:T(8,128)(2,1)S(1)}, bf16[1408,256]{1,0:T(8,128)(2,1)S(1)}, u32[]{:S(2)}, u32[]{:S(2)}) collective-permute-start(bf16[1408,256]{1,0:T(8,128)(2,1)S(1)} %get-tuple-element.68), channel_id=1, source_target_pairs={{0,24},{8,0},{16,8},{24,16},{32,56},{40,32},{48,40},{56,48},{64,88... | collective-permute-start | bytes 2162696 | tf_op jit(solution)/shard_map/ppermute | solution.py:39
  98.8 17.2 %collective-permute-start.14 = (bf16[1408,256]{1,0:T(8,128)(2,1)S(1)}, bf16[1408,256]{1,0:T(8,128)(2,1)S(1)}, u32[]{:S(2)}, u32[]{:S(2)}) collective-permute-start(bf16[1408,256]{1,0:T(8,128)(2,1)S(1)} %get-tuple-element.69), channel_id=1, source_target_pairs={{0,32},{8,40},{16,48},{24,56},{32,64},{40,72},{48,80},{56,88},{64,... | collective-permute-start | bytes 2162696 | tf_op jit(solution)/shard_map/ppermute | solution.py:39
  99.1 18.2 %collective-permute-start.15 = (bf16[1408,256]{1,0:T(8,128)(2,1)S(1)}, bf16[1408,256]{1,0:T(8,128)(2,1)S(1)}, u32[]{:S(2)}, u32[]{:S(2)}) collective-permute-start(bf16[1408,256]{1,0:T(8,128)(2,1)S(1)} %get-tuple-element.70), channel_id=1, source_target_pairs={{0,96},{8,104},{16,112},{24,120},{32,0},{40,8},{48,16},{56,24},{64... | collective-permute-start | bytes 2162696 | tf_op jit(solution)/shard_map/ppermute | solution.py:39
  117.2 24.6 %collective-permute-start.17 = (bf16[2048,256]{1,0:T(8,128)(2,1)S(1)}, bf16[2048,256]{1,0:T(8,128)(2,1)S(1)}, u32[]{:S(2)}, u32[]{:S(2)}) collective-permute-start(bf16[2048,256]{1,0:T(8,128)(2,1)S(1)} %pad_maximum_fusion.refs_0_), channel_id=1, source_target_pairs={{0,24},{8,0},{16,8},{24,16},{32,56},{40,32},{48,40},{56,48},{64,88... | collective-permute-start | bytes 3145736 | tf_op jit(solution)/shard_map/ppermute | solution.py:39
  118.9 23.7 %collective-permute-start.16 = (bf16[2048,256]{1,0:T(8,128)(2,1)S(1)}, bf16[2048,256]{1,0:T(8,128)(2,1)S(1)}, u32[]{:S(2)}, u32[]{:S(2)}) collective-permute-start(bf16[2048,256]{1,0:T(8,128)(2,1)S(1)} %pad_maximum_fusion.refs_0_), channel_id=1, source_target_pairs={{0,8},{8,16},{16,24},{24,0},{32,40},{40,48},{48,56},{56,32},{64,72... | collective-permute-start | bytes 3145736 | tf_op jit(solution)/shard_map/ppermute | solution.py:39
  119.3 23.7 %collective-permute-start.19 = (bf16[2048,256]{1,0:T(8,128)(2,1)S(1)}, bf16[2048,256]{1,0:T(8,128)(2,1)S(1)}, u32[]{:S(2)}, u32[]{:S(2)}) collective-permute-start(bf16[2048,256]{1,0:T(8,128)(2,1)S(1)} %pad_maximum_fusion.1.refs_5_), channel_id=1, source_target_pairs={{0,96},{8,104},{16,112},{24,120},{32,0},{40,8},{48,16},{56,24},{64... | collective-permute-start | bytes 3145736 | tf_op jit(solution)/shard_map/ppermute | solution.py:39
  119.8 23.2 %collective-permute-start.18 = (bf16[2048,256]{1,0:T(8,128)(2,1)S(1)}, bf16[2048,256]{1,0:T(8,128)(2,1)S(1)}, u32[]{:S(2)}, u32[]{:S(2)}) collective-permute-start(bf16[2048,256]{1,0:T(8,128)(2,1)S(1)} %pad_maximum_fusion.1.refs_5_), channel_id=1, source_target_pairs={{0,32},{8,40},{16,48},{24,56},{32,64},{40,72},{48,80},{56,88},{64,... | collective-permute-start | bytes 3145736 | tf_op jit(solution)/shard_map/ppermute | solution.py:39
  143.1 11.6 %collective-permute-start.20 = (bf16[1024,256]{1,0:T(8,128)(2,1)S(1)}, bf16[1024,256]{1,0:T(8,128)(2,1)S(1)}, u32[]{:S(2)}, u32[]{:S(2)}) collective-permute-start(bf16[1024,256]{1,0:T(8,128)(2,1)S(1)} %get-tuple-element.85), channel_id=1, source_target_pairs={{0,8},{8,16},{16,24},{24,0},{32,40},{40,48},{48,56},{56,32},{64,72... | collective-permute-start | bytes 1572872 | tf_op jit(solution)/shard_map/ppermute | solution.py:39
  143.5 11.3 %collective-permute-start.21 = (bf16[1024,256]{1,0:T(8,128)(2,1)S(1)}, bf16[1024,256]{1,0:T(8,128)(2,1)S(1)}, u32[]{:S(2)}, u32[]{:S(2)}) collective-permute-start(bf16[1024,256]{1,0:T(8,128)(2,1)S(1)} %get-tuple-element.86), channel_id=1, source_target_pairs={{0,24},{8,0},{16,8},{24,16},{32,56},{40,32},{48,40},{56,48},{64,88... | collective-permute-start | bytes 1572872 | tf_op jit(solution)/shard_map/ppermute | solution.py:39
  146.4 10.0 %collective-permute-start.22 = (bf16[1024,256]{1,0:T(8,128)(2,1)S(1)}, bf16[1024,256]{1,0:T(8,128)(2,1)S(1)}, u32[]{:S(2)}, u32[]{:S(2)}) collective-permute-start(bf16[1024,256]{1,0:T(8,128)(2,1)S(1)} %get-tuple-element.87), channel_id=1, source_target_pairs={{0,32},{8,40},{16,48},{24,56},{32,64},{40,72},{48,80},{56,88},{64,... | collective-permute-start | bytes 1572872 | tf_op jit(solution)/shard_map/ppermute | solution.py:39
  149.4 10.4 %collective-permute-start.23 = (bf16[1024,256]{1,0:T(8,128)(2,1)S(1)}, bf16[1024,256]{1,0:T(8,128)(2,1)S(1)}, u32[]{:S(2)}, u32[]{:S(2)}) collective-permute-start(bf16[1024,256]{1,0:T(8,128)(2,1)S(1)} %get-tuple-element.88), channel_id=1, source_target_pairs={{0,96},{8,104},{16,112},{24,120},{32,0},{40,8},{48,16},{56,24},{64... | collective-permute-start | bytes 1572872 | tf_op jit(solution)/shard_map/ppermute | solution.py:39
  167.5 5.8 %collective-permute-start.24 = (bf16[1024,256]{1,0:T(8,128)(2,1)S(1)}, bf16[1024,256]{1,0:T(8,128)(2,1)S(1)}, u32[]{:S(2)}, u32[]{:S(2)}) collective-permute-start(bf16[1024,256]{1,0:T(8,128)(2,1)S(1)} %get-tuple-element.91), channel_id=1, source_target_pairs={{0,1},{1,0},{2,3},{3,2},{4,5},{5,4},{6,7},{7,6},{8,9},{9,8},{10,11... | collective-permute-start | bytes 1572872 | tf_op jit(solution)/shard_map/ppermute | solution.py:406
  172.7 10.7 %collective-permute-start.25 = (bf16[2,1024,256]{2,1,0:T(8,128)(2,1)S(1)}, bf16[2,1024,256]{2,1,0:T(8,128)(2,1)S(1)}, u32[]{:S(2)}, u32[]{:S(2)}) collective-permute-start(bf16[2,1024,256]{2,1,0:T(8,128)(2,1)S(1)} %project_out_2.2), channel_id=1, source_target_pairs={{0,1},{1,0},{2,3},{3,2},{4,5},{5,4},{6,7},{7,6},{8,9},{9,8},{10,11... | collective-permute-start | bytes 3145736 | tf_op jit(solution)/shard_map/ppermute | solution.py:406
  173.2 16.4 %collective-permute-start.28 = (bf16[1024,256]{1,0:T(8,128)(2,1)S(1)}, bf16[1024,256]{1,0:T(8,128)(2,1)S(1)}, u32[]{:S(2)}, u32[]{:S(2)}) collective-permute-start(bf16[1024,256]{1,0:T(8,128)(2,1)S(1)} %get-tuple-element.97), channel_id=1, source_target_pairs={{0,1},{1,0},{2,3},{3,2},{4,5},{5,4},{6,7},{7,6},{8,9},{9,8},{10,11... | collective-permute-start | bytes 1572872 | tf_op jit(solution)/shard_map/ppermute | solution.py:406
  173.4 9.9 %collective-permute-start.26 = (bf16[512,256]{1,0:T(8,128)(2,1)S(1)}, bf16[512,256]{1,0:T(8,128)(2,1)S(1)}, u32[]{:S(2)}, u32[]{:S(2)}) collective-permute-start(bf16[512,256]{1,0:T(8,128)(2,1)S(1)} %get-tuple-element.92), channel_id=1, source_target_pairs={{0,2},{1,3},{2,4},{3,5},{4,6},{5,7},{6,0},{7,1},{8,10},{9,11},{10,... | collective-permute-start | bytes 786440 | tf_op jit(solution)/shard_map/ppermute | solution.py:407
  174.6 8.4 %collective-permute-start.27 = (bf16[512,256]{1,0:T(8,128)(2,1)S(1)}, bf16[512,256]{1,0:T(8,128)(2,1)S(1)}, u32[]{:S(2)}, u32[]{:S(2)}) collective-permute-start(bf16[512,256]{1,0:T(8,128)(2,1)S(1)} %get-tuple-element.94), channel_id=1, source_target_pairs={{0,6},{1,7},{2,0},{3,1},{4,2},{5,3},{6,4},{7,5},{8,14},{9,15},{10,... | collective-permute-start | bytes 786440 | tf_op jit(solution)/shard_map/ppermute | solution.py:407
  183.7 13.7 %collective-permute-start.30 = (bf16[1024,256]{1,0:T(8,128)(2,1)S(1)}, bf16[1024,256]{1,0:T(8,128)(2,1)S(1)}, u32[]{:S(2)}, u32[]{:S(2)}) collective-permute-start(bf16[1024,256]{1,0:T(8,128)(2,1)S(1)} %get-tuple-element.98), channel_id=1, source_target_pairs={{0,6},{1,7},{2,0},{3,1},{4,2},{5,3},{6,4},{7,5},{8,14},{9,15},{10,... | collective-permute-start | bytes 1572872 | tf_op jit(solution)/shard_map/ppermute | solution.py:407
  186.7 14.1 %collective-permute-start.29 = (bf16[1024,256]{1,0:T(8,128)(2,1)S(1)}, bf16[1024,256]{1,0:T(8,128)(2,1)S(1)}, u32[]{:S(2)}, u32[]{:S(2)}) collective-permute-start(bf16[1024,256]{1,0:T(8,128)(2,1)S(1)} %get-tuple-element.95), channel_id=1, source_target_pairs={{0,2},{1,3},{2,4},{3,5},{4,6},{5,7},{6,0},{7,1},{8,10},{9,11},{10,... | collective-permute-start | bytes 1572872 | tf_op jit(solution)/shard_map/ppermute | solution.py:407

commit v7 on v6

--- a/solution.py
+++ b/solution.py
@@ -357,6 +357,22 @@
 
 def forward_kernel(*refs):
     half = refs[4].shape[0]
+    if half > 1024:
+
+        def together(sem):
+            copies = [
+                pltpu.make_async_copy(
+                    refs[i].at[pl.ds(i % 2 * half, half), :], refs[4 + i], sem.at[i]
+                )
+                for i in range(4)
+            ]
+            for one in copies:
+                one.start()
+            for one in copies:
+                one.wait()
+
+        pl.run_scoped(together, pltpu.SemaphoreType.DMA((4,)))
+        return
     steps = 8 if half % 128 == 0 else 2
     chunk = half // steps
 

time: 203 us -> 204 us (level)
  no operation moved by 1% of the time
where the time goes in v7:
time: 204 us; the launch traced here: 203 us
  Pallas kernels  63.5 us (31%)
  waiting for transfers between devices  56.3 us (28%)
  starting transfers between devices  55.3 us (27%)
  local copies, waits for them, and re-layouts  16.7 us (8%)
  other arithmetic  7.1 us (3%)
  matrix products  3.37 us (2%)
    ppermute x24, waiting for transfers between devices, send(): lax.ppermute(value, 'req', torus(step, 0) if along == 0 else torus(0, step))  37 us
    ppermute x24, starting transfers between devices, send(): lax.ppermute(value, 'req', torus(step, 0) if along == 0 else torus(0, step))  36.4 us
    pallas_call x4, Pallas kernels, project_out(): pl.pallas_call(functools.partial(project_out_kernel, blocks), out_shape=s...  20.6 us
    pallas_call x1, Pallas kernels, attention(): pl.pallas_call(attend_kernel, out_shape=jax.ShapeDtypeStruct((NE, 1024, 2...  19.3 us
    pallas_call x1, Pallas kernels, project_early(): pl.pallas_call(early_kernel, out_shape=(jax.ShapeDtypeStruct((4, 2, 16, 2...  14.5 us
    ppermute x4, waiting for transfers between devices, exchange(): lax.ppermute(value, 'exp', [(i, (i + 2 * step) % 8) for i in range(8)])  12.7 us
    unnamed x61, local copies, waits for them, and re-layouts  8.86 us
    all_to_all x1, starting transfers between devices, body(): received = lax.all_to_all(outgoing, 'req', 0, 0, tiled=True)  7.34 us
  transfers between devices with their start and end apart: 33, of which 16 were waited for; matrix products, arithmetic and copies ran while one was open for 10% of the time, Pallas kernels for 26%

profile of v7, /device:TPU:6, one launch (start us, length us, event | category | flops | bytes accessed | tf_op | source)
XLA Modules:
  0.0 202.8 jit_solution(3744046257457341669)
XLA Ops:
  0.0 1.7 copy.41
  2.4 0.8 constant_dynamic-update-slice_fusion.3
  3.2 0.7 constant_dynamic-update-slice_fusion.6
  4.5 0.9 pad_maximum_fusion.2
  5.4 0.8 collective-permute-start.1
  6.2 2.4 %collective-permute-start = (bf16[1216,256]{1,0:T(8,128)(2,1)}, bf16[1216,256]{1,0:T(8,128)(2,1)S(1)}, u32[]{:S(2)}, u32[]{:S(2)}) collective-permute-start(bf16[1216,256]{1,0:T(8,128)(2,1)} %pad_maximum_fusion.2), channel_id=1, source_target_pairs={{0,32},{8,40},{16,48},{24,56},{32,64},{40,72},{48,80},{56,88},{64,... | collective-permute-start | bytes 1867784 | tf_op jit(solution)/shard_map/ppermute | solution.py:39
  8.7 1.0 pad_maximum_fusion.3
  9.7 4.0 %collective-permute-start.3 = (bf16[1216,256]{1,0:T(8,128)(2,1)}, bf16[1216,256]{1,0:T(8,128)(2,1)S(1)}, u32[]{:S(2)}, u32[]{:S(2)}) collective-permute-start(bf16[1216,256]{1,0:T(8,128)(2,1)} %pad_maximum_fusion.3), channel_id=1, source_target_pairs={{0,24},{8,0},{16,8},{24,16},{32,56},{40,32},{48,40},{56,48},{64,88... | collective-permute-start | bytes 1867784 | tf_op jit(solution)/shard_map/ppermute | solution.py:39
  13.8 0.7 select_reduce_fusion.2.index_ref
  15.1 2.3 %pack.1 = bf16[16,96,512]{2,1,0:T(8,128)(2,1)} custom-call(s32[16]{0:T(128)} %select_reduce_fusion.2.index_ref, bf16[4,64,512]{2,1,0:T(8,128)(2,1)} %store_ref.1, bf16[64,256]{1,0:T(8,128)(2,1)} %bitcast.46), custom_call_target="tpu_custom_call" | custom-call | flops 3449999872 | bytes 1048576 | tf_op jit(solution)/shard_map/pack/pallas_call | solution.py:74
  17.5 7.3 %all-to-all-start = ((bf16[16,96,512]{2,1,0:T(8,128)(2,1)}), bf16[16,96,512]{2,1,0:T(8,128)(2,1)}, u32[]{:S(2)}, u32[]{:S(2)}) async-start(bf16[16,96,512]{2,1,0:T(8,128)(2,1)} %pack.1), calls=%async_computation | async-start | bytes 3145728 | tf_op jit(solution)/shard_map/all_to_all | solution.py:487
  25.1 0.7 pad_add_fusion.info_ref
  25.8 3.4 %fusion.5 = f32[1024,8]{0,1:T(8,128)S(1)} fusion(bf16[1024,2048]{1,0:T(8,128)(2,1)} %x_ref.3, bf16[2048,8]{0,1:T(8,128)(2,1)S(1)} %copy-done.18), kind=kOutput, calls=%fused_computation.41 | convolution fusion | flops 33554432 | bytes 4259840 | tf_op jit(solution)/shard_map/dot_general | solution.py:519
  29.2 13.4 %collective-permute-done.3.refs_3_ = bf16[1216,256]{1,0:T(8,128)(2,1)S(1)} collective-permute-done((bf16[1216,256]{1,0:T(8,128)(2,1)}, bf16[1216,256]{1,0:T(8,128)(2,1)S(1)}, u32[]{:S(2)}, u32[]{:S(2)}) %collective-permute-start.3) | collective-permute-done | bytes 622624 | tf_op jit(solution)/shard_map/ppermute | solution.py:39
  42.6 4.3 %collective-permute-done.2.refs_2_ = bf16[1216,256]{1,0:T(8,128)(2,1)S(1)} collective-permute-done((bf16[1216,256]{1,0:T(8,128)(2,1)}, bf16[1216,256]{1,0:T(8,128)(2,1)S(1)}, u32[]{:S(2)}, u32[]{:S(2)}) %collective-permute-start.2) | collective-permute-done | bytes 622624 | tf_op jit(solution)/shard_map/ppermute | solution.py:39
  46.8 0.8 slice_dynamic-update-slice_fusion.3
  47.7 0.8 slice_dynamic-update-slice_fusion.2
  48.6 0.8 slice_dynamic-update-slice_fusion.1
  49.4 2.0 collective-permute-start.5
  51.4 3.2 %collective-permute-start.9 = (bf16[608,256]{1,0:T(8,128)(2,1)S(1)}, bf16[608,256]{1,0:T(8,128)(2,1)S(1)}, u32[]{:S(2)}, u32[]{:S(2)}) collective-permute-start(bf16[608,256]{1,0:T(8,128)(2,1)S(1)} %get-tuple-element.60), channel_id=1, source_target_pairs={{0,24},{8,0},{16,8},{24,16},{32,56},{40,32},{48,40},{56,48},{64,88... | collective-permute-start | bytes 933896 | tf_op jit(solution)/shard_map/ppermute | solution.py:39
  54.6 0.8 slice_dynamic-update-slice_fusion
  55.4 1.3 collective-permute-done.8
  56.7 0.7 constant_dynamic-update-slice_fusion.4
  57.4 4.6 %collective-permute-done.9 = bf16[608,256]{1,0:T(8,128)(2,1)S(1)} collective-permute-done((bf16[608,256]{1,0:T(8,128)(2,1)S(1)}, bf16[608,256]{1,0:T(8,128)(2,1)S(1)}, u32[]{:S(2)}, u32[]{:S(2)}) %collective-permute-start.9) | collective-permute-done | bytes 311328 | tf_op jit(solution)/shard_map/ppermute | solution.py:39
  62.9 2.9 %collective-permute-start.10 = (bf16[2816,256]{1,0:T(8,128)(2,1)}, bf16[2816,256]{1,0:T(8,128)(2,1)}, u32[]{:S(2)}, u32[]{:S(2)}) collective-permute-start(bf16[2816,256]{1,0:T(8,128)(2,1)} %slice_dynamic-update-slice_fusion.4.refs_3_), channel_id=1, source_target_pairs={{0,32},{8,40},{16,48},{24,56},{32,64},{40,72},{48,80},{56,88},{64,... | collective-permute-start | bytes 4325384 | tf_op jit(solution)/shard_map/ppermute | solution.py:39
  65.9 0.7 constant_dynamic-update-slice_fusion
  66.6 0.7 slice_dynamic-update-slice_fusion.5.refs_0_
  67.3 3.7 %collective-permute-start.7 = (bf16[2816,256]{1,0:T(8,128)(2,1)}, bf16[2816,256]{1,0:T(8,128)(2,1)}, u32[]{:S(2)}, u32[]{:S(2)}) collective-permute-start(bf16[2816,256]{1,0:T(8,128)(2,1)} %slice_dynamic-update-slice_fusion.5.refs_0_), channel_id=1, source_target_pairs={{0,24},{8,0},{16,8},{24,16},{32,56},{40,32},{48,40},{56,48},{64,88... | collective-permute-start | bytes 4325384 | tf_op jit(solution)/shard_map/ppermute | solution.py:39
  71.1 1.1 copy.34.routes_ref
  72.4 1.0 copy.32
  73.4 1.2 broadcast_multiply_fusion.gates_ref
  74.8 0.9 copy-done.14
  75.7 0.7 slice.109
  76.5 2.2 %pick_down.1 = bf16[4,16,256]{2,1,0:T(8,128)(2,1)} custom-call(s32[13]{0:T(128)} %pad_add_fusion.info_ref, bf16[16,96,512]{2,1,0:T(8,128)(2,1)} %all-to-all-done.recv_ref.recv_hbm), custom_call_target="tpu_custom_call" | custom-call | flops 2300000000 | bytes 1048576 | tf_op jit(solution)/shard_map/pick_down/pallas_call | solution.py:104
  78.7 1.5 broadcast_in_dim.5
  80.2 4.5 %all-to-all-start.1 = ((bf16[8,4,16,256]{3,2,1,0:T(8,128)(2,1)}), bf16[8,4,16,256]{3,2,1,0:T(8,128)(2,1)}, u32[]{:S(2)}, u32[]{:S(2)}) async-start(bf16[8,4,16,256]{3,2,1,0:T(8,128)(2,1)} %broadcast_in_dim.5), calls=%async_computation.1 | async-start | bytes 524288 | tf_op jit(solution)/shard_map/all_to_all | solution.py:529
  84.7 1.1 pad_maximum_fusion.1.refs_5_
  85.8 6.5 %all-to-all-done.1.down_ref = bf16[8,4,16,256]{3,2,1,0:T(8,128)(2,1)} async-done(((bf16[8,4,16,256]{3,2,1,0:T(8,128)(2,1)}), bf16[8,4,16,256]{3,2,1,0:T(8,128)(2,1)}, u32[]{:S(2)}, u32[]{:S(2)}) %all-to-all-start.1) | async-done | bytes 262176 | tf_op jit(solution)/shard_map/all_to_all | solution.py:529
  92.4 4.0 %forward_kernel.4 = (bf16[1408,256]{1,0:T(8,128)(2,1)S(1)}, bf16[1408,256]{1,0:T(8,128)(2,1)S(1)}, bf16[1408,256]{1,0:T(8,128)(2,1)S(1)}, bf16[1408,256]{1,0:T(8,128)(2,1)S(1)}) custom-call(bf16[2816,256]{1,0:T(8,128)(2,1)} %collective-permute-done.6.refs_0_.refs_1_, bf16[2816,256]{1,0:T(8,128)(2,1)} %collective-permute-done.7.refs_1_.refs_2_, ...), custom_call_target="tpu_custom_call" | custom-call | flops 2300000000 | bytes 1048576 | tf_op jit(solution)/shard_map/forward_kernel/pallas_call | solution.py:347
  96.4 3.3 %collective-permute-start.13 = (bf16[1408,256]{1,0:T(8,128)(2,1)S(1)}, bf16[1408,256]{1,0:T(8,128)(2,1)S(1)}, u32[]{:S(2)}, u32[]{:S(2)}) collective-permute-start(bf16[1408,256]{1,0:T(8,128)(2,1)S(1)} %get-tuple-element.68), channel_id=1, source_target_pairs={{0,24},{8,0},{16,8},{24,16},{32,56},{40,32},{48,40},{56,48},{64,88... | collective-permute-start | bytes 2162696 | tf_op jit(solution)/shard_map/ppermute | solution.py:39
  100.0 1.7 collective-permute-start.15
  101.8 14.5 %project_early.1 = (bf16[4,2,16,256]{3,2,1,0:T(8,128)(2,1)S(1)}, f32[4,4,256,256]{3,2,1,0:T(8,128)S(1)}) custom-call(s32[13]{0:T(128)S(1)} %copy-done.7, s32[1024,2]{1,0:T(8,128)S(1)} %copy-done.6, bf16[1024,2048]{1,0:T(8,128)(2,1)S(1)} %copy-done.1, bf16[2816,256]{1,0:T(8,128)(2,1)} %slice_dynamic-update-slice_fusion.5.refs_0_, ...), custom_call_target="tpu_custom_call" | custom-call | flops 17250000896 | bytes 1048576 | tf_op jit(solution)/shard_map/project_early/pallas_call | solution.py:179
  116.2 0.7 collective-permute-done.14.refs_2_
  117.0 1.2 collective-permute-done.15.refs_3_
  118.2 1.7 collective-permute-start.17
  120.7 2.7 %collective-permute-start.18 = (bf16[2048,256]{1,0:T(8,128)(2,1)S(1)}, bf16[2048,256]{1,0:T(8,128)(2,1)S(1)}, u32[]{:S(2)}, u32[]{:S(2)}) collective-permute-start(bf16[2048,256]{1,0:T(8,128)(2,1)S(1)} %pad_maximum_fusion.1.refs_5_), channel_id=1, source_target_pairs={{0,32},{8,40},{16,48},{24,56},{32,64},{40,72},{48,80},{56,88},{64,... | collective-permute-start | bytes 3145736 | tf_op jit(solution)/shard_map/ppermute | solution.py:39
  123.4 19.3 %attention.1.lhs_ref = bf16[8,1024,256]{2,1,0:T(8,128)(2,1)S(1)} custom-call(s32[13]{0:T(128)S(1)} %copy-done.7, s32[1024,2]{1,0:T(8,128)S(1)} %copy-done.6, bf16[8,4,16,256]{3,2,1,0:T(8,128)(2,1)} %all-to-all-done.1.down_ref, bf16[1024,2048]{1,0:T(8,128)(2,1)S(1)} %copy-done.1, bf16[4,2,16,256]{3,2,1,0:T(8,128)(2,1)S(1)} %get-tuple-element.74.up_ref, ...), custom_call_target="tpu_custom_call" | custom-call | flops 25300000768 | bytes 1048576 | tf_op jit(solution)/shard_map/attention/pallas_call | solution.py:258
  142.8 0.8 collective-permute-done.16.refs_0_.refs_1_
  144.4 3.0 %collective-permute-start.21 = (bf16[1024,256]{1,0:T(8,128)(2,1)S(1)}, bf16[1024,256]{1,0:T(8,128)(2,1)S(1)}, u32[]{:S(2)}, u32[]{:S(2)}) collective-permute-start(bf16[1024,256]{1,0:T(8,128)(2,1)S(1)} %get-tuple-element.86), channel_id=1, source_target_pairs={{0,24},{8,0},{16,8},{24,16},{32,56},{40,32},{48,40},{56,48},{64,88... | collective-permute-start | bytes 1572872 | tf_op jit(solution)/shard_map/ppermute | solution.py:39
  147.4 3.0 %collective-permute-start.22 = (bf16[1024,256]{1,0:T(8,128)(2,1)S(1)}, bf16[1024,256]{1,0:T(8,128)(2,1)S(1)}, u32[]{:S(2)}, u32[]{:S(2)}) collective-permute-start(bf16[1024,256]{1,0:T(8,128)(2,1)S(1)} %get-tuple-element.87), channel_id=1, source_target_pairs={{0,32},{8,40},{16,48},{24,56},{32,64},{40,72},{48,80},{56,88},{64,... | collective-permute-start | bytes 1572872 | tf_op jit(solution)/shard_map/ppermute | solution.py:39
  150.3 5.4 %collective-permute-done.20.refs_3_ = bf16[1024,256]{1,0:T(8,128)(2,1)S(1)} collective-permute-done((bf16[1024,256]{1,0:T(8,128)(2,1)S(1)}, bf16[1024,256]{1,0:T(8,128)(2,1)S(1)}, u32[]{:S(2)}, u32[]{:S(2)}) %collective-permute-start.20) | collective-permute-done | bytes 524320 | tf_op jit(solution)/shard_map/ppermute | solution.py:39
  155.7 1.7 collective-permute-done.22.refs_8_
  157.3 3.4 %collective-permute-done.23.refs_9_ = bf16[1024,256]{1,0:T(8,128)(2,1)S(1)} collective-permute-done((bf16[1024,256]{1,0:T(8,128)(2,1)S(1)}, bf16[1024,256]{1,0:T(8,128)(2,1)S(1)}, u32[]{:S(2)}, u32[]{:S(2)}) %collective-permute-start.23) | collective-permute-done | bytes 524320 | tf_op jit(solution)/shard_map/ppermute | solution.py:39
  160.8 7.6 %project_out_3.1 = (bf16[1024,256]{1,0:T(8,128)(2,1)S(1)}, bf16[1024,256]{1,0:T(8,128)(2,1)S(1)}, bf16[1024,256]{1,0:T(8,128)(2,1)S(1)}) custom-call(s32[3]{0:T(128)S(1)} %pad_add_fusion.1.place_ref, f32[1024,8]{1,0:T(8,128)S(1)} %broadcast_multiply_fusion.gates_ref, bf16[8,1024,256]{2,1,0:T(8,128)(2,1)S(1)} %attention.1.lhs_ref, ...), custom_call_target="tpu_custom_call" | custom-call | flops 7590000128 | bytes 1048576 | tf_op jit(solution)/shard_map/project_out_3/pallas_call | solution.py:331
  168.5 5.1 %project_out_2.2 = bf16[2,1024,256]{2,1,0:T(8,128)(2,1)S(1)} custom-call(s32[3]{0:T(128)S(1)} %pad_add_fusion.1.place_ref, f32[1024,8]{1,0:T(8,128)S(1)} %broadcast_multiply_fusion.gates_ref, bf16[8,1024,256]{2,1,0:T(8,128)(2,1)S(1)} %attention.1.lhs_ref, bf16[2048,256]{1,0:T(8,128)(2,1)S(1)} %pad_maximum_fusion.refs_0_, ...), custom_call_target="tpu_custom_call" | custom-call | flops 5059999744 | bytes 1048576 | tf_op jit(solution)/shard_map/project_out_2/pallas_call | solution.py:331
  174.3 1.2 collective-permute-start.26
  175.6 2.1 %collective-permute-start.27 = (bf16[512,256]{1,0:T(8,128)(2,1)S(1)}, bf16[512,256]{1,0:T(8,128)(2,1)S(1)}, u32[]{:S(2)}, u32[]{:S(2)}) collective-permute-start(bf16[512,256]{1,0:T(8,128)(2,1)S(1)} %get-tuple-element.94), channel_id=1, source_target_pairs={{0,6},{1,7},{2,0},{3,1},{4,2},{5,3},{6,4},{7,5},{8,14},{9,15},{10,... | collective-permute-start | bytes 786440 | tf_op jit(solution)/shard_map/ppermute | solution.py:423
  177.6 5.0 %project_out_2.3.mine_ref = bf16[2,1024,256]{2,1,0:T(8,128)(2,1)S(1)} custom-call(s32[3]{0:T(128)S(1)} %pad_add_fusion.1.place_ref, f32[1024,8]{1,0:T(8,128)S(1)} %broadcast_multiply_fusion.gates_ref, bf16[8,1024,256]{2,1,0:T(8,128)(2,1)S(1)} %attention.1.lhs_ref, bf16[2048,256]{1,0:T(8,128)(2,1)S(1)} %pad_maximum_fusion.refs_0_, ...), custom_call_target="tpu_custom_call" | custom-call | flops 5059999744 | bytes 1048576 | tf_op jit(solution)/shard_map/project_out_2/pallas_call | solution.py:331
  182.7 1.2 collective-permute-done.27.high_ref
  184.6 3.0 %collective-permute-start.30 = (bf16[1024,256]{1,0:T(8,128)(2,1)S(1)}, bf16[1024,256]{1,0:T(8,128)(2,1)S(1)}, u32[]{:S(2)}, u32[]{:S(2)}) collective-permute-start(bf16[1024,256]{1,0:T(8,128)(2,1)S(1)} %get-tuple-element.98), channel_id=1, source_target_pairs={{0,6},{1,7},{2,0},{3,1},{4,2},{5,3},{6,4},{7,5},{8,14},{9,15},{10,... | collective-permute-start | bytes 1572872 | tf_op jit(solution)/shard_map/ppermute | solution.py:423
  187.6 2.9 %project_out_1.1 = bf16[1,1024,256]{2,1,0:T(8,128)(2,1)S(1)} custom-call(s32[3]{0:T(128)S(1)} %pad_add_fusion.1.place_ref, f32[1024,8]{1,0:T(8,128)S(1)} %broadcast_multiply_fusion.gates_ref, bf16[8,1024,256]{2,1,0:T(8,128)(2,1)S(1)} %attention.1.lhs_ref, bf16[2048,256]{1,0:T(8,128)(2,1)S(1)} %pad_maximum_fusion.refs_0_, ...), custom_call_target="tpu_custom_call" | custom-call | flops 2529999872 | bytes 1048576 | tf_op jit(solution)/shard_map/project_out_1/pallas_call | solution.py:331
  190.5 7.8 %collective-permute-done.30 = bf16[1024,256]{1,0:T(8,128)(2,1)S(1)} collective-permute-done((bf16[1024,256]{1,0:T(8,128)(2,1)S(1)}, bf16[1024,256]{1,0:T(8,128)(2,1)S(1)}, u32[]{:S(2)}, u32[]{:S(2)}) %collective-permute-start.30) | collective-permute-done | bytes 524320 | tf_op jit(solution)/shard_map/ppermute | solution.py:423
  198.3 3.4 %collective-permute-done.29 = bf16[1024,256]{1,0:T(8,128)(2,1)S(1)} collective-permute-done((bf16[1024,256]{1,0:T(8,128)(2,1)S(1)}, bf16[1024,256]{1,0:T(8,128)(2,1)S(1)}, u32[]{:S(2)}, u32[]{:S(2)}) %collective-permute-start.29) | collective-permute-done | bytes 524320 | tf_op jit(solution)/shard_map/ppermute | solution.py:423
  201.7 1.1 fusion.2
  (116 shorter events, 7.7 us)
Async XLA Ops:
  0.0 14.5 %copy-start = (bf16[4,2048,16]{1,2,0:T(8,128)(2,1)S(1)}, bf16[4,2048,16]{1,2,0:T(8,128)(2,1)}, u32[]{:S(2)}) copy-start(bf16[4,2048,16]{1,2,0:T(8,128)(2,1)} %param.25) | copy-start | bytes 786436
  0.0 2.1 %copy-start.12 = (bf16[128,8,256]{2,1,0:T(8,128)(2,1)S(1)}, bf16[128,8,256]{2,1,0:T(8,128)(2,1)}, u32[]{:S(2)}) copy-start(bf16[128,8,256]{2,1,0:T(8,128)(2,1)} %param.23) | copy-start | bytes 1572868
  2.1 2.4 %copy-start.8 = (bf16[64,8,2,128]{3,1,2,0:T(8,128)(2,1)}, bf16[64,8,2,128]{3,1,2,0:T(8,128)(2,1)S(1)}, u32[]{:S(2)}) copy-start(bf16[64,8,2,128]{3,1,2,0:T(8,128)(2,1)S(1)} %copy.43) | copy-start | bytes 786436
  2.1 1.1 copy-start.15
  2.3 1.6 copy-start.17
  4.5 9.2 %copy-start.21 = (s32[64]{0:T(128)S(1)}, s32[64]{0:T(128)}, u32[]{:S(2)}) copy-start(s32[64]{0:T(128)} %param.18) | copy-start | bytes 772
  5.4 23.8 %collective-permute-start.1 = (bf16[1216,256]{1,0:T(8,128)(2,1)}, bf16[1216,256]{1,0:T(8,128)(2,1)S(1)}, u32[]{:S(2)}, u32[]{:S(2)}) collective-permute-start(bf16[1216,256]{1,0:T(8,128)(2,1)} %pad_maximum_fusion.2), channel_id=1, source_target_pairs={{0,96},{8,104},{16,112},{24,120},{32,0},{40,8},{48,16},{56,24},{64... | collective-permute-start | bytes 1867784 | tf_op jit(solution)/shard_map/ppermute | solution.py:39
  6.2 23.0 %collective-permute-start = (bf16[1216,256]{1,0:T(8,128)(2,1)}, bf16[1216,256]{1,0:T(8,128)(2,1)S(1)}, u32[]{:S(2)}, u32[]{:S(2)}) collective-permute-start(bf16[1216,256]{1,0:T(8,128)(2,1)} %pad_maximum_fusion.2), channel_id=1, source_target_pairs={{0,32},{8,40},{16,48},{24,56},{32,64},{40,72},{48,80},{56,88},{64,... | collective-permute-start | bytes 1867784 | tf_op jit(solution)/shard_map/ppermute | solution.py:39
  8.7 1.0 copy-start.10
  9.7 32.9 %collective-permute-start.3 = (bf16[1216,256]{1,0:T(8,128)(2,1)}, bf16[1216,256]{1,0:T(8,128)(2,1)S(1)}, u32[]{:S(2)}, u32[]{:S(2)}) collective-permute-start(bf16[1216,256]{1,0:T(8,128)(2,1)} %pad_maximum_fusion.3), channel_id=1, source_target_pairs={{0,24},{8,0},{16,8},{24,16},{32,56},{40,32},{48,40},{56,48},{64,88... | collective-permute-start | bytes 1867784 | tf_op jit(solution)/shard_map/ppermute | solution.py:39
  13.7 33.1 %collective-permute-start.2 = (bf16[1216,256]{1,0:T(8,128)(2,1)}, bf16[1216,256]{1,0:T(8,128)(2,1)S(1)}, u32[]{:S(2)}, u32[]{:S(2)}) collective-permute-start(bf16[1216,256]{1,0:T(8,128)(2,1)} %pad_maximum_fusion.3), channel_id=1, source_target_pairs={{0,8},{8,16},{16,24},{24,0},{32,40},{40,48},{48,56},{56,32},{64,72... | collective-permute-start | bytes 1867784 | tf_op jit(solution)/shard_map/ppermute | solution.py:39
  17.4 7.5 %copy-start.22 = (s32[64]{0:T(128)S(1)}, s32[64]{0:T(128)}, u32[]{:S(2)}) copy-start(s32[64]{0:T(128)} %param.20) | copy-start | bytes 772
  17.4 7.5 %copy-start.23 = (s32[4]{0:T(128)S(1)}, s32[4]{0:T(128)}, u32[]{:S(2)}) copy-start(s32[4]{0:T(128)} %param.19) | copy-start | bytes 52
  17.4 7.7 %copy-start.19 = (s32[4]{0:T(128)S(1)}, s32[4]{0:T(128)}, u32[]{:S(2)}) copy-start(s32[4]{0:T(128)} %param.17) | copy-start | bytes 52
  17.4 8.4 %copy-start.18 = (bf16[2048,8]{0,1:T(8,128)(2,1)S(1)}, bf16[2048,8]{0,1:T(8,128)(2,1)}, u32[]{:S(2)}) copy-start(bf16[2048,8]{0,1:T(8,128)(2,1)} %param.21) | copy-start | bytes 98308
  17.5 59.1 %all-to-all-start = ((bf16[16,96,512]{2,1,0:T(8,128)(2,1)}), bf16[16,96,512]{2,1,0:T(8,128)(2,1)}, u32[]{:S(2)}, u32[]{:S(2)}) async-start(bf16[16,96,512]{2,1,0:T(8,128)(2,1)} %pack.1), calls=%async_computation | async-start | bytes 3145728 | tf_op jit(solution)/shard_map/all_to_all | solution.py:487
  29.2 45.5 %copy-start.2 = (bf16[1216,256]{1,0:T(8,128)(2,1)}, bf16[1216,256]{1,0:T(8,128)(2,1)S(1)}, u32[]{:S(2)}) copy-start(bf16[1216,256]{1,0:T(8,128)(2,1)S(1)} %collective-permute-done.1.refs_1_) | copy-start | bytes 1867780
  29.2 45.5 %copy-start.3 = (bf16[1216,256]{1,0:T(8,128)(2,1)}, bf16[1216,256]{1,0:T(8,128)(2,1)S(1)}, u32[]{:S(2)}) copy-start(bf16[1216,256]{1,0:T(8,128)(2,1)S(1)} %collective-permute-done.refs_0_) | copy-start | bytes 1867780
  42.6 32.2 %copy-start.4 = (bf16[1216,256]{1,0:T(8,128)(2,1)}, bf16[1216,256]{1,0:T(8,128)(2,1)S(1)}, u32[]{:S(2)}) copy-start(bf16[1216,256]{1,0:T(8,128)(2,1)S(1)} %collective-permute-done.3.refs_3_) | copy-start | bytes 1867780
  46.8 1.7 copy-start.5
  48.5 8.2 %collective-permute-start.8 = (bf16[608,256]{1,0:T(8,128)(2,1)S(1)}, bf16[608,256]{1,0:T(8,128)(2,1)S(1)}, u32[]{:S(2)}, u32[]{:S(2)}) collective-permute-start(bf16[608,256]{1,0:T(8,128)(2,1)S(1)} %get-tuple-element.59), channel_id=1, source_target_pairs={{0,8},{8,16},{16,24},{24,0},{32,40},{40,48},{48,56},{56,32},{64,72... | collective-permute-start | bytes 933896 | tf_op jit(solution)/shard_map/ppermute | solution.py:39
  48.6 22.4 %copy-start.20 = (s32[4]{0:T(128)S(1)}, s32[4]{0:T(128)}, u32[]{:S(2)}) copy-start(s32[4]{0:T(128)} %param.16) | copy-start | bytes 52
  48.6 22.5 %copy-start.16 = (s32[1024,2]{0,1:T(2,128)S(1)}, s32[1024,2]{0,1:T(2,128)}, u32[]{:S(2)}) copy-start(s32[1024,2]{0,1:T(2,128)} %param.15) | copy-start | bytes 24580
  49.4 16.5 %collective-permute-start.4 = (bf16[608,256]{1,0:T(8,128)(2,1)S(1)}, bf16[608,256]{1,0:T(8,128)(2,1)S(1)}, u32[]{:S(2)}, u32[]{:S(2)}) collective-permute-start(bf16[608,256]{1,0:T(8,128)(2,1)S(1)} %get-tuple-element.57), channel_id=1, source_target_pairs={{0,32},{8,40},{16,48},{24,56},{32,64},{40,72},{48,80},{56,88},{64,... | collective-permute-start | bytes 933896 | tf_op jit(solution)/shard_map/ppermute | solution.py:39
  49.4 17.2 %collective-permute-start.5 = (bf16[608,256]{1,0:T(8,128)(2,1)S(1)}, bf16[608,256]{1,0:T(8,128)(2,1)S(1)}, u32[]{:S(2)}, u32[]{:S(2)}) collective-permute-start(bf16[608,256]{1,0:T(8,128)(2,1)S(1)} %get-tuple-element.58), channel_id=1, source_target_pairs={{0,96},{8,104},{16,112},{24,120},{32,0},{40,8},{48,16},{56,24},{64... | collective-permute-start | bytes 933896 | tf_op jit(solution)/shard_map/ppermute | solution.py:39
  51.4 10.6 %collective-permute-start.9 = (bf16[608,256]{1,0:T(8,128)(2,1)S(1)}, bf16[608,256]{1,0:T(8,128)(2,1)S(1)}, u32[]{:S(2)}, u32[]{:S(2)}) collective-permute-start(bf16[608,256]{1,0:T(8,128)(2,1)S(1)} %get-tuple-element.60), channel_id=1, source_target_pairs={{0,24},{8,0},{16,8},{24,16},{32,56},{40,32},{48,40},{56,48},{64,88... | collective-permute-start | bytes 933896 | tf_op jit(solution)/shard_map/ppermute | solution.py:39
  62.0 11.5 %copy-start.13 = (bf16[608,256]{1,0:T(8,128)(2,1)}, bf16[608,256]{1,0:T(8,128)(2,1)S(1)}, u32[]{:S(2)}) copy-start(bf16[608,256]{1,0:T(8,128)(2,1)S(1)} %collective-permute-done.9) | copy-start | bytes 933892
  62.6 29.7 %collective-permute-start.11 = (bf16[2816,256]{1,0:T(8,128)(2,1)}, bf16[2816,256]{1,0:T(8,128)(2,1)}, u32[]{:S(2)}, u32[]{:S(2)}) collective-permute-start(bf16[2816,256]{1,0:T(8,128)(2,1)} %slice_dynamic-update-slice_fusion.4.refs_3_), channel_id=1, source_target_pairs={{0,96},{8,104},{16,112},{24,120},{32,0},{40,8},{48,16},{56,24},{64... | collective-permute-start | bytes 4325384 | tf_op jit(solution)/shard_map/ppermute | solution.py:39
  62.9 29.4 %collective-permute-start.10 = (bf16[2816,256]{1,0:T(8,128)(2,1)}, bf16[2816,256]{1,0:T(8,128)(2,1)}, u32[]{:S(2)}, u32[]{:S(2)}) collective-permute-start(bf16[2816,256]{1,0:T(8,128)(2,1)} %slice_dynamic-update-slice_fusion.4.refs_3_), channel_id=1, source_target_pairs={{0,32},{8,40},{16,48},{24,56},{32,64},{40,72},{48,80},{56,88},{64,... | collective-permute-start | bytes 4325384 | tf_op jit(solution)/shard_map/ppermute | solution.py:39
  66.6 8.1 %copy-start.11 = (bf16[608,256]{1,0:T(8,128)(2,1)}, bf16[608,256]{1,0:T(8,128)(2,1)S(1)}, u32[]{:S(2)}) copy-start(bf16[608,256]{1,0:T(8,128)(2,1)S(1)} %collective-permute-done.5) | copy-start | bytes 933892
  67.3 25.1 %collective-permute-start.7 = (bf16[2816,256]{1,0:T(8,128)(2,1)}, bf16[2816,256]{1,0:T(8,128)(2,1)}, u32[]{:S(2)}, u32[]{:S(2)}) collective-permute-start(bf16[2816,256]{1,0:T(8,128)(2,1)} %slice_dynamic-update-slice_fusion.5.refs_0_), channel_id=1, source_target_pairs={{0,24},{8,0},{16,8},{24,16},{32,56},{40,32},{48,40},{56,48},{64,88... | collective-permute-start | bytes 4325384 | tf_op jit(solution)/shard_map/ppermute | solution.py:39
  71.0 21.4 %collective-permute-start.6 = (bf16[2816,256]{1,0:T(8,128)(2,1)}, bf16[2816,256]{1,0:T(8,128)(2,1)}, u32[]{:S(2)}, u32[]{:S(2)}) collective-permute-start(bf16[2816,256]{1,0:T(8,128)(2,1)} %slice_dynamic-update-slice_fusion.5.refs_0_), channel_id=1, source_target_pairs={{0,8},{8,16},{16,24},{24,0},{32,40},{40,48},{48,56},{56,32},{64,72... | collective-permute-start | bytes 4325384 | tf_op jit(solution)/shard_map/ppermute | solution.py:39
  74.7 1.0 copy-start.14
  74.7 1.7 slice-start.1
  74.7 1.7 copy-start.9
  74.7 1.7 slice-start.4
  74.8 1.6 slice-start
  76.5 8.2 %slice-start.2 = ((bf16[1216,256]{1,0:T(8,128)(2,1)}), bf16[512,256]{1,0:T(8,128)(2,1)S(1)}, s32[]{:S(2)}) async-start(bf16[1216,256]{1,0:T(8,128)(2,1)} %copy-done.4), calls=%async_computation.4 | async-start | bytes 524288 | tf_op jit(solution)/shard_map/slice | solution.py:512
  76.5 8.2 %slice-start.3 = ((bf16[1216,256]{1,0:T(8,128)(2,1)}), bf16[512,256]{1,0:T(8,128)(2,1)S(1)}, s32[]{:S(2)}) async-start(bf16[1216,256]{1,0:T(8,128)(2,1)} %copy-done.5), calls=%async_computation.5 | async-start | bytes 524288 | tf_op jit(solution)/shard_map/slice | solution.py:511
  80.2 12.1 %all-to-all-start.1 = ((bf16[8,4,16,256]{3,2,1,0:T(8,128)(2,1)}), bf16[8,4,16,256]{3,2,1,0:T(8,128)(2,1)}, u32[]{:S(2)}, u32[]{:S(2)}) async-start(bf16[8,4,16,256]{3,2,1,0:T(8,128)(2,1)} %broadcast_in_dim.5), calls=%async_computation.1 | async-start | bytes 524288 | tf_op jit(solution)/shard_map/all_to_all | solution.py:529
  85.8 16.0 %copy-start.6 = (s32[1024,2]{1,0:T(8,128)S(1)}, s32[1024,2]{1,0:T(8,128)}, u32[]{:S(2)}) copy-start(s32[1024,2]{1,0:T(8,128)} %copy.34.routes_ref) | copy-start | bytes 24580
  85.8 15.9 %copy-start.7 = (s32[13]{0:T(128)S(1)}, s32[13]{0:T(128)}, u32[]{:S(2)}) copy-start(s32[13]{0:T(128)} %pad_add_fusion.info_ref) | copy-start | bytes 160
  92.3 9.4 %copy-start.1 = (bf16[1024,2048]{1,0:T(8,128)(2,1)S(1)}, bf16[1024,2048]{1,0:T(8,128)(2,1)}, u32[]{:S(2)}) copy-start(bf16[1024,2048]{1,0:T(8,128)(2,1)} %x_ref.3) | copy-start | bytes 12582916
  96.3 19.9 %collective-permute-start.12 = (bf16[1408,256]{1,0:T(8,128)(2,1)S(1)}, bf16[1408,256]{1,0:T(8,128)(2,1)S(1)}, u32[]{:S(2)}, u32[]{:S(2)}) collective-permute-start(bf16[1408,256]{1,0:T(8,128)(2,1)S(1)} %get-tuple-element.67), channel_id=1, source_target_pairs={{0,8},{8,16},{16,24},{24,0},{32,40},{40,48},{48,56},{56,32},{64,72... | collective-permute-start | bytes 2162696 | tf_op jit(solution)/shard_map/ppermute | solution.py:39
  96.4 19.8 %collective-permute-start.13 = (bf16[1408,256]{1,0:T(8,128)(2,1)S(1)}, bf16[1408,256]{1,0:T(8,128)(2,1)S(1)}, u32[]{:S(2)}, u32[]{:S(2)}) collective-permute-start(bf16[1408,256]{1,0:T(8,128)(2,1)S(1)} %get-tuple-element.68), channel_id=1, source_target_pairs={{0,24},{8,0},{16,8},{24,16},{32,56},{40,32},{48,40},{56,48},{64,88... | collective-permute-start | bytes 2162696 | tf_op jit(solution)/shard_map/ppermute | solution.py:39
  99.7 17.2 %collective-permute-start.14 = (bf16[1408,256]{1,0:T(8,128)(2,1)S(1)}, bf16[1408,256]{1,0:T(8,128)(2,1)S(1)}, u32[]{:S(2)}, u32[]{:S(2)}) collective-permute-start(bf16[1408,256]{1,0:T(8,128)(2,1)S(1)} %get-tuple-element.69), channel_id=1, source_target_pairs={{0,32},{8,40},{16,48},{24,56},{32,64},{40,72},{48,80},{56,88},{64,... | collective-permute-start | bytes 2162696 | tf_op jit(solution)/shard_map/ppermute | solution.py:39
  100.0 18.2 %collective-permute-start.15 = (bf16[1408,256]{1,0:T(8,128)(2,1)S(1)}, bf16[1408,256]{1,0:T(8,128)(2,1)S(1)}, u32[]{:S(2)}, u32[]{:S(2)}) collective-permute-start(bf16[1408,256]{1,0:T(8,128)(2,1)S(1)} %get-tuple-element.70), channel_id=1, source_target_pairs={{0,96},{8,104},{16,112},{24,120},{32,0},{40,8},{48,16},{56,24},{64... | collective-permute-start | bytes 2162696 | tf_op jit(solution)/shard_map/ppermute | solution.py:39
  118.2 24.6 %collective-permute-start.17 = (bf16[2048,256]{1,0:T(8,128)(2,1)S(1)}, bf16[2048,256]{1,0:T(8,128)(2,1)S(1)}, u32[]{:S(2)}, u32[]{:S(2)}) collective-permute-start(bf16[2048,256]{1,0:T(8,128)(2,1)S(1)} %pad_maximum_fusion.refs_0_), channel_id=1, source_target_pairs={{0,24},{8,0},{16,8},{24,16},{32,56},{40,32},{48,40},{56,48},{64,88... | collective-permute-start | bytes 3145736 | tf_op jit(solution)/shard_map/ppermute | solution.py:39
  119.8 23.7 %collective-permute-start.16 = (bf16[2048,256]{1,0:T(8,128)(2,1)S(1)}, bf16[2048,256]{1,0:T(8,128)(2,1)S(1)}, u32[]{:S(2)}, u32[]{:S(2)}) collective-permute-start(bf16[2048,256]{1,0:T(8,128)(2,1)S(1)} %pad_maximum_fusion.refs_0_), channel_id=1, source_target_pairs={{0,8},{8,16},{16,24},{24,0},{32,40},{40,48},{48,56},{56,32},{64,72... | collective-permute-start | bytes 3145736 | tf_op jit(solution)/shard_map/ppermute | solution.py:39
  120.2 23.7 %collective-permute-start.19 = (bf16[2048,256]{1,0:T(8,128)(2,1)S(1)}, bf16[2048,256]{1,0:T(8,128)(2,1)S(1)}, u32[]{:S(2)}, u32[]{:S(2)}) collective-permute-start(bf16[2048,256]{1,0:T(8,128)(2,1)S(1)} %pad_maximum_fusion.1.refs_5_), channel_id=1, source_target_pairs={{0,96},{8,104},{16,112},{24,120},{32,0},{40,8},{48,16},{56,24},{64... | collective-permute-start | bytes 3145736 | tf_op jit(solution)/shard_map/ppermute | solution.py:39
  120.7 23.2 %collective-permute-start.18 = (bf16[2048,256]{1,0:T(8,128)(2,1)S(1)}, bf16[2048,256]{1,0:T(8,128)(2,1)S(1)}, u32[]{:S(2)}, u32[]{:S(2)}) collective-permute-start(bf16[2048,256]{1,0:T(8,128)(2,1)S(1)} %pad_maximum_fusion.1.refs_5_), channel_id=1, source_target_pairs={{0,32},{8,40},{16,48},{24,56},{32,64},{40,72},{48,80},{56,88},{64,... | collective-permute-start | bytes 3145736 | tf_op jit(solution)/shard_map/ppermute | solution.py:39
  144.1 11.6 %collective-permute-start.20 = (bf16[1024,256]{1,0:T(8,128)(2,1)S(1)}, bf16[1024,256]{1,0:T(8,128)(2,1)S(1)}, u32[]{:S(2)}, u32[]{:S(2)}) collective-permute-start(bf16[1024,256]{1,0:T(8,128)(2,1)S(1)} %get-tuple-element.85), channel_id=1, source_target_pairs={{0,8},{8,16},{16,24},{24,0},{32,40},{40,48},{48,56},{56,32},{64,72... | collective-permute-start | bytes 1572872 | tf_op jit(solution)/shard_map/ppermute | solution.py:39
  144.4 11.3 %collective-permute-start.21 = (bf16[1024,256]{1,0:T(8,128)(2,1)S(1)}, bf16[1024,256]{1,0:T(8,128)(2,1)S(1)}, u32[]{:S(2)}, u32[]{:S(2)}) collective-permute-start(bf16[1024,256]{1,0:T(8,128)(2,1)S(1)} %get-tuple-element.86), channel_id=1, source_target_pairs={{0,24},{8,0},{16,8},{24,16},{32,56},{40,32},{48,40},{56,48},{64,88... | collective-permute-start | bytes 1572872 | tf_op jit(solution)/shard_map/ppermute | solution.py:39
  147.4 10.0 %collective-permute-start.22 = (bf16[1024,256]{1,0:T(8,128)(2,1)S(1)}, bf16[1024,256]{1,0:T(8,128)(2,1)S(1)}, u32[]{:S(2)}, u32[]{:S(2)}) collective-permute-start(bf16[1024,256]{1,0:T(8,128)(2,1)S(1)} %get-tuple-element.87), channel_id=1, source_target_pairs={{0,32},{8,40},{16,48},{24,56},{32,64},{40,72},{48,80},{56,88},{64,... | collective-permute-start | bytes 1572872 | tf_op jit(solution)/shard_map/ppermute | solution.py:39
  150.3 10.4 %collective-permute-start.23 = (bf16[1024,256]{1,0:T(8,128)(2,1)S(1)}, bf16[1024,256]{1,0:T(8,128)(2,1)S(1)}, u32[]{:S(2)}, u32[]{:S(2)}) collective-permute-start(bf16[1024,256]{1,0:T(8,128)(2,1)S(1)} %get-tuple-element.88), channel_id=1, source_target_pairs={{0,96},{8,104},{16,112},{24,120},{32,0},{40,8},{48,16},{56,24},{64... | collective-permute-start | bytes 1572872 | tf_op jit(solution)/shard_map/ppermute | solution.py:39
  168.4 5.8 %collective-permute-start.24 = (bf16[1024,256]{1,0:T(8,128)(2,1)S(1)}, bf16[1024,256]{1,0:T(8,128)(2,1)S(1)}, u32[]{:S(2)}, u32[]{:S(2)}) collective-permute-start(bf16[1024,256]{1,0:T(8,128)(2,1)S(1)} %get-tuple-element.91), channel_id=1, source_target_pairs={{0,1},{1,0},{2,3},{3,2},{4,5},{5,4},{6,7},{7,6},{8,9},{9,8},{10,11... | collective-permute-start | bytes 1572872 | tf_op jit(solution)/shard_map/ppermute | solution.py:422
  173.6 10.7 %collective-permute-start.25 = (bf16[2,1024,256]{2,1,0:T(8,128)(2,1)S(1)}, bf16[2,1024,256]{2,1,0:T(8,128)(2,1)S(1)}, u32[]{:S(2)}, u32[]{:S(2)}) collective-permute-start(bf16[2,1024,256]{2,1,0:T(8,128)(2,1)S(1)} %project_out_2.2), channel_id=1, source_target_pairs={{0,1},{1,0},{2,3},{3,2},{4,5},{5,4},{6,7},{7,6},{8,9},{9,8},{10,11... | collective-permute-start | bytes 3145736 | tf_op jit(solution)/shard_map/ppermute | solution.py:422
  174.1 16.4 %collective-permute-start.28 = (bf16[1024,256]{1,0:T(8,128)(2,1)S(1)}, bf16[1024,256]{1,0:T(8,128)(2,1)S(1)}, u32[]{:S(2)}, u32[]{:S(2)}) collective-permute-start(bf16[1024,256]{1,0:T(8,128)(2,1)S(1)} %get-tuple-element.97), channel_id=1, source_target_pairs={{0,1},{1,0},{2,3},{3,2},{4,5},{5,4},{6,7},{7,6},{8,9},{9,8},{10,11... | collective-permute-start | bytes 1572872 | tf_op jit(solution)/shard_map/ppermute | solution.py:422
  174.3 9.9 %collective-permute-start.26 = (bf16[512,256]{1,0:T(8,128)(2,1)S(1)}, bf16[512,256]{1,0:T(8,128)(2,1)S(1)}, u32[]{:S(2)}, u32[]{:S(2)}) collective-permute-start(bf16[512,256]{1,0:T(8,128)(2,1)S(1)} %get-tuple-element.92), channel_id=1, source_target_pairs={{0,2},{1,3},{2,4},{3,5},{4,6},{5,7},{6,0},{7,1},{8,10},{9,11},{10,... | collective-permute-start | bytes 786440 | tf_op jit(solution)/shard_map/ppermute | solution.py:423
  175.6 8.4 %collective-permute-start.27 = (bf16[512,256]{1,0:T(8,128)(2,1)S(1)}, bf16[512,256]{1,0:T(8,128)(2,1)S(1)}, u32[]{:S(2)}, u32[]{:S(2)}) collective-permute-start(bf16[512,256]{1,0:T(8,128)(2,1)S(1)} %get-tuple-element.94), channel_id=1, source_target_pairs={{0,6},{1,7},{2,0},{3,1},{4,2},{5,3},{6,4},{7,5},{8,14},{9,15},{10,... | collective-permute-start | bytes 786440 | tf_op jit(solution)/shard_map/ppermute | solution.py:423
  184.6 13.7 %collective-permute-start.30 = (bf16[1024,256]{1,0:T(8,128)(2,1)S(1)}, bf16[1024,256]{1,0:T(8,128)(2,1)S(1)}, u32[]{:S(2)}, u32[]{:S(2)}) collective-permute-start(bf16[1024,256]{1,0:T(8,128)(2,1)S(1)} %get-tuple-element.98), channel_id=1, source_target_pairs={{0,6},{1,7},{2,0},{3,1},{4,2},{5,3},{6,4},{7,5},{8,14},{9,15},{10,... | collective-permute-start | bytes 1572872 | tf_op jit(solution)/shard_map/ppermute | solution.py:423
  187.6 14.1 %collective-permute-start.29 = (bf16[1024,256]{1,0:T(8,128)(2,1)S(1)}, bf16[1024,256]{1,0:T(8,128)(2,1)S(1)}, u32[]{:S(2)}, u32[]{:S(2)}) collective-permute-start(bf16[1024,256]{1,0:T(8,128)(2,1)S(1)} %get-tuple-element.95), channel_id=1, source_target_pairs={{0,2},{1,3},{2,4},{3,5},{4,6},{5,7},{6,0},{7,1},{8,10},{9,11},{10,... | collective-permute-start | bytes 1572872 | tf_op jit(solution)/shard_map/ppermute | solution.py:423
